TPU v7x, 256 devices: a whole 4x4x8 slice. The times are simulated.
256 devices in a mesh: tm: 16 (over z, core), mp: 8 (over y, x_hi), batch: 2 (over x_lo).
Axes of the slice: x: 4 (x_hi: 2, x_lo: 2; x = x_hi * 2 + x_lo), y: 4, z: 8, core: 2. Of those that a mesh axis runs over, the one named last changes fastest.
Arguments:
- frames: bfloat16 [32768, 1024], P(('batch', 'tm')), parts along dimension 0, may hold values from -40 to 40
- norm_gain: float32 [1024], replicated, may hold values from 0.5 to 1.5
- qkv_weight: bfloat16 [3, 1024, 1024], P(None, None, 'mp'), may hold values from -2 to 2
- out_weight: bfloat16 [1024, 1024], P('mp'), may hold values from -0.1875 to 0.1875
- cotangent: bfloat16 [32768, 1024], P(('batch', 'tm')), parts along dimension 0, may hold values from -6 to 6
- pad_mask: int32 [32768], P('batch'), parts along dimension 0, may hold values from 0 to 1, as said below
- utt_lengths: int32 [16], P('batch'), parts along dimension 0, may hold values from 1 to 4096, 16384 in all
Outputs:
- frame_grad: bfloat16 [32768, 1024], P(('batch', 'tm'), 'mp'), parts along dimension 0
- qkv_grad: float32 [6, 1024, 1024], P('batch', 'tm', 'mp'), parts along dimension 0
- out_grad: float32 [2048, 1024], P(('batch', 'mp'), 'tm'), parts along dimension 0
There are 2 independent parts, one for each index of `batch`. A program takes and returns all parts, laid end to end along the dimension named above; an argument that names none is the same for every part. Nothing has to cross between parts.
Inputs may be any that keep to these rules, and one draw needn't show every extreme that they name: `pad_mask`: in each aligned block of 256 frames, the padding frames form the tail of the block, fewer than 128 of them. `utt_lengths`: 8 lengths that sum to 16384; the largest is exactly 4096.
All inputs are finite; a program needn't handle non-finite values.
Results may differ from a plain program's by a relative error of at most 0.012.
The roundings to bfloat16 on the way count: a program that leaves them out, or rounds other values in their place, can miss the bound.
Values may be sent and summed in bfloat16 or wider, within the bound.
No kernel may reach another device: no remote copies, remote signals or barrier semaphores. Data moves between devices by JAX's collectives and lax.ppermute only.
A program may use at most 64 MiB of HBM per device.

v0:
```python
import jax
import jax.numpy as jnp
from jax import lax
from jax.sharding import PartitionSpec as P

HS = 128
CH = 32


EPSILON = 1e-05


def with_halo(block, sides, width):
    for axis, dim in sides:
        count = lax.axis_size(axis)
        forward = [(i, i + 1) for i in range(count - 1)]
        backward = [(target, source) for source, target in forward]
        low = lax.ppermute(
            lax.slice_in_dim(block, block.shape[dim] - width, None, axis=dim), axis, forward
        )
        high = lax.ppermute(lax.slice_in_dim(block, 0, width, axis=dim), axis, backward)
        block = jnp.concatenate([low, block, high], axis=dim)
    return block


def cut_along(x, dim, count):
    dims = x.shape
    pieces = x.reshape(*dims[:dim], count, dims[dim] // count, *dims[dim + 1 :])
    return jnp.moveaxis(pieces, dim, 0)


def sent_and_summed(x, axis, dim):
    pieces = cut_along(x, dim, lax.axis_size(axis))
    arrived = lax.all_to_all(pieces, axis, split_axis=0, concat_axis=0, tiled=True)
    return arrived.astype(jnp.float32).sum(axis=0)


def layer_norm(frames, norm_gain):
    values = frames.astype(jnp.float32)
    center = values - jnp.mean(values, axis=-1, keepdims=True)
    inverse = lax.rsqrt(jnp.mean(center * center, axis=-1, keepdims=True) + EPSILON)
    normal_form = center * inverse
    return (normal_form, inverse, (normal_form * norm_gain).astype(jnp.bfloat16))


def norm_backward(incoming, normal_form, inverse, norm_gain):
    scaled = incoming * norm_gain
    mean_grad = jnp.mean(scaled, axis=-1, keepdims=True)
    mean_proj = jnp.mean(scaled * normal_form, axis=-1, keepdims=True)
    return inverse * (scaled - mean_grad - normal_form * mean_proj)


def windows(block_rows):
    block_count = block_rows.shape[0] - 2
    return jnp.concatenate(
        [block_rows[:block_count], block_rows[1 : block_count + 1], block_rows[2:]], axis=1
    )


def fold_keys(window):
    block_width = window.shape[1] // 3
    trailing = [(0, 0)] * (window.ndim - 1)
    pieces = [
        jnp.pad(
            window[:, offset * block_width : (offset + 1) * block_width],
            [(offset, 2 - offset)] + trailing,
        )
        for offset in range(3)
    ]
    return pieces[0] + pieces[1] + pieces[2]


def permitted(query_start, query_count, key_start, key_count, pad_mask, utt_lengths):
    utt_ends = jnp.cumsum(utt_lengths)
    query_pos = query_start + jnp.arange(query_count, dtype=jnp.int32)
    key_pos = key_start + jnp.arange(key_count, dtype=jnp.int32)

    def segment(positions):
        return jnp.sum((utt_ends[None, :] <= positions[:, None]).astype(jnp.int32), axis=1)

    padded = jnp.pad(pad_mask, 2 * CH)
    live_keys = lax.dynamic_slice(
        padded, (jnp.asarray(key_start + 2 * CH, jnp.int32),), (key_count,)
    )
    query_cells = query_pos.reshape(-1, CH)
    query_seg = segment(query_pos).reshape(-1, CH)
    key_cells = windows(key_pos.reshape(-1, CH))
    key_seg = windows(segment(key_pos).reshape(-1, CH))
    key_live = windows(live_keys.reshape(-1, CH))
    same_utt = query_seg[:, :, None] == key_seg[:, None, :]
    return same_utt & (
        (key_live[:, None, :] == 1) | (query_cells[:, :, None] == key_cells[:, None, :])
    )


def attend(queries, grad_rows, key_blocks, value_blocks, allowed):
    score_scale = HS ** (-0.5)
    key_win = windows(key_blocks)
    value_win = windows(value_blocks)
    scores = (
        jnp.einsum("cihd,cjhd->chij", queries, key_win, preferred_element_type=jnp.float32)
        * score_scale
    )
    scores = jnp.where(allowed[:, None], scores, -1e30)
    row_max = jnp.max(scores, axis=-1, keepdims=True)
    weights = jnp.exp(scores - row_max)
    attn_probs = weights / jnp.sum(weights, axis=-1, keepdims=True)
    rounded = attn_probs.astype(jnp.bfloat16)
    mixed_out = jnp.einsum(
        "chij,cjhd->cihd", rounded, value_win, preferred_element_type=jnp.float32
    ).astype(jnp.bfloat16)
    prob_grad = jnp.einsum(
        "cihd,cjhd->chij", grad_rows, value_win, preferred_element_type=jnp.float32
    )
    centre = jnp.sum(attn_probs * prob_grad, axis=-1, keepdims=True)
    score_grad = (attn_probs * (prob_grad - centre) * score_scale).astype(jnp.bfloat16)
    query_grad = jnp.einsum(
        "chij,cjhd->cihd", score_grad, key_win, preferred_element_type=jnp.float32
    )
    key_grad = fold_keys(
        jnp.einsum("chij,cihd->cjhd", score_grad, queries, preferred_element_type=jnp.float32)
    )
    value_grad = fold_keys(
        jnp.einsum("chij,cihd->cjhd", rounded, grad_rows, preferred_element_type=jnp.float32)
    )
    return (mixed_out, query_grad, key_grad, value_grad)


def on_device(frames, norm_gain, qkv_weight, out_weight, cotangent, pad_mask, utt_lengths):
    frame_rows = frames.shape[0]
    head_cols = qkv_weight.shape[2]
    heads_here = head_cols // HS
    first_row = lax.axis_index("tm") * frame_rows
    normal_form, inverse, normed = layer_norm(frames, norm_gain)
    projected = jnp.einsum(
        "rd,mdh->mrh", normed, qkv_weight, preferred_element_type=jnp.float32
    ).astype(jnp.bfloat16)
    live_rows = lax.dynamic_slice(pad_mask, (first_row,), (frame_rows,))
    masked = cotangent * live_rows.astype(jnp.bfloat16)[:, None]
    grad_heads = jnp.dot(masked, out_weight.T, preferred_element_type=jnp.float32).astype(
        jnp.bfloat16
    )

    def blocks(tensor):
        return tensor.reshape(-1, CH, heads_here, HS)

    stacked = jnp.concatenate([projected, grad_heads[None]], axis=0)
    extended = with_halo(stacked, (("tm", 1),), 2 * CH)
    query_rim = extended[:, CH:-CH]
    allowed = permitted(
        first_row - CH,
        frame_rows + 2 * CH,
        first_row - 2 * CH,
        frame_rows + 4 * CH,
        pad_mask,
        utt_lengths,
    )
    mixed_ext, query_ext, key_ext, value_ext = attend(
        blocks(query_rim[0]),
        blocks(query_rim[3]),
        blocks(extended[1]),
        blocks(extended[2]),
        allowed,
    )
    mixed_out = mixed_ext[1:-1]
    query_grad = query_ext[1:-1]
    key_grad = key_ext[2:-2]
    value_grad = value_ext[2:-2]
    all_grads = (
        jnp.stack([query_grad, key_grad, value_grad])
        .reshape(3, frame_rows, head_cols)
        .astype(jnp.bfloat16)
    )
    mixed_rows = mixed_out.reshape(frame_rows, head_cols)
    weight_terms = jnp.einsum("rd,mrh->mdh", normed, all_grads, preferred_element_type=jnp.float32)
    out_terms = jnp.einsum("rh,rd->hd", mixed_rows, masked, preferred_element_type=jnp.float32)
    qkv_grad, out_grad = (
        sent_and_summed(weight_terms.astype(jnp.bfloat16), "tm", 1),
        sent_and_summed(out_terms.astype(jnp.bfloat16), "tm", 1),
    )
    incoming = jnp.einsum("mrh,mdh->rd", all_grads, qkv_weight, preferred_element_type=jnp.float32)
    frame_grad = sent_and_summed(
        norm_backward(incoming, normal_form, inverse, norm_gain).astype(jnp.bfloat16), "mp", 1
    )
    return (frame_grad.astype(jnp.bfloat16), qkv_grad, out_grad)


def solution(mesh):
    placed = (
        P(("batch", "tm"), None),
        P(),
        P(None, None, "mp"),
        P("mp", None),
        P(("batch", "tm"), None),
        P("batch"),
        P("batch"),
    )
    return jax.shard_map(
        on_device,
        mesh=mesh,
        in_specs=placed,
        out_specs=(P(("batch", "tm"), "mp"), P("batch", "tm", "mp"), P(("batch", "mp"), "tm")),
        check_vma=False,
    )
```

profile of v0, /device:TPU:1, one launch (start us, length us, event | category | flops | bytes accessed | tf_op | source)
XLA Modules:
  0.0 137.9 jit_solution(8353201642219619879)
XLA Ops:
  0.6 0.0 copy-start
  0.7 2.9 %copy.28 = bf16[1024,1024]{0,1:T(8,128)(2,1)S(1)} copy(bf16[1024,1024]{1,0:T(8,128)(2,1)} %param.7) | data formatting | bytes 4194304 | tf_op args[0]
  3.6 0.0 copy-start.10
  3.6 0.0 copy-start.25
  3.6 0.4 convert_reduce_fusion
  4.0 0.6 fusion.12
  4.7 2.3 %fusion.36 = bf16[1,1024,128]{2,1,0:T(8,128)(2,1)S(1)} fusion(bf16[128,1024]{1,0:T(8,128)(2,1)S(1)} %copy-done.25, bf16[1024,1024]{1,0:T(8,128)(2,1)} %param.11, bf16[1024]{0:T(1024)(128)(2,1)S(1)} %dynamic-slice_convert_fusion), kind=kOutput, calls=%fused_computation.43 | convolution fusion | flops 269615104 | bytes 2623488 | tf_op jit(solution)/shard_map/dot_general | solution.py:140
  7.1 0.0 copy-start.26
  7.1 1.4 %fusion.20 = bf16[3,1024,128]{2,1,0:T(8,128)(2,1)S(1)} fusion(bf16[3,1024,128]{2,1,0:T(8,128)(2,1)S(1)} %copy-done, bf16[1024,1024]{0,1:T(8,128)(2,1)S(1)} %copy.28, f32[1024]{0:T(1024)S(1)} %copy-done.20, f32[1024]{0:T(1024)S(1)} %add_rsqrt_fusion, f32[1024]{0:T(1024)S(1)} %broadcast_multiply_fusion.2), kind=kOutput, calls=%fused_computation.28 | convolution fusion | flops 810942464 | bytes 3682304 | tf_op jit(solution)/shard_map/rd,mdh->mrh/dot_general | solution.py:135
  8.5 0.9 copy-done.1
  9.4 0.6 pad_maximum_fusion.16
  10.0 4.9 %collective-permute-start = (bf16[4,64,128]{2,1,0:T(8,128)(2,1)}, bf16[4,64,128]{2,1,0:T(8,128)(2,1)S(1)}, u32[]{:S(2)}, u32[]{:S(2)}) collective-permute-start(bf16[4,64,128]{2,1,0:T(8,128)(2,1)} %get-tuple-element.25), channel_id=1, source_target_pairs={{0,16},{16,32},{32,48},{48,64},{64,80},{80,96},{96,112},{112,128},... | collective-permute-start | bytes 196616 | tf_op jit(solution)/shard_map/ppermute | solution.py:18
  15.0 1.9 %collective-permute-start.1 = (bf16[4,64,128]{2,1,0:T(8,128)(2,1)S(1)}, bf16[4,64,128]{2,1,0:T(8,128)(2,1)S(1)}, u32[]{:S(2)}, u32[]{:S(2)}) collective-permute-start(bf16[4,64,128]{2,1,0:T(8,128)(2,1)S(1)} %get-tuple-element.26), channel_id=1, source_target_pairs={{16,0},{32,16},{48,32},{64,48},{80,64},{96,80},{112,96},{128,112},... | collective-permute-start | bytes 196616 | tf_op jit(solution)/shard_map/ppermute | solution.py:21
  16.9 0.6 add_add_fusion.1
  17.5 0.2 reduce-window.8
  17.7 0.1 convert_reduce_fusion.4
  17.8 0.1 convert_reduce_fusion.3
  17.9 0.7 eq.39
  18.6 0.1 fusion.73
  18.7 0.1 slice.198
  18.7 0.1 slice.202
  18.8 0.1 slice.200
  18.9 0.1 pad_dynamic-slice_fusion.1
  19.0 0.1 concatenate.47
  19.0 0.1 concatenate.48
  19.1 0.1 concatenate.49
  19.2 0.7 pad_add_fusion.4
  19.9 0.7 add_compare_fusion
  20.6 0.0 collective-permute-done
  20.6 1.9 %pad_maximum_fusion.8 = (bf16[1,1088,128]{2,1,0:T(8,128)(2,1)S(1)}, bf16[1,1088,128]{2,1,0:T(8,128)(2,1)}, bf16[1,1088,128]{2,1,0:T(8,128)(2,1)S(1)}) fusion(bf16[4,64,128]{2,1,0:T(8,128)(2,1)S(1)} %collective-permute-done, bf16[1,1024,128]{2,1,0:T(8,128)(2,1)S(1)} %fusion.36, bf16[3,1024,128]{2,1,0:T(8,128)(2,1)} %copy-done.1, ...), kind=kLoop, calls=%fused_computation.66 | loop fusion | flops 2506752 | bytes 2015232 | tf_op jit(solution)/shard_map/concatenate | solution.py:22
  22.5 1.1 pad_maximum_fusion.5
  23.6 0.7 copy-done.4
  24.3 1.4 fusion.49
  25.7 2.7 %fusion.74 = (f32[34,32]{1,0:T(8,128)S(1)}, f32[34,32,96]{2,1,0:T(8,128)}) fusion(bf16[34,32,128]{2,1,0:T(8,128)(2,1)} %bitcast.84, bf16[34,32,1,128]{3,1,0,2:T(8,128)(2,1)} %bitcast.88, bf16[34,32,1,128]{3,1,0,2:T(8,128)(2,1)} %bitcast.86, bf16[34,32,1,128]{3,1,0,2:T(8,128)(2,1)} %bitcast.92, s32[34,96]{1,0:T(8,128)S(1)} %copy-done.14, ...), kind=kOutput, calls=%fused_computation.115 | convolution fusion | flops 30081120 | bytes 1574336 | tf_op jit(solution)/shard_map/sub | solution.py:106
  28.3 2.4 %fusion.35 = bf16[34,32,1,128]{3,1,0,2:T(8,128)(2,1)} fusion(bf16[34,32,1,128]{3,1,0,2:T(8,128)(2,1)} %bitcast.97, bf16[34,32,1,128]{3,1,0,2:T(8,128)(2,1)} %bitcast.91, bf16[34,32,1,128]{3,1,0,2:T(8,128)(2,1)} %bitcast.95, f32[34,32,96]{2,1,0:T(8,128)} %get-tuple-element.37, f32[34,32]{1,0:T(8,128)S(1)} %get-tuple-element.36), kind=kOutput, calls=%fused_computation.42 | convolution fusion | flops 29593600 | bytes 1536256 | tf_op jit(solution)/shard_map/chij,cjhd->cihd/dot_general | solution.py:109
  30.7 8.2 %fusion.34 = bf16[34,32,1,128]{3,1,0,2:T(8,128)(2,1)} fusion(f32[34,32,96]{2,1,0:T(8,128)} %fusion.49, bf16[34,32,1,128]{3,1,0,2:T(8,128)(2,1)} %bitcast.89, bf16[34,32,1,128]{3,1,0,2:T(8,128)(2,1)} %bitcast.87, bf16[34,32,1,128]{3,1,0,2:T(8,128)(2,1)} %bitcast.93, f32[34,32,96]{2,1,0:T(8,128)} %get-tuple-element.37, f32[34,32]{1,0:T(8,128)S(1)} %get-tuple-element.36), kind=kOutput, calls=%fused_computation.41 | convolution fusion | flops 30117024 | bytes 1954048 | tf_op jit(solution)/shard_map/chij,cjhd->cihd/dot_general | solution.py:117
  39.0 9.3 %convolution_bitcast_fusion.1 = f32[34,96,1,128]{3,1,0,2:T(8,128)} fusion(bf16[34,32,128]{2,1,0:T(8,128)(2,1)} %bitcast.85, f32[34,32,96]{2,1,0:T(8,128)} %fusion.49, f32[34,32,96]{2,1,0:T(8,128)} %get-tuple-element.37, f32[34,32]{1,0:T(8,128)S(1)} %get-tuple-element.36), kind=kOutput, calls=%fused_computation.24 | convolution fusion | flops 27471008 | bytes 2789632 | tf_op jit(solution)/shard_map/chij,cihd->cjhd/dot_general | solution.py:121
  48.3 3.2 %convolution_bitcast_fusion = f32[34,96,1,128]{3,1,0,2:T(8,128)} fusion(bf16[34,32,128]{2,1,0:T(8,128)(2,1)S(1)} %bitcast.83, f32[34,32,96]{2,1,0:T(8,128)} %get-tuple-element.37, f32[34,32]{1,0:T(8,128)S(1)} %get-tuple-element.36), kind=kOutput, calls=%fused_computation.23 | convolution fusion | flops 26947584 | bytes 2371840 | tf_op jit(solution)/shard_map/chij,cihd->cjhd/dot_general | solution.py:124
  51.5 0.5 fusion.31
  52.1 0.9 copy.34
  52.9 9.9 %all-to-all-start.2 = ((bf16[16,128,64]{1,2,0:T(8,128)(2,1)}), bf16[16,128,64]{1,2,0:T(8,128)(2,1)S(1)}, u32[]{:S(2)}, u32[]{:S(2)}) async-start(bf16[16,128,64]{1,2,0:T(8,128)(2,1)} %bitcast.37), calls=%async_computation.2 | async-start | bytes 524288 | tf_op jit(solution)/shard_map/all_to_all | solution.py:34
  62.8 1.7 %fusion.70 = (f32[34,32,1,128]{3,1,0,2:T(8,128)S(1)}, f32[34,32,1,128]{3,1,0,2:T(8,128)S(1)}, f32[34,32,1,128]{3,1,0,2:T(8,128)S(1)}) fusion(f32[34,96,1,128]{3,1,0,2:T(8,128)} %convolution_bitcast_fusion.1), kind=kLoop, calls=%fused_computation.111 | loop fusion | bytes 3342336 | tf_op jit(solution)/shard_map/slice | solution.py:65
  64.5 0.3 copy-done.3
  64.8 0.1 fusion.71
  64.9 0.0 copy-start.21
  65.0 0.2 fusion.48
  65.1 0.2 fusion.47
  65.3 0.0 copy-start.8
  65.3 0.5 copy-done.7
  65.8 0.2 copy-done.8
  66.0 2.1 %fusion.21 = bf16[3,1024,128]{1,2,0:T(8,128)(2,1)} fusion(bf16[1024,1024]{0,1:T(8,128)(2,1)S(1)} %copy.28, f32[1024]{0:T(1024)S(1)} %copy-done.21, f32[1024]{0:T(1024)S(1)} %copy-done.18, f32[1024]{0:T(1024)S(1)} %copy-done.12, bf16[1,1024,128]{2,1,0:T(8,128)(2,1)S(1)} %bitcast.103, bf16[1,1024,128]{2,1,0:T(8,128)(2,1)S(1)} %bitcast.101, ...), kind=kOutput, calls=%fused_computation.29 | convolution fusion | flops 811728896 | bytes 3682304 | tf_op jit(solution)/shard_map/rd,mrh->mdh/dot_general | solution.py:175
  68.1 2.3 %copy.32 = bf16[3,1024,128]{2,1,0:T(8,128)(2,1)} copy(bf16[3,1024,128]{1,2,0:T(8,128)(2,1)} %fusion.21) | data formatting | bytes 1572864 | tf_op jit(solution)/shard_map/convert_element_type | solution.py:178
  70.4 2.1 %copy.33 = bf16[16,3,64,128]{3,2,1,0:T(8,128)(2,1)} copy(bf16[16,3,64,128]{3,2,0,1:T(8,128)(2,1)} %bitcast.81) | data formatting | bytes 1572864 | tf_op jit(solution)/shard_map/transpose | solution.py:29
  72.5 2.1 %all-to-all-done.2 = bf16[16,128,64]{1,2,0:T(8,128)(2,1)S(1)} async-done(((bf16[16,128,64]{1,2,0:T(8,128)(2,1)}), bf16[16,128,64]{1,2,0:T(8,128)(2,1)S(1)}, u32[]{:S(2)}, u32[]{:S(2)}) %all-to-all-start.2) | async-done | bytes 262176 | tf_op jit(solution)/shard_map/all_to_all | solution.py:34
  74.5 5.1 %all-to-all-start.1 = ((bf16[16,3,64,128]{3,2,1,0:T(8,128)(2,1)}), bf16[16,3,64,128]{3,2,1,0:T(8,128)(2,1)}, u32[]{:S(2)}, u32[]{:S(2)}) async-start(bf16[16,3,64,128]{3,2,1,0:T(8,128)(2,1)} %copy.33), calls=%async_computation.1 | async-start | bytes 1572864 | tf_op jit(solution)/shard_map/all_to_all | solution.py:34
  79.7 2.6 %fusion.13 = (f32[1024]{0:T(1024)S(1)}, f32[1024]{0:T(1024)S(1)}, f32[1024,1024,1]{0,1,2:T(8,128)S(1)}) fusion(f32[1024]{0:T(1024)S(1)} %copy-done.21, f32[1024]{0:T(1024)S(1)} %copy-done.18, f32[1024]{0:T(1024)S(1)} %copy-done.12, bf16[1024,1024]{0,1:T(8,128)(2,1)S(1)} %copy.28, bf16[3,1024,128]{2,1,0:T(8,128)(2,1)S(1)} %copy-done, ...), kind=kOutput, calls=%fused_computation.16 | convolution fusion | flops 813430784 | bytes 7884800 | tf_op jit(solution)/shard_map/mrh,mdh->rd/dot_general | solution.py:181
  82.3 2.6 %fusion.11 = bf16[1024,1024]{0,1:T(8,128)(2,1)} fusion(bf16[1024,1024]{0,1:T(8,128)(2,1)S(1)} %copy.28, f32[1024,1024,1]{0,1,2:T(8,128)S(1)} %get-tuple-element.38, f32[1024]{0:T(1024)S(1)} %broadcast_multiply_fusion, f32[1024]{0:T(1024)S(1)} %broadcast_multiply_fusion.1, f32[1024]{0:T(1024)S(1)} %copy-done.21, f32[1024]{0:T(1024)S(1)} %copy-done.18, ...), kind=kLoop, calls=%fused_computation.13 | loop fusion | flops 9437184 | bytes 8409088 | tf_op jit(solution)/shard_map/convert_element_type | solution.py:183
  84.9 17.5 %all-to-all-done.1 = bf16[16,3,64,128]{3,2,1,0:T(8,128)(2,1)} async-done(((bf16[16,3,64,128]{3,2,1,0:T(8,128)(2,1)}), bf16[16,3,64,128]{3,2,1,0:T(8,128)(2,1)}, u32[]{:S(2)}, u32[]{:S(2)}) %all-to-all-start.1) | async-done | bytes 786464 | tf_op jit(solution)/shard_map/all_to_all | solution.py:34
  102.5 6.7 %all-to-all-start = ((bf16[8,1024,128]{1,2,0:T(8,128)(2,1)}), bf16[8,1024,128]{1,2,0:T(8,128)(2,1)S(1)}, u32[]{:S(2)}, u32[]{:S(2)}) async-start(bf16[8,1024,128]{1,2,0:T(8,128)(2,1)} %bitcast.80), calls=%async_computation | async-start | bytes 4194304 | tf_op jit(solution)/shard_map/all_to_all | solution.py:34
  109.1 0.7 convert_reduce_fusion.2
  109.8 1.9 %convert_reduce_fusion.1 = f32[3,64,128]{2,1,0:T(8,128)} fusion(bf16[16,3,64,128]{3,2,1,0:T(8,128)(2,1)} %all-to-all-done.1), kind=kLoop, calls=%fused_computation.22 | loop fusion | flops 761856 | bytes 884736 | tf_op jit(solution)/shard_map/reduce_sum | solution.py:35
  111.7 25.1 %all-to-all-done = bf16[8,1024,128]{1,2,0:T(8,128)(2,1)S(1)} async-done(((bf16[8,1024,128]{1,2,0:T(8,128)(2,1)}), bf16[8,1024,128]{1,2,0:T(8,128)(2,1)S(1)}, u32[]{:S(2)}, u32[]{:S(2)}) %all-to-all-start) | async-done | bytes 2097184 | tf_op jit(solution)/shard_map/all_to_all | solution.py:34
  136.7 0.4 reduce_sum.110
  137.1 0.8 copy.35
  (56 shorter events, 0.2 us)
Async XLA Ops:
  0.6 6.4 %copy-start = (bf16[3,1024,128]{2,1,0:T(8,128)(2,1)S(1)}, bf16[3,1024,128]{2,1,0:T(8,128)(2,1)}, u32[]{:S(2)}) copy-start(bf16[3,1024,128]{2,1,0:T(8,128)(2,1)} %param.9) | copy-start | bytes 2359300
  3.6 1.0 copy-start.10
  3.6 1.1 copy-start.25
  4.0 3.0 %copy-start.11 = (f32[1024]{0:T(1024)}, f32[1024]{0:T(1024)S(1)}, u32[]{:S(2)}) copy-start(f32[1024]{0:T(1024)S(1)} %broadcast_multiply_fusion.2) | copy-start | bytes 12292
  4.6 2.5 %copy-start.20 = (f32[1024]{0:T(1024)S(1)}, f32[1024]{0:T(1024)}, u32[]{:S(2)}) copy-start(f32[1024]{0:T(1024)} %param.8) | copy-start | bytes 12292
  4.6 3.9 %copy-start.17 = (f32[1024]{0:T(1024)}, f32[1024]{0:T(1024)S(1)}, u32[]{:S(2)}) copy-start(f32[1024]{0:T(1024)S(1)} %add_rsqrt_fusion) | copy-start | bytes 12292
  4.7 3.8 %copy-start.22 = (bf16[1024]{0:T(1024)(128)(2,1)}, bf16[1024]{0:T(1024)(128)(2,1)S(1)}, u32[]{:S(2)}) copy-start(bf16[1024]{0:T(1024)(128)(2,1)S(1)} %dynamic-slice_convert_fusion) | copy-start | bytes 6148
  7.1 10.5 %copy-start.26 = (s32[8]{0:T(128)S(1)}, s32[8]{0:T(128)}, u32[]{:S(2)}) copy-start(s32[8]{0:T(128)} %param.13) | copy-start | bytes 100
  8.5 0.9 copy-start.1
  10.0 10.6 %collective-permute-start = (bf16[4,64,128]{2,1,0:T(8,128)(2,1)}, bf16[4,64,128]{2,1,0:T(8,128)(2,1)S(1)}, u32[]{:S(2)}, u32[]{:S(2)}) collective-permute-start(bf16[4,64,128]{2,1,0:T(8,128)(2,1)} %get-tuple-element.25), channel_id=1, source_target_pairs={{0,16},{16,32},{32,48},{48,64},{64,80},{80,96},{96,112},{112,128},... | collective-permute-start | bytes 196616 | tf_op jit(solution)/shard_map/ppermute | solution.py:18
  15.0 5.6 %collective-permute-start.1 = (bf16[4,64,128]{2,1,0:T(8,128)(2,1)S(1)}, bf16[4,64,128]{2,1,0:T(8,128)(2,1)S(1)}, u32[]{:S(2)}, u32[]{:S(2)}) collective-permute-start(bf16[4,64,128]{2,1,0:T(8,128)(2,1)S(1)} %get-tuple-element.26), channel_id=1, source_target_pairs={{16,0},{32,16},{48,32},{64,48},{80,64},{96,80},{112,96},{128,112},... | collective-permute-start | bytes 196616 | tf_op jit(solution)/shard_map/ppermute | solution.py:21
  19.2 3.3 %copy-start.2 = (bf16[3,1024,128]{2,1,0:T(8,128)(2,1)S(1)}, bf16[3,1024,128]{2,1,0:T(8,128)(2,1)}, u32[]{:S(2)}) copy-start(bf16[3,1024,128]{2,1,0:T(8,128)(2,1)} %copy-done.1) | copy-start | bytes 2359300
  22.5 3.2 %copy-start.5 = (bf16[1,1088,128]{2,1,0:T(8,128)(2,1)}, bf16[1,1088,128]{2,1,0:T(8,128)(2,1)S(1)}, u32[]{:S(2)}) copy-start(bf16[1,1088,128]{2,1,0:T(8,128)(2,1)S(1)} %get-tuple-element.21) | copy-start | bytes 835588
  22.5 3.2 %copy-start.6 = (bf16[1,1088,128]{2,1,0:T(8,128)(2,1)}, bf16[1,1088,128]{2,1,0:T(8,128)(2,1)S(1)}, u32[]{:S(2)}) copy-start(bf16[1,1088,128]{2,1,0:T(8,128)(2,1)S(1)} %get-tuple-element.24) | copy-start | bytes 835588
  23.6 0.7 copy-start.4
  23.6 2.1 %copy-start.13 = (s32[34,96]{1,0:T(8,128)S(1)}, s32[34,96]{1,0:T(8,128)}, u32[]{:S(2)}) copy-start(s32[34,96]{1,0:T(8,128)} %get-tuple-element.39) | copy-start | bytes 39172
  23.6 2.1 %copy-start.14 = (s32[34,96]{1,0:T(8,128)S(1)}, s32[34,96]{1,0:T(8,128)}, u32[]{:S(2)}) copy-start(s32[34,96]{1,0:T(8,128)} %get-tuple-element.40) | copy-start | bytes 39172
  23.6 2.1 %copy-start.15 = (s32[34,32]{1,0:T(8,128)S(1)}, s32[34,32]{1,0:T(8,128)}, u32[]{:S(2)}) copy-start(s32[34,32]{1,0:T(8,128)} %eq.39) | copy-start | bytes 13060
  23.6 2.1 %copy-start.16 = (s32[34,32]{1,0:T(8,128)S(1)}, s32[34,32]{1,0:T(8,128)}, u32[]{:S(2)}) copy-start(s32[34,32]{1,0:T(8,128)} %add_add_fusion.1) | copy-start | bytes 13060
  23.6 2.1 %copy-start.19 = (pred[34,96]{1,0:T(8,128)(4,1)S(1)}, pred[34,96]{1,0:T(8,128)(4,1)}, u32[]{:S(2)}) copy-start(pred[34,96]{1,0:T(8,128)(4,1)} %add_compare_fusion) | copy-start | bytes 9796
  48.3 3.2 %copy-start.9 = (bf16[34,32,1,128]{3,1,0,2:T(8,128)(2,1)S(1)}, bf16[34,32,1,128]{3,1,0,2:T(8,128)(2,1)}, u32[]{:S(2)}) copy-start(bf16[34,32,1,128]{3,1,0,2:T(8,128)(2,1)} %fusion.34) | copy-start | bytes 835588
  48.3 3.2 %slice-start = ((bf16[34,32,1,128]{3,1,0,2:T(8,128)(2,1)}), bf16[32,32,1,128]{3,1,0,2:T(8,128)(2,1)S(1)}, s32[]{:S(2)}) async-start(bf16[34,32,1,128]{3,1,0,2:T(8,128)(2,1)} %fusion.35), calls=%async_computation.3 | async-start | bytes 524288 | tf_op jit(solution)/shard_map/slice | solution.py:165
  48.3 3.3 %copy-start.23 = (bf16[1024]{0:T(1024)(128)(2,1)S(1)}, bf16[1024]{0:T(1024)(128)(2,1)}, u32[]{:S(2)}) copy-start(bf16[1024]{0:T(1024)(128)(2,1)} %copy-done.22) | copy-start | bytes 6148
  48.3 3.3 %copy-start.24 = (bf16[1024,1024]{1,0:T(8,128)(2,1)S(1)}, bf16[1024,1024]{1,0:T(8,128)(2,1)}, u32[]{:S(2)}) copy-start(bf16[1024,1024]{1,0:T(8,128)(2,1)} %param.11) | copy-start | bytes 6291460
  52.9 21.6 %all-to-all-start.2 = ((bf16[16,128,64]{1,2,0:T(8,128)(2,1)}), bf16[16,128,64]{1,2,0:T(8,128)(2,1)S(1)}, u32[]{:S(2)}, u32[]{:S(2)}) async-start(bf16[16,128,64]{1,2,0:T(8,128)(2,1)} %bitcast.37), calls=%async_computation.2 | async-start | bytes 524288 | tf_op jit(solution)/shard_map/all_to_all | solution.py:34
  62.8 2.0 %copy-start.3 = (f32[34,96,1,128]{3,1,0,2:T(8,128)S(1)}, f32[34,96,1,128]{3,1,0,2:T(8,128)}, u32[]{:S(2)}) copy-start(f32[34,96,1,128]{3,1,0,2:T(8,128)} %convolution_bitcast_fusion) | copy-start | bytes 5013508
  64.9 1.1 copy-start.12
  64.9 1.1 copy-start.18
  64.9 1.1 copy-start.21
  65.1 0.7 copy-start.7
  65.3 0.7 copy-start.8
  74.5 27.9 %all-to-all-start.1 = ((bf16[16,3,64,128]{3,2,1,0:T(8,128)(2,1)}), bf16[16,3,64,128]{3,2,1,0:T(8,128)(2,1)}, u32[]{:S(2)}, u32[]{:S(2)}) async-start(bf16[16,3,64,128]{3,2,1,0:T(8,128)(2,1)} %copy.33), calls=%async_computation.1 | async-start | bytes 1572864 | tf_op jit(solution)/shard_map/all_to_all | solution.py:34
  102.5 34.3 %all-to-all-start = ((bf16[8,1024,128]{1,2,0:T(8,128)(2,1)}), bf16[8,1024,128]{1,2,0:T(8,128)(2,1)S(1)}, u32[]{:S(2)}, u32[]{:S(2)}) async-start(bf16[8,1024,128]{1,2,0:T(8,128)(2,1)} %bitcast.80), calls=%async_computation | async-start | bytes 4194304 | tf_op jit(solution)/shard_map/all_to_all | solution.py:34
where the time goes:
time: 139 us; the launch traced here: 138 us
  waiting for transfers between devices  44.7 us (32%)
  matrix products  36.1 us (26%)
  starting transfers between devices  28.5 us (21%)
  local copies, waits for them, and re-layouts  14.7 us (11%)
  other arithmetic  12.8 us (9%)
    all_to_all x3, waiting for transfers between devices, sent_and_summed(): lax.all_to_all(pieces, axis, split_axis=0, concat_axis=0, tiled=True)  44.7 us
    all_to_all x3, starting transfers between devices, sent_and_summed(): lax.all_to_all(pieces, axis, split_axis=0, concat_axis=0, tiled=True)  21.7 us
    dot_general x1, matrix products, attend(): jnp.einsum('chij,cihd->cjhd', score_grad, queries, preferred_element_type...  9.29 us
    dot_general x1, matrix products, attend(): jnp.einsum('chij,cjhd->cihd', score_grad, key_win, preferred_element_type...  8.23 us
    unnamed x56, local copies, waits for them, and re-layouts  6.44 us
    ppermute x1, starting transfers between devices, with_halo(): lax.ppermute(lax.slice_in_dim(block, block.shape[dim] - width, None, axis...  4.92 us
    dot_general x1, matrix products, attend(): jnp.einsum('chij,cihd->cjhd', rounded, grad_rows, preferred_element_type=...  3.21 us
    concatenate x2, other arithmetic, with_halo(): block = jnp.concatenate([low, block, high], axis=dim)  2.96 us
  transfers between devices with their start and end apart: 5, of which 3 were waited for; matrix products, arithmetic and copies ran while one was open for 14% of the time, Pallas kernels for 0%

commit v1 on v0

v1 whole, which is shorter than its diff:
```python
import jax
import jax.numpy as jnp
from jax import lax
from jax.experimental import pallas as pl
from jax.experimental.pallas import tpu as pltpu
from jax.sharding import PartitionSpec as P

HS = 128
CH = 32
HALO = 64
EPSILON = 1e-05
SCALE = HS ** (-0.5)
F32 = jnp.float32
BF16 = jnp.bfloat16


def rows_by_rows(left, right):
    return lax.dot_general(left, right, (((1,), (1,)), ((), ())), preferred_element_type=F32)


def cols_by_cols(left, right):
    return lax.dot_general(left, right, (((0,), (0,)), ((), ())), preferred_element_type=F32)


def plain(left, right):
    return jnp.dot(left, right, preferred_element_type=F32)


def normalised(values):
    values = values.astype(F32)
    center = values - jnp.mean(values, axis=-1, keepdims=True)
    inverse = lax.rsqrt(jnp.mean(center * center, axis=-1, keepdims=True) + EPSILON)
    return center * inverse, inverse


def pad_rows(pad_ref, first, count):
    total = pad_ref.shape[0]
    return [pad_ref[pl.ds(jnp.clip(first + i, 0, total - 1), 1), :] for i in range(count)]


def as_columns(rows):
    height = -(-len(rows) // 8) * 8
    full = jnp.concatenate(rows + [jnp.zeros_like(rows[0])] * (height - len(rows)), axis=0)
    return full.T


def project_body(frames_ref, gain_ref, qkv_ref, out_ref, cot_ref, pad_ref, proj_ref, normed_ref, w_scr):
    step = pl.program_id(0)
    rows = frames_ref.shape[0]

    @pl.when(step == 0)
    def _():
        for m in range(3):
            w_scr[:, m * HS : (m + 1) * HS] = qkv_ref[m]

    normal_form, _ = normalised(frames_ref[...])
    normed = (normal_form * gain_ref[...]).astype(BF16)
    normed_ref[...] = normed
    qkv = plain(normed, w_scr[...]).astype(BF16)
    for m in range(3):
        proj_ref[m] = qkv[:, m * HS : (m + 1) * HS]
    per_step = rows // 128
    first = (lax.axis_index("tm") * pl.num_programs(0) + step) * per_step
    live = as_columns([r.astype(F32) for r in pad_rows(pad_ref, first, per_step)])
    live = jnp.concatenate([live[:, i : i + 1] for i in range(per_step)], axis=0)
    grads = rows_by_rows(cot_ref[...], out_ref[...])
    proj_ref[3] = jnp.where(live == 1.0, grads, 0.0).astype(BF16)


def project(frames, gain, qkv_weight, out_weight, cotangent, pad2d):
    count, width = frames.shape
    rows = 256
    whole = lambda *shape: pl.BlockSpec(shape, lambda i: (0,) * len(shape))
    return pl.pallas_call(
        project_body,
        grid=(count // rows,),
        in_specs=[
            pl.BlockSpec((rows, width), lambda i: (i, 0)),
            whole(1, width),
            whole(*qkv_weight.shape),
            whole(*out_weight.shape),
            pl.BlockSpec((rows, width), lambda i: (i, 0)),
            whole(*pad2d.shape),
        ],
        out_specs=[
            pl.BlockSpec((4, rows, HS), lambda i: (0, i, 0)),
            pl.BlockSpec((rows, width), lambda i: (i, 0)),
        ],
        out_shape=[
            jax.ShapeDtypeStruct((4, count, HS), BF16),
            jax.ShapeDtypeStruct((count, width), BF16),
        ],
        scratch_shapes=[pltpu.VMEM((width, 3 * HS), BF16)],
        compiler_params=pltpu.CompilerParams(vmem_limit_bytes=48 << 20),
        name="project",
    )(frames, gain, qkv_weight, out_weight, cotangent, pad2d)


def attend_body(len_ref, proj_ref, halo_ref, gain_ref, qkv_ref, out_ref, pad_ref, grads_ref, mixed_ref, x_scr):
    count = proj_ref.shape[1]
    tiles = count // 128 + 1
    shard = lax.axis_index("tm")
    first_block = shard * (count // 128) - 1
    normal_form, _ = normalised(halo_ref[0])
    normed = (normal_form * gain_ref[...]).astype(BF16)
    blocks = tiles + 1
    live_rows = [r.astype(F32) for r in pad_rows(pad_ref, first_block, blocks)]
    live_cols = as_columns(live_rows)
    halo_live = jnp.concatenate([live_cols[HALO:, 0:1], live_cols[:HALO, blocks - 1 : blocks]], axis=0)
    zeros = jnp.zeros((HALO, HS), BF16)
    for m in range(4):
        if m < 3:
            part = plain(normed, qkv_ref[m])
        else:
            part = jnp.where(halo_live == 1.0, rows_by_rows(halo_ref[1], out_ref[...]), 0.0)
        part = part.astype(BF16)
        x_scr[m, 0:HALO, :] = zeros
        x_scr[m, HALO : 2 * HALO, :] = part[:HALO]
        x_scr[m, 2 * HALO : 2 * HALO + count, :] = proj_ref[m]
        x_scr[m, 2 * HALO + count : 3 * HALO + count, :] = part[HALO:]
        x_scr[m, 3 * HALO + count :, :] = zeros

    ends = []
    total = 0
    for u in range(len_ref.shape[0]):
        total = total + len_ref[u]
        ends.append(total)

    def segment(positions):
        found = jnp.zeros(positions.shape, jnp.int32)
        for end in ends:
            found = found + jnp.where(positions >= end, 1, 0)
        return found.astype(F32)

    lane = lax.broadcasted_iota(jnp.int32, (1, 128), 1)
    codes = []
    for b in range(blocks):
        at = (first_block + b) * 128 + lane
        codes.append(jnp.where((live_rows[b] == 1.0) & (at >= 0), segment(at), -1.0))
    code_cols = as_columns(codes)

    keys = 192
    key_at = lax.broadcasted_iota(jnp.int32, (keys, 128), 0)
    query_at = lax.broadcasted_iota(jnp.int32, (keys, 128), 1)
    apart = key_at // CH - query_at // CH
    in_band = (apart >= 0) & (apart <= 2)
    same = key_at == query_at + CH

    carry_k = carry_v = None
    for t in range(tiles):
        base = 128 * t
        q = x_scr[0, base + HALO : base + HALO + 128, :]
        g = x_scr[3, base + HALO : base + HALO + 128, :]
        k = x_scr[1, base + CH : base + CH + keys, :]
        v = x_scr[2, base + CH : base + CH + keys, :]
        query_seg = segment((first_block + t) * 128 + HALO + lane)
        code = jnp.concatenate([code_cols[CH:, t : t + 1], code_cols[: keys - 96, t + 1 : t + 2]], axis=0)
        allowed = in_band & ((code == query_seg) | same)
        scores = jnp.where(allowed, rows_by_rows(k, q) * SCALE, -1e30)
        weights = jnp.exp(scores - jnp.max(scores, axis=0, keepdims=True))
        probs = weights * (1.0 / jnp.sum(weights, axis=0, keepdims=True))
        rounded = probs.astype(BF16)
        prob_grad = rows_by_rows(v, g)
        centre = jnp.sum(probs * prob_grad, axis=0, keepdims=True)
        score_grad = (probs * (prob_grad - centre) * SCALE).astype(BF16)
        mixed = cols_by_cols(rounded, v).astype(BF16)
        query_grad = cols_by_cols(score_grad, k).astype(BF16)
        key_grad = plain(score_grad, q)
        value_grad = plain(rounded, g)
        live = jnp.concatenate([live_cols[HALO:, t : t + 1], live_cols[:HALO, t + 1 : t + 2]], axis=0)
        mixed = jnp.where(live == 1.0, mixed, jnp.zeros_like(mixed))
        lo, hi = (HALO if t == 0 else 0), (HALO if t == tiles - 1 else 128)
        at = base - HALO
        mixed_ref[at + lo : at + hi, :] = mixed[lo:hi]
        grads_ref[at + lo : at + hi, 0:HS] = query_grad[lo:hi]
        if t > 0:
            key_grad = jnp.concatenate([key_grad[:64] + carry_k, key_grad[64:]], axis=0)
            value_grad = jnp.concatenate([value_grad[:64] + carry_v, value_grad[64:]], axis=0)
        carry_k, carry_v = key_grad[128:], value_grad[128:]
        lo, hi = (96 if t == 0 else 0), (96 if t == tiles - 1 else 128)
        at = base - 96
        grads_ref[at + lo : at + hi, HS : 2 * HS] = key_grad[lo:hi].astype(BF16)
        grads_ref[at + lo : at + hi, 2 * HS : 3 * HS] = value_grad[lo:hi].astype(BF16)


def attend(lengths, proj, halo, gain, qkv_weight, out_weight, pad2d):
    count = proj.shape[1]
    vmem = pl.BlockSpec(memory_space=pltpu.VMEM)
    return pl.pallas_call(
        attend_body,
        in_specs=[pl.BlockSpec(memory_space=pltpu.SMEM)] + [vmem] * 6,
        out_specs=[vmem, vmem],
        out_shape=[
            jax.ShapeDtypeStruct((count, 3 * HS), BF16),
            jax.ShapeDtypeStruct((count, HS), BF16),
        ],
        scratch_shapes=[pltpu.VMEM((4, count + 4 * HALO, HS), BF16)],
        compiler_params=pltpu.CompilerParams(vmem_limit_bytes=48 << 20),
        name="attend",
    )(lengths, proj, halo, gain, qkv_weight, out_weight, pad2d)


def input_body(frames_ref, gain_ref, qkv_ref, grads_ref, term_ref, w_scr):
    @pl.when(pl.program_id(0) == 0)
    def _():
        for m in range(3):
            w_scr[:, m * HS : (m + 1) * HS] = qkv_ref[m]

    incoming = rows_by_rows(grads_ref[...], w_scr[...])
    normal_form, inverse = normalised(frames_ref[...])
    scaled = incoming * gain_ref[...]
    mean_grad = jnp.mean(scaled, axis=-1, keepdims=True)
    mean_proj = jnp.mean(scaled * normal_form, axis=-1, keepdims=True)
    result = (inverse * (scaled - mean_grad - normal_form * mean_proj)).astype(BF16)
    for p in range(term_ref.shape[0]):
        term_ref[p] = result[:, p * 128 : (p + 1) * 128]


def input_terms(frames, gain, qkv_weight, grads):
    count, width = frames.shape
    rows = 256
    whole = lambda *shape: pl.BlockSpec(shape, lambda i: (0,) * len(shape))
    return pl.pallas_call(
        input_body,
        grid=(count // rows,),
        in_specs=[
            pl.BlockSpec((rows, width), lambda i: (i, 0)),
            whole(1, width),
            whole(*qkv_weight.shape),
            pl.BlockSpec((rows, 3 * HS), lambda i: (i, 0)),
        ],
        out_specs=pl.BlockSpec((width // 128, rows, 128), lambda i: (0, i, 0)),
        out_shape=jax.ShapeDtypeStruct((width // 128, count, 128), BF16),
        scratch_shapes=[pltpu.VMEM((width, 3 * HS), BF16)],
        compiler_params=pltpu.CompilerParams(vmem_limit_bytes=48 << 20),
        name="input_terms",
    )(frames, gain, qkv_weight, grads)


def weight_body(normed_ref, cot_ref, grads_ref, mixed_ref, term_ref):
    shards, _, part, _ = term_ref.shape
    qkv = cols_by_cols(normed_ref[...], grads_ref[...]).astype(BF16)
    out = cols_by_cols(cot_ref[...], mixed_ref[...]).astype(BF16)
    for s in range(shards):
        for m in range(3):
            term_ref[s, m] = qkv[s * part : (s + 1) * part, m * HS : (m + 1) * HS]
        term_ref[s, 3] = out[s * part : (s + 1) * part]


def weight_terms(normed, cotangent, grads, mixed, shards):
    count, width = normed.shape
    vmem = pl.BlockSpec(memory_space=pltpu.VMEM)
    return pl.pallas_call(
        weight_body,
        in_specs=[vmem] * 4,
        out_specs=vmem,
        out_shape=jax.ShapeDtypeStruct((shards, 4, width // shards, HS), BF16),
        compiler_params=pltpu.CompilerParams(vmem_limit_bytes=48 << 20),
        name="weight_terms",
    )(normed, cotangent, grads, mixed)


def on_device(frames, norm_gain, qkv_weight, out_weight, cotangent, pad_mask, utt_lengths):
    shards = lax.axis_size("tm")
    up = [(i, i + 1) for i in range(shards - 1)]
    down = [(i + 1, i) for i in range(shards - 1)]
    ends = jnp.stack([frames[-HALO:], cotangent[-HALO:]])
    starts = jnp.stack([frames[:HALO], cotangent[:HALO]])
    halo = jnp.concatenate([lax.ppermute(ends, "tm", up), lax.ppermute(starts, "tm", down)], axis=1)
    gain = norm_gain[None, :]
    pad2d = pad_mask.reshape(-1, 128)
    proj, normed = project(frames, gain, qkv_weight, out_weight, cotangent, pad2d)
    grads, mixed = attend(utt_lengths, proj, halo, gain, qkv_weight, out_weight, pad2d)
    terms = input_terms(frames, gain, qkv_weight, grads)
    weights = weight_terms(normed, cotangent, grads, mixed, shards)
    terms = lax.all_to_all(terms, "mp", 0, 0, tiled=True)
    weights = lax.all_to_all(weights, "tm", 0, 0, tiled=True)
    frame_grad = terms.astype(F32).sum(axis=0).astype(BF16)
    summed = weights.astype(F32).sum(axis=0)
    return frame_grad, summed[:3], summed[3].T


def solution(mesh):
    placed = (
        P(("batch", "tm"), None),
        P(),
        P(None, None, "mp"),
        P("mp", None),
        P(("batch", "tm"), None),
        P("batch"),
        P("batch"),
    )
    return jax.shard_map(
        on_device,
        mesh=mesh,
        in_specs=placed,
        out_specs=(P(("batch", "tm"), "mp"), P("batch", "tm", "mp"), P(("batch", "mp"), "tm")),
        check_vma=False,
    )
```

time: 139 us -> 96.9 us (0.70)
  matrix products: 36.1 us -> 0 us
  Pallas kernels: 0 us -> 18.3 us
  local copies, waits for them, and re-layouts: 14.7 us -> 2.51 us
  other arithmetic: 12.8 us -> 2.93 us
  starting transfers between devices: 28.5 us -> 22.5 us
  waiting for transfers between devices: 44.7 us -> 49.5 us
    dot_general x10 -> x0, matrix products: 33.5 us -> none  [the longest x1 9.29 us: attend(): jnp.einsum('chij,cihd->cjhd', score_grad, queries, preferred_element_type...]
    pallas_call x0 -> x4, Pallas kernels: none -> 18.3 us  [the longest x1 5.27 us: project(): pl.pallas_call(project_body, grid=(count // rows,), in_specs=[pl.BlockSpe...]
    unnamed x56 -> x12, local copies, waits for them, and re-layouts: 6.44 us -> 0.03 us
    all_to_all x3 -> x2, starting transfers between devices: 21.7 us -> 15.4 us  [the longest x1 8.97 us: on_device(): weights = lax.all_to_all(weights, 'tm', 0, 0, tiled=True)]
    all_to_all x3 -> x2, waiting for transfers between devices: 44.7 us -> 49.4 us  [the longest x1 25.3 us: on_device(): weights = lax.all_to_all(weights, 'tm', 0, 0, tiled=True)]
    concatenate x3 -> x1, other arithmetic: 3.67 us -> 0.04 us  [on_device(): jnp.concatenate([lax.ppermute(ends, 'tm', up), lax.ppermute(starts, 'tm',...]
    convert_element_type x2 -> x0, local copies, waits for them, and re-layouts: 3.15 us -> none  [the longest x1 2.3 us: on_device(): weight_terms.astype(jnp.bfloat16)]
    sub x1 -> x0, matrix products: 2.67 us -> none  [attend(): weights = jnp.exp(scores - row_max)]
  transfers between devices with their start and end apart: 5 -> 4, of which waited for: 3 -> 2; matrix products, arithmetic and copies ran while one was open for 14% -> 3% of each run, Pallas kernels for 0% -> 10%
where the time goes in v1:
time: 96.9 us; the launch traced here: 96.5 us
  waiting for transfers between devices  49.5 us (51%)
  starting transfers between devices  22.5 us (23%)
  Pallas kernels  18.3 us (19%)
  other arithmetic  2.93 us (3%)
  local copies, waits for them, and re-layouts  2.51 us (3%)
    all_to_all x1, waiting for transfers between devices, on_device(): weights = lax.all_to_all(weights, 'tm', 0, 0, tiled=True)  25.3 us
    all_to_all x1, waiting for transfers between devices, on_device(): terms = lax.all_to_all(terms, 'mp', 0, 0, tiled=True)  24.2 us
    all_to_all x1, starting transfers between devices, on_device(): weights = lax.all_to_all(weights, 'tm', 0, 0, tiled=True)  8.97 us
    all_to_all x1, starting transfers between devices, on_device(): terms = lax.all_to_all(terms, 'mp', 0, 0, tiled=True)  6.44 us
    pallas_call x1, Pallas kernels, project(): pl.pallas_call(project_body, grid=(count // rows,), in_specs=[pl.BlockSpe...  5.27 us
    ppermute x1, starting transfers between devices, on_device(): lax.ppermute(starts, 'tm', down)  5.15 us
    pallas_call x1, Pallas kernels, attend(): pl.pallas_call(attend_body, in_specs=[pl.BlockSpec(memory_space=pltpu.SME...  4.53 us
    pallas_call x1, Pallas kernels, weight_terms(): pl.pallas_call(weight_body, in_specs=[vmem] * 4, out_specs=vmem, out_shap...  4.42 us
  transfers between devices with their start and end apart: 4, of which 2 were waited for; matrix products, arithmetic and copies ran while one was open for 3% of the time, Pallas kernels for 10%

profile of v1, /device:TPU:1, one launch (start us, length us, event | category | flops | bytes accessed | tf_op | source)
XLA Modules:
  0.0 96.5 jit_solution(2304276612495308610)
XLA Ops:
  0.6 0.0 copy-start.1
  0.6 0.0 copy-start.2
  0.7 0.0 copy-start.3
  0.7 0.0 copy-start.4
  0.7 1.2 %slice_bitcast_fusion.2 = (bf16[1,64,1024]{2,1,0:T(8,128)(2,1)S(1)}, bf16[1,64,1024]{2,1,0:T(8,128)(2,1)S(1)}, bf16[1,64,1024]{2,1,0:T(8,128)(2,1)S(1)}, bf16[1,64,1024]{2,1,0:T(8,128)(2,1)S(1)}) fusion(bf16[1024,1024]{1,0:T(8,128)(2,1)} %cot_ref.3, bf16[1024,1024]{1,0:T(8,128)(2,1)} %frames_ref.3), kind=kLoop, calls=%fused_computation.6 | loop fusion | bytes 1048576 | tf_op jit(solution)/shard_map/stack | solution.py:267
  1.9 5.1 %collective-permute-start.1 = (bf16[2,64,1024]{2,1,0:T(8,128)(2,1)S(1)}, bf16[2,64,1024]{2,1,0:T(8,128)(2,1)S(1)}, u32[]{:S(2)}, u32[]{:S(2)}) collective-permute-start(bf16[2,64,1024]{2,1,0:T(8,128)(2,1)S(1)} %pad_maximum_fusion.2), channel_id=1, source_target_pairs={{16,0},{32,16},{48,32},{64,48},{80,64},{96,80},{112,96},{128,112},... | collective-permute-start | bytes 786440 | tf_op jit(solution)/shard_map/ppermute | solution.py:269
  7.1 1.9 %collective-permute-start = (bf16[2,64,1024]{2,1,0:T(8,128)(2,1)S(1)}, bf16[2,64,1024]{2,1,0:T(8,128)(2,1)S(1)}, u32[]{:S(2)}, u32[]{:S(2)}) collective-permute-start(bf16[2,64,1024]{2,1,0:T(8,128)(2,1)S(1)} %pad_maximum_fusion.1), channel_id=1, source_target_pairs={{0,16},{16,32},{32,48},{48,64},{64,80},{80,96},{96,112},{112,128},... | collective-permute-start | bytes 786440 | tf_op jit(solution)/shard_map/ppermute | solution.py:269
  9.0 0.0 copy-done.1
  9.1 0.0 copy-done.2
  9.1 0.0 copy-done.3
  9.1 0.0 copy-done.4
  9.1 0.0 copy-start.5
  9.1 5.3 %project.1 = (bf16[4,1024,128]{2,1,0:T(8,128)(2,1)S(1)}, bf16[1024,1024]{1,0:T(8,128)(2,1)S(1)}) custom-call(bf16[1024,1024]{1,0:T(8,128)(2,1)} %frames_ref.3, f32[1,1024]{1,0:T(1,128)S(1)} %bitcast.16, bf16[3,1024,128]{2,1,0:T(8,128)(2,1)S(1)} %copy-done.1, bf16[128,1024]{1,0:T(8,128)(2,1)S(1)} %copy-done.2, bf16[1024,1024]{1,0:T(8,128)(2,1)} %cot_ref.3, ...), custom_call_target="tpu_custom_call" | custom-call | tf_op jit(solution)/shard_map/project/pallas_call | solution.py:74
  14.4 0.0 copy-start
  14.4 0.0 collective-permute-done.1
  14.4 0.0 collective-permute-done
  14.5 0.0 copy-done.5
  14.5 4.5 %attend.1 = (bf16[1024,384]{1,0:T(8,128)(2,1)S(1)}, bf16[1024,128]{1,0:T(8,128)(2,1)S(1)}) custom-call(s32[8]{0:T(128)S(1)} %copy-done.5, bf16[4,1024,128]{2,1,0:T(8,128)(2,1)S(1)} %get-tuple-element.7.proj_ref, bf16[2,128,1024]{2,1,0:T(8,128)(2,1)S(1)} %pad_maximum_fusion.halo_ref, f32[1,1024]{1,0:T(1,128)S(1)} %bitcast.17, ...), custom_call_target="tpu_custom_call" | custom-call | tf_op jit(solution)/shard_map/attend/pallas_call | solution.py:189
  19.0 0.0 copy-done
  19.0 4.1 %input_terms.1 = bf16[8,1024,128]{2,1,0:T(8,128)(2,1)} custom-call(bf16[1024,1024]{1,0:T(8,128)(2,1)S(1)} %copy-done, f32[1,1024]{1,0:T(1,128)S(1)} %bitcast.18, bf16[3,1024,128]{2,1,0:T(8,128)(2,1)S(1)} %copy-done.1, bf16[1024,384]{1,0:T(8,128)(2,1)S(1)} %get-tuple-element.8.grads_ref), custom_call_target="tpu_custom_call" | custom-call | tf_op jit(solution)/shard_map/input_terms/pallas_call | solution.py:223
  23.1 6.4 %all-to-all-start = ((bf16[8,1024,128]{2,1,0:T(8,128)(2,1)}), bf16[8,1024,128]{2,1,0:T(8,128)(2,1)}, u32[]{:S(2)}, u32[]{:S(2)}) async-start(bf16[8,1024,128]{2,1,0:T(8,128)(2,1)} %input_terms.1), calls=%async_computation | async-start | bytes 4194304 | tf_op jit(solution)/shard_map/all_to_all | solution.py:276
  29.5 4.4 %weight_terms.1 = bf16[16,4,64,128]{3,2,1,0:T(8,128)(2,1)} custom-call(bf16[1024,1024]{1,0:T(8,128)(2,1)S(1)} %get-tuple-element.9.normed_ref, bf16[1024,1024]{1,0:T(8,128)(2,1)} %cot_ref.3, bf16[1024,384]{1,0:T(8,128)(2,1)S(1)} %get-tuple-element.8.grads_ref, bf16[1024,128]{1,0:T(8,128)(2,1)S(1)} %get-tuple-element.10.mixed_ref), custom_call_target="tpu_custom_call" | custom-call | tf_op jit(solution)/shard_map/weight_terms/pallas_call | solution.py:253
  34.0 24.2 %all-to-all-done = bf16[8,1024,128]{2,1,0:T(8,128)(2,1)} async-done(((bf16[8,1024,128]{2,1,0:T(8,128)(2,1)}), bf16[8,1024,128]{2,1,0:T(8,128)(2,1)}, u32[]{:S(2)}, u32[]{:S(2)}) %all-to-all-start) | async-done | bytes 2097184 | tf_op jit(solution)/shard_map/all_to_all | solution.py:276
  58.1 9.0 %all-to-all-start.1 = ((bf16[16,4,64,128]{3,2,1,0:T(8,128)(2,1)}), bf16[16,4,64,128]{3,2,1,0:T(8,128)(2,1)S(1)}, u32[]{:S(2)}, u32[]{:S(2)}) async-start(bf16[16,4,64,128]{3,2,1,0:T(8,128)(2,1)} %weight_terms.1), calls=%async_computation.1 | async-start | bytes 2097152 | tf_op jit(solution)/shard_map/all_to_all | solution.py:277
  67.1 2.6 %reduce_sum.21 = bf16[1024,128]{1,0:T(8,128)(2,1)} reduce(bf16[8,1024,128]{2,1,0:T(8,128)(2,1)} %all-to-all-done, bf16[]{:T(256)} %constant.2.clone.1), dimensions={0}, to_apply=%region_0.0 | reduce | flops 917504 | bytes 2359298 | tf_op jit(solution)/shard_map/reduce_sum | solution.py:278
  69.7 25.3 %all-to-all-done.1 = bf16[16,4,64,128]{3,2,1,0:T(8,128)(2,1)S(1)} async-done(((bf16[16,4,64,128]{3,2,1,0:T(8,128)(2,1)}), bf16[16,4,64,128]{3,2,1,0:T(8,128)(2,1)S(1)}, u32[]{:S(2)}, u32[]{:S(2)}) %all-to-all-start.1) | async-done | bytes 1048608 | tf_op jit(solution)/shard_map/all_to_all | solution.py:277
  95.0 0.2 convert_reduce_fusion
  95.2 0.6 slice_bitcast_fusion.4
  95.8 0.6 slice.24
  (3 shorter events, 0.1 us)
Async XLA Ops:
  0.6 8.4 %copy-start.1 = (bf16[3,1024,128]{2,1,0:T(8,128)(2,1)S(1)}, bf16[3,1024,128]{2,1,0:T(8,128)(2,1)}, u32[]{:S(2)}) copy-start(bf16[3,1024,128]{2,1,0:T(8,128)(2,1)} %qkv_ref.5) | copy-start | bytes 2359300
  0.6 8.4 %copy-start.2 = (bf16[128,1024]{1,0:T(8,128)(2,1)S(1)}, bf16[128,1024]{1,0:T(8,128)(2,1)}, u32[]{:S(2)}) copy-start(bf16[128,1024]{1,0:T(8,128)(2,1)} %out_ref.3) | copy-start | bytes 786436
  0.7 8.4 %copy-start.3 = (s32[16384]{0:T(1024)S(1)}, s32[16384]{0:T(1024)}, u32[]{:S(2)}) copy-start(s32[16384]{0:T(1024)} %param.12) | copy-start | bytes 196612
  0.7 8.4 %copy-start.4 = (f32[1024]{0:T(1024)S(1)}, f32[1024]{0:T(1024)}, u32[]{:S(2)}) copy-start(f32[1024]{0:T(1024)} %param.8) | copy-start | bytes 12292
  1.9 12.5 %collective-permute-start.1 = (bf16[2,64,1024]{2,1,0:T(8,128)(2,1)S(1)}, bf16[2,64,1024]{2,1,0:T(8,128)(2,1)S(1)}, u32[]{:S(2)}, u32[]{:S(2)}) collective-permute-start(bf16[2,64,1024]{2,1,0:T(8,128)(2,1)S(1)} %pad_maximum_fusion.2), channel_id=1, source_target_pairs={{16,0},{32,16},{48,32},{64,48},{80,64},{96,80},{112,96},{128,112},... | collective-permute-start | bytes 786440 | tf_op jit(solution)/shard_map/ppermute | solution.py:269
  7.1 7.3 %collective-permute-start = (bf16[2,64,1024]{2,1,0:T(8,128)(2,1)S(1)}, bf16[2,64,1024]{2,1,0:T(8,128)(2,1)S(1)}, u32[]{:S(2)}, u32[]{:S(2)}) collective-permute-start(bf16[2,64,1024]{2,1,0:T(8,128)(2,1)S(1)} %pad_maximum_fusion.1), channel_id=1, source_target_pairs={{0,16},{16,32},{32,48},{48,64},{64,80},{80,96},{96,112},{112,128},... | collective-permute-start | bytes 786440 | tf_op jit(solution)/shard_map/ppermute | solution.py:269
  9.1 5.4 %copy-start.5 = (s32[8]{0:T(128)S(1)}, s32[8]{0:T(128)}, u32[]{:S(2)}) copy-start(s32[8]{0:T(128)} %len_ref.1) | copy-start | bytes 100
  14.4 4.6 %copy-start = (bf16[1024,1024]{1,0:T(8,128)(2,1)S(1)}, bf16[1024,1024]{1,0:T(8,128)(2,1)}, u32[]{:S(2)}) copy-start(bf16[1024,1024]{1,0:T(8,128)(2,1)} %frames_ref.3) | copy-start | bytes 6291460
  23.1 35.0 %all-to-all-start = ((bf16[8,1024,128]{2,1,0:T(8,128)(2,1)}), bf16[8,1024,128]{2,1,0:T(8,128)(2,1)}, u32[]{:S(2)}, u32[]{:S(2)}) async-start(bf16[8,1024,128]{2,1,0:T(8,128)(2,1)} %input_terms.1), calls=%async_computation | async-start | bytes 4194304 | tf_op jit(solution)/shard_map/all_to_all | solution.py:276
  58.1 36.9 %all-to-all-start.1 = ((bf16[16,4,64,128]{3,2,1,0:T(8,128)(2,1)}), bf16[16,4,64,128]{3,2,1,0:T(8,128)(2,1)S(1)}, u32[]{:S(2)}, u32[]{:S(2)}) async-start(bf16[16,4,64,128]{3,2,1,0:T(8,128)(2,1)} %weight_terms.1), calls=%async_computation.1 | async-start | bytes 2097152 | tf_op jit(solution)/shard_map/all_to_all | solution.py:277

commit v2 on v1

--- a/solution.py
+++ b/solution.py
@@ -200,7 +200,11 @@
     )(lengths, proj, halo, gain, qkv_weight, out_weight, pad2d)
 
 
-def input_body(frames_ref, gain_ref, qkv_ref, grads_ref, term_ref, w_scr):
+def input_body(frames_ref, gain_ref, qkv_ref, grads_ref, *rest):
+    outs, w_scr = rest[:-1], rest[-1]
+    place = lax.axis_index("mp")
+    y, xh = place // 2, place % 2
+
     @pl.when(pl.program_id(0) == 0)
     def _():
         for m in range(3):
@@ -212,52 +216,95 @@
     mean_grad = jnp.mean(scaled, axis=-1, keepdims=True)
     mean_proj = jnp.mean(scaled * normal_form, axis=-1, keepdims=True)
     result = (inverse * (scaled - mean_grad - normal_form * mean_proj)).astype(BF16)
-    for p in range(term_ref.shape[0]):
-        term_ref[p] = result[:, p * 128 : (p + 1) * 128]
-
-
-def input_terms(frames, gain, qkv_weight, grads):
+    if len(outs) == 4:
+        for p in range(4):
+            for k in range(4):
+
+                @pl.when((p - y) % 4 == k)
+                def _():
+                    for h in range(2):
+                        at = (2 * p + h) * 128
+                        outs[k][h] = result[:, at : at + 128]
+    else:
+        for p in range(4):
+            low = result[:, 256 * p : 256 * p + 128]
+            high = result[:, 256 * p + 128 : 256 * p + 256]
+            away = (p - y + 4) % 4
+            outs[0][away] = jnp.where(xh == 0, low, high)
+            outs[1][away] = jnp.where(xh == 0, high, low)
+
+
+def input_terms(frames, gain, qkv_weight, grads, half, pair_first):
     count, width = frames.shape
     rows = 256
+    steps = count // rows // 2
+    first = half * steps
     whole = lambda *shape: pl.BlockSpec(shape, lambda i: (0,) * len(shape))
+    lead, n_outs = (4, 2) if pair_first else (2, 4)
     return pl.pallas_call(
         input_body,
-        grid=(count // rows,),
+        grid=(steps,),
         in_specs=[
-            pl.BlockSpec((rows, width), lambda i: (i, 0)),
+            pl.BlockSpec((rows, width), lambda i: (i + first, 0)),
             whole(1, width),
             whole(*qkv_weight.shape),
-            pl.BlockSpec((rows, 3 * HS), lambda i: (i, 0)),
-        ],
-        out_specs=pl.BlockSpec((width // 128, rows, 128), lambda i: (0, i, 0)),
-        out_shape=jax.ShapeDtypeStruct((width // 128, count, 128), BF16),
+            pl.BlockSpec((rows, 3 * HS), lambda i: (i + first, 0)),
+        ],
+        out_specs=[pl.BlockSpec((lead, rows, 128), lambda i: (0, i, 0))] * n_outs,
+        out_shape=[jax.ShapeDtypeStruct((lead, count // 2, 128), BF16)] * n_outs,
         scratch_shapes=[pltpu.VMEM((width, 3 * HS), BF16)],
         compiler_params=pltpu.CompilerParams(vmem_limit_bytes=48 << 20),
-        name="input_terms",
+        name="input_terms_pair" if pair_first else "input_terms_ring",
     )(frames, gain, qkv_weight, grads)
 
 
-def weight_body(normed_ref, cot_ref, grads_ref, mixed_ref, term_ref):
-    shards, _, part, _ = term_ref.shape
+def weight_body(normed_ref, cot_ref, grads_ref, mixed_ref, keep_ref, send_ref):
+    place = lax.axis_index("tm")
+    core, zl, zh = place % 2, (place // 2) % 2, place // 4
     qkv = cols_by_cols(normed_ref[...], grads_ref[...]).astype(BF16)
     out = cols_by_cols(cot_ref[...], mixed_ref[...]).astype(BF16)
-    for s in range(shards):
-        for m in range(3):
-            term_ref[s, m] = qkv[s * part : (s + 1) * part, m * HS : (m + 1) * HS]
-        term_ref[s, 3] = out[s * part : (s + 1) * part]
-
-
-def weight_terms(normed, cotangent, grads, mixed, shards):
+    full = jnp.concatenate([qkv, out], axis=1)
+    for h in range(4):
+        away = (h - zh + 4) % 4
+        for l in range(2):
+            side = (l - zl + 2) % 2
+            at = (2 * h + l) * 128
+            low, high = full[at : at + 64], full[at + 64 : at + 128]
+            keep = jnp.where(core == 0, low, high)
+            send = jnp.where(core == 0, high, low)
+            for m in range(4):
+                keep_ref[side, away, m] = keep[:, m * HS : (m + 1) * HS]
+                send_ref[side, away, m] = send[:, m * HS : (m + 1) * HS]
+
+
+def weight_terms(normed, cotangent, grads, mixed):
     count, width = normed.shape
     vmem = pl.BlockSpec(memory_space=pltpu.VMEM)
+    part = jax.ShapeDtypeStruct((2, 4, 4, width // 16, HS), BF16)
     return pl.pallas_call(
         weight_body,
         in_specs=[vmem] * 4,
-        out_specs=vmem,
-        out_shape=jax.ShapeDtypeStruct((shards, 4, width // shards, HS), BF16),
+        out_specs=[vmem] * 2,
+        out_shape=[part] * 2,
         compiler_params=pltpu.CompilerParams(vmem_limit_bytes=48 << 20),
         name="weight_terms",
     )(normed, cotangent, grads, mixed)
+
+
+def shifted(x, axis, by):
+    size = lax.axis_size(axis)
+    return lax.ppermute(x, axis, [(i, (i + by) % size) for i in range(size)])
+
+
+def swapped(x, axis, bit):
+    return lax.ppermute(x, axis, [(i, i ^ bit) for i in range(lax.axis_size(axis))])
+
+
+def total(*parts):
+    summed = parts[0].astype(F32)
+    for part in parts[1:]:
+        summed = summed + part.astype(F32)
+    return summed
 
 
 def on_device(frames, norm_gain, qkv_weight, out_weight, cotangent, pad_mask, utt_lengths):
@@ -271,12 +318,27 @@
     pad2d = pad_mask.reshape(-1, 128)
     proj, normed = project(frames, gain, qkv_weight, out_weight, cotangent, pad2d)
     grads, mixed = attend(utt_lengths, proj, halo, gain, qkv_weight, out_weight, pad2d)
-    terms = input_terms(frames, gain, qkv_weight, grads)
-    weights = weight_terms(normed, cotangent, grads, mixed, shards)
-    terms = lax.all_to_all(terms, "mp", 0, 0, tiled=True)
-    weights = lax.all_to_all(weights, "tm", 0, 0, tiled=True)
-    frame_grad = terms.astype(F32).sum(axis=0).astype(BF16)
-    summed = weights.astype(F32).sum(axis=0)
+    keep, send = weight_terms(normed, cotangent, grads, mixed)
+    other = swapped(send, "tm", 1)
+    (frames_b, grads_b), _ = lax.optimization_barrier(((frames, grads), send))
+    near, across = input_terms(frames_b, gain, qkv_weight, grads_b, 1, True)
+    across = swapped(across, "mp", 1)
+    ring = input_terms(frames_b, gain, qkv_weight, grads_b, 0, False)
+    ring_in = [shifted(ring[k], "mp", 2 * k) for k in (2, 1, 3)]
+    stay = total(keep[0], other[0]).astype(BF16)
+    cross = swapped(total(keep[1], other[1]).astype(BF16), "tm", 2)
+    pair = [total(stay[k], cross[k]) for k in range(4)]
+    far = [shifted(pair[k].astype(BF16), "tm", 4 * k) for k in (2, 1, 3)]
+    col = [total(near[k], across[k]) for k in range(4)]
+    col_in = [shifted(col[k].astype(BF16), "mp", 2 * k) for k in (2, 1, 3)]
+    xh = lax.axis_index("mp") % 2
+    both = total(ring[0], *ring_in).astype(BF16)
+    mine = lax.dynamic_index_in_dim(both, xh, 0, False)
+    theirs = swapped(lax.dynamic_index_in_dim(both, 1 - xh, 0, False), "mp", 1)
+    first_half = total(mine, theirs).astype(BF16)
+    second_half = total(col[0], *col_in).astype(BF16)
+    frame_grad = jnp.concatenate([first_half, second_half], axis=0)
+    summed = total(pair[0], *far)
     return frame_grad, summed[:3], summed[3].T
 
 

time: 96.9 us -> 77.4 us (0.80)
  waiting for transfers between devices: 49.5 us -> 9.03 us
  starting transfers between devices: 22.5 us -> 39.4 us
  local copies, waits for them, and re-layouts: 2.51 us -> 4.37 us
    all_to_all x2 -> x0, waiting for transfers between devices: 49.4 us -> none  [the longest x1 25.3 us: on_device(): weights = lax.all_to_all(weights, 'tm', 0, 0, tiled=True)]
    ppermute x0 -> x13, starting transfers between devices: none -> 32.5 us  [the longest x9 23.8 us: shifted(): return lax.ppermute(x, axis, [(i, (i + by) % size) for i in range(size)])]
    all_to_all x2 -> x0, starting transfers between devices: 15.4 us -> none  [the longest x1 8.97 us: on_device(): weights = lax.all_to_all(weights, 'tm', 0, 0, tiled=True)]
    ppermute x0 -> x13, waiting for transfers between devices: none -> 8.62 us  [the longest x9 8.4 us: shifted(): return lax.ppermute(x, axis, [(i, (i + by) % size) for i in range(size)])]
    ppermute x1, starting transfers between devices: 5.15 us -> 1.92 us  [on_device(): lax.ppermute(starts, 'tm', down)]
    ppermute x1, starting transfers between devices: 1.92 us -> 4.94 us  [on_device(): lax.ppermute(ends, 'tm', up)]
    reduce_sum x2 -> x0, other arithmetic: 2.84 us -> none  [the longest x1 2.65 us: on_device(): frame_grad = terms.astype(F32).sum(axis=0).astype(BF16)]
    convert_element_type x0 -> x6, other arithmetic: none -> 2.75 us  [the longest x1 1.25 us: on_device(): both = total(ring[0], *ring_in).astype(BF16)]
  transfers between devices with their start and end apart: 4 -> 15, of which waited for: 2 -> 7; matrix products, arithmetic and copies ran while one was open for 3% -> 5% of each run, Pallas kernels for 10% -> 10%
where the time goes in v2:
time: 77.4 us; the launch traced here: 76.5 us
  starting transfers between devices  39.4 us (51%)
  Pallas kernels  19.2 us (25%)
  waiting for transfers between devices  9.03 us (12%)
  local copies, waits for them, and re-layouts  4.37 us (6%)
  other arithmetic  3.61 us (5%)
  between operations  0.86 us (1%)
    ppermute x9, starting transfers between devices, shifted(): return lax.ppermute(x, axis, [(i, (i + by) % size) for i in range(size)])  23.8 us
    ppermute x4, starting transfers between devices, swapped(): lax.ppermute(x, axis, [(i, i ^ bit) for i in range(lax.axis_size(axis))])  8.72 us
    ppermute x9, waiting for transfers between devices, shifted(): return lax.ppermute(x, axis, [(i, (i + by) % size) for i in range(size)])  8.4 us
    pallas_call x1, Pallas kernels, project(): pl.pallas_call(project_body, grid=(count // rows,), in_specs=[pl.BlockSpe...  5.28 us
    ppermute x1, starting transfers between devices, on_device(): lax.ppermute(ends, 'tm', up)  4.94 us
    pallas_call x2, Pallas kernels, input_terms(): pl.pallas_call(input_body, grid=(steps,), in_specs=[pl.BlockSpec((rows, w...  4.78 us
    pallas_call x1, Pallas kernels, weight_terms(): pl.pallas_call(weight_body, in_specs=[vmem] * 4, out_specs=[vmem] * 2, ou...  4.64 us
    pallas_call x1, Pallas kernels, attend(): pl.pallas_call(attend_body, in_specs=[pl.BlockSpec(memory_space=pltpu.SME...  4.53 us
  transfers between devices with their start and end apart: 15, of which 7 were waited for; matrix products, arithmetic and copies ran while one was open for 5% of the time, Pallas kernels for 10%

profile of v2, /device:TPU:1, one launch (start us, length us, event | category | flops | bytes accessed | tf_op | source)
XLA Modules:
  0.0 76.5 jit_solution(12795589298544571012)
XLA Ops:
  0.6 0.0 copy-start.8
  0.6 0.0 copy-start.5
  0.7 0.0 copy-start.4
  0.7 0.0 copy-start.1
  0.7 1.2 %slice_bitcast_fusion.2 = (bf16[1,64,1024]{2,1,0:T(8,128)(2,1)S(1)}, bf16[1,64,1024]{2,1,0:T(8,128)(2,1)S(1)}, bf16[1,64,1024]{2,1,0:T(8,128)(2,1)S(1)}, bf16[1,64,1024]{2,1,0:T(8,128)(2,1)S(1)}) fusion(bf16[1024,1024]{1,0:T(8,128)(2,1)} %cot_ref.3, bf16[1024,1024]{1,0:T(8,128)(2,1)} %frames_ref.3), kind=kLoop, calls=%fused_computation.34 | loop fusion | bytes 1048576 | tf_op jit(solution)/shard_map/stack | solution.py:314
  1.9 4.9 %collective-permute-start = (bf16[2,64,1024]{2,1,0:T(8,128)(2,1)S(1)}, bf16[2,64,1024]{2,1,0:T(8,128)(2,1)S(1)}, u32[]{:S(2)}, u32[]{:S(2)}) collective-permute-start(bf16[2,64,1024]{2,1,0:T(8,128)(2,1)S(1)} %pad_maximum_fusion.1), channel_id=1, source_target_pairs={{0,16},{16,32},{32,48},{48,64},{64,80},{80,96},{96,112},{112,128},... | collective-permute-start | bytes 786440 | tf_op jit(solution)/shard_map/ppermute | solution.py:316
  6.9 1.9 %collective-permute-start.1 = (bf16[2,64,1024]{2,1,0:T(8,128)(2,1)S(1)}, bf16[2,64,1024]{2,1,0:T(8,128)(2,1)S(1)}, u32[]{:S(2)}, u32[]{:S(2)}) collective-permute-start(bf16[2,64,1024]{2,1,0:T(8,128)(2,1)S(1)} %pad_maximum_fusion.2), channel_id=1, source_target_pairs={{16,0},{32,16},{48,32},{64,48},{80,64},{96,80},{112,96},{128,112},... | collective-permute-start | bytes 786440 | tf_op jit(solution)/shard_map/ppermute | solution.py:316
  8.8 0.0 copy-done.8
  8.8 0.0 copy-done.5
  8.9 0.0 copy-done.4
  8.9 0.0 copy-done.1
  8.9 0.0 copy-start.9
  8.9 5.3 %project.1 = (bf16[4,1024,128]{2,1,0:T(8,128)(2,1)S(1)}, bf16[1024,1024]{1,0:T(8,128)(2,1)S(1)}) custom-call(bf16[1024,1024]{1,0:T(8,128)(2,1)} %frames_ref.3, f32[1,1024]{1,0:T(1,128)S(1)} %bitcast.71, bf16[3,1024,128]{2,1,0:T(8,128)(2,1)S(1)} %copy-done.1, bf16[128,1024]{1,0:T(8,128)(2,1)S(1)} %copy-done.4, bf16[1024,1024]{1,0:T(8,128)(2,1)} %cot_ref.3, ...), custom_call_target="tpu_custom_call" | custom-call | tf_op jit(solution)/shard_map/project/pallas_call | solution.py:74
  14.2 0.0 collective-permute-done
  14.2 0.4 collective-permute-done.1
  14.6 0.0 copy-done.9
  14.7 4.5 %attend.1 = (bf16[1024,384]{1,0:T(8,128)(2,1)S(1)}, bf16[1024,128]{1,0:T(8,128)(2,1)S(1)}) custom-call(s32[8]{0:T(128)S(1)} %copy-done.9, bf16[4,1024,128]{2,1,0:T(8,128)(2,1)S(1)} %get-tuple-element.17.proj_ref, bf16[2,128,1024]{2,1,0:T(8,128)(2,1)S(1)} %pad_maximum_fusion.halo_ref, f32[1,1024]{1,0:T(1,128)S(1)} %bitcast.72, ...), custom_call_target="tpu_custom_call" | custom-call | tf_op jit(solution)/shard_map/attend/pallas_call | solution.py:189
  19.2 0.0 copy-start.2
  19.2 0.0 copy-start
  19.2 4.6 %weight_terms.1 = (bf16[2,4,4,64,128]{4,3,2,1,0:T(8,128)(2,1)S(1)}, bf16[2,4,4,64,128]{4,3,2,1,0:T(8,128)(2,1)}) custom-call(bf16[1024,1024]{1,0:T(8,128)(2,1)S(1)} %get-tuple-element.19.normed_ref, bf16[1024,1024]{1,0:T(8,128)(2,1)} %cot_ref.3, bf16[1024,384]{1,0:T(8,128)(2,1)S(1)} %get-tuple-element.23.grads_ref, ...), custom_call_target="tpu_custom_call" | custom-call | tf_op jit(solution)/shard_map/weight_terms/pallas_call | solution.py:284
  23.8 0.0 copy-done.2
  23.8 0.0 copy-done
  23.9 2.8 %input_terms_ring.1 = (bf16[2,512,128]{2,1,0:T(8,128)(2,1)S(1)}, bf16[2,512,128]{2,1,0:T(8,128)(2,1)}, bf16[2,512,128]{2,1,0:T(8,128)(2,1)}, bf16[2,512,128]{2,1,0:T(8,128)(2,1)}) custom-call(bf16[1024,1024]{1,0:T(8,128)(2,1)S(1)} %copy-done, f32[1,1024]{1,0:T(1,128)S(1)} %bitcast.73, bf16[3,1024,128]{2,1,0:T(8,128)(2,1)S(1)} %copy-done.1, ...), custom_call_target="tpu_custom_call" | custom-call | tf_op jit(solution)/shard_map/input_terms_ring/pallas_call | solution.py:244
  26.6 0.0 copy-start.6
  26.6 0.7 copy-done.6
  27.3 2.9 %collective-permute-start.2 = (bf16[2,512,128]{2,1,0:T(8,128)(2,1)}, bf16[2,512,128]{2,1,0:T(8,128)(2,1)}, u32[]{:S(2)}, u32[]{:S(2)}) collective-permute-start(bf16[2,512,128]{2,1,0:T(8,128)(2,1)} %get-tuple-element.25), channel_id=1, source_target_pairs={{0,8},{2,10},{4,12},{6,14},{8,0},{10,2},{12,4},{14,6},{1,9},{3,11}... | collective-permute-start | bytes 786440 | tf_op jit(solution)/shard_map/ppermute | solution.py:296
  30.2 0.4 collective-permute-start.3
  30.6 2.3 %collective-permute-start.4 = (bf16[2,512,128]{2,1,0:T(8,128)(2,1)}, bf16[2,512,128]{2,1,0:T(8,128)(2,1)}, u32[]{:S(2)}, u32[]{:S(2)}) collective-permute-start(bf16[2,512,128]{2,1,0:T(8,128)(2,1)} %get-tuple-element.27), channel_id=1, source_target_pairs={{0,12},{2,14},{4,0},{6,2},{8,4},{10,6},{12,8},{14,10},{1,13},{3,15... | collective-permute-start | bytes 786440 | tf_op jit(solution)/shard_map/ppermute | solution.py:296
  32.9 0.0 collective-permute-start.10
  32.9 0.0 copy-start.3
  32.9 1.1 %copy-done.3 = bf16[1024,384]{1,0:T(8,128)(2,1)S(1)} copy-done((bf16[1024,384]{1,0:T(8,128)(2,1)S(1)}, bf16[1024,384]{1,0:T(8,128)(2,1)}, u32[]{:S(2)}) %copy-start.3) | copy-done | bytes 786456
  34.1 0.0 copy-start.7
  34.1 2.0 %input_terms_pair.1 = (bf16[4,512,128]{2,1,0:T(8,128)(2,1)S(1)}, bf16[4,512,128]{2,1,0:T(8,128)(2,1)S(1)}) custom-call(bf16[1024,1024]{1,0:T(8,128)(2,1)S(1)} %copy-done, f32[1,1024]{1,0:T(1,128)S(1)} %bitcast.74, bf16[3,1024,128]{2,1,0:T(8,128)(2,1)S(1)} %copy-done.1, bf16[1024,384]{1,0:T(8,128)(2,1)S(1)} %copy-done.3), custom_call_target="tpu_custom_call" | custom-call | tf_op jit(solution)/shard_map/input_terms_pair/pallas_call | solution.py:244
  36.1 2.8 %collective-permute-start.6 = (bf16[4,512,128]{2,1,0:T(8,128)(2,1)S(1)}, bf16[4,512,128]{2,1,0:T(8,128)(2,1)S(1)}, u32[]{:S(2)}, u32[]{:S(2)}) collective-permute-start(bf16[4,512,128]{2,1,0:T(8,128)(2,1)S(1)} %get-tuple-element.29), channel_id=1, source_target_pairs={{0,2},{2,0},{4,6},{6,4},{8,10},{10,8},{12,14},{14,12},{1,3},{3,1},... | collective-permute-start | bytes 1572872 | tf_op jit(solution)/shard_map/ppermute | solution.py:300
  38.9 0.0 collective-permute-done.2
  38.9 3.1 %collective-permute-done.3 = bf16[2,512,128]{2,1,0:T(8,128)(2,1)} collective-permute-done((bf16[2,512,128]{2,1,0:T(8,128)(2,1)}, bf16[2,512,128]{2,1,0:T(8,128)(2,1)}, u32[]{:S(2)}, u32[]{:S(2)}) %collective-permute-start.3) | collective-permute-done | bytes 262176 | tf_op jit(solution)/shard_map/ppermute | solution.py:296
  42.0 0.0 collective-permute-done.4
  42.0 0.0 copy-done.7
  42.0 1.2 %add_convert_fusion.2 = bf16[2,512,128]{2,1,0:T(8,128)(2,1)S(1)} fusion(bf16[2,512,128]{2,1,0:T(8,128)(2,1)} %collective-permute-done.4, bf16[2,512,128]{2,1,0:T(8,128)(2,1)} %collective-permute-done.3, bf16[2,512,128]{2,1,0:T(8,128)(2,1)} %collective-permute-done.2, bf16[2,512,128]{2,1,0:T(8,128)(2,1)S(1)} %copy-done.7), kind=kLoop, calls=%fused_computation.3 | loop fusion | flops 1048576 | bytes 1310720 | tf_op jit(solution)/shard_map/convert_element_type | solution.py:335
  43.3 1.9 %collective-permute-start.5 = (bf16[512,128]{1,0:T(8,128)(2,1)S(1)}, bf16[512,128]{1,0:T(8,128)(2,1)S(1)}, u32[]{:S(2)}, u32[]{:S(2)}) collective-permute-start(bf16[512,128]{1,0:T(8,128)(2,1)S(1)} %dynamic-slice_bitcast_fusion), channel_id=1, source_target_pairs={{0,2},{2,0},{4,6},{6,4},{8,10},{10,8},{12,14},{14,12},{1,3},{3,1},... | collective-permute-start | bytes 393224 | tf_op jit(solution)/shard_map/ppermute | solution.py:300
  45.2 0.0 collective-permute-done.10
  45.2 1.2 %add_convert_fusion.1 = (bf16[1,4,4,64,128]{4,3,2,1,0:T(8,128)(2,1)S(1)}, bf16[4,4,64,128]{3,2,1,0:T(8,128)(2,1)S(1)}) fusion(bf16[2,4,4,64,128]{4,3,2,1,0:T(8,128)(2,1)} %collective-permute-done.10, bf16[2,4,4,64,128]{4,3,2,1,0:T(8,128)(2,1)S(1)} %get-tuple-element.30), kind=kLoop, calls=%fused_computation.2 | loop fusion | flops 1048576 | bytes 1572864 | tf_op jit(solution)/shard_map/convert_element_type | solution.py:328
  46.4 4.0 %collective-permute-start.11 = (bf16[4,4,64,128]{3,2,1,0:T(8,128)(2,1)S(1)}, bf16[4,4,64,128]{3,2,1,0:T(8,128)(2,1)S(1)}, u32[]{:S(2)}, u32[]{:S(2)}) collective-permute-start(bf16[4,4,64,128]{3,2,1,0:T(8,128)(2,1)S(1)} %get-tuple-element.36), channel_id=1, source_target_pairs={{0,32},{16,48},{32,0},{48,16},{64,96},{80,112},{96,64},{112,80},{1... | collective-permute-start | bytes 786440 | tf_op jit(solution)/shard_map/ppermute | solution.py:300
  50.4 0.2 collective-permute-done.6
  50.6 0.1 fusion.5
  50.7 1.6 %collective-permute-start.7 = (bf16[512,128]{1,0:T(8,128)(2,1)S(1)}, bf16[512,128]{1,0:T(8,128)(2,1)S(1)}, u32[]{:S(2)}, u32[]{:S(2)}) collective-permute-start(bf16[512,128]{1,0:T(8,128)(2,1)S(1)} %get-tuple-element.37), channel_id=1, source_target_pairs={{0,8},{2,10},{4,12},{6,14},{8,0},{10,2},{12,4},{14,6},{1,9},{3,11}... | collective-permute-start | bytes 393224 | tf_op jit(solution)/shard_map/ppermute | solution.py:296
  52.4 1.4 %collective-permute-start.8 = (bf16[512,128]{1,0:T(8,128)(2,1)S(1)}, bf16[512,128]{1,0:T(8,128)(2,1)S(1)}, u32[]{:S(2)}, u32[]{:S(2)}) collective-permute-start(bf16[512,128]{1,0:T(8,128)(2,1)S(1)} %get-tuple-element.39), channel_id=1, source_target_pairs={{0,4},{2,6},{4,8},{6,10},{8,12},{10,14},{12,0},{14,2},{1,5},{3,7},... | collective-permute-start | bytes 393224 | tf_op jit(solution)/shard_map/ppermute | solution.py:296
  53.8 1.3 %collective-permute-start.9 = (bf16[512,128]{1,0:T(8,128)(2,1)S(1)}, bf16[512,128]{1,0:T(8,128)(2,1)S(1)}, u32[]{:S(2)}, u32[]{:S(2)}) collective-permute-start(bf16[512,128]{1,0:T(8,128)(2,1)S(1)} %get-tuple-element.38), channel_id=1, source_target_pairs={{0,12},{2,14},{4,0},{6,2},{8,4},{10,6},{12,8},{14,10},{1,13},{3,15... | collective-permute-start | bytes 393224 | tf_op jit(solution)/shard_map/ppermute | solution.py:296
  55.1 0.0 collective-permute-done.5
  55.1 1.1 %collective-permute-done.7 = bf16[512,128]{1,0:T(8,128)(2,1)S(1)} collective-permute-done((bf16[512,128]{1,0:T(8,128)(2,1)S(1)}, bf16[512,128]{1,0:T(8,128)(2,1)S(1)}, u32[]{:S(2)}, u32[]{:S(2)}) %collective-permute-start.7) | collective-permute-done | bytes 131104 | tf_op jit(solution)/shard_map/ppermute | solution.py:296
  56.2 1.4 %collective-permute-done.8 = bf16[512,128]{1,0:T(8,128)(2,1)S(1)} collective-permute-done((bf16[512,128]{1,0:T(8,128)(2,1)S(1)}, bf16[512,128]{1,0:T(8,128)(2,1)S(1)}, u32[]{:S(2)}, u32[]{:S(2)}) %collective-permute-start.8) | collective-permute-done | bytes 131104 | tf_op jit(solution)/shard_map/ppermute | solution.py:296
  57.6 1.7 %collective-permute-done.9 = bf16[512,128]{1,0:T(8,128)(2,1)S(1)} collective-permute-done((bf16[512,128]{1,0:T(8,128)(2,1)S(1)}, bf16[512,128]{1,0:T(8,128)(2,1)S(1)}, u32[]{:S(2)}, u32[]{:S(2)}) %collective-permute-start.9) | collective-permute-done | bytes 131104 | tf_op jit(solution)/shard_map/ppermute | solution.py:296
  59.3 0.1 fusion.4
  59.3 0.0 collective-permute-done.11
  59.4 0.1 fusion.15
  59.4 10.3 %collective-permute-start.12 = (bf16[4,64,128]{2,1,0:T(8,128)(2,1)S(1)}, bf16[4,64,128]{2,1,0:T(8,128)(2,1)S(1)}, u32[]{:S(2)}, u32[]{:S(2)}) collective-permute-start(bf16[4,64,128]{2,1,0:T(8,128)(2,1)S(1)} %get-tuple-element.40), channel_id=1, source_target_pairs={{0,128},{16,144},{32,160},{48,176},{64,192},{80,208},{96,224},{112... | collective-permute-start | bytes 196616 | tf_op jit(solution)/shard_map/ppermute | solution.py:296
  69.8 0.0 collective-permute-start.13
  69.8 3.6 %collective-permute-start.14 = (bf16[4,64,128]{2,1,0:T(8,128)(2,1)S(1)}, bf16[4,64,128]{2,1,0:T(8,128)(2,1)S(1)}, u32[]{:S(2)}, u32[]{:S(2)}) collective-permute-start(bf16[4,64,128]{2,1,0:T(8,128)(2,1)S(1)} %get-tuple-element.41), channel_id=1, source_target_pairs={{0,192},{16,208},{32,224},{48,240},{64,0},{80,16},{96,32},{112,48}... | collective-permute-start | bytes 196616 | tf_op jit(solution)/shard_map/ppermute | solution.py:296
  73.4 0.7 pad_maximum_fusion.3
  74.1 0.0 collective-permute-done.12
  74.1 1.1 %collective-permute-done.13 = bf16[4,64,128]{2,1,0:T(8,128)(2,1)S(1)} collective-permute-done((bf16[4,64,128]{2,1,0:T(8,128)(2,1)S(1)}, bf16[4,64,128]{2,1,0:T(8,128)(2,1)S(1)}, u32[]{:S(2)}, u32[]{:S(2)}) %collective-permute-start.13) | collective-permute-done | bytes 65568 | tf_op jit(solution)/shard_map/ppermute | solution.py:296
  75.2 0.0 collective-permute-done.14
  75.2 0.6 slice.122
  75.9 0.6 slice_bitcast_fusion.8
  (6 shorter events, 0.2 us)
Async XLA Ops:
  0.6 8.2 %copy-start.8 = (f32[1024]{0:T(1024)S(1)}, f32[1024]{0:T(1024)}, u32[]{:S(2)}) copy-start(f32[1024]{0:T(1024)} %param.8) | copy-start | bytes 12292
  0.6 8.2 %copy-start.5 = (s32[16384]{0:T(1024)S(1)}, s32[16384]{0:T(1024)}, u32[]{:S(2)}) copy-start(s32[16384]{0:T(1024)} %param.12) | copy-start | bytes 196612
  0.7 8.2 %copy-start.4 = (bf16[128,1024]{1,0:T(8,128)(2,1)S(1)}, bf16[128,1024]{1,0:T(8,128)(2,1)}, u32[]{:S(2)}) copy-start(bf16[128,1024]{1,0:T(8,128)(2,1)} %out_ref.3) | copy-start | bytes 786436
  0.7 8.2 %copy-start.1 = (bf16[3,1024,128]{2,1,0:T(8,128)(2,1)S(1)}, bf16[3,1024,128]{2,1,0:T(8,128)(2,1)}, u32[]{:S(2)}) copy-start(bf16[3,1024,128]{2,1,0:T(8,128)(2,1)} %qkv_ref.7) | copy-start | bytes 2359300
  1.9 12.3 %collective-permute-start = (bf16[2,64,1024]{2,1,0:T(8,128)(2,1)S(1)}, bf16[2,64,1024]{2,1,0:T(8,128)(2,1)S(1)}, u32[]{:S(2)}, u32[]{:S(2)}) collective-permute-start(bf16[2,64,1024]{2,1,0:T(8,128)(2,1)S(1)} %pad_maximum_fusion.1), channel_id=1, source_target_pairs={{0,16},{16,32},{32,48},{48,64},{64,80},{80,96},{96,112},{112,128},... | collective-permute-start | bytes 786440 | tf_op jit(solution)/shard_map/ppermute | solution.py:316
  6.9 7.7 %collective-permute-start.1 = (bf16[2,64,1024]{2,1,0:T(8,128)(2,1)S(1)}, bf16[2,64,1024]{2,1,0:T(8,128)(2,1)S(1)}, u32[]{:S(2)}, u32[]{:S(2)}) collective-permute-start(bf16[2,64,1024]{2,1,0:T(8,128)(2,1)S(1)} %pad_maximum_fusion.2), channel_id=1, source_target_pairs={{16,0},{32,16},{48,32},{64,48},{80,64},{96,80},{112,96},{128,112},... | collective-permute-start | bytes 786440 | tf_op jit(solution)/shard_map/ppermute | solution.py:316
  8.9 5.8 %copy-start.9 = (s32[8]{0:T(128)S(1)}, s32[8]{0:T(128)}, u32[]{:S(2)}) copy-start(s32[8]{0:T(128)} %len_ref.1) | copy-start | bytes 100
  19.2 4.7 %copy-start.2 = (bf16[1024,384]{1,0:T(8,128)(2,1)}, bf16[1024,384]{1,0:T(8,128)(2,1)S(1)}, u32[]{:S(2)}) copy-start(bf16[1024,384]{1,0:T(8,128)(2,1)S(1)} %get-tuple-element.23.grads_ref) | copy-start | bytes 2359300
  19.2 4.7 %copy-start = (bf16[1024,1024]{1,0:T(8,128)(2,1)S(1)}, bf16[1024,1024]{1,0:T(8,128)(2,1)}, u32[]{:S(2)}) copy-start(bf16[1024,1024]{1,0:T(8,128)(2,1)} %frames_ref.3) | copy-start | bytes 6291460
  26.6 0.7 copy-start.6
  27.3 11.6 %collective-permute-start.2 = (bf16[2,512,128]{2,1,0:T(8,128)(2,1)}, bf16[2,512,128]{2,1,0:T(8,128)(2,1)}, u32[]{:S(2)}, u32[]{:S(2)}) collective-permute-start(bf16[2,512,128]{2,1,0:T(8,128)(2,1)} %get-tuple-element.25), channel_id=1, source_target_pairs={{0,8},{2,10},{4,12},{6,14},{8,0},{10,2},{12,4},{14,6},{1,9},{3,11}... | collective-permute-start | bytes 786440 | tf_op jit(solution)/shard_map/ppermute | solution.py:296
  30.2 11.8 %collective-permute-start.3 = (bf16[2,512,128]{2,1,0:T(8,128)(2,1)}, bf16[2,512,128]{2,1,0:T(8,128)(2,1)}, u32[]{:S(2)}, u32[]{:S(2)}) collective-permute-start(bf16[2,512,128]{2,1,0:T(8,128)(2,1)} %get-tuple-element.26), channel_id=1, source_target_pairs={{0,4},{2,6},{4,8},{6,10},{8,12},{10,14},{12,0},{14,2},{1,5},{3,7},... | collective-permute-start | bytes 786440 | tf_op jit(solution)/shard_map/ppermute | solution.py:296
  30.6 11.4 %collective-permute-start.4 = (bf16[2,512,128]{2,1,0:T(8,128)(2,1)}, bf16[2,512,128]{2,1,0:T(8,128)(2,1)}, u32[]{:S(2)}, u32[]{:S(2)}) collective-permute-start(bf16[2,512,128]{2,1,0:T(8,128)(2,1)} %get-tuple-element.27), channel_id=1, source_target_pairs={{0,12},{2,14},{4,0},{6,2},{8,4},{10,6},{12,8},{14,10},{1,13},{3,15... | collective-permute-start | bytes 786440 | tf_op jit(solution)/shard_map/ppermute | solution.py:296
  32.9 12.3 %collective-permute-start.10 = (bf16[2,4,4,64,128]{4,3,2,1,0:T(8,128)(2,1)}, bf16[2,4,4,64,128]{4,3,2,1,0:T(8,128)(2,1)}, u32[]{:S(2)}, u32[]{:S(2)}) collective-permute-start(bf16[2,4,4,64,128]{4,3,2,1,0:T(8,128)(2,1)} %get-tuple-element.21), channel_id=1, source_target_pairs={{0,16},{16,0},{32,48},{48,32},{64,80},{80,64},{96,112},{112,96},{1... | collective-permute-start | bytes 1572872 | tf_op jit(solution)/shard_map/ppermute | solution.py:300
  32.9 1.1 %copy-start.3 = (bf16[1024,384]{1,0:T(8,128)(2,1)S(1)}, bf16[1024,384]{1,0:T(8,128)(2,1)}, u32[]{:S(2)}) copy-start(bf16[1024,384]{1,0:T(8,128)(2,1)} %copy-done.2) | copy-start | bytes 2359300
  34.1 8.0 %copy-start.7 = (bf16[2,512,128]{2,1,0:T(8,128)(2,1)S(1)}, bf16[2,512,128]{2,1,0:T(8,128)(2,1)}, u32[]{:S(2)}) copy-start(bf16[2,512,128]{2,1,0:T(8,128)(2,1)} %copy-done.6) | copy-start | bytes 786436
  36.1 14.6 %collective-permute-start.6 = (bf16[4,512,128]{2,1,0:T(8,128)(2,1)S(1)}, bf16[4,512,128]{2,1,0:T(8,128)(2,1)S(1)}, u32[]{:S(2)}, u32[]{:S(2)}) collective-permute-start(bf16[4,512,128]{2,1,0:T(8,128)(2,1)S(1)} %get-tuple-element.29), channel_id=1, source_target_pairs={{0,2},{2,0},{4,6},{6,4},{8,10},{10,8},{12,14},{14,12},{1,3},{3,1},... | collective-permute-start | bytes 1572872 | tf_op jit(solution)/shard_map/ppermute | solution.py:300
  43.3 11.7 %collective-permute-start.5 = (bf16[512,128]{1,0:T(8,128)(2,1)S(1)}, bf16[512,128]{1,0:T(8,128)(2,1)S(1)}, u32[]{:S(2)}, u32[]{:S(2)}) collective-permute-start(bf16[512,128]{1,0:T(8,128)(2,1)S(1)} %dynamic-slice_bitcast_fusion), channel_id=1, source_target_pairs={{0,2},{2,0},{4,6},{6,4},{8,10},{10,8},{12,14},{14,12},{1,3},{3,1},... | collective-permute-start | bytes 393224 | tf_op jit(solution)/shard_map/ppermute | solution.py:300
  46.4 12.9 %collective-permute-start.11 = (bf16[4,4,64,128]{3,2,1,0:T(8,128)(2,1)S(1)}, bf16[4,4,64,128]{3,2,1,0:T(8,128)(2,1)S(1)}, u32[]{:S(2)}, u32[]{:S(2)}) collective-permute-start(bf16[4,4,64,128]{3,2,1,0:T(8,128)(2,1)S(1)} %get-tuple-element.36), channel_id=1, source_target_pairs={{0,32},{16,48},{32,0},{48,16},{64,96},{80,112},{96,64},{112,80},{1... | collective-permute-start | bytes 786440 | tf_op jit(solution)/shard_map/ppermute | solution.py:300
  50.7 5.4 %collective-permute-start.7 = (bf16[512,128]{1,0:T(8,128)(2,1)S(1)}, bf16[512,128]{1,0:T(8,128)(2,1)S(1)}, u32[]{:S(2)}, u32[]{:S(2)}) collective-permute-start(bf16[512,128]{1,0:T(8,128)(2,1)S(1)} %get-tuple-element.37), channel_id=1, source_target_pairs={{0,8},{2,10},{4,12},{6,14},{8,0},{10,2},{12,4},{14,6},{1,9},{3,11}... | collective-permute-start | bytes 393224 | tf_op jit(solution)/shard_map/ppermute | solution.py:296
  52.4 5.2 %collective-permute-start.8 = (bf16[512,128]{1,0:T(8,128)(2,1)S(1)}, bf16[512,128]{1,0:T(8,128)(2,1)S(1)}, u32[]{:S(2)}, u32[]{:S(2)}) collective-permute-start(bf16[512,128]{1,0:T(8,128)(2,1)S(1)} %get-tuple-element.39), channel_id=1, source_target_pairs={{0,4},{2,6},{4,8},{6,10},{8,12},{10,14},{12,0},{14,2},{1,5},{3,7},... | collective-permute-start | bytes 393224 | tf_op jit(solution)/shard_map/ppermute | solution.py:296
  53.8 5.5 %collective-permute-start.9 = (bf16[512,128]{1,0:T(8,128)(2,1)S(1)}, bf16[512,128]{1,0:T(8,128)(2,1)S(1)}, u32[]{:S(2)}, u32[]{:S(2)}) collective-permute-start(bf16[512,128]{1,0:T(8,128)(2,1)S(1)} %get-tuple-element.38), channel_id=1, source_target_pairs={{0,12},{2,14},{4,0},{6,2},{8,4},{10,6},{12,8},{14,10},{1,13},{3,15... | collective-permute-start | bytes 393224 | tf_op jit(solution)/shard_map/ppermute | solution.py:296
  59.4 14.6 %collective-permute-start.12 = (bf16[4,64,128]{2,1,0:T(8,128)(2,1)S(1)}, bf16[4,64,128]{2,1,0:T(8,128)(2,1)S(1)}, u32[]{:S(2)}, u32[]{:S(2)}) collective-permute-start(bf16[4,64,128]{2,1,0:T(8,128)(2,1)S(1)} %get-tuple-element.40), channel_id=1, source_target_pairs={{0,128},{16,144},{32,160},{48,176},{64,192},{80,208},{96,224},{112... | collective-permute-start | bytes 196616 | tf_op jit(solution)/shard_map/ppermute | solution.py:296
  69.8 5.4 %collective-permute-start.13 = (bf16[4,64,128]{2,1,0:T(8,128)(2,1)S(1)}, bf16[4,64,128]{2,1,0:T(8,128)(2,1)S(1)}, u32[]{:S(2)}, u32[]{:S(2)}) collective-permute-start(bf16[4,64,128]{2,1,0:T(8,128)(2,1)S(1)} %get-tuple-element.42), channel_id=1, source_target_pairs={{0,64},{16,80},{32,96},{48,112},{64,128},{80,144},{96,160},{112,17... | collective-permute-start | bytes 196616 | tf_op jit(solution)/shard_map/ppermute | solution.py:296
  69.8 5.4 %collective-permute-start.14 = (bf16[4,64,128]{2,1,0:T(8,128)(2,1)S(1)}, bf16[4,64,128]{2,1,0:T(8,128)(2,1)S(1)}, u32[]{:S(2)}, u32[]{:S(2)}) collective-permute-start(bf16[4,64,128]{2,1,0:T(8,128)(2,1)S(1)} %get-tuple-element.41), channel_id=1, source_target_pairs={{0,192},{16,208},{32,224},{48,240},{64,0},{80,16},{96,32},{112,48}... | collective-permute-start | bytes 196616 | tf_op jit(solution)/shard_map/ppermute | solution.py:296

commit v3 on v1

--- a/solution.py
+++ b/solution.py
@@ -200,7 +200,10 @@
     )(lengths, proj, halo, gain, qkv_weight, out_weight, pad2d)
 
 
-def input_body(frames_ref, gain_ref, qkv_ref, grads_ref, term_ref, w_scr):
+def input_body(frames_ref, gain_ref, qkv_ref, grads_ref, *rest):
+    outs, w_scr = rest[:-1], rest[-1]
+    y = lax.axis_index("mp") // 2
+
     @pl.when(pl.program_id(0) == 0)
     def _():
         for m in range(3):
@@ -212,8 +215,14 @@
     mean_grad = jnp.mean(scaled, axis=-1, keepdims=True)
     mean_proj = jnp.mean(scaled * normal_form, axis=-1, keepdims=True)
     result = (inverse * (scaled - mean_grad - normal_form * mean_proj)).astype(BF16)
-    for p in range(term_ref.shape[0]):
-        term_ref[p] = result[:, p * 128 : (p + 1) * 128]
+    for p in range(4):
+        for k in range(4):
+
+            @pl.when((p - y + 4) % 4 == k)
+            def _():
+                for h in range(2):
+                    at = (2 * p + h) * 128
+                    outs[k][h] = result[:, at : at + 128]
 
 
 def input_terms(frames, gain, qkv_weight, grads):
@@ -229,35 +238,80 @@
             whole(*qkv_weight.shape),
             pl.BlockSpec((rows, 3 * HS), lambda i: (i, 0)),
         ],
-        out_specs=pl.BlockSpec((width // 128, rows, 128), lambda i: (0, i, 0)),
-        out_shape=jax.ShapeDtypeStruct((width // 128, count, 128), BF16),
+        out_specs=[pl.BlockSpec((2, rows, 128), lambda i: (0, i, 0))] * 4,
+        out_shape=[jax.ShapeDtypeStruct((2, count, 128), BF16)] * 4,
         scratch_shapes=[pltpu.VMEM((width, 3 * HS), BF16)],
         compiler_params=pltpu.CompilerParams(vmem_limit_bytes=48 << 20),
         name="input_terms",
     )(frames, gain, qkv_weight, grads)
 
 
-def weight_body(normed_ref, cot_ref, grads_ref, mixed_ref, term_ref):
-    shards, _, part, _ = term_ref.shape
-    qkv = cols_by_cols(normed_ref[...], grads_ref[...]).astype(BF16)
-    out = cols_by_cols(cot_ref[...], mixed_ref[...]).astype(BF16)
-    for s in range(shards):
-        for m in range(3):
-            term_ref[s, m] = qkv[s * part : (s + 1) * part, m * HS : (m + 1) * HS]
-        term_ref[s, 3] = out[s * part : (s + 1) * part]
-
-
-def weight_terms(normed, cotangent, grads, mixed, shards):
+def weight_body(normed_ref, cot_ref, grads_ref, mixed_ref, keep_ref, send_ref):
+    core = lax.axis_index("tm") % 2
+    qkv = cols_by_cols(grads_ref[...], normed_ref[...]).astype(BF16)
+    out = cols_by_cols(mixed_ref[...], cot_ref[...]).astype(BF16)
+    full = jnp.concatenate([qkv, out], axis=0)
+    for z in range(8):
+        both = full[:, z * 128 : (z + 1) * 128].T
+        low, high = both[:64], both[64:]
+        keep = jnp.where(core == 0, low, high)
+        send = jnp.where(core == 0, high, low)
+        for m in range(4):
+            keep_ref[z, m] = keep[:, m * HS : (m + 1) * HS]
+            send_ref[z, m] = send[:, m * HS : (m + 1) * HS]
+
+
+def weight_terms(normed, cotangent, grads, mixed):
     count, width = normed.shape
     vmem = pl.BlockSpec(memory_space=pltpu.VMEM)
+    part = jax.ShapeDtypeStruct((8, 4, width // 16, HS), BF16)
     return pl.pallas_call(
         weight_body,
         in_specs=[vmem] * 4,
-        out_specs=vmem,
-        out_shape=jax.ShapeDtypeStruct((shards, 4, width // shards, HS), BF16),
+        out_specs=[vmem] * 2,
+        out_shape=[part] * 2,
         compiler_params=pltpu.CompilerParams(vmem_limit_bytes=48 << 20),
         name="weight_terms",
     )(normed, cotangent, grads, mixed)
+
+
+def finish_body(parts_ref, qkv_ref, out_ref):
+    for m in range(4):
+        summed = parts_ref[0, m].astype(F32)
+        for z in range(1, 8):
+            summed = summed + parts_ref[z, m].astype(F32)
+        if m < 3:
+            qkv_ref[m] = summed
+        else:
+            out_ref[...] = summed.T
+
+
+def finish(parts):
+    vmem = pl.BlockSpec(memory_space=pltpu.VMEM)
+    part = parts.shape[2]
+    return pl.pallas_call(
+        finish_body,
+        in_specs=[vmem],
+        out_specs=[vmem] * 2,
+        out_shape=[jax.ShapeDtypeStruct((3, part, HS), F32), jax.ShapeDtypeStruct((HS, part), F32)],
+        name="finish",
+    )(parts)
+
+
+def shifted(x, axis, by):
+    size = lax.axis_size(axis)
+    return lax.ppermute(x, axis, [(i, (i + by) % size) for i in range(size)])
+
+
+def swapped(x, axis, bit):
+    return lax.ppermute(x, axis, [(i, i ^ bit) for i in range(lax.axis_size(axis))])
+
+
+def total(*parts):
+    summed = parts[0].astype(F32)
+    for part in parts[1:]:
+        summed = summed + part.astype(F32)
+    return summed
 
 
 def on_device(frames, norm_gain, qkv_weight, out_weight, cotangent, pad_mask, utt_lengths):
@@ -271,13 +325,22 @@
     pad2d = pad_mask.reshape(-1, 128)
     proj, normed = project(frames, gain, qkv_weight, out_weight, cotangent, pad2d)
     grads, mixed = attend(utt_lengths, proj, halo, gain, qkv_weight, out_weight, pad2d)
-    terms = input_terms(frames, gain, qkv_weight, grads)
-    weights = weight_terms(normed, cotangent, grads, mixed, shards)
-    terms = lax.all_to_all(terms, "mp", 0, 0, tiled=True)
-    weights = lax.all_to_all(weights, "tm", 0, 0, tiled=True)
-    frame_grad = terms.astype(F32).sum(axis=0).astype(BF16)
-    summed = weights.astype(F32).sum(axis=0)
-    return frame_grad, summed[:3], summed[3].T
+    keep, send = weight_terms(normed, cotangent, grads, mixed)
+    other = swapped(send, "tm", 1)
+    (frames_b, grads_b), _ = lax.optimization_barrier(((frames, grads), keep))
+    ring = input_terms(frames_b, gain, qkv_weight, grads_b)
+    ring_in = [shifted(ring[k], "mp", 2 * k) for k in (2, 1, 3)]
+    (keep, other), _ = lax.optimization_barrier(((keep, other), ring[0]))
+    chip = total(keep, other).astype(BF16)
+    same_core = [[c + 2 * z for z in range(shards // 2)] for c in range(2)]
+    weights = lax.all_to_all(chip, "tm", 0, 0, tiled=True, axis_index_groups=same_core)
+    xh = lax.axis_index("mp") % 2
+    both = total(ring[0], *ring_in).astype(BF16)
+    mine = lax.dynamic_index_in_dim(both, xh, 0, False)
+    theirs = swapped(lax.dynamic_index_in_dim(both, 1 - xh, 0, False), "mp", 1)
+    frame_grad = total(mine, theirs).astype(BF16)
+    qkv_grad, out_grad = finish(weights)
+    return frame_grad, qkv_grad, out_grad
 
 
 def solution(mesh):

time: 96.9 us -> 71.3 us (0.74)
  the two profiles are of different devices: /device:TPU:1 before, /device:TPU:102 now
where the time goes in v3:
time: 71.3 us; the launch traced here: 70.9 us
  starting transfers between devices  22.6 us (32%)
  waiting for transfers between devices  21.8 us (31%)
  Pallas kernels  18.7 us (26%)
  local copies, waits for them, and re-layouts  3.62 us (5%)
  other arithmetic  3.33 us (5%)
  between operations  0.83 us (1%)
    ppermute x3, waiting for transfers between devices, shifted(): return lax.ppermute(x, axis, [(i, (i + by) % size) for i in range(size)])  13.9 us
    ppermute x2, waiting for transfers between devices, swapped(): lax.ppermute(x, axis, [(i, i ^ bit) for i in range(lax.axis_size(axis))])  7.97 us
    ppermute x3, starting transfers between devices, shifted(): return lax.ppermute(x, axis, [(i, (i + by) % size) for i in range(size)])  6.5 us
    all_to_all x1, starting transfers between devices, on_device(): lax.all_to_all(chip, 'tm', 0, 0, tiled=True, axis_index_groups=same_core)  5.8 us
    pallas_call x1, Pallas kernels, project(): pl.pallas_call(project_body, grid=(count // rows,), in_specs=[pl.BlockSpe...  5.28 us
    ppermute x2, starting transfers between devices, swapped(): lax.ppermute(x, axis, [(i, i ^ bit) for i in range(lax.axis_size(axis))])  4.7 us
    pallas_call x1, Pallas kernels, attend(): pl.pallas_call(attend_body, in_specs=[pl.BlockSpec(memory_space=pltpu.SME...  4.52 us
    pallas_call x1, Pallas kernels, input_terms(): pl.pallas_call(input_body, grid=(count // rows,), in_specs=[pl.BlockSpec(...  3.97 us
  transfers between devices with their start and end apart: 8, of which 4 were waited for; matrix products, arithmetic and copies ran while one was open for 5% of the time, Pallas kernels for 13%

profile of v3, /device:TPU:102, one launch (start us, length us, event | category | flops | bytes accessed | tf_op | source)
XLA Modules:
  0.0 70.9 jit_solution(1981964831204008973)
XLA Ops:
  0.6 0.0 copy-start.4
  0.6 0.0 copy-start.3
  0.7 0.0 copy-start.2
  0.7 0.0 copy-start.1
  0.7 1.2 %slice_bitcast_fusion.2 = (bf16[1,64,1024]{2,1,0:T(8,128)(2,1)S(1)}, bf16[1,64,1024]{2,1,0:T(8,128)(2,1)S(1)}, bf16[1,64,1024]{2,1,0:T(8,128)(2,1)S(1)}, bf16[1,64,1024]{2,1,0:T(8,128)(2,1)S(1)}) fusion(bf16[1024,1024]{1,0:T(8,128)(2,1)} %cot_ref.3, bf16[1024,1024]{1,0:T(8,128)(2,1)} %frames_ref.2), kind=kLoop, calls=%fused_computation.10 | loop fusion | bytes 1048576 | tf_op jit(solution)/shard_map/stack | solution.py:321
  1.9 1.9 %collective-permute-start = (bf16[2,64,1024]{2,1,0:T(8,128)(2,1)S(1)}, bf16[2,64,1024]{2,1,0:T(8,128)(2,1)S(1)}, u32[]{:S(2)}, u32[]{:S(2)}) collective-permute-start(bf16[2,64,1024]{2,1,0:T(8,128)(2,1)S(1)} %pad_maximum_fusion.1), channel_id=1, source_target_pairs={{0,16},{16,32},{32,48},{48,64},{64,80},{80,96},{96,112},{112,128},... | collective-permute-start | bytes 786440 | tf_op jit(solution)/shard_map/ppermute | solution.py:323
  3.9 3.6 %collective-permute-start.1 = (bf16[2,64,1024]{2,1,0:T(8,128)(2,1)S(1)}, bf16[2,64,1024]{2,1,0:T(8,128)(2,1)S(1)}, u32[]{:S(2)}, u32[]{:S(2)}) collective-permute-start(bf16[2,64,1024]{2,1,0:T(8,128)(2,1)S(1)} %pad_maximum_fusion.2), channel_id=1, source_target_pairs={{16,0},{32,16},{48,32},{64,48},{80,64},{96,80},{112,96},{128,112},... | collective-permute-start | bytes 786440 | tf_op jit(solution)/shard_map/ppermute | solution.py:323
  7.5 0.0 copy-done.4
  7.6 0.0 copy-done.3
  7.6 0.0 copy-done.2
  7.6 0.0 copy-done.1
  7.6 0.0 copy-start.5
  7.6 5.3 %project.1 = (bf16[4,1024,128]{2,1,0:T(8,128)(2,1)S(1)}, bf16[1024,1024]{1,0:T(8,128)(2,1)S(1)}) custom-call(bf16[1024,1024]{1,0:T(8,128)(2,1)} %frames_ref.2, f32[1,1024]{1,0:T(1,128)S(1)} %bitcast.17, bf16[3,1024,128]{2,1,0:T(8,128)(2,1)S(1)} %copy-done.1, bf16[128,1024]{1,0:T(8,128)(2,1)S(1)} %copy-done.2, bf16[1024,1024]{1,0:T(8,128)(2,1)} %cot_ref.3, ...), custom_call_target="tpu_custom_call" | custom-call | tf_op jit(solution)/shard_map/project/pallas_call | solution.py:74
  12.9 0.0 collective-permute-done
  12.9 0.0 collective-permute-done.1
  13.0 0.0 copy-done.5
  13.0 4.5 %attend.1 = (bf16[1024,384]{1,0:T(8,128)(2,1)S(1)}, bf16[1024,128]{1,0:T(8,128)(2,1)S(1)}) custom-call(s32[8]{0:T(128)S(1)} %copy-done.5, bf16[4,1024,128]{2,1,0:T(8,128)(2,1)S(1)} %get-tuple-element.19.proj_ref, bf16[2,128,1024]{2,1,0:T(8,128)(2,1)S(1)} %pad_maximum_fusion.halo_ref, f32[1,1024]{1,0:T(1,128)S(1)} %bitcast.18, ...), custom_call_target="tpu_custom_call" | custom-call | tf_op jit(solution)/shard_map/attend/pallas_call | solution.py:189
  17.5 0.0 copy-start
  17.5 3.1 %weight_terms.1 = (bf16[8,4,64,128]{3,2,1,0:T(8,128)(2,1)S(1)}, bf16[8,4,64,128]{3,2,1,0:T(8,128)(2,1)S(1)}) custom-call(bf16[1024,1024]{1,0:T(8,128)(2,1)S(1)} %get-tuple-element.21.normed_ref, bf16[1024,1024]{1,0:T(8,128)(2,1)} %cot_ref.3, bf16[1024,384]{1,0:T(8,128)(2,1)S(1)} %get-tuple-element.25.grads_ref, bf16[1024,128]{1,0:T(8,128)(2,1)S(1)} %get-tuple-element.22.mixed_ref), custom_call_target="tpu_custom_call" | custom-call | tf_op jit(solution)/shard_map/weight_terms/pallas_call | solution.py:268
  20.6 3.2 %collective-permute-start.6 = (bf16[8,4,64,128]{3,2,1,0:T(8,128)(2,1)S(1)}, bf16[8,4,64,128]{3,2,1,0:T(8,128)(2,1)S(1)}, u32[]{:S(2)}, u32[]{:S(2)}) collective-permute-start(bf16[8,4,64,128]{3,2,1,0:T(8,128)(2,1)S(1)} %get-tuple-element.30), channel_id=1, source_target_pairs={{0,16},{16,0},{32,48},{48,32},{64,80},{80,64},{96,112},{112,96},{1... | collective-permute-start | bytes 1572872 | tf_op jit(solution)/shard_map/ppermute | solution.py:307
  23.9 0.0 copy-done
  23.9 4.0 %input_terms.1 = (bf16[2,1024,128]{2,1,0:T(8,128)(2,1)S(1)}, bf16[2,1024,128]{2,1,0:T(8,128)(2,1)S(1)}, bf16[2,1024,128]{2,1,0:T(8,128)(2,1)S(1)}, bf16[2,1024,128]{2,1,0:T(8,128)(2,1)S(1)}) custom-call(bf16[1024,1024]{1,0:T(8,128)(2,1)S(1)} %copy-done, f32[1,1024]{1,0:T(1,128)S(1)} %bitcast.19, bf16[3,1024,128]{2,1,0:T(8,128)(2,1)S(1)} %copy-done.1, ...), custom_call_target="tpu_custom_call" | custom-call | tf_op jit(solution)/shard_map/input_terms/pallas_call | solution.py:232
  27.8 3.3 %collective-permute-start.2 = (bf16[2,1024,128]{2,1,0:T(8,128)(2,1)S(1)}, bf16[2,1024,128]{2,1,0:T(8,128)(2,1)S(1)}, u32[]{:S(2)}, u32[]{:S(2)}) collective-permute-start(bf16[2,1024,128]{2,1,0:T(8,128)(2,1)S(1)} %get-tuple-element.27), channel_id=1, source_target_pairs={{0,8},{2,10},{4,12},{6,14},{8,0},{10,2},{12,4},{14,6},{1,9},{3,11}... | collective-permute-start | bytes 1572872 | tf_op jit(solution)/shard_map/ppermute | solution.py:303
  31.1 0.7 collective-permute-start.3
  31.8 2.6 %collective-permute-start.4 = (bf16[2,1024,128]{2,1,0:T(8,128)(2,1)S(1)}, bf16[2,1024,128]{2,1,0:T(8,128)(2,1)}, u32[]{:S(2)}, u32[]{:S(2)}) collective-permute-start(bf16[2,1024,128]{2,1,0:T(8,128)(2,1)S(1)} %get-tuple-element.29), channel_id=1, source_target_pairs={{0,12},{2,14},{4,0},{6,2},{8,4},{10,6},{12,8},{14,10},{1,13},{3,15... | collective-permute-start | bytes 1572872 | tf_op jit(solution)/shard_map/ppermute | solution.py:303
  34.3 0.0 collective-permute-done.6
  34.3 1.0 %add_convert_fusion = bf16[8,4,64,128]{3,2,1,0:T(8,128)(2,1)} fusion(bf16[8,4,64,128]{3,2,1,0:T(8,128)(2,1)S(1)} %collective-permute-done.6, bf16[8,4,64,128]{3,2,1,0:T(8,128)(2,1)S(1)} %get-tuple-element.31), kind=kLoop, calls=%fused_computation | loop fusion | flops 1048576 | bytes 1572864 | tf_op jit(solution)/shard_map/convert_element_type | solution.py:334
  35.3 5.8 %all-to-all-start = ((bf16[8,4,64,128]{3,2,1,0:T(8,128)(2,1)}), bf16[8,4,64,128]{3,2,1,0:T(8,128)(2,1)S(1)}, u32[]{:S(2)}, u32[]{:S(2)}) async-start(bf16[8,4,64,128]{3,2,1,0:T(8,128)(2,1)} %add_convert_fusion), calls=%async_computation | async-start | bytes 1048576 | tf_op jit(solution)/shard_map/all_to_all | solution.py:336
  41.1 3.1 %collective-permute-done.2 = bf16[2,1024,128]{2,1,0:T(8,128)(2,1)S(1)} collective-permute-done((bf16[2,1024,128]{2,1,0:T(8,128)(2,1)S(1)}, bf16[2,1024,128]{2,1,0:T(8,128)(2,1)S(1)}, u32[]{:S(2)}, u32[]{:S(2)}) %collective-permute-start.2) | collective-permute-done | bytes 524320 | tf_op jit(solution)/shard_map/ppermute | solution.py:303
  44.3 10.4 %collective-permute-done.3 = bf16[2,1024,128]{2,1,0:T(8,128)(2,1)} collective-permute-done((bf16[2,1024,128]{2,1,0:T(8,128)(2,1)S(1)}, bf16[2,1024,128]{2,1,0:T(8,128)(2,1)}, u32[]{:S(2)}, u32[]{:S(2)}) %collective-permute-start.3) | collective-permute-done | bytes 524320 | tf_op jit(solution)/shard_map/ppermute | solution.py:303
  54.6 0.4 collective-permute-done.4
  55.0 1.5 %add_convert_fusion.1 = bf16[2,1024,128]{2,1,0:T(8,128)(2,1)S(1)} fusion(bf16[2,1024,128]{2,1,0:T(8,128)(2,1)} %collective-permute-done.4, bf16[2,1024,128]{2,1,0:T(8,128)(2,1)} %collective-permute-done.3, bf16[2,1024,128]{2,1,0:T(8,128)(2,1)S(1)} %collective-permute-done.2, bf16[2,1024,128]{2,1,0:T(8,128)(2,1)S(1)} %get-tuple-element.26), kind=kLoop, calls=%fused_computation.1 | loop fusion | flops 2097152 | bytes 2621440 | tf_op jit(solution)/shard_map/convert_element_type | solution.py:338
  56.5 1.5 %collective-permute-start.5 = (bf16[1024,128]{1,0:T(8,128)(2,1)S(1)}, bf16[1024,128]{1,0:T(8,128)(2,1)S(1)}, u32[]{:S(2)}, u32[]{:S(2)}) collective-permute-start(bf16[1024,128]{1,0:T(8,128)(2,1)S(1)} %dynamic-slice_bitcast_fusion), channel_id=1, source_target_pairs={{0,2},{2,0},{4,6},{6,4},{8,10},{10,8},{12,14},{14,12},{1,3},{3,1},... | collective-permute-start | bytes 786440 | tf_op jit(solution)/shard_map/ppermute | solution.py:307
  58.0 8.0 %collective-permute-done.5 = bf16[1024,128]{1,0:T(8,128)(2,1)S(1)} collective-permute-done((bf16[1024,128]{1,0:T(8,128)(2,1)S(1)}, bf16[1024,128]{1,0:T(8,128)(2,1)S(1)}, u32[]{:S(2)}, u32[]{:S(2)}) %collective-permute-start.5) | collective-permute-done | bytes 262176 | tf_op jit(solution)/shard_map/ppermute | solution.py:307
  66.0 0.8 %fusion = bf16[1024,128]{1,0:T(8,128)(2,1)} fusion(bf16[1024,128]{1,0:T(8,128)(2,1)S(1)} %collective-permute-done.5, bf16[2,1024,128]{2,1,0:T(8,128)(2,1)S(1)} %add_convert_fusion.1, s32[]{:T(128)S(6)} %select_n.15), kind=kLoop, calls=%fused_computation.4 | loop fusion | flops 524288 | bytes 786436 | tf_op jit(solution)/shard_map/convert_element_type | solution.py:341
  66.7 0.0 all-to-all-done.parts_ref
  66.7 0.0 copy-start.6
  66.8 0.8 %copy-done.6 = bf16[8,4,64,128]{3,2,1,0:T(8,128)(2,1)} copy-done((bf16[8,4,64,128]{3,2,1,0:T(8,128)(2,1)}, bf16[8,4,64,128]{3,2,1,0:T(8,128)(2,1)S(1)}, u32[]{:S(2)}) %copy-start.6) | copy-done | bytes 524312
  67.6 1.8 %finish.1 = (f32[3,64,128]{2,1,0:T(8,128)}, f32[128,64]{1,0:T(8,128)}) custom-call(bf16[8,4,64,128]{3,2,1,0:T(8,128)(2,1)} %copy-done.6), custom_call_target="tpu_custom_call" | custom-call | tf_op jit(solution)/shard_map/finish/pallas_call | solution.py:292
  69.3 1.5 %copy.10 = f32[128,64]{0,1:T(8,128)} copy(f32[128,64]{1,0:T(8,128)} %get-tuple-element.37) | data formatting | bytes 65536
  (4 shorter events, 0.1 us)
Async XLA Ops:
  0.6 6.9 %copy-start.4 = (f32[1024]{0:T(1024)S(1)}, f32[1024]{0:T(1024)}, u32[]{:S(2)}) copy-start(f32[1024]{0:T(1024)} %param.8) | copy-start | bytes 12292
  0.6 6.9 %copy-start.3 = (s32[16384]{0:T(1024)S(1)}, s32[16384]{0:T(1024)}, u32[]{:S(2)}) copy-start(s32[16384]{0:T(1024)} %param.12) | copy-start | bytes 196612
  0.7 6.9 %copy-start.2 = (bf16[128,1024]{1,0:T(8,128)(2,1)S(1)}, bf16[128,1024]{1,0:T(8,128)(2,1)}, u32[]{:S(2)}) copy-start(bf16[128,1024]{1,0:T(8,128)(2,1)} %out_ref.3) | copy-start | bytes 786436
  0.7 6.9 %copy-start.1 = (bf16[3,1024,128]{2,1,0:T(8,128)(2,1)S(1)}, bf16[3,1024,128]{2,1,0:T(8,128)(2,1)}, u32[]{:S(2)}) copy-start(bf16[3,1024,128]{2,1,0:T(8,128)(2,1)} %qkv_ref.5) | copy-start | bytes 2359300
  1.9 11.0 %collective-permute-start = (bf16[2,64,1024]{2,1,0:T(8,128)(2,1)S(1)}, bf16[2,64,1024]{2,1,0:T(8,128)(2,1)S(1)}, u32[]{:S(2)}, u32[]{:S(2)}) collective-permute-start(bf16[2,64,1024]{2,1,0:T(8,128)(2,1)S(1)} %pad_maximum_fusion.1), channel_id=1, source_target_pairs={{0,16},{16,32},{32,48},{48,64},{64,80},{80,96},{96,112},{112,128},... | collective-permute-start | bytes 786440 | tf_op jit(solution)/shard_map/ppermute | solution.py:323
  3.9 9.0 %collective-permute-start.1 = (bf16[2,64,1024]{2,1,0:T(8,128)(2,1)S(1)}, bf16[2,64,1024]{2,1,0:T(8,128)(2,1)S(1)}, u32[]{:S(2)}, u32[]{:S(2)}) collective-permute-start(bf16[2,64,1024]{2,1,0:T(8,128)(2,1)S(1)} %pad_maximum_fusion.2), channel_id=1, source_target_pairs={{16,0},{32,16},{48,32},{64,48},{80,64},{96,80},{112,96},{128,112},... | collective-permute-start | bytes 786440 | tf_op jit(solution)/shard_map/ppermute | solution.py:323
  7.6 5.4 %copy-start.5 = (s32[8]{0:T(128)S(1)}, s32[8]{0:T(128)}, u32[]{:S(2)}) copy-start(s32[8]{0:T(128)} %len_ref.1) | copy-start | bytes 100
  17.5 6.4 %copy-start = (bf16[1024,1024]{1,0:T(8,128)(2,1)S(1)}, bf16[1024,1024]{1,0:T(8,128)(2,1)}, u32[]{:S(2)}) copy-start(bf16[1024,1024]{1,0:T(8,128)(2,1)} %frames_ref.2) | copy-start | bytes 6291460
  20.6 13.7 %collective-permute-start.6 = (bf16[8,4,64,128]{3,2,1,0:T(8,128)(2,1)S(1)}, bf16[8,4,64,128]{3,2,1,0:T(8,128)(2,1)S(1)}, u32[]{:S(2)}, u32[]{:S(2)}) collective-permute-start(bf16[8,4,64,128]{3,2,1,0:T(8,128)(2,1)S(1)} %get-tuple-element.30), channel_id=1, source_target_pairs={{0,16},{16,0},{32,48},{48,32},{64,80},{80,64},{96,112},{112,96},{1... | collective-permute-start | bytes 1572872 | tf_op jit(solution)/shard_map/ppermute | solution.py:307
  27.8 16.4 %collective-permute-start.2 = (bf16[2,1024,128]{2,1,0:T(8,128)(2,1)S(1)}, bf16[2,1024,128]{2,1,0:T(8,128)(2,1)S(1)}, u32[]{:S(2)}, u32[]{:S(2)}) collective-permute-start(bf16[2,1024,128]{2,1,0:T(8,128)(2,1)S(1)} %get-tuple-element.27), channel_id=1, source_target_pairs={{0,8},{2,10},{4,12},{6,14},{8,0},{10,2},{12,4},{14,6},{1,9},{3,11}... | collective-permute-start | bytes 1572872 | tf_op jit(solution)/shard_map/ppermute | solution.py:303
  31.1 23.5 %collective-permute-start.3 = (bf16[2,1024,128]{2,1,0:T(8,128)(2,1)S(1)}, bf16[2,1024,128]{2,1,0:T(8,128)(2,1)}, u32[]{:S(2)}, u32[]{:S(2)}) collective-permute-start(bf16[2,1024,128]{2,1,0:T(8,128)(2,1)S(1)} %get-tuple-element.28), channel_id=1, source_target_pairs={{0,4},{2,6},{4,8},{6,10},{8,12},{10,14},{12,0},{14,2},{1,5},{3,7},... | collective-permute-start | bytes 1572872 | tf_op jit(solution)/shard_map/ppermute | solution.py:303
  31.8 23.2 %collective-permute-start.4 = (bf16[2,1024,128]{2,1,0:T(8,128)(2,1)S(1)}, bf16[2,1024,128]{2,1,0:T(8,128)(2,1)}, u32[]{:S(2)}, u32[]{:S(2)}) collective-permute-start(bf16[2,1024,128]{2,1,0:T(8,128)(2,1)S(1)} %get-tuple-element.29), channel_id=1, source_target_pairs={{0,12},{2,14},{4,0},{6,2},{8,4},{10,6},{12,8},{14,10},{1,13},{3,15... | collective-permute-start | bytes 1572872 | tf_op jit(solution)/shard_map/ppermute | solution.py:303
  35.3 31.4 %all-to-all-start = ((bf16[8,4,64,128]{3,2,1,0:T(8,128)(2,1)}), bf16[8,4,64,128]{3,2,1,0:T(8,128)(2,1)S(1)}, u32[]{:S(2)}, u32[]{:S(2)}) async-start(bf16[8,4,64,128]{3,2,1,0:T(8,128)(2,1)} %add_convert_fusion), calls=%async_computation | async-start | bytes 1048576 | tf_op jit(solution)/shard_map/all_to_all | solution.py:336
  56.5 9.5 %collective-permute-start.5 = (bf16[1024,128]{1,0:T(8,128)(2,1)S(1)}, bf16[1024,128]{1,0:T(8,128)(2,1)S(1)}, u32[]{:S(2)}, u32[]{:S(2)}) collective-permute-start(bf16[1024,128]{1,0:T(8,128)(2,1)S(1)} %dynamic-slice_bitcast_fusion), channel_id=1, source_target_pairs={{0,2},{2,0},{4,6},{6,4},{8,10},{10,8},{12,14},{14,12},{1,3},{3,1},... | collective-permute-start | bytes 786440 | tf_op jit(solution)/shard_map/ppermute | solution.py:307
  66.7 0.8 %copy-start.6 = (bf16[8,4,64,128]{3,2,1,0:T(8,128)(2,1)}, bf16[8,4,64,128]{3,2,1,0:T(8,128)(2,1)S(1)}, u32[]{:S(2)}) copy-start(bf16[8,4,64,128]{3,2,1,0:T(8,128)(2,1)S(1)} %all-to-all-done.parts_ref) | copy-start | bytes 1572868

commit v4 on v2

--- a/solution.py
+++ b/solution.py
@@ -259,28 +259,24 @@
 
 
 def weight_body(normed_ref, cot_ref, grads_ref, mixed_ref, keep_ref, send_ref):
-    place = lax.axis_index("tm")
-    core, zl, zh = place % 2, (place // 2) % 2, place // 4
-    qkv = cols_by_cols(normed_ref[...], grads_ref[...]).astype(BF16)
-    out = cols_by_cols(cot_ref[...], mixed_ref[...]).astype(BF16)
-    full = jnp.concatenate([qkv, out], axis=1)
-    for h in range(4):
-        away = (h - zh + 4) % 4
-        for l in range(2):
-            side = (l - zl + 2) % 2
-            at = (2 * h + l) * 128
-            low, high = full[at : at + 64], full[at + 64 : at + 128]
-            keep = jnp.where(core == 0, low, high)
-            send = jnp.where(core == 0, high, low)
-            for m in range(4):
-                keep_ref[side, away, m] = keep[:, m * HS : (m + 1) * HS]
-                send_ref[side, away, m] = send[:, m * HS : (m + 1) * HS]
+    core = lax.axis_index("tm") % 2
+    qkv = cols_by_cols(grads_ref[...], normed_ref[...]).astype(BF16)
+    out = cols_by_cols(mixed_ref[...], cot_ref[...]).astype(BF16)
+    full = jnp.concatenate([qkv, out], axis=0)
+    for z in range(8):
+        both = full[:, z * 128 : (z + 1) * 128].T
+        low, high = both[:64], both[64:]
+        keep = jnp.where(core == 0, low, high)
+        send = jnp.where(core == 0, high, low)
+        for m in range(4):
+            keep_ref[z, m] = keep[:, m * HS : (m + 1) * HS]
+            send_ref[z, m] = send[:, m * HS : (m + 1) * HS]
 
 
 def weight_terms(normed, cotangent, grads, mixed):
     count, width = normed.shape
     vmem = pl.BlockSpec(memory_space=pltpu.VMEM)
-    part = jax.ShapeDtypeStruct((2, 4, 4, width // 16, HS), BF16)
+    part = jax.ShapeDtypeStruct((8, 4, width // 16, HS), BF16)
     return pl.pallas_call(
         weight_body,
         in_specs=[vmem] * 4,
@@ -320,26 +316,31 @@
     grads, mixed = attend(utt_lengths, proj, halo, gain, qkv_weight, out_weight, pad2d)
     keep, send = weight_terms(normed, cotangent, grads, mixed)
     other = swapped(send, "tm", 1)
-    (frames_b, grads_b), _ = lax.optimization_barrier(((frames, grads), send))
-    near, across = input_terms(frames_b, gain, qkv_weight, grads_b, 1, True)
+    (frames_p, grads_p), _ = lax.optimization_barrier(((frames, grads), keep))
+    near, across = input_terms(frames_p, gain, qkv_weight, grads_p, 1, True)
     across = swapped(across, "mp", 1)
-    ring = input_terms(frames_b, gain, qkv_weight, grads_b, 0, False)
+    (frames_r, grads_r), _ = lax.optimization_barrier(((frames, grads), near))
+    ring = input_terms(frames_r, gain, qkv_weight, grads_r, 0, False)
     ring_in = [shifted(ring[k], "mp", 2 * k) for k in (2, 1, 3)]
-    stay = total(keep[0], other[0]).astype(BF16)
-    cross = swapped(total(keep[1], other[1]).astype(BF16), "tm", 2)
-    pair = [total(stay[k], cross[k]) for k in range(4)]
-    far = [shifted(pair[k].astype(BF16), "tm", 4 * k) for k in (2, 1, 3)]
+    (keep, other), _ = lax.optimization_barrier(((keep, other), ring[0]))
+    chip = total(keep, other).astype(BF16)
+    same_core = [[c + 2 * z for z in range(shards // 2)] for c in range(2)]
+    weights = lax.all_to_all(chip, "tm", 0, 0, tiled=True, axis_index_groups=same_core)
     col = [total(near[k], across[k]) for k in range(4)]
     col_in = [shifted(col[k].astype(BF16), "mp", 2 * k) for k in (2, 1, 3)]
+    ring_in, _ = lax.optimization_barrier((ring_in, [c.astype(BF16) for c in col[1:]]))
     xh = lax.axis_index("mp") % 2
-    both = total(ring[0], *ring_in).astype(BF16)
-    mine = lax.dynamic_index_in_dim(both, xh, 0, False)
-    theirs = swapped(lax.dynamic_index_in_dim(both, 1 - xh, 0, False), "mp", 1)
-    first_half = total(mine, theirs).astype(BF16)
+
+    def both(side):
+        return total(*[lax.dynamic_index_in_dim(r, side, 0, False) for r in (ring[0], *ring_in)])
+
+    theirs = swapped(both(1 - xh).astype(BF16), "mp", 1)
+    first_half = total(both(xh), theirs).astype(BF16)
     second_half = total(col[0], *col_in).astype(BF16)
     frame_grad = jnp.concatenate([first_half, second_half], axis=0)
-    summed = total(pair[0], *far)
-    return frame_grad, summed[:3], summed[3].T
+    qkv_grad = weights[:, :3].astype(F32).sum(axis=0)
+    out_grad = weights[:, 3].astype(F32).sum(axis=0)
+    return frame_grad, qkv_grad, out_grad.T
 
 
 def solution(mesh):

time: 77.4 us -> 69.3 us (0.90)
  starting transfers between devices: 39.4 us -> 27.4 us
  other arithmetic: 3.61 us -> 6.5 us
  waiting for transfers between devices: 9.03 us -> 10.8 us
    ppermute x9 -> x6, starting transfers between devices: 23.8 us -> 8.26 us  [shifted(): return lax.ppermute(x, axis, [(i, (i + by) % size) for i in range(size)])]
    all_to_all x0 -> x1, starting transfers between devices: none -> 9.19 us  [on_device(): lax.all_to_all(chip, 'tm', 0, 0, tiled=True, axis_index_groups=same_core)]
    ppermute x4 -> x3, starting transfers between devices: 8.72 us -> 3.05 us  [swapped(): lax.ppermute(x, axis, [(i, i ^ bit) for i in range(lax.axis_size(axis))])]
    ppermute x9 -> x6, waiting for transfers between devices: 8.4 us -> 3.53 us  [shifted(): return lax.ppermute(x, axis, [(i, (i + by) % size) for i in range(size)])]
    all_to_all x0 -> x1, waiting for transfers between devices: none -> 4.48 us  [on_device(): lax.all_to_all(chip, 'tm', 0, 0, tiled=True, axis_index_groups=same_core)]
    ppermute x4 -> x3, waiting for transfers between devices: 0.21 us -> 2.42 us  [swapped(): lax.ppermute(x, axis, [(i, i ^ bit) for i in range(lax.axis_size(axis))])]
    reduce_sum x0 -> x2, other arithmetic: none -> 1.33 us  [the longest x1 0.69 us: on_device(): qkv_grad = weights[:, :3].astype(F32).sum(axis=0)]
    convert_element_type x1, other arithmetic: 0.09 us -> 1.01 us  [on_device(): second_half = total(col[0], *col_in).astype(BF16)]
  transfers between devices with their start and end apart: 15 -> 12, of which waited for: 7 -> 5; matrix products, arithmetic and copies ran while one was open for 5% -> 7% of each run, Pallas kernels for 10% -> 16%
where the time goes in v4:
time: 69.3 us; the launch traced here: 68.9 us
  starting transfers between devices  27.4 us (40%)
  Pallas kernels  19.4 us (28%)
  waiting for transfers between devices  10.8 us (16%)
  other arithmetic  6.5 us (9%)
  local copies, waits for them, and re-layouts  3.92 us (6%)
  between operations  0.87 us (1%)
    all_to_all x1, starting transfers between devices, on_device(): lax.all_to_all(chip, 'tm', 0, 0, tiled=True, axis_index_groups=same_core)  9.19 us
    ppermute x6, starting transfers between devices, shifted(): return lax.ppermute(x, axis, [(i, (i + by) % size) for i in range(size)])  8.26 us
    pallas_call x2, Pallas kernels, input_terms(): pl.pallas_call(input_body, grid=(steps,), in_specs=[pl.BlockSpec((rows, w...  5.45 us
    pallas_call x1, Pallas kernels, project(): pl.pallas_call(project_body, grid=(count // rows,), in_specs=[pl.BlockSpe...  5.28 us
    ppermute x1, starting transfers between devices, on_device(): lax.ppermute(ends, 'tm', up)  4.94 us
    pallas_call x1, Pallas kernels, attend(): pl.pallas_call(attend_body, in_specs=[pl.BlockSpec(memory_space=pltpu.SME...  4.54 us
    all_to_all x1, waiting for transfers between devices, on_device(): lax.all_to_all(chip, 'tm', 0, 0, tiled=True, axis_index_groups=same_core)  4.48 us
    pallas_call x1, Pallas kernels, weight_terms(): pl.pallas_call(weight_body, in_specs=[vmem] * 4, out_specs=[vmem] * 2, ou...  4.12 us
  transfers between devices with their start and end apart: 12, of which 5 were waited for; matrix products, arithmetic and copies ran while one was open for 7% of the time, Pallas kernels for 16%

profile of v4, /device:TPU:1, one launch (start us, length us, event | category | flops | bytes accessed | tf_op | source)
XLA Modules:
  0.0 68.9 jit_solution(3498221075848524446)
XLA Ops:
  0.6 0.0 copy-start.10
  0.6 0.0 copy-start.7
  0.7 0.0 copy-start.4
  0.7 0.0 copy-start.1
  0.7 1.2 %slice_bitcast_fusion.2 = (bf16[1,64,1024]{2,1,0:T(8,128)(2,1)S(1)}, bf16[1,64,1024]{2,1,0:T(8,128)(2,1)S(1)}, bf16[1,64,1024]{2,1,0:T(8,128)(2,1)S(1)}, bf16[1,64,1024]{2,1,0:T(8,128)(2,1)S(1)}) fusion(bf16[1024,1024]{1,0:T(8,128)(2,1)} %cot_ref.3, bf16[1024,1024]{1,0:T(8,128)(2,1)} %frames_ref.3), kind=kLoop, calls=%fused_computation.23 | loop fusion | bytes 1048576 | tf_op jit(solution)/shard_map/stack | solution.py:310
  1.9 4.9 %collective-permute-start = (bf16[2,64,1024]{2,1,0:T(8,128)(2,1)S(1)}, bf16[2,64,1024]{2,1,0:T(8,128)(2,1)S(1)}, u32[]{:S(2)}, u32[]{:S(2)}) collective-permute-start(bf16[2,64,1024]{2,1,0:T(8,128)(2,1)S(1)} %pad_maximum_fusion.1), channel_id=1, source_target_pairs={{0,16},{16,32},{32,48},{48,64},{64,80},{80,96},{96,112},{112,128},... | collective-permute-start | bytes 786440 | tf_op jit(solution)/shard_map/ppermute | solution.py:312
  6.9 1.9 %collective-permute-start.1 = (bf16[2,64,1024]{2,1,0:T(8,128)(2,1)S(1)}, bf16[2,64,1024]{2,1,0:T(8,128)(2,1)S(1)}, u32[]{:S(2)}, u32[]{:S(2)}) collective-permute-start(bf16[2,64,1024]{2,1,0:T(8,128)(2,1)S(1)} %pad_maximum_fusion.2), channel_id=1, source_target_pairs={{16,0},{32,16},{48,32},{64,48},{80,64},{96,80},{112,96},{128,112},... | collective-permute-start | bytes 786440 | tf_op jit(solution)/shard_map/ppermute | solution.py:312
  8.8 0.0 copy-done.10
  8.8 0.0 copy-done.7
  8.9 0.0 copy-done.4
  8.9 0.0 copy-done.1
  8.9 0.0 copy-start.11
  8.9 5.3 %project.1 = (bf16[4,1024,128]{2,1,0:T(8,128)(2,1)S(1)}, bf16[1024,1024]{1,0:T(8,128)(2,1)S(1)}) custom-call(bf16[1024,1024]{1,0:T(8,128)(2,1)} %frames_ref.3, f32[1,1024]{1,0:T(1,128)S(1)} %bitcast.33, bf16[3,1024,128]{2,1,0:T(8,128)(2,1)S(1)} %copy-done.1, bf16[128,1024]{1,0:T(8,128)(2,1)S(1)} %copy-done.4, bf16[1024,1024]{1,0:T(8,128)(2,1)} %cot_ref.3, ...), custom_call_target="tpu_custom_call" | custom-call | tf_op jit(solution)/shard_map/project/pallas_call | solution.py:74
  14.2 0.0 collective-permute-done
  14.2 0.4 collective-permute-done.1
  14.6 0.0 copy-done.11
  14.7 4.5 %attend.1 = (bf16[1024,384]{1,0:T(8,128)(2,1)S(1)}, bf16[1024,128]{1,0:T(8,128)(2,1)S(1)}) custom-call(s32[8]{0:T(128)S(1)} %copy-done.11, bf16[4,1024,128]{2,1,0:T(8,128)(2,1)S(1)} %get-tuple-element.24.proj_ref, bf16[2,128,1024]{2,1,0:T(8,128)(2,1)S(1)} %pad_maximum_fusion.halo_ref, f32[1,1024]{1,0:T(1,128)S(1)} %bitcast.34, ...), custom_call_target="tpu_custom_call" | custom-call | tf_op jit(solution)/shard_map/attend/pallas_call | solution.py:189
  19.2 0.0 copy-start.2
  19.2 0.0 copy-start
  19.2 4.1 %weight_terms.1 = (bf16[8,4,64,128]{3,2,1,0:T(8,128)(2,1)S(1)}, bf16[8,4,64,128]{3,2,1,0:T(8,128)(2,1)}) custom-call(bf16[1024,1024]{1,0:T(8,128)(2,1)S(1)} %get-tuple-element.26.normed_ref, bf16[1024,1024]{1,0:T(8,128)(2,1)} %cot_ref.3, bf16[1024,384]{1,0:T(8,128)(2,1)S(1)} %get-tuple-element.33.grads_ref, bf16[1024,128]{1,0:T(8,128)(2,1)S(1)} %get-tuple-element.27.mixed_ref), custom_call_target="tpu_custom_call" | custom-call | tf_op jit(solution)/shard_map/weight_terms/pallas_call | solution.py:280
  23.3 0.0 collective-permute-start.10
  23.3 0.0 copy-done.2
  23.3 0.0 copy-done
  23.3 2.7 %input_terms_pair.1 = (bf16[4,512,128]{2,1,0:T(8,128)(2,1)S(1)}, bf16[4,512,128]{2,1,0:T(8,128)(2,1)}) custom-call(bf16[1024,1024]{1,0:T(8,128)(2,1)S(1)} %copy-done, f32[1,1024]{1,0:T(1,128)S(1)} %bitcast.35, bf16[3,1024,128]{2,1,0:T(8,128)(2,1)S(1)} %copy-done.1, bf16[1024,384]{1,0:T(8,128)(2,1)S(1)} %get-tuple-element.33.grads_ref), custom_call_target="tpu_custom_call" | custom-call | tf_op jit(solution)/shard_map/input_terms_pair/pallas_call | solution.py:244
  26.0 0.0 copy-start.5
  26.1 0.8 %copy-done.5 = bf16[4,512,128]{2,1,0:T(8,128)(2,1)} copy-done((bf16[4,512,128]{2,1,0:T(8,128)(2,1)}, bf16[4,512,128]{2,1,0:T(8,128)(2,1)S(1)}, u32[]{:S(2)}) %copy-start.5) | copy-done | bytes 524312
  26.9 2.7 %collective-permute-start.5 = (bf16[4,512,128]{2,1,0:T(8,128)(2,1)}, bf16[4,512,128]{2,1,0:T(8,128)(2,1)}, u32[]{:S(2)}, u32[]{:S(2)}) collective-permute-start(bf16[4,512,128]{2,1,0:T(8,128)(2,1)} %get-tuple-element.38), channel_id=1, source_target_pairs={{0,2},{2,0},{4,6},{6,4},{8,10},{10,8},{12,14},{14,12},{1,3},{3,1},... | collective-permute-start | bytes 1572872 | tf_op jit(solution)/shard_map/ppermute | solution.py:296
  29.6 0.0 copy-start.3
  29.6 1.1 %copy-done.3 = bf16[1024,384]{1,0:T(8,128)(2,1)S(1)} copy-done((bf16[1024,384]{1,0:T(8,128)(2,1)S(1)}, bf16[1024,384]{1,0:T(8,128)(2,1)}, u32[]{:S(2)}) %copy-start.3) | copy-done | bytes 786456
  30.7 2.7 %input_terms_ring.1 = (bf16[2,512,128]{2,1,0:T(8,128)(2,1)S(1)}, bf16[2,512,128]{2,1,0:T(8,128)(2,1)}, bf16[2,512,128]{2,1,0:T(8,128)(2,1)}, bf16[2,512,128]{2,1,0:T(8,128)(2,1)}) custom-call(bf16[1024,1024]{1,0:T(8,128)(2,1)S(1)} %copy-done, f32[1,1024]{1,0:T(1,128)S(1)} %bitcast.36, bf16[3,1024,128]{2,1,0:T(8,128)(2,1)S(1)} %copy-done.1, ...), custom_call_target="tpu_custom_call" | custom-call | tf_op jit(solution)/shard_map/input_terms_ring/pallas_call | solution.py:244
  33.5 0.0 copy-start.8
  33.5 0.7 %copy-done.8 = bf16[2,512,128]{2,1,0:T(8,128)(2,1)} copy-done((bf16[2,512,128]{2,1,0:T(8,128)(2,1)}, bf16[2,512,128]{2,1,0:T(8,128)(2,1)S(1)}, u32[]{:S(2)}) %copy-start.8) | copy-done | bytes 262168
  34.2 0.0 copy-start.6
  34.2 0.0 copy-start.9
  34.2 2.9 %collective-permute-start.2 = (bf16[2,512,128]{2,1,0:T(8,128)(2,1)}, bf16[2,512,128]{2,1,0:T(8,128)(2,1)S(1)}, u32[]{:S(2)}, u32[]{:S(2)}) collective-permute-start(bf16[2,512,128]{2,1,0:T(8,128)(2,1)} %get-tuple-element.35), channel_id=1, source_target_pairs={{0,8},{2,10},{4,12},{6,14},{8,0},{10,2},{12,4},{14,6},{1,9},{3,11}... | collective-permute-start | bytes 786440 | tf_op jit(solution)/shard_map/ppermute | solution.py:292
  37.1 0.4 collective-permute-start.3
  37.5 2.3 %collective-permute-start.4 = (bf16[2,512,128]{2,1,0:T(8,128)(2,1)}, bf16[2,512,128]{2,1,0:T(8,128)(2,1)S(1)}, u32[]{:S(2)}, u32[]{:S(2)}) collective-permute-start(bf16[2,512,128]{2,1,0:T(8,128)(2,1)} %get-tuple-element.37), channel_id=1, source_target_pairs={{0,12},{2,14},{4,0},{6,2},{8,4},{10,6},{12,8},{14,10},{1,13},{3,15... | collective-permute-start | bytes 786440 | tf_op jit(solution)/shard_map/ppermute | solution.py:292
  39.8 0.0 collective-permute-done.10
  39.8 2.0 %add_convert_fusion = bf16[8,4,64,128]{3,2,1,0:T(8,128)(2,1)} fusion(bf16[8,4,64,128]{3,2,1,0:T(8,128)(2,1)} %collective-permute-done.10, bf16[8,4,64,128]{3,2,1,0:T(8,128)(2,1)S(1)} %get-tuple-element.43), kind=kLoop, calls=%fused_computation | loop fusion | flops 1048576 | bytes 1572864 | tf_op jit(solution)/shard_map/convert_element_type | solution.py:326
  41.8 9.2 %all-to-all-start = ((bf16[8,4,64,128]{3,2,1,0:T(8,128)(2,1)}), bf16[8,4,64,128]{3,2,1,0:T(8,128)(2,1)S(1)}, u32[]{:S(2)}, u32[]{:S(2)}) async-start(bf16[8,4,64,128]{3,2,1,0:T(8,128)(2,1)} %add_convert_fusion), calls=%async_computation | async-start | bytes 1048576 | tf_op jit(solution)/shard_map/all_to_all | solution.py:328
  51.0 0.0 collective-permute-done.5
  51.0 0.0 copy-done.6
  51.0 1.1 %fusion.5 = (bf16[512,128]{1,0:T(8,128)(2,1)S(1)}, bf16[512,128]{1,0:T(8,128)(2,1)S(1)}, bf16[512,128]{1,0:T(8,128)(2,1)S(1)}) fusion(bf16[4,512,128]{2,1,0:T(8,128)(2,1)} %collective-permute-done.5, bf16[4,512,128]{2,1,0:T(8,128)(2,1)S(1)} %copy-done.6), kind=kLoop, calls=%fused_computation.18 | loop fusion | flops 786432 | bytes 1179648 | tf_op jit(solution)/shard_map/convert_element_type | solution.py:331
  52.2 0.0 collective-permute-done.2
  52.2 0.0 collective-permute-done.3
  52.2 0.0 collective-permute-done.4
  52.2 0.0 copy-done.9
  52.2 0.1 fusion.7
  52.3 0.3 collective-permute-start.6
  52.6 0.0 collective-permute-start.7
  52.6 0.8 %collective-permute-start.8 = (bf16[512,128]{1,0:T(8,128)(2,1)S(1)}, bf16[512,128]{1,0:T(8,128)(2,1)S(1)}, u32[]{:S(2)}, u32[]{:S(2)}) collective-permute-start(bf16[512,128]{1,0:T(8,128)(2,1)S(1)} %get-tuple-element.51), channel_id=1, source_target_pairs={{0,4},{2,6},{4,8},{6,10},{8,12},{10,14},{12,0},{14,2},{1,5},{3,7},... | collective-permute-start | bytes 393224 | tf_op jit(solution)/shard_map/ppermute | solution.py:292
  53.4 1.8 %collective-permute-start.9 = (bf16[512,128]{1,0:T(8,128)(2,1)S(1)}, bf16[512,128]{1,0:T(8,128)(2,1)S(1)}, u32[]{:S(2)}, u32[]{:S(2)}) collective-permute-start(bf16[512,128]{1,0:T(8,128)(2,1)S(1)} %get-tuple-element.50), channel_id=1, source_target_pairs={{0,12},{2,14},{4,0},{6,2},{8,4},{10,6},{12,8},{14,10},{1,13},{3,15... | collective-permute-start | bytes 393224 | tf_op jit(solution)/shard_map/ppermute | solution.py:292
  55.3 2.4 %collective-permute-done.6 = bf16[512,128]{1,0:T(8,128)(2,1)S(1)} collective-permute-done((bf16[512,128]{1,0:T(8,128)(2,1)S(1)}, bf16[512,128]{1,0:T(8,128)(2,1)S(1)}, u32[]{:S(2)}, u32[]{:S(2)}) %collective-permute-start.6) | collective-permute-done | bytes 131104 | tf_op jit(solution)/shard_map/ppermute | solution.py:296
  57.7 0.1 fusion.3
  57.8 0.2 collective-permute-done.7
  58.0 3.3 %collective-permute-done.8 = bf16[512,128]{1,0:T(8,128)(2,1)S(1)} collective-permute-done((bf16[512,128]{1,0:T(8,128)(2,1)S(1)}, bf16[512,128]{1,0:T(8,128)(2,1)S(1)}, u32[]{:S(2)}, u32[]{:S(2)}) %collective-permute-start.8) | collective-permute-done | bytes 131104 | tf_op jit(solution)/shard_map/ppermute | solution.py:292
  61.3 0.0 collective-permute-done.9
  61.3 1.0 %fusion.2 = bf16[512,128]{1,0:T(8,128)(2,1)S(1)} fusion(bf16[512,128]{1,0:T(8,128)(2,1)S(1)} %collective-permute-done.9, bf16[512,128]{1,0:T(8,128)(2,1)S(1)} %collective-permute-done.8, bf16[512,128]{1,0:T(8,128)(2,1)S(1)} %collective-permute-done.7, bf16[4,512,128]{2,1,0:T(8,128)(2,1)} %collective-permute-done.5, bf16[4,512,128]{2,1,0:T(8,128)(2,1)S(1)} %copy-done.6), kind=kLoop, calls=%fused_computation.9 | loop fusion | flops 655360 | bytes 786432 | tf_op jit(solution)/shard_map/convert_element_type | solution.py:339
  62.3 0.7 %pad_maximum_fusion.3 = bf16[1024,128]{1,0:T(8,128)(2,1)} fusion(bf16[512,128]{1,0:T(8,128)(2,1)S(1)} %fusion.2, bf16[512,128]{1,0:T(8,128)(2,1)S(1)} %fusion.3), kind=kLoop, calls=%fused_computation.5 | loop fusion | flops 524288 | bytes 524288 | tf_op jit(solution)/shard_map/concatenate | solution.py:340
  63.1 4.5 %all-to-all-done = bf16[8,4,64,128]{3,2,1,0:T(8,128)(2,1)S(1)} async-done(((bf16[8,4,64,128]{3,2,1,0:T(8,128)(2,1)}), bf16[8,4,64,128]{3,2,1,0:T(8,128)(2,1)S(1)}, u32[]{:S(2)}, u32[]{:S(2)}) %all-to-all-start) | async-done | bytes 524320 | tf_op jit(solution)/shard_map/all_to_all | solution.py:328
  67.5 0.7 %convert_reduce_fusion = f32[3,64,128]{2,1,0:T(8,128)} fusion(bf16[8,4,64,128]{3,2,1,0:T(8,128)(2,1)S(1)} %all-to-all-done), kind=kLoop, calls=%fused_computation.1 | loop fusion | flops 368640 | bytes 491520 | tf_op jit(solution)/shard_map/reduce_sum | solution.py:341
  68.2 0.6 convert_reduce_fusion.1
  (3 shorter events, 0.1 us)
Async XLA Ops:
  0.6 8.2 %copy-start.10 = (f32[1024]{0:T(1024)S(1)}, f32[1024]{0:T(1024)}, u32[]{:S(2)}) copy-start(f32[1024]{0:T(1024)} %param.8) | copy-start | bytes 12292
  0.6 8.2 %copy-start.7 = (s32[16384]{0:T(1024)S(1)}, s32[16384]{0:T(1024)}, u32[]{:S(2)}) copy-start(s32[16384]{0:T(1024)} %param.12) | copy-start | bytes 196612
  0.7 8.2 %copy-start.4 = (bf16[128,1024]{1,0:T(8,128)(2,1)S(1)}, bf16[128,1024]{1,0:T(8,128)(2,1)}, u32[]{:S(2)}) copy-start(bf16[128,1024]{1,0:T(8,128)(2,1)} %out_ref.3) | copy-start | bytes 786436
  0.7 8.2 %copy-start.1 = (bf16[3,1024,128]{2,1,0:T(8,128)(2,1)S(1)}, bf16[3,1024,128]{2,1,0:T(8,128)(2,1)}, u32[]{:S(2)}) copy-start(bf16[3,1024,128]{2,1,0:T(8,128)(2,1)} %qkv_ref.7) | copy-start | bytes 2359300
  1.9 12.3 %collective-permute-start = (bf16[2,64,1024]{2,1,0:T(8,128)(2,1)S(1)}, bf16[2,64,1024]{2,1,0:T(8,128)(2,1)S(1)}, u32[]{:S(2)}, u32[]{:S(2)}) collective-permute-start(bf16[2,64,1024]{2,1,0:T(8,128)(2,1)S(1)} %pad_maximum_fusion.1), channel_id=1, source_target_pairs={{0,16},{16,32},{32,48},{48,64},{64,80},{80,96},{96,112},{112,128},... | collective-permute-start | bytes 786440 | tf_op jit(solution)/shard_map/ppermute | solution.py:312
  6.9 7.7 %collective-permute-start.1 = (bf16[2,64,1024]{2,1,0:T(8,128)(2,1)S(1)}, bf16[2,64,1024]{2,1,0:T(8,128)(2,1)S(1)}, u32[]{:S(2)}, u32[]{:S(2)}) collective-permute-start(bf16[2,64,1024]{2,1,0:T(8,128)(2,1)S(1)} %pad_maximum_fusion.2), channel_id=1, source_target_pairs={{16,0},{32,16},{48,32},{64,48},{80,64},{96,80},{112,96},{128,112},... | collective-permute-start | bytes 786440 | tf_op jit(solution)/shard_map/ppermute | solution.py:312
  8.9 5.8 %copy-start.11 = (s32[8]{0:T(128)S(1)}, s32[8]{0:T(128)}, u32[]{:S(2)}) copy-start(s32[8]{0:T(128)} %len_ref.1) | copy-start | bytes 100
  19.2 4.1 %copy-start.2 = (bf16[1024,384]{1,0:T(8,128)(2,1)}, bf16[1024,384]{1,0:T(8,128)(2,1)S(1)}, u32[]{:S(2)}) copy-start(bf16[1024,384]{1,0:T(8,128)(2,1)S(1)} %get-tuple-element.33.grads_ref) | copy-start | bytes 2359300
  19.2 4.1 %copy-start = (bf16[1024,1024]{1,0:T(8,128)(2,1)S(1)}, bf16[1024,1024]{1,0:T(8,128)(2,1)}, u32[]{:S(2)}) copy-start(bf16[1024,1024]{1,0:T(8,128)(2,1)} %frames_ref.3) | copy-start | bytes 6291460
  23.3 16.4 %collective-permute-start.10 = (bf16[8,4,64,128]{3,2,1,0:T(8,128)(2,1)}, bf16[8,4,64,128]{3,2,1,0:T(8,128)(2,1)}, u32[]{:S(2)}, u32[]{:S(2)}) collective-permute-start(bf16[8,4,64,128]{3,2,1,0:T(8,128)(2,1)} %get-tuple-element.42), channel_id=1, source_target_pairs={{0,16},{16,0},{32,48},{48,32},{64,80},{80,64},{96,112},{112,96},{1... | collective-permute-start | bytes 1572872 | tf_op jit(solution)/shard_map/ppermute | solution.py:296
  26.0 0.8 %copy-start.5 = (bf16[4,512,128]{2,1,0:T(8,128)(2,1)}, bf16[4,512,128]{2,1,0:T(8,128)(2,1)S(1)}, u32[]{:S(2)}) copy-start(bf16[4,512,128]{2,1,0:T(8,128)(2,1)S(1)} %get-tuple-element.31) | copy-start | bytes 1572868
  26.9 24.1 %collective-permute-start.5 = (bf16[4,512,128]{2,1,0:T(8,128)(2,1)}, bf16[4,512,128]{2,1,0:T(8,128)(2,1)}, u32[]{:S(2)}, u32[]{:S(2)}) collective-permute-start(bf16[4,512,128]{2,1,0:T(8,128)(2,1)} %get-tuple-element.38), channel_id=1, source_target_pairs={{0,2},{2,0},{4,6},{6,4},{8,10},{10,8},{12,14},{14,12},{1,3},{3,1},... | collective-permute-start | bytes 1572872 | tf_op jit(solution)/shard_map/ppermute | solution.py:296
  29.6 1.1 %copy-start.3 = (bf16[1024,384]{1,0:T(8,128)(2,1)S(1)}, bf16[1024,384]{1,0:T(8,128)(2,1)}, u32[]{:S(2)}) copy-start(bf16[1024,384]{1,0:T(8,128)(2,1)} %copy-done.2) | copy-start | bytes 2359300
  33.5 0.7 %copy-start.8 = (bf16[2,512,128]{2,1,0:T(8,128)(2,1)}, bf16[2,512,128]{2,1,0:T(8,128)(2,1)S(1)}, u32[]{:S(2)}) copy-start(bf16[2,512,128]{2,1,0:T(8,128)(2,1)S(1)} %get-tuple-element.34) | copy-start | bytes 786436
  34.2 16.8 %copy-start.6 = (bf16[4,512,128]{2,1,0:T(8,128)(2,1)S(1)}, bf16[4,512,128]{2,1,0:T(8,128)(2,1)}, u32[]{:S(2)}) copy-start(bf16[4,512,128]{2,1,0:T(8,128)(2,1)} %copy-done.5) | copy-start | bytes 1572868
  34.2 18.0 %copy-start.9 = (bf16[2,512,128]{2,1,0:T(8,128)(2,1)S(1)}, bf16[2,512,128]{2,1,0:T(8,128)(2,1)}, u32[]{:S(2)}) copy-start(bf16[2,512,128]{2,1,0:T(8,128)(2,1)} %copy-done.8) | copy-start | bytes 786436
  34.2 18.0 %collective-permute-start.2 = (bf16[2,512,128]{2,1,0:T(8,128)(2,1)}, bf16[2,512,128]{2,1,0:T(8,128)(2,1)S(1)}, u32[]{:S(2)}, u32[]{:S(2)}) collective-permute-start(bf16[2,512,128]{2,1,0:T(8,128)(2,1)} %get-tuple-element.35), channel_id=1, source_target_pairs={{0,8},{2,10},{4,12},{6,14},{8,0},{10,2},{12,4},{14,6},{1,9},{3,11}... | collective-permute-start | bytes 786440 | tf_op jit(solution)/shard_map/ppermute | solution.py:292
  37.1 15.1 %collective-permute-start.3 = (bf16[2,512,128]{2,1,0:T(8,128)(2,1)}, bf16[2,512,128]{2,1,0:T(8,128)(2,1)S(1)}, u32[]{:S(2)}, u32[]{:S(2)}) collective-permute-start(bf16[2,512,128]{2,1,0:T(8,128)(2,1)} %get-tuple-element.36), channel_id=1, source_target_pairs={{0,4},{2,6},{4,8},{6,10},{8,12},{10,14},{12,0},{14,2},{1,5},{3,7},... | collective-permute-start | bytes 786440 | tf_op jit(solution)/shard_map/ppermute | solution.py:292
  37.5 14.7 %collective-permute-start.4 = (bf16[2,512,128]{2,1,0:T(8,128)(2,1)}, bf16[2,512,128]{2,1,0:T(8,128)(2,1)S(1)}, u32[]{:S(2)}, u32[]{:S(2)}) collective-permute-start(bf16[2,512,128]{2,1,0:T(8,128)(2,1)} %get-tuple-element.37), channel_id=1, source_target_pairs={{0,12},{2,14},{4,0},{6,2},{8,4},{10,6},{12,8},{14,10},{1,13},{3,15... | collective-permute-start | bytes 786440 | tf_op jit(solution)/shard_map/ppermute | solution.py:292
  41.8 25.7 %all-to-all-start = ((bf16[8,4,64,128]{3,2,1,0:T(8,128)(2,1)}), bf16[8,4,64,128]{3,2,1,0:T(8,128)(2,1)S(1)}, u32[]{:S(2)}, u32[]{:S(2)}) async-start(bf16[8,4,64,128]{3,2,1,0:T(8,128)(2,1)} %add_convert_fusion), calls=%async_computation | async-start | bytes 1048576 | tf_op jit(solution)/shard_map/all_to_all | solution.py:328
  52.3 5.4 %collective-permute-start.6 = (bf16[512,128]{1,0:T(8,128)(2,1)S(1)}, bf16[512,128]{1,0:T(8,128)(2,1)S(1)}, u32[]{:S(2)}, u32[]{:S(2)}) collective-permute-start(bf16[512,128]{1,0:T(8,128)(2,1)S(1)} %fusion.7), channel_id=1, source_target_pairs={{0,2},{2,0},{4,6},{6,4},{8,10},{10,8},{12,14},{14,12},{1,3},{3,1},... | collective-permute-start | bytes 393224 | tf_op jit(solution)/shard_map/ppermute | solution.py:296
  52.6 5.4 %collective-permute-start.7 = (bf16[512,128]{1,0:T(8,128)(2,1)S(1)}, bf16[512,128]{1,0:T(8,128)(2,1)S(1)}, u32[]{:S(2)}, u32[]{:S(2)}) collective-permute-start(bf16[512,128]{1,0:T(8,128)(2,1)S(1)} %get-tuple-element.49), channel_id=1, source_target_pairs={{0,8},{2,10},{4,12},{6,14},{8,0},{10,2},{12,4},{14,6},{1,9},{3,11}... | collective-permute-start | bytes 393224 | tf_op jit(solution)/shard_map/ppermute | solution.py:292
  52.6 8.7 %collective-permute-start.8 = (bf16[512,128]{1,0:T(8,128)(2,1)S(1)}, bf16[512,128]{1,0:T(8,128)(2,1)S(1)}, u32[]{:S(2)}, u32[]{:S(2)}) collective-permute-start(bf16[512,128]{1,0:T(8,128)(2,1)S(1)} %get-tuple-element.51), channel_id=1, source_target_pairs={{0,4},{2,6},{4,8},{6,10},{8,12},{10,14},{12,0},{14,2},{1,5},{3,7},... | collective-permute-start | bytes 393224 | tf_op jit(solution)/shard_map/ppermute | solution.py:292
  53.4 7.9 %collective-permute-start.9 = (bf16[512,128]{1,0:T(8,128)(2,1)S(1)}, bf16[512,128]{1,0:T(8,128)(2,1)S(1)}, u32[]{:S(2)}, u32[]{:S(2)}) collective-permute-start(bf16[512,128]{1,0:T(8,128)(2,1)S(1)} %get-tuple-element.50), channel_id=1, source_target_pairs={{0,12},{2,14},{4,0},{6,2},{8,4},{10,6},{12,8},{14,10},{1,13},{3,15... | collective-permute-start | bytes 393224 | tf_op jit(solution)/shard_map/ppermute | solution.py:292

commit v5 on v4

--- a/solution.py
+++ b/solution.py
@@ -91,7 +91,7 @@
             jax.ShapeDtypeStruct((count, width), BF16),
         ],
         scratch_shapes=[pltpu.VMEM((width, 3 * HS), BF16)],
-        compiler_params=pltpu.CompilerParams(vmem_limit_bytes=48 << 20),
+        compiler_params=pltpu.CompilerParams(vmem_limit_bytes=20 << 20),
         name="project",
     )(frames, gain, qkv_weight, out_weight, cotangent, pad2d)
 
@@ -195,13 +195,12 @@
             jax.ShapeDtypeStruct((count, HS), BF16),
         ],
         scratch_shapes=[pltpu.VMEM((4, count + 4 * HALO, HS), BF16)],
-        compiler_params=pltpu.CompilerParams(vmem_limit_bytes=48 << 20),
+        compiler_params=pltpu.CompilerParams(vmem_limit_bytes=20 << 20),
         name="attend",
     )(lengths, proj, halo, gain, qkv_weight, out_weight, pad2d)
 
 
-def input_body(frames_ref, gain_ref, qkv_ref, grads_ref, *rest):
-    outs, w_scr = rest[:-1], rest[-1]
+def input_body(frames_ref, gain_ref, qkv_ref, grads_ref, near_ref, across_ref, w_scr):
     place = lax.axis_index("mp")
     y, xh = place // 2, place % 2
 
@@ -216,45 +215,32 @@
     mean_grad = jnp.mean(scaled, axis=-1, keepdims=True)
     mean_proj = jnp.mean(scaled * normal_form, axis=-1, keepdims=True)
     result = (inverse * (scaled - mean_grad - normal_form * mean_proj)).astype(BF16)
-    if len(outs) == 4:
-        for p in range(4):
-            for k in range(4):
-
-                @pl.when((p - y) % 4 == k)
-                def _():
-                    for h in range(2):
-                        at = (2 * p + h) * 128
-                        outs[k][h] = result[:, at : at + 128]
-    else:
-        for p in range(4):
-            low = result[:, 256 * p : 256 * p + 128]
-            high = result[:, 256 * p + 128 : 256 * p + 256]
-            away = (p - y + 4) % 4
-            outs[0][away] = jnp.where(xh == 0, low, high)
-            outs[1][away] = jnp.where(xh == 0, high, low)
-
-
-def input_terms(frames, gain, qkv_weight, grads, half, pair_first):
+    for p in range(4):
+        low = result[:, 256 * p : 256 * p + 128]
+        high = result[:, 256 * p + 128 : 256 * p + 256]
+        away = (p - y + 4) % 4
+        near_ref[away] = jnp.where(xh == 0, low, high)
+        across_ref[away] = jnp.where(xh == 0, high, low)
+
+
+def input_terms(frames, gain, qkv_weight, grads):
     count, width = frames.shape
     rows = 256
-    steps = count // rows // 2
-    first = half * steps
     whole = lambda *shape: pl.BlockSpec(shape, lambda i: (0,) * len(shape))
-    lead, n_outs = (4, 2) if pair_first else (2, 4)
     return pl.pallas_call(
         input_body,
-        grid=(steps,),
+        grid=(count // rows,),
         in_specs=[
-            pl.BlockSpec((rows, width), lambda i: (i + first, 0)),
+            pl.BlockSpec((rows, width), lambda i: (i, 0)),
             whole(1, width),
             whole(*qkv_weight.shape),
-            pl.BlockSpec((rows, 3 * HS), lambda i: (i + first, 0)),
-        ],
-        out_specs=[pl.BlockSpec((lead, rows, 128), lambda i: (0, i, 0))] * n_outs,
-        out_shape=[jax.ShapeDtypeStruct((lead, count // 2, 128), BF16)] * n_outs,
+            pl.BlockSpec((rows, 3 * HS), lambda i: (i, 0)),
+        ],
+        out_specs=[pl.BlockSpec((4, rows, 128), lambda i: (0, i, 0))] * 2,
+        out_shape=[jax.ShapeDtypeStruct((4, count, 128), BF16)] * 2,
         scratch_shapes=[pltpu.VMEM((width, 3 * HS), BF16)],
-        compiler_params=pltpu.CompilerParams(vmem_limit_bytes=48 << 20),
-        name="input_terms_pair" if pair_first else "input_terms_ring",
+        compiler_params=pltpu.CompilerParams(vmem_limit_bytes=20 << 20),
+        name="input_terms",
     )(frames, gain, qkv_weight, grads)
 
 
@@ -282,7 +268,7 @@
         in_specs=[vmem] * 4,
         out_specs=[vmem] * 2,
         out_shape=[part] * 2,
-        compiler_params=pltpu.CompilerParams(vmem_limit_bytes=48 << 20),
+        compiler_params=pltpu.CompilerParams(vmem_limit_bytes=20 << 20),
         name="weight_terms",
     )(normed, cotangent, grads, mixed)
 
@@ -314,30 +300,18 @@
     pad2d = pad_mask.reshape(-1, 128)
     proj, normed = project(frames, gain, qkv_weight, out_weight, cotangent, pad2d)
     grads, mixed = attend(utt_lengths, proj, halo, gain, qkv_weight, out_weight, pad2d)
+    near, across = input_terms(frames, gain, qkv_weight, grads)
+    across = swapped(across, "mp", 1)
+    (normed, cotangent, grads, mixed), _ = lax.optimization_barrier(((normed, cotangent, grads, mixed), near))
     keep, send = weight_terms(normed, cotangent, grads, mixed)
     other = swapped(send, "tm", 1)
-    (frames_p, grads_p), _ = lax.optimization_barrier(((frames, grads), keep))
-    near, across = input_terms(frames_p, gain, qkv_weight, grads_p, 1, True)
-    across = swapped(across, "mp", 1)
-    (frames_r, grads_r), _ = lax.optimization_barrier(((frames, grads), near))
-    ring = input_terms(frames_r, gain, qkv_weight, grads_r, 0, False)
-    ring_in = [shifted(ring[k], "mp", 2 * k) for k in (2, 1, 3)]
-    (keep, other), _ = lax.optimization_barrier(((keep, other), ring[0]))
     chip = total(keep, other).astype(BF16)
     same_core = [[c + 2 * z for z in range(shards // 2)] for c in range(2)]
     weights = lax.all_to_all(chip, "tm", 0, 0, tiled=True, axis_index_groups=same_core)
+    (near, across), _ = lax.optimization_barrier(((near, across), chip))
     col = [total(near[k], across[k]) for k in range(4)]
     col_in = [shifted(col[k].astype(BF16), "mp", 2 * k) for k in (2, 1, 3)]
-    ring_in, _ = lax.optimization_barrier((ring_in, [c.astype(BF16) for c in col[1:]]))
-    xh = lax.axis_index("mp") % 2
-
-    def both(side):
-        return total(*[lax.dynamic_index_in_dim(r, side, 0, False) for r in (ring[0], *ring_in)])
-
-    theirs = swapped(both(1 - xh).astype(BF16), "mp", 1)
-    first_half = total(both(xh), theirs).astype(BF16)
-    second_half = total(col[0], *col_in).astype(BF16)
-    frame_grad = jnp.concatenate([first_half, second_half], axis=0)
+    frame_grad = total(col[0], *col_in).astype(BF16)
     qkv_grad = weights[:, :3].astype(F32).sum(axis=0)
     out_grad = weights[:, 3].astype(F32).sum(axis=0)
     return frame_grad, qkv_grad, out_grad.T

time: 69.3 us -> 72.3 us (1.043)
  waiting for transfers between devices: 10.8 us -> 24.1 us
  Pallas kernels: 19.4 us -> 13.4 us
  starting transfers between devices: 27.4 us -> 22.1 us
  local copies, waits for them, and re-layouts: 3.92 us -> 5.81 us
  other arithmetic: 6.5 us -> 5.56 us
    ppermute x3 -> x2, waiting for transfers between devices: 2.42 us -> 13 us  [swapped(): lax.ppermute(x, axis, [(i, i ^ bit) for i in range(lax.axis_size(axis))])]
    ppermute x6 -> x3, waiting for transfers between devices: 3.53 us -> 11.1 us  [shifted(): return lax.ppermute(x, axis, [(i, (i + by) % size) for i in range(size)])]
    all_to_all x1, waiting for transfers between devices: 4.48 us -> 0.01 us  [on_device(): lax.all_to_all(chip, 'tm', 0, 0, tiled=True, axis_index_groups=same_core)]
    ppermute x6 -> x3, starting transfers between devices: 8.26 us -> 4.57 us  [shifted(): return lax.ppermute(x, axis, [(i, (i + by) % size) for i in range(size)])]
    ppermute x1, starting transfers between devices: 1.92 us -> 5.15 us  [on_device(): lax.ppermute(starts, 'tm', down)]
    ppermute x1, starting transfers between devices: 4.94 us -> 1.92 us  [on_device(): lax.ppermute(ends, 'tm', up)]
    pallas_call x1, Pallas kernels: 4.12 us -> 1.41 us  [weight_terms(): pl.pallas_call(weight_body, in_specs=[vmem] * 4, out_specs=[vmem] * 2, ou...]
    unnamed x24 -> x20, local copies, waits for them, and re-layouts: 2.7 us -> 4.53 us
  transfers between devices with their start and end apart: 12 -> 8, of which waited for: 5 -> 4; matrix products, arithmetic and copies ran while one was open for 7% -> 6% of each run, Pallas kernels for 16% -> 7%
where the time goes in v5:
time: 72.3 us; the launch traced here: 71.8 us
  waiting for transfers between devices  24.1 us (33%)
  starting transfers between devices  22.1 us (31%)
  Pallas kernels  13.4 us (19%)
  local copies, waits for them, and re-layouts  5.81 us (8%)
  other arithmetic  5.56 us (8%)
  between operations  0.81 us (1%)
    ppermute x2, waiting for transfers between devices, swapped(): lax.ppermute(x, axis, [(i, i ^ bit) for i in range(lax.axis_size(axis))])  13 us
    ppermute x3, waiting for transfers between devices, shifted(): return lax.ppermute(x, axis, [(i, (i + by) % size) for i in range(size)])  11.1 us
    all_to_all x1, starting transfers between devices, on_device(): lax.all_to_all(chip, 'tm', 0, 0, tiled=True, axis_index_groups=same_core)  7.73 us
    ppermute x1, starting transfers between devices, on_device(): lax.ppermute(starts, 'tm', down)  5.15 us
    ppermute x3, starting transfers between devices, shifted(): return lax.ppermute(x, axis, [(i, (i + by) % size) for i in range(size)])  4.57 us
    unnamed x20, local copies, waits for them, and re-layouts  4.53 us
    pallas_call x1, Pallas kernels, attend(): pl.pallas_call(attend_body, in_specs=[pl.BlockSpec(memory_space=pltpu.SME...  4.51 us
    pallas_call x1, Pallas kernels, input_terms(): pl.pallas_call(input_body, grid=(count // rows,), in_specs=[pl.BlockSpec(...  3.89 us
  transfers between devices with their start and end apart: 8, of which 4 were waited for; matrix products, arithmetic and copies ran while one was open for 6% of the time, Pallas kernels for 7%

profile of v5, /device:TPU:1, one launch (start us, length us, event | category | flops | bytes accessed | tf_op | source)
XLA Modules:
  0.0 71.8 jit_solution(11306819916842318741)
XLA Ops:
  0.6 0.0 copy-start
  0.6 0.0 copy-start.8
  0.7 1.3 %slice_bitcast_fusion.2 = (bf16[1,64,1024]{2,1,0:T(8,128)(2,1)S(1)}, bf16[1,64,1024]{2,1,0:T(8,128)(2,1)S(1)}, bf16[1,64,1024]{2,1,0:T(8,128)(2,1)S(1)}, bf16[1,64,1024]{2,1,0:T(8,128)(2,1)S(1)}) fusion(bf16[1024,1024]{1,0:T(8,128)(2,1)} %cot_ref.2, bf16[1024,1024]{1,0:T(8,128)(2,1)} %frames_ref.3), kind=kLoop, calls=%fused_computation.18 | loop fusion | bytes 1048576 | tf_op jit(solution)/shard_map/stack | solution.py:296
  2.0 5.1 %collective-permute-start.1 = (bf16[2,64,1024]{2,1,0:T(8,128)(2,1)S(1)}, bf16[2,64,1024]{2,1,0:T(8,128)(2,1)S(1)}, u32[]{:S(2)}, u32[]{:S(2)}) collective-permute-start(bf16[2,64,1024]{2,1,0:T(8,128)(2,1)S(1)} %pad_maximum_fusion.2), channel_id=1, source_target_pairs={{16,0},{32,16},{48,32},{64,48},{80,64},{96,80},{112,96},{128,112},... | collective-permute-start | bytes 786440 | tf_op jit(solution)/shard_map/ppermute | solution.py:298
  7.2 1.9 %collective-permute-start = (bf16[2,64,1024]{2,1,0:T(8,128)(2,1)S(1)}, bf16[2,64,1024]{2,1,0:T(8,128)(2,1)S(1)}, u32[]{:S(2)}, u32[]{:S(2)}) collective-permute-start(bf16[2,64,1024]{2,1,0:T(8,128)(2,1)S(1)} %pad_maximum_fusion.1), channel_id=1, source_target_pairs={{0,16},{16,32},{32,48},{48,64},{64,80},{80,96},{96,112},{112,128},... | collective-permute-start | bytes 786440 | tf_op jit(solution)/shard_map/ppermute | solution.py:298
  9.1 0.0 copy-done
  9.1 0.0 copy-done.8
  9.1 0.0 copy-start.1
  9.1 1.6 %copy-done.1 = bf16[1024,1024]{1,0:T(8,128)(2,1)S(1)} copy-done((bf16[1024,1024]{1,0:T(8,128)(2,1)S(1)}, bf16[1024,1024]{1,0:T(8,128)(2,1)}, u32[]{:S(2)}) %copy-start.1) | copy-done | bytes 2097176
  10.7 0.0 copy-start.3
  10.7 1.1 %copy-done.3 = bf16[3,1024,128]{2,1,0:T(8,128)(2,1)S(1)} copy-done((bf16[3,1024,128]{2,1,0:T(8,128)(2,1)S(1)}, bf16[3,1024,128]{2,1,0:T(8,128)(2,1)}, u32[]{:S(2)}) %copy-start.3) | copy-done | bytes 786456
  11.8 0.0 copy-start.5
  11.8 0.9 %copy-done.5 = bf16[128,1024]{1,0:T(8,128)(2,1)S(1)} copy-done((bf16[128,1024]{1,0:T(8,128)(2,1)S(1)}, bf16[128,1024]{1,0:T(8,128)(2,1)}, u32[]{:S(2)}) %copy-start.5) | copy-done | bytes 262168
  12.8 0.0 copy-start.7
  12.8 0.8 %copy-done.7 = s32[16384]{0:T(1024)S(1)} copy-done((s32[16384]{0:T(1024)S(1)}, s32[16384]{0:T(1024)}, u32[]{:S(2)}) %copy-start.7) | copy-done | bytes 65560
  13.6 0.0 copy-start.4
  13.6 0.0 copy-start.6
  13.6 0.0 copy-start.9
  13.6 3.6 %project.1 = (bf16[4,1024,128]{2,1,0:T(8,128)(2,1)S(1)}, bf16[1024,1024]{1,0:T(8,128)(2,1)S(1)}) custom-call(bf16[1024,1024]{1,0:T(8,128)(2,1)S(1)} %copy-done, f32[1,1024]{1,0:T(1,128)S(1)} %bitcast.27, bf16[3,1024,128]{2,1,0:T(8,128)(2,1)S(1)} %copy-done.3, bf16[128,1024]{1,0:T(8,128)(2,1)S(1)} %copy-done.5, bf16[1024,1024]{1,0:T(8,128)(2,1)S(1)} %copy-done.1, ...), custom_call_target="tpu_custom_call" | custom-call | tf_op jit(solution)/shard_map/project/pallas_call | solution.py:74
  17.3 0.0 collective-permute-done.1
  17.3 0.0 collective-permute-done
  17.3 0.0 copy-done.4
  17.4 0.0 copy-done.6
  17.4 0.0 copy-done.9
  17.4 4.5 %attend.1 = (bf16[1024,384]{1,0:T(8,128)(2,1)S(1)}, bf16[1024,128]{1,0:T(8,128)(2,1)S(1)}) custom-call(s32[8]{0:T(128)S(1)} %copy-done.9, bf16[4,1024,128]{2,1,0:T(8,128)(2,1)S(1)} %get-tuple-element.17.proj_ref, bf16[2,128,1024]{2,1,0:T(8,128)(2,1)S(1)} %pad_maximum_fusion.halo_ref, f32[1,1024]{1,0:T(1,128)S(1)} %bitcast.28, ...), custom_call_target="tpu_custom_call" | custom-call | tf_op jit(solution)/shard_map/attend/pallas_call | solution.py:189
  21.9 0.0 copy-start.2
  21.9 3.9 %input_terms.1 = (bf16[4,1024,128]{2,1,0:T(8,128)(2,1)S(1)}, bf16[4,1024,128]{2,1,0:T(8,128)(2,1)S(1)}) custom-call(bf16[1024,1024]{1,0:T(8,128)(2,1)S(1)} %copy-done, f32[1,1024]{1,0:T(1,128)S(1)} %bitcast.29, bf16[3,1024,128]{2,1,0:T(8,128)(2,1)S(1)} %copy-done.4, bf16[1024,384]{1,0:T(8,128)(2,1)S(1)} %get-tuple-element.25.grads_ref), custom_call_target="tpu_custom_call" | custom-call | tf_op jit(solution)/shard_map/input_terms/pallas_call | solution.py:230
  25.8 2.6 %collective-permute-start.2 = (bf16[4,1024,128]{2,1,0:T(8,128)(2,1)S(1)}, bf16[4,1024,128]{2,1,0:T(8,128)(2,1)}, u32[]{:S(2)}, u32[]{:S(2)}) collective-permute-start(bf16[4,1024,128]{2,1,0:T(8,128)(2,1)S(1)} %get-tuple-element.20), channel_id=1, source_target_pairs={{0,2},{2,0},{4,6},{6,4},{8,10},{10,8},{12,14},{14,12},{1,3},{3,1},... | collective-permute-start | bytes 3145736 | tf_op jit(solution)/shard_map/ppermute | solution.py:282
  28.4 0.0 copy-done.2
  28.4 1.4 %weight_terms.1 = (bf16[8,4,64,128]{3,2,1,0:T(8,128)(2,1)S(1)}, bf16[8,4,64,128]{3,2,1,0:T(8,128)(2,1)S(1)}) custom-call(bf16[1024,1024]{1,0:T(8,128)(2,1)S(1)} %get-tuple-element.23.normed_ref, bf16[1024,1024]{1,0:T(8,128)(2,1)S(1)} %copy-done.2, bf16[1024,384]{1,0:T(8,128)(2,1)S(1)} %get-tuple-element.25.grads_ref, ...), custom_call_target="tpu_custom_call" | custom-call | tf_op jit(solution)/shard_map/weight_terms/pallas_call | solution.py:266
  29.8 0.1 collective-permute-start.3
  29.9 1.9 %collective-permute-done.3 = bf16[8,4,64,128]{3,2,1,0:T(8,128)(2,1)S(1)} collective-permute-done((bf16[8,4,64,128]{3,2,1,0:T(8,128)(2,1)S(1)}, bf16[8,4,64,128]{3,2,1,0:T(8,128)(2,1)S(1)}, u32[]{:S(2)}, u32[]{:S(2)}) %collective-permute-start.3) | collective-permute-done | bytes 524320 | tf_op jit(solution)/shard_map/ppermute | solution.py:282
  31.8 1.0 %add_convert_fusion = bf16[8,4,64,128]{3,2,1,0:T(8,128)(2,1)} fusion(bf16[8,4,64,128]{3,2,1,0:T(8,128)(2,1)S(1)} %collective-permute-done.3, bf16[8,4,64,128]{3,2,1,0:T(8,128)(2,1)S(1)} %get-tuple-element.27), kind=kLoop, calls=%fused_computation | loop fusion | flops 1048576 | bytes 1572864 | tf_op jit(solution)/shard_map/convert_element_type | solution.py:308
  32.8 7.7 %all-to-all-start = ((bf16[8,4,64,128]{3,2,1,0:T(8,128)(2,1)}), bf16[8,4,64,128]{3,2,1,0:T(8,128)(2,1)S(1)}, u32[]{:S(2)}, u32[]{:S(2)}) async-start(bf16[8,4,64,128]{3,2,1,0:T(8,128)(2,1)} %add_convert_fusion), calls=%async_computation | async-start | bytes 1048576 | tf_op jit(solution)/shard_map/all_to_all | solution.py:310
  40.6 11.1 %collective-permute-done.2 = bf16[4,1024,128]{2,1,0:T(8,128)(2,1)} collective-permute-done((bf16[4,1024,128]{2,1,0:T(8,128)(2,1)S(1)}, bf16[4,1024,128]{2,1,0:T(8,128)(2,1)}, u32[]{:S(2)}, u32[]{:S(2)}) %collective-permute-start.2) | collective-permute-done | bytes 1048608 | tf_op jit(solution)/shard_map/ppermute | solution.py:282
  51.7 1.3 %fusion.3 = (bf16[1024,128]{1,0:T(8,128)(2,1)S(1)}, bf16[1024,128]{1,0:T(8,128)(2,1)S(1)}, bf16[1024,128]{1,0:T(8,128)(2,1)S(1)}) fusion(bf16[4,1024,128]{2,1,0:T(8,128)(2,1)} %collective-permute-done.2, bf16[4,1024,128]{2,1,0:T(8,128)(2,1)S(1)} %get-tuple-element.29), kind=kLoop, calls=%fused_computation.10 | loop fusion | flops 1572864 | bytes 2359296 | tf_op jit(solution)/shard_map/convert_element_type | solution.py:313
  53.0 3.1 %collective-permute-start.4 = (bf16[1024,128]{1,0:T(8,128)(2,1)S(1)}, bf16[1024,128]{1,0:T(8,128)(2,1)S(1)}, u32[]{:S(2)}, u32[]{:S(2)}) collective-permute-start(bf16[1024,128]{1,0:T(8,128)(2,1)S(1)} %get-tuple-element.31), channel_id=1, source_target_pairs={{0,8},{2,10},{4,12},{6,14},{8,0},{10,2},{12,4},{14,6},{1,9},{3,11}... | collective-permute-start | bytes 786440 | tf_op jit(solution)/shard_map/ppermute | solution.py:278
  56.1 0.8 %collective-permute-start.6 = (bf16[1024,128]{1,0:T(8,128)(2,1)S(1)}, bf16[1024,128]{1,0:T(8,128)(2,1)S(1)}, u32[]{:S(2)}, u32[]{:S(2)}) collective-permute-start(bf16[1024,128]{1,0:T(8,128)(2,1)S(1)} %get-tuple-element.32), channel_id=1, source_target_pairs={{0,12},{2,14},{4,0},{6,2},{8,4},{10,6},{12,8},{14,10},{1,13},{3,15... | collective-permute-start | bytes 786440 | tf_op jit(solution)/shard_map/ppermute | solution.py:278
  56.9 0.7 collective-permute-start.5
  57.6 4.3 %collective-permute-done.4 = bf16[1024,128]{1,0:T(8,128)(2,1)S(1)} collective-permute-done((bf16[1024,128]{1,0:T(8,128)(2,1)S(1)}, bf16[1024,128]{1,0:T(8,128)(2,1)S(1)}, u32[]{:S(2)}, u32[]{:S(2)}) %collective-permute-start.4) | collective-permute-done | bytes 262176 | tf_op jit(solution)/shard_map/ppermute | solution.py:278
  61.9 6.7 %collective-permute-done.6 = bf16[1024,128]{1,0:T(8,128)(2,1)S(1)} collective-permute-done((bf16[1024,128]{1,0:T(8,128)(2,1)S(1)}, bf16[1024,128]{1,0:T(8,128)(2,1)S(1)}, u32[]{:S(2)}, u32[]{:S(2)}) %collective-permute-start.6) | collective-permute-done | bytes 262176 | tf_op jit(solution)/shard_map/ppermute | solution.py:278
  68.6 0.0 collective-permute-done.5
  68.7 1.8 %fusion.2 = bf16[1024,128]{1,0:T(8,128)(2,1)} fusion(bf16[1024,128]{1,0:T(8,128)(2,1)S(1)} %collective-permute-done.6, bf16[1024,128]{1,0:T(8,128)(2,1)S(1)} %collective-permute-done.5, bf16[1024,128]{1,0:T(8,128)(2,1)S(1)} %collective-permute-done.4, bf16[4,1024,128]{2,1,0:T(8,128)(2,1)} %collective-permute-done.2, ...), kind=kLoop, calls=%fused_computation.6 | loop fusion | flops 1310720 | bytes 1572864 | tf_op jit(solution)/shard_map/convert_element_type | solution.py:314
  70.5 0.0 all-to-all-done
  70.5 0.6 convert_reduce_fusion.1
  71.1 0.7 convert_reduce_fusion
  (3 shorter events, 0.1 us)
Async XLA Ops:
  0.6 8.5 %copy-start = (bf16[1024,1024]{1,0:T(8,128)(2,1)S(1)}, bf16[1024,1024]{1,0:T(8,128)(2,1)}, u32[]{:S(2)}) copy-start(bf16[1024,1024]{1,0:T(8,128)(2,1)} %frames_ref.3) | copy-start | bytes 6291460
  0.6 8.5 %copy-start.8 = (f32[1024]{0:T(1024)S(1)}, f32[1024]{0:T(1024)}, u32[]{:S(2)}) copy-start(f32[1024]{0:T(1024)} %param.8) | copy-start | bytes 12292
  2.0 15.3 %collective-permute-start.1 = (bf16[2,64,1024]{2,1,0:T(8,128)(2,1)S(1)}, bf16[2,64,1024]{2,1,0:T(8,128)(2,1)S(1)}, u32[]{:S(2)}, u32[]{:S(2)}) collective-permute-start(bf16[2,64,1024]{2,1,0:T(8,128)(2,1)S(1)} %pad_maximum_fusion.2), channel_id=1, source_target_pairs={{16,0},{32,16},{48,32},{64,48},{80,64},{96,80},{112,96},{128,112},... | collective-permute-start | bytes 786440 | tf_op jit(solution)/shard_map/ppermute | solution.py:298
  7.2 10.1 %collective-permute-start = (bf16[2,64,1024]{2,1,0:T(8,128)(2,1)S(1)}, bf16[2,64,1024]{2,1,0:T(8,128)(2,1)S(1)}, u32[]{:S(2)}, u32[]{:S(2)}) collective-permute-start(bf16[2,64,1024]{2,1,0:T(8,128)(2,1)S(1)} %pad_maximum_fusion.1), channel_id=1, source_target_pairs={{0,16},{16,32},{32,48},{48,64},{64,80},{80,96},{96,112},{112,128},... | collective-permute-start | bytes 786440 | tf_op jit(solution)/shard_map/ppermute | solution.py:298
  9.1 1.6 %copy-start.1 = (bf16[1024,1024]{1,0:T(8,128)(2,1)S(1)}, bf16[1024,1024]{1,0:T(8,128)(2,1)}, u32[]{:S(2)}) copy-start(bf16[1024,1024]{1,0:T(8,128)(2,1)} %cot_ref.2) | copy-start | bytes 6291460
  10.7 1.1 %copy-start.3 = (bf16[3,1024,128]{2,1,0:T(8,128)(2,1)S(1)}, bf16[3,1024,128]{2,1,0:T(8,128)(2,1)}, u32[]{:S(2)}) copy-start(bf16[3,1024,128]{2,1,0:T(8,128)(2,1)} %qkv_ref.5) | copy-start | bytes 2359300
  11.8 0.9 %copy-start.5 = (bf16[128,1024]{1,0:T(8,128)(2,1)S(1)}, bf16[128,1024]{1,0:T(8,128)(2,1)}, u32[]{:S(2)}) copy-start(bf16[128,1024]{1,0:T(8,128)(2,1)} %out_ref.3) | copy-start | bytes 786436
  12.8 0.8 %copy-start.7 = (s32[16384]{0:T(1024)S(1)}, s32[16384]{0:T(1024)}, u32[]{:S(2)}) copy-start(s32[16384]{0:T(1024)} %param.12) | copy-start | bytes 196612
  13.6 3.7 %copy-start.4 = (bf16[3,1024,128]{2,1,0:T(8,128)(2,1)S(1)}, bf16[3,1024,128]{2,1,0:T(8,128)(2,1)}, u32[]{:S(2)}) copy-start(bf16[3,1024,128]{2,1,0:T(8,128)(2,1)} %qkv_ref.5) | copy-start | bytes 2359300
  13.6 3.7 %copy-start.6 = (bf16[128,1024]{1,0:T(8,128)(2,1)S(1)}, bf16[128,1024]{1,0:T(8,128)(2,1)}, u32[]{:S(2)}) copy-start(bf16[128,1024]{1,0:T(8,128)(2,1)} %out_ref.3) | copy-start | bytes 786436
  13.6 3.7 %copy-start.9 = (s32[8]{0:T(128)S(1)}, s32[8]{0:T(128)}, u32[]{:S(2)}) copy-start(s32[8]{0:T(128)} %len_ref.1) | copy-start | bytes 100
  21.9 6.5 %copy-start.2 = (bf16[1024,1024]{1,0:T(8,128)(2,1)S(1)}, bf16[1024,1024]{1,0:T(8,128)(2,1)}, u32[]{:S(2)}) copy-start(bf16[1024,1024]{1,0:T(8,128)(2,1)} %cot_ref.2) | copy-start | bytes 6291460
  25.8 25.9 %collective-permute-start.2 = (bf16[4,1024,128]{2,1,0:T(8,128)(2,1)S(1)}, bf16[4,1024,128]{2,1,0:T(8,128)(2,1)}, u32[]{:S(2)}, u32[]{:S(2)}) collective-permute-start(bf16[4,1024,128]{2,1,0:T(8,128)(2,1)S(1)} %get-tuple-element.20), channel_id=1, source_target_pairs={{0,2},{2,0},{4,6},{6,4},{8,10},{10,8},{12,14},{14,12},{1,3},{3,1},... | collective-permute-start | bytes 3145736 | tf_op jit(solution)/shard_map/ppermute | solution.py:282
  29.8 2.0 %collective-permute-start.3 = (bf16[8,4,64,128]{3,2,1,0:T(8,128)(2,1)S(1)}, bf16[8,4,64,128]{3,2,1,0:T(8,128)(2,1)S(1)}, u32[]{:S(2)}, u32[]{:S(2)}) collective-permute-start(bf16[8,4,64,128]{3,2,1,0:T(8,128)(2,1)S(1)} %get-tuple-element.28), channel_id=1, source_target_pairs={{0,16},{16,0},{32,48},{48,32},{64,80},{80,64},{96,112},{112,96},{1... | collective-permute-start | bytes 1572872 | tf_op jit(solution)/shard_map/ppermute | solution.py:282
  32.8 37.6 %all-to-all-start = ((bf16[8,4,64,128]{3,2,1,0:T(8,128)(2,1)}), bf16[8,4,64,128]{3,2,1,0:T(8,128)(2,1)S(1)}, u32[]{:S(2)}, u32[]{:S(2)}) async-start(bf16[8,4,64,128]{3,2,1,0:T(8,128)(2,1)} %add_convert_fusion), calls=%async_computation | async-start | bytes 1048576 | tf_op jit(solution)/shard_map/all_to_all | solution.py:310
  53.0 8.9 %collective-permute-start.4 = (bf16[1024,128]{1,0:T(8,128)(2,1)S(1)}, bf16[1024,128]{1,0:T(8,128)(2,1)S(1)}, u32[]{:S(2)}, u32[]{:S(2)}) collective-permute-start(bf16[1024,128]{1,0:T(8,128)(2,1)S(1)} %get-tuple-element.31), channel_id=1, source_target_pairs={{0,8},{2,10},{4,12},{6,14},{8,0},{10,2},{12,4},{14,6},{1,9},{3,11}... | collective-permute-start | bytes 786440 | tf_op jit(solution)/shard_map/ppermute | solution.py:278
  56.1 12.5 %collective-permute-start.6 = (bf16[1024,128]{1,0:T(8,128)(2,1)S(1)}, bf16[1024,128]{1,0:T(8,128)(2,1)S(1)}, u32[]{:S(2)}, u32[]{:S(2)}) collective-permute-start(bf16[1024,128]{1,0:T(8,128)(2,1)S(1)} %get-tuple-element.32), channel_id=1, source_target_pairs={{0,12},{2,14},{4,0},{6,2},{8,4},{10,6},{12,8},{14,10},{1,13},{3,15... | collective-permute-start | bytes 786440 | tf_op jit(solution)/shard_map/ppermute | solution.py:278
  56.9 11.7 %collective-permute-start.5 = (bf16[1024,128]{1,0:T(8,128)(2,1)S(1)}, bf16[1024,128]{1,0:T(8,128)(2,1)S(1)}, u32[]{:S(2)}, u32[]{:S(2)}) collective-permute-start(bf16[1024,128]{1,0:T(8,128)(2,1)S(1)} %get-tuple-element.33), channel_id=1, source_target_pairs={{0,4},{2,6},{4,8},{6,10},{8,12},{10,14},{12,0},{14,2},{1,5},{3,7},... | collective-permute-start | bytes 786440 | tf_op jit(solution)/shard_map/ppermute | solution.py:278

commit v6 on v5

--- a/solution.py
+++ b/solution.py
@@ -96,7 +96,19 @@
     )(frames, gain, qkv_weight, out_weight, cotangent, pad2d)
 
 
-def attend_body(len_ref, proj_ref, halo_ref, gain_ref, qkv_ref, out_ref, pad_ref, grads_ref, mixed_ref, x_scr):
+def backward_body(
+    len_ref, proj_ref, halo_ref, gain_ref, qkv_ref, out_ref, pad_ref, frames_hbm, normed_hbm, cot_hbm,
+    near_ref, across_ref, ring0_ref, ring1_ref, ring2_ref, ring3_ref, keep_ref, send_ref,
+    x_scr, grads_ref, mixed_ref, w_scr, frames_ref, normed_ref, cot_ref, sems,
+):
+    fetches = [
+        pltpu.make_async_copy(source, target, sems.at[i])
+        for i, (source, target) in enumerate(
+            [(frames_hbm, frames_ref), (normed_hbm, normed_ref), (cot_hbm, cot_ref)]
+        )
+    ]
+    for fetch in fetches:
+        fetch.start()
     count = proj_ref.shape[1]
     tiles = count // 128 + 1
     shard = lax.axis_index("tm")
@@ -145,6 +157,31 @@
     apart = key_at // CH - query_at // CH
     in_band = (apart >= 0) & (apart <= 2)
     same = key_at == query_at + CH
+
+    place = lax.axis_index("mp")
+    owners = [((place // 2 + k) % 4) * 2 + (place + s) % 2 for k in range(4) for s in range(2)]
+    spans = [pl.ds(pl.multiple_of(owner * 128, 128), 128) for owner in owners]
+    for m in range(3):
+        for j, span in enumerate(spans):
+            w_scr[j * 128 : (j + 1) * 128, m * HS : (m + 1) * HS] = qkv_ref[m, span, :]
+    gain = jnp.concatenate([gain_ref[:, span] for span in spans], axis=1)
+    ring_refs = (ring0_ref, ring1_ref, ring2_ref, ring3_ref)
+
+    def input_rows(at, rows):
+        incoming = rows_by_rows(grads_ref[at : at + rows, :], w_scr[...])
+        frames = jnp.concatenate([frames_ref[at : at + rows, span] for span in spans], axis=1)
+        normal_form, inverse = normalised(frames)
+        scaled = incoming * gain
+        mean_grad = jnp.mean(scaled, axis=-1, keepdims=True)
+        mean_proj = jnp.mean(scaled * normal_form, axis=-1, keepdims=True)
+        result = (inverse * (scaled - mean_grad - normal_form * mean_proj)).astype(BF16)
+        to = at % (count // 2)
+        for j in range(8):
+            part = result[:, j * 128 : (j + 1) * 128]
+            if at < count // 2:
+                ring_refs[j // 2][j % 2, to : to + rows, :] = part
+            else:
+                (near_ref, across_ref)[j % 2][j // 2, to : to + rows, :] = part
 
     carry_k = carry_v = None
     for t in range(tiles):
@@ -183,69 +220,14 @@
         grads_ref[at + lo : at + hi, 2 * HS : 3 * HS] = value_grad[lo:hi].astype(BF16)
 
 
-def attend(lengths, proj, halo, gain, qkv_weight, out_weight, pad2d):
-    count = proj.shape[1]
-    vmem = pl.BlockSpec(memory_space=pltpu.VMEM)
-    return pl.pallas_call(
-        attend_body,
-        in_specs=[pl.BlockSpec(memory_space=pltpu.SMEM)] + [vmem] * 6,
-        out_specs=[vmem, vmem],
-        out_shape=[
-            jax.ShapeDtypeStruct((count, 3 * HS), BF16),
-            jax.ShapeDtypeStruct((count, HS), BF16),
-        ],
-        scratch_shapes=[pltpu.VMEM((4, count + 4 * HALO, HS), BF16)],
-        compiler_params=pltpu.CompilerParams(vmem_limit_bytes=20 << 20),
-        name="attend",
-    )(lengths, proj, halo, gain, qkv_weight, out_weight, pad2d)
-
-
-def input_body(frames_ref, gain_ref, qkv_ref, grads_ref, near_ref, across_ref, w_scr):
-    place = lax.axis_index("mp")
-    y, xh = place // 2, place % 2
-
-    @pl.when(pl.program_id(0) == 0)
-    def _():
-        for m in range(3):
-            w_scr[:, m * HS : (m + 1) * HS] = qkv_ref[m]
-
-    incoming = rows_by_rows(grads_ref[...], w_scr[...])
-    normal_form, inverse = normalised(frames_ref[...])
-    scaled = incoming * gain_ref[...]
-    mean_grad = jnp.mean(scaled, axis=-1, keepdims=True)
-    mean_proj = jnp.mean(scaled * normal_form, axis=-1, keepdims=True)
-    result = (inverse * (scaled - mean_grad - normal_form * mean_proj)).astype(BF16)
-    for p in range(4):
-        low = result[:, 256 * p : 256 * p + 128]
-        high = result[:, 256 * p + 128 : 256 * p + 256]
-        away = (p - y + 4) % 4
-        near_ref[away] = jnp.where(xh == 0, low, high)
-        across_ref[away] = jnp.where(xh == 0, high, low)
-
-
-def input_terms(frames, gain, qkv_weight, grads):
-    count, width = frames.shape
-    rows = 256
-    whole = lambda *shape: pl.BlockSpec(shape, lambda i: (0,) * len(shape))
-    return pl.pallas_call(
-        input_body,
-        grid=(count // rows,),
-        in_specs=[
-            pl.BlockSpec((rows, width), lambda i: (i, 0)),
-            whole(1, width),
-            whole(*qkv_weight.shape),
-            pl.BlockSpec((rows, 3 * HS), lambda i: (i, 0)),
-        ],
-        out_specs=[pl.BlockSpec((4, rows, 128), lambda i: (0, i, 0))] * 2,
-        out_shape=[jax.ShapeDtypeStruct((4, count, 128), BF16)] * 2,
-        scratch_shapes=[pltpu.VMEM((width, 3 * HS), BF16)],
-        compiler_params=pltpu.CompilerParams(vmem_limit_bytes=20 << 20),
-        name="input_terms",
-    )(frames, gain, qkv_weight, grads)
-
-
-def weight_body(normed_ref, cot_ref, grads_ref, mixed_ref, keep_ref, send_ref):
-    core = lax.axis_index("tm") % 2
+        if t == 2:
+            fetches[0].wait()
+        if t >= 2 and t % 2 == 0:
+            input_rows(base - 256, 256)
+
+    fetches[1].wait()
+    fetches[2].wait()
+    core = shard % 2
     qkv = cols_by_cols(grads_ref[...], normed_ref[...]).astype(BF16)
     out = cols_by_cols(mixed_ref[...], cot_ref[...]).astype(BF16)
     full = jnp.concatenate([qkv, out], axis=0)
@@ -259,18 +241,29 @@
             send_ref[z, m] = send[:, m * HS : (m + 1) * HS]
 
 
-def weight_terms(normed, cotangent, grads, mixed):
-    count, width = normed.shape
+def backward(lengths, proj, halo, gain, qkv_weight, out_weight, pad2d, frames, normed, cotangent):
+    count, width = frames.shape
     vmem = pl.BlockSpec(memory_space=pltpu.VMEM)
-    part = jax.ShapeDtypeStruct((8, 4, width // 16, HS), BF16)
+    half = count // 2
+    shapes = [(4, half, 128)] * 2 + [(2, half, 128)] * 4 + [(8, 4, width // 16, HS)] * 2
     return pl.pallas_call(
-        weight_body,
-        in_specs=[vmem] * 4,
-        out_specs=[vmem] * 2,
-        out_shape=[part] * 2,
-        compiler_params=pltpu.CompilerParams(vmem_limit_bytes=20 << 20),
-        name="weight_terms",
-    )(normed, cotangent, grads, mixed)
+        backward_body,
+        in_specs=[pl.BlockSpec(memory_space=pltpu.SMEM)] + [vmem] * 6 + [pl.BlockSpec(memory_space=pl.ANY)] * 3,
+        out_specs=[vmem] * len(shapes),
+        out_shape=[jax.ShapeDtypeStruct(shape, BF16) for shape in shapes],
+        scratch_shapes=[
+            pltpu.VMEM((4, count + 4 * HALO, HS), BF16),
+            pltpu.VMEM((count, 3 * HS), BF16),
+            pltpu.VMEM((count, HS), BF16),
+            pltpu.VMEM((width, 3 * HS), BF16),
+            pltpu.VMEM((count, width), BF16),
+            pltpu.VMEM((count, width), BF16),
+            pltpu.VMEM((count, width), BF16),
+            pltpu.SemaphoreType.DMA((3,)),
+        ],
+        compiler_params=pltpu.CompilerParams(vmem_limit_bytes=40 << 20),
+        name="backward",
+    )(lengths, proj, halo, gain, qkv_weight, out_weight, pad2d, frames, normed, cotangent)
 
 
 def shifted(x, axis, by):
@@ -299,19 +292,22 @@
     gain = norm_gain[None, :]
     pad2d = pad_mask.reshape(-1, 128)
     proj, normed = project(frames, gain, qkv_weight, out_weight, cotangent, pad2d)
-    grads, mixed = attend(utt_lengths, proj, halo, gain, qkv_weight, out_weight, pad2d)
-    near, across = input_terms(frames, gain, qkv_weight, grads)
+    near, across, *ring, keep, send = backward(
+        utt_lengths, proj, halo, gain, qkv_weight, out_weight, pad2d, frames, normed, cotangent
+    )
+    other = swapped(send, "tm", 1)
     across = swapped(across, "mp", 1)
-    (normed, cotangent, grads, mixed), _ = lax.optimization_barrier(((normed, cotangent, grads, mixed), near))
-    keep, send = weight_terms(normed, cotangent, grads, mixed)
-    other = swapped(send, "tm", 1)
+    ring_in = [shifted(ring[k], "mp", 2 * k) for k in (2, 1, 3)]
     chip = total(keep, other).astype(BF16)
     same_core = [[c + 2 * z for z in range(shards // 2)] for c in range(2)]
     weights = lax.all_to_all(chip, "tm", 0, 0, tiled=True, axis_index_groups=same_core)
-    (near, across), _ = lax.optimization_barrier(((near, across), chip))
     col = [total(near[k], across[k]) for k in range(4)]
     col_in = [shifted(col[k].astype(BF16), "mp", 2 * k) for k in (2, 1, 3)]
-    frame_grad = total(col[0], *col_in).astype(BF16)
+    ring_in, _ = lax.optimization_barrier((ring_in, [c.astype(BF16) for c in col[1:]]))
+    theirs = swapped(total(ring[0][1], *[r[1] for r in ring_in]).astype(BF16), "mp", 1)
+    first_half = total(total(ring[0][0], *[r[0] for r in ring_in]), theirs).astype(BF16)
+    second_half = total(col[0], *col_in).astype(BF16)
+    frame_grad = jnp.concatenate([first_half, second_half], axis=0)
     qkv_grad = weights[:, :3].astype(F32).sum(axis=0)
     out_grad = weights[:, 3].astype(F32).sum(axis=0)
     return frame_grad, qkv_grad, out_grad.T

time: 72.3 us -> 73.1 us (1.011)
  starting transfers between devices: 22.1 us -> 27.5 us
  waiting for transfers between devices: 24.1 us -> 21.6 us
  other arithmetic: 5.56 us -> 3.51 us
    all_to_all x1, waiting for transfers between devices: 0.01 us -> 6.7 us  [on_device(): lax.all_to_all(chip, 'tm', 0, 0, tiled=True, axis_index_groups=same_core)]
    ppermute x2 -> x3, waiting for transfers between devices: 13 us -> 7.29 us  [swapped(): lax.ppermute(x, axis, [(i, i ^ bit) for i in range(lax.axis_size(axis))])]
    ppermute x3 -> x6, starting transfers between devices: 4.57 us -> 9.76 us  [shifted(): return lax.ppermute(x, axis, [(i, (i + by) % size) for i in range(size)])]
    ppermute x3 -> x6, waiting for transfers between devices: 11.1 us -> 7.62 us  [shifted(): return lax.ppermute(x, axis, [(i, (i + by) % size) for i in range(size)])]
    convert_element_type x2 -> x3, other arithmetic: 3.14 us -> 0.31 us  [the longest x1 0.1 us: on_device(): c.astype(BF16)]
    ppermute x2 -> x3, starting transfers between devices: 2.71 us -> 2.93 us  [swapped(): lax.ppermute(x, axis, [(i, i ^ bit) for i in range(lax.axis_size(axis))])]
    pallas_call x3 -> x1, Pallas kernels: 9.81 us -> 9.84 us  [backward(): pl.pallas_call(backward_body, in_specs=[pl.BlockSpec(memory_space=pltpu.S...]
    unnamed x20 -> x18, local copies, waits for them, and re-layouts: 4.53 us -> 4.53 us
  transfers between devices with their start and end apart: 8 -> 12, of which waited for: 4 -> 7; matrix products, arithmetic and copies ran while one was open for 6% -> 2% of each run, Pallas kernels for 7% -> 5%
where the time goes in v6:
time: 73.1 us; the launch traced here: 72.7 us
  starting transfers between devices  27.5 us (38%)
  waiting for transfers between devices  21.6 us (30%)
  Pallas kernels  13.5 us (18%)
  local copies, waits for them, and re-layouts  5.81 us (8%)
  other arithmetic  3.51 us (5%)
  between operations  0.8 us (1%)
    pallas_call x1, Pallas kernels, backward(): pl.pallas_call(backward_body, in_specs=[pl.BlockSpec(memory_space=pltpu.S...  9.84 us
    ppermute x6, starting transfers between devices, shifted(): return lax.ppermute(x, axis, [(i, (i + by) % size) for i in range(size)])  9.76 us
    all_to_all x1, starting transfers between devices, on_device(): lax.all_to_all(chip, 'tm', 0, 0, tiled=True, axis_index_groups=same_core)  7.73 us
    ppermute x6, waiting for transfers between devices, shifted(): return lax.ppermute(x, axis, [(i, (i + by) % size) for i in range(size)])  7.62 us
    ppermute x3, waiting for transfers between devices, swapped(): lax.ppermute(x, axis, [(i, i ^ bit) for i in range(lax.axis_size(axis))])  7.29 us
    all_to_all x1, waiting for transfers between devices, on_device(): lax.all_to_all(chip, 'tm', 0, 0, tiled=True, axis_index_groups=same_core)  6.7 us
    ppermute x1, starting transfers between devices, on_device(): lax.ppermute(starts, 'tm', down)  5.15 us
    unnamed x18, local copies, waits for them, and re-layouts  4.53 us
  transfers between devices with their start and end apart: 12, of which 7 were waited for; matrix products, arithmetic and copies ran while one was open for 2% of the time, Pallas kernels for 5%

profile of v6, /device:TPU:1, one launch (start us, length us, event | category | flops | bytes accessed | tf_op | source)
XLA Modules:
  0.0 72.7 jit_solution(16157034975449740527)
XLA Ops:
  0.6 0.0 copy-start
  0.6 0.0 copy-start.7
  0.7 1.3 %slice_bitcast_fusion.2 = (bf16[1,64,1024]{2,1,0:T(8,128)(2,1)S(1)}, bf16[1,64,1024]{2,1,0:T(8,128)(2,1)S(1)}, bf16[1,64,1024]{2,1,0:T(8,128)(2,1)S(1)}, bf16[1,64,1024]{2,1,0:T(8,128)(2,1)S(1)}) fusion(bf16[1024,1024]{1,0:T(8,128)(2,1)} %cot_hbm.1, bf16[1024,1024]{1,0:T(8,128)(2,1)} %frames_hbm.1), kind=kLoop, calls=%fused_computation.23 | loop fusion | bytes 1048576 | tf_op jit(solution)/shard_map/stack | solution.py:289
  2.0 5.1 %collective-permute-start.1 = (bf16[2,64,1024]{2,1,0:T(8,128)(2,1)S(1)}, bf16[2,64,1024]{2,1,0:T(8,128)(2,1)S(1)}, u32[]{:S(2)}, u32[]{:S(2)}) collective-permute-start(bf16[2,64,1024]{2,1,0:T(8,128)(2,1)S(1)} %pad_maximum_fusion.2), channel_id=1, source_target_pairs={{16,0},{32,16},{48,32},{64,48},{80,64},{96,80},{112,96},{128,112},... | collective-permute-start | bytes 786440 | tf_op jit(solution)/shard_map/ppermute | solution.py:291
  7.2 1.9 %collective-permute-start = (bf16[2,64,1024]{2,1,0:T(8,128)(2,1)S(1)}, bf16[2,64,1024]{2,1,0:T(8,128)(2,1)S(1)}, u32[]{:S(2)}, u32[]{:S(2)}) collective-permute-start(bf16[2,64,1024]{2,1,0:T(8,128)(2,1)S(1)} %pad_maximum_fusion.1), channel_id=1, source_target_pairs={{0,16},{16,32},{32,48},{48,64},{64,80},{80,96},{96,112},{112,128},... | collective-permute-start | bytes 786440 | tf_op jit(solution)/shard_map/ppermute | solution.py:291
  9.1 0.0 copy-done
  9.1 0.0 copy-done.7
  9.1 0.0 copy-start.1
  9.1 1.6 %copy-done.1 = bf16[1024,1024]{1,0:T(8,128)(2,1)S(1)} copy-done((bf16[1024,1024]{1,0:T(8,128)(2,1)S(1)}, bf16[1024,1024]{1,0:T(8,128)(2,1)}, u32[]{:S(2)}) %copy-start.1) | copy-done | bytes 2097176
  10.7 0.0 copy-start.3
  10.7 1.1 %copy-done.3 = bf16[3,1024,128]{2,1,0:T(8,128)(2,1)S(1)} copy-done((bf16[3,1024,128]{2,1,0:T(8,128)(2,1)S(1)}, bf16[3,1024,128]{2,1,0:T(8,128)(2,1)}, u32[]{:S(2)}) %copy-start.3) | copy-done | bytes 786456
  11.8 0.0 copy-start.5
  11.8 0.9 %copy-done.5 = bf16[128,1024]{1,0:T(8,128)(2,1)S(1)} copy-done((bf16[128,1024]{1,0:T(8,128)(2,1)S(1)}, bf16[128,1024]{1,0:T(8,128)(2,1)}, u32[]{:S(2)}) %copy-start.5) | copy-done | bytes 262168
  12.8 0.0 copy-start.6
  12.8 0.8 %copy-done.6 = s32[16384]{0:T(1024)S(1)} copy-done((s32[16384]{0:T(1024)S(1)}, s32[16384]{0:T(1024)}, u32[]{:S(2)}) %copy-start.6) | copy-done | bytes 65560
  13.6 0.0 copy-start.2
  13.6 0.0 copy-start.4
  13.6 0.0 copy-start.8
  13.6 3.6 %project.1 = (bf16[4,1024,128]{2,1,0:T(8,128)(2,1)S(1)}, bf16[1024,1024]{1,0:T(8,128)(2,1)S(1)}) custom-call(bf16[1024,1024]{1,0:T(8,128)(2,1)S(1)} %copy-done, f32[1,1024]{1,0:T(1,128)S(1)} %bitcast.33, bf16[3,1024,128]{2,1,0:T(8,128)(2,1)S(1)} %copy-done.3, bf16[128,1024]{1,0:T(8,128)(2,1)S(1)} %copy-done.5, bf16[1024,1024]{1,0:T(8,128)(2,1)S(1)} %copy-done.1, ...), custom_call_target="tpu_custom_call" | custom-call | tf_op jit(solution)/shard_map/project/pallas_call | solution.py:74
  17.3 0.0 collective-permute-done.1
  17.3 0.0 collective-permute-done
  17.4 0.0 copy-done.2
  17.4 0.0 copy-done.4
  17.4 0.0 copy-done.8
  17.4 9.8 %backward.1 = (bf16[4,512,128]{2,1,0:T(8,128)(2,1)S(1)}, bf16[4,512,128]{2,1,0:T(8,128)(2,1)S(1)}, bf16[2,512,128]{2,1,0:T(8,128)(2,1)S(1)}, bf16[2,512,128]{2,1...) custom-call(s32[8]{0:T(128)S(1)} %copy-done.8, ...), custom_call_target="tpu_custom_call" | custom-call | tf_op jit(solution)/shard_map/backward/pallas_call | solution.py:249
  27.2 2.6 %collective-permute-start.5 = (bf16[4,512,128]{2,1,0:T(8,128)(2,1)S(1)}, bf16[4,512,128]{2,1,0:T(8,128)(2,1)S(1)}, u32[]{:S(2)}, u32[]{:S(2)}) collective-permute-start(bf16[4,512,128]{2,1,0:T(8,128)(2,1)S(1)} %get-tuple-element.23), channel_id=1, source_target_pairs={{0,2},{2,0},{4,6},{6,4},{8,10},{10,8},{12,14},{14,12},{1,3},{3,1},... | collective-permute-start | bytes 1572872 | tf_op jit(solution)/shard_map/ppermute | solution.py:275
  29.8 0.0 collective-permute-start.10
  29.8 2.9 %collective-permute-start.2 = (bf16[2,512,128]{2,1,0:T(8,128)(2,1)S(1)}, bf16[2,512,128]{2,1,0:T(8,128)(2,1)S(1)}, u32[]{:S(2)}, u32[]{:S(2)}) collective-permute-start(bf16[2,512,128]{2,1,0:T(8,128)(2,1)S(1)} %get-tuple-element.19), channel_id=1, source_target_pairs={{0,8},{2,10},{4,12},{6,14},{8,0},{10,2},{12,4},{14,6},{1,9},{3,11}... | collective-permute-start | bytes 786440 | tf_op jit(solution)/shard_map/ppermute | solution.py:271
  32.8 0.4 collective-permute-start.3
  33.2 2.3 %collective-permute-start.4 = (bf16[2,512,128]{2,1,0:T(8,128)(2,1)S(1)}, bf16[2,512,128]{2,1,0:T(8,128)(2,1)S(1)}, u32[]{:S(2)}, u32[]{:S(2)}) collective-permute-start(bf16[2,512,128]{2,1,0:T(8,128)(2,1)S(1)} %get-tuple-element.21), channel_id=1, source_target_pairs={{0,12},{2,14},{4,0},{6,2},{8,4},{10,6},{12,8},{14,10},{1,13},{3,15... | collective-permute-start | bytes 786440 | tf_op jit(solution)/shard_map/ppermute | solution.py:271
  35.4 6.4 %collective-permute-done.5 = bf16[4,512,128]{2,1,0:T(8,128)(2,1)S(1)} collective-permute-done((bf16[4,512,128]{2,1,0:T(8,128)(2,1)S(1)}, bf16[4,512,128]{2,1,0:T(8,128)(2,1)S(1)}, u32[]{:S(2)}, u32[]{:S(2)}) %collective-permute-start.5) | collective-permute-done | bytes 524320 | tf_op jit(solution)/shard_map/ppermute | solution.py:275
  41.8 0.1 fusion.5
  41.9 0.0 collective-permute-done.2
  41.9 3.3 %collective-permute-done.3 = bf16[2,512,128]{2,1,0:T(8,128)(2,1)S(1)} collective-permute-done((bf16[2,512,128]{2,1,0:T(8,128)(2,1)S(1)}, bf16[2,512,128]{2,1,0:T(8,128)(2,1)S(1)}, u32[]{:S(2)}, u32[]{:S(2)}) %collective-permute-start.3) | collective-permute-done | bytes 262176 | tf_op jit(solution)/shard_map/ppermute | solution.py:271
  45.2 0.0 collective-permute-done.4
  45.2 0.0 collective-permute-done.10
  45.2 1.0 %add_convert_fusion = bf16[8,4,64,128]{3,2,1,0:T(8,128)(2,1)} fusion(bf16[8,4,64,128]{3,2,1,0:T(8,128)(2,1)S(1)} %collective-permute-done.10, bf16[8,4,64,128]{3,2,1,0:T(8,128)(2,1)S(1)} %get-tuple-element.27), kind=kLoop, calls=%fused_computation | loop fusion | flops 1048576 | bytes 1572864 | tf_op jit(solution)/shard_map/convert_element_type | solution.py:301
  46.2 7.7 %all-to-all-start = ((bf16[8,4,64,128]{3,2,1,0:T(8,128)(2,1)}), bf16[8,4,64,128]{3,2,1,0:T(8,128)(2,1)S(1)}, u32[]{:S(2)}, u32[]{:S(2)}) async-start(bf16[8,4,64,128]{3,2,1,0:T(8,128)(2,1)} %add_convert_fusion), calls=%async_computation | async-start | bytes 1048576 | tf_op jit(solution)/shard_map/all_to_all | solution.py:303
  53.9 0.1 fusion.7
  54.0 0.3 collective-permute-start.6
  54.3 2.7 %collective-permute-start.7 = (bf16[512,128]{1,0:T(8,128)(2,1)S(1)}, bf16[512,128]{1,0:T(8,128)(2,1)S(1)}, u32[]{:S(2)}, u32[]{:S(2)}) collective-permute-start(bf16[512,128]{1,0:T(8,128)(2,1)S(1)} %get-tuple-element.33), channel_id=1, source_target_pairs={{0,8},{2,10},{4,12},{6,14},{8,0},{10,2},{12,4},{14,6},{1,9},{3,11}... | collective-permute-start | bytes 393224 | tf_op jit(solution)/shard_map/ppermute | solution.py:271
  57.0 1.0 %collective-permute-start.9 = (bf16[512,128]{1,0:T(8,128)(2,1)S(1)}, bf16[512,128]{1,0:T(8,128)(2,1)S(1)}, u32[]{:S(2)}, u32[]{:S(2)}) collective-permute-start(bf16[512,128]{1,0:T(8,128)(2,1)S(1)} %get-tuple-element.34), channel_id=1, source_target_pairs={{0,12},{2,14},{4,0},{6,2},{8,4},{10,6},{12,8},{14,10},{1,13},{3,15... | collective-permute-start | bytes 393224 | tf_op jit(solution)/shard_map/ppermute | solution.py:271
  58.0 0.5 collective-permute-start.8
  58.5 0.9 %collective-permute-done.6 = bf16[512,128]{1,0:T(8,128)(2,1)S(1)} collective-permute-done((bf16[512,128]{1,0:T(8,128)(2,1)S(1)}, bf16[512,128]{1,0:T(8,128)(2,1)S(1)}, u32[]{:S(2)}, u32[]{:S(2)}) %collective-permute-start.6) | collective-permute-done | bytes 131104 | tf_op jit(solution)/shard_map/ppermute | solution.py:275
  59.4 0.1 fusion.3
  59.5 0.4 collective-permute-done.7
  59.9 3.0 %collective-permute-done.9 = bf16[512,128]{1,0:T(8,128)(2,1)S(1)} collective-permute-done((bf16[512,128]{1,0:T(8,128)(2,1)S(1)}, bf16[512,128]{1,0:T(8,128)(2,1)S(1)}, u32[]{:S(2)}, u32[]{:S(2)}) %collective-permute-start.9) | collective-permute-done | bytes 131104 | tf_op jit(solution)/shard_map/ppermute | solution.py:271
  62.9 0.9 %collective-permute-done.8 = bf16[512,128]{1,0:T(8,128)(2,1)S(1)} collective-permute-done((bf16[512,128]{1,0:T(8,128)(2,1)S(1)}, bf16[512,128]{1,0:T(8,128)(2,1)S(1)}, u32[]{:S(2)}, u32[]{:S(2)}) %collective-permute-start.8) | collective-permute-done | bytes 131104 | tf_op jit(solution)/shard_map/ppermute | solution.py:271
  63.8 0.1 fusion.2
  64.0 0.7 pad_maximum_fusion.3
  64.7 6.7 %all-to-all-done = bf16[8,4,64,128]{3,2,1,0:T(8,128)(2,1)S(1)} async-done(((bf16[8,4,64,128]{3,2,1,0:T(8,128)(2,1)}), bf16[8,4,64,128]{3,2,1,0:T(8,128)(2,1)S(1)}, u32[]{:S(2)}, u32[]{:S(2)}) %all-to-all-start) | async-done | bytes 524320 | tf_op jit(solution)/shard_map/all_to_all | solution.py:303
  71.4 0.6 convert_reduce_fusion.1
  72.0 0.7 convert_reduce_fusion
  (3 shorter events, 0.1 us)
Async XLA Ops:
  0.6 8.5 %copy-start = (bf16[1024,1024]{1,0:T(8,128)(2,1)S(1)}, bf16[1024,1024]{1,0:T(8,128)(2,1)}, u32[]{:S(2)}) copy-start(bf16[1024,1024]{1,0:T(8,128)(2,1)} %frames_hbm.1) | copy-start | bytes 6291460
  0.6 8.5 %copy-start.7 = (f32[1024]{0:T(1024)S(1)}, f32[1024]{0:T(1024)}, u32[]{:S(2)}) copy-start(f32[1024]{0:T(1024)} %param.8) | copy-start | bytes 12292
  2.0 15.3 %collective-permute-start.1 = (bf16[2,64,1024]{2,1,0:T(8,128)(2,1)S(1)}, bf16[2,64,1024]{2,1,0:T(8,128)(2,1)S(1)}, u32[]{:S(2)}, u32[]{:S(2)}) collective-permute-start(bf16[2,64,1024]{2,1,0:T(8,128)(2,1)S(1)} %pad_maximum_fusion.2), channel_id=1, source_target_pairs={{16,0},{32,16},{48,32},{64,48},{80,64},{96,80},{112,96},{128,112},... | collective-permute-start | bytes 786440 | tf_op jit(solution)/shard_map/ppermute | solution.py:291
  7.2 10.1 %collective-permute-start = (bf16[2,64,1024]{2,1,0:T(8,128)(2,1)S(1)}, bf16[2,64,1024]{2,1,0:T(8,128)(2,1)S(1)}, u32[]{:S(2)}, u32[]{:S(2)}) collective-permute-start(bf16[2,64,1024]{2,1,0:T(8,128)(2,1)S(1)} %pad_maximum_fusion.1), channel_id=1, source_target_pairs={{0,16},{16,32},{32,48},{48,64},{64,80},{80,96},{96,112},{112,128},... | collective-permute-start | bytes 786440 | tf_op jit(solution)/shard_map/ppermute | solution.py:291
  9.1 1.6 %copy-start.1 = (bf16[1024,1024]{1,0:T(8,128)(2,1)S(1)}, bf16[1024,1024]{1,0:T(8,128)(2,1)}, u32[]{:S(2)}) copy-start(bf16[1024,1024]{1,0:T(8,128)(2,1)} %cot_hbm.1) | copy-start | bytes 6291460
  10.7 1.1 %copy-start.3 = (bf16[3,1024,128]{2,1,0:T(8,128)(2,1)S(1)}, bf16[3,1024,128]{2,1,0:T(8,128)(2,1)}, u32[]{:S(2)}) copy-start(bf16[3,1024,128]{2,1,0:T(8,128)(2,1)} %qkv_ref.3) | copy-start | bytes 2359300
  11.8 0.9 %copy-start.5 = (bf16[128,1024]{1,0:T(8,128)(2,1)S(1)}, bf16[128,1024]{1,0:T(8,128)(2,1)}, u32[]{:S(2)}) copy-start(bf16[128,1024]{1,0:T(8,128)(2,1)} %out_ref.3) | copy-start | bytes 786436
  12.8 0.8 %copy-start.6 = (s32[16384]{0:T(1024)S(1)}, s32[16384]{0:T(1024)}, u32[]{:S(2)}) copy-start(s32[16384]{0:T(1024)} %param.12) | copy-start | bytes 196612
  13.6 3.7 %copy-start.2 = (bf16[1024,1024]{1,0:T(8,128)(2,1)S(1)}, bf16[1024,1024]{1,0:T(8,128)(2,1)}, u32[]{:S(2)}) copy-start(bf16[1024,1024]{1,0:T(8,128)(2,1)} %cot_hbm.1) | copy-start | bytes 6291460
  13.6 3.7 %copy-start.4 = (bf16[3,1024,128]{2,1,0:T(8,128)(2,1)S(1)}, bf16[3,1024,128]{2,1,0:T(8,128)(2,1)}, u32[]{:S(2)}) copy-start(bf16[3,1024,128]{2,1,0:T(8,128)(2,1)} %qkv_ref.3) | copy-start | bytes 2359300
  13.6 3.7 %copy-start.8 = (s32[8]{0:T(128)S(1)}, s32[8]{0:T(128)}, u32[]{:S(2)}) copy-start(s32[8]{0:T(128)} %len_ref.1) | copy-start | bytes 100
  27.2 14.6 %collective-permute-start.5 = (bf16[4,512,128]{2,1,0:T(8,128)(2,1)S(1)}, bf16[4,512,128]{2,1,0:T(8,128)(2,1)S(1)}, u32[]{:S(2)}, u32[]{:S(2)}) collective-permute-start(bf16[4,512,128]{2,1,0:T(8,128)(2,1)S(1)} %get-tuple-element.23), channel_id=1, source_target_pairs={{0,2},{2,0},{4,6},{6,4},{8,10},{10,8},{12,14},{14,12},{1,3},{3,1},... | collective-permute-start | bytes 1572872 | tf_op jit(solution)/shard_map/ppermute | solution.py:275
  29.8 15.4 %collective-permute-start.10 = (bf16[8,4,64,128]{3,2,1,0:T(8,128)(2,1)S(1)}, bf16[8,4,64,128]{3,2,1,0:T(8,128)(2,1)S(1)}, u32[]{:S(2)}, u32[]{:S(2)}) collective-permute-start(bf16[8,4,64,128]{3,2,1,0:T(8,128)(2,1)S(1)} %get-tuple-element.28), channel_id=1, source_target_pairs={{0,16},{16,0},{32,48},{48,32},{64,80},{80,64},{96,112},{112,96},{1... | collective-permute-start | bytes 1572872 | tf_op jit(solution)/shard_map/ppermute | solution.py:275
  29.8 12.1 %collective-permute-start.2 = (bf16[2,512,128]{2,1,0:T(8,128)(2,1)S(1)}, bf16[2,512,128]{2,1,0:T(8,128)(2,1)S(1)}, u32[]{:S(2)}, u32[]{:S(2)}) collective-permute-start(bf16[2,512,128]{2,1,0:T(8,128)(2,1)S(1)} %get-tuple-element.19), channel_id=1, source_target_pairs={{0,8},{2,10},{4,12},{6,14},{8,0},{10,2},{12,4},{14,6},{1,9},{3,11}... | collective-permute-start | bytes 786440 | tf_op jit(solution)/shard_map/ppermute | solution.py:271
  32.8 12.4 %collective-permute-start.3 = (bf16[2,512,128]{2,1,0:T(8,128)(2,1)S(1)}, bf16[2,512,128]{2,1,0:T(8,128)(2,1)S(1)}, u32[]{:S(2)}, u32[]{:S(2)}) collective-permute-start(bf16[2,512,128]{2,1,0:T(8,128)(2,1)S(1)} %get-tuple-element.20), channel_id=1, source_target_pairs={{0,4},{2,6},{4,8},{6,10},{8,12},{10,14},{12,0},{14,2},{1,5},{3,7},... | collective-permute-start | bytes 786440 | tf_op jit(solution)/shard_map/ppermute | solution.py:271
  33.2 12.0 %collective-permute-start.4 = (bf16[2,512,128]{2,1,0:T(8,128)(2,1)S(1)}, bf16[2,512,128]{2,1,0:T(8,128)(2,1)S(1)}, u32[]{:S(2)}, u32[]{:S(2)}) collective-permute-start(bf16[2,512,128]{2,1,0:T(8,128)(2,1)S(1)} %get-tuple-element.21), channel_id=1, source_target_pairs={{0,12},{2,14},{4,0},{6,2},{8,4},{10,6},{12,8},{14,10},{1,13},{3,15... | collective-permute-start | bytes 786440 | tf_op jit(solution)/shard_map/ppermute | solution.py:271
  46.2 25.2 %all-to-all-start = ((bf16[8,4,64,128]{3,2,1,0:T(8,128)(2,1)}), bf16[8,4,64,128]{3,2,1,0:T(8,128)(2,1)S(1)}, u32[]{:S(2)}, u32[]{:S(2)}) async-start(bf16[8,4,64,128]{3,2,1,0:T(8,128)(2,1)} %add_convert_fusion), calls=%async_computation | async-start | bytes 1048576 | tf_op jit(solution)/shard_map/all_to_all | solution.py:303
  54.0 5.4 %collective-permute-start.6 = (bf16[512,128]{1,0:T(8,128)(2,1)S(1)}, bf16[512,128]{1,0:T(8,128)(2,1)S(1)}, u32[]{:S(2)}, u32[]{:S(2)}) collective-permute-start(bf16[512,128]{1,0:T(8,128)(2,1)S(1)} %fusion.7), channel_id=1, source_target_pairs={{0,2},{2,0},{4,6},{6,4},{8,10},{10,8},{12,14},{14,12},{1,3},{3,1},... | collective-permute-start | bytes 393224 | tf_op jit(solution)/shard_map/ppermute | solution.py:275
  54.3 5.6 %collective-permute-start.7 = (bf16[512,128]{1,0:T(8,128)(2,1)S(1)}, bf16[512,128]{1,0:T(8,128)(2,1)S(1)}, u32[]{:S(2)}, u32[]{:S(2)}) collective-permute-start(bf16[512,128]{1,0:T(8,128)(2,1)S(1)} %get-tuple-element.33), channel_id=1, source_target_pairs={{0,8},{2,10},{4,12},{6,14},{8,0},{10,2},{12,4},{14,6},{1,9},{3,11}... | collective-permute-start | bytes 393224 | tf_op jit(solution)/shard_map/ppermute | solution.py:271
  57.0 5.9 %collective-permute-start.9 = (bf16[512,128]{1,0:T(8,128)(2,1)S(1)}, bf16[512,128]{1,0:T(8,128)(2,1)S(1)}, u32[]{:S(2)}, u32[]{:S(2)}) collective-permute-start(bf16[512,128]{1,0:T(8,128)(2,1)S(1)} %get-tuple-element.34), channel_id=1, source_target_pairs={{0,12},{2,14},{4,0},{6,2},{8,4},{10,6},{12,8},{14,10},{1,13},{3,15... | collective-permute-start | bytes 393224 | tf_op jit(solution)/shard_map/ppermute | solution.py:271
  58.0 5.9 %collective-permute-start.8 = (bf16[512,128]{1,0:T(8,128)(2,1)S(1)}, bf16[512,128]{1,0:T(8,128)(2,1)S(1)}, u32[]{:S(2)}, u32[]{:S(2)}) collective-permute-start(bf16[512,128]{1,0:T(8,128)(2,1)S(1)} %get-tuple-element.35), channel_id=1, source_target_pairs={{0,4},{2,6},{4,8},{6,10},{8,12},{10,14},{12,0},{14,2},{1,5},{3,7},... | collective-permute-start | bytes 393224 | tf_op jit(solution)/shard_map/ppermute | solution.py:271

commit v7 on v6

--- a/solution.py
+++ b/solution.py
@@ -91,7 +91,7 @@
             jax.ShapeDtypeStruct((count, width), BF16),
         ],
         scratch_shapes=[pltpu.VMEM((width, 3 * HS), BF16)],
-        compiler_params=pltpu.CompilerParams(vmem_limit_bytes=20 << 20),
+        compiler_params=pltpu.CompilerParams(vmem_limit_bytes=48 << 20),
         name="project",
     )(frames, gain, qkv_weight, out_weight, cotangent, pad2d)
 
@@ -301,6 +301,7 @@
     chip = total(keep, other).astype(BF16)
     same_core = [[c + 2 * z for z in range(shards // 2)] for c in range(2)]
     weights = lax.all_to_all(chip, "tm", 0, 0, tiled=True, axis_index_groups=same_core)
+    (near, across, ring_in), _ = lax.optimization_barrier(((near, across, ring_in), chip))
     col = [total(near[k], across[k]) for k in range(4)]
     col_in = [shifted(col[k].astype(BF16), "mp", 2 * k) for k in (2, 1, 3)]
     ring_in, _ = lax.optimization_barrier((ring_in, [c.astype(BF16) for c in col[1:]]))

time: 73.1 us -> 59.5 us (0.81)
  waiting for transfers between devices: 21.6 us -> 9.04 us
  local copies, waits for them, and re-layouts: 5.81 us -> 1.25 us
  other arithmetic: 3.51 us -> 5.43 us
  Pallas kernels: 13.5 us -> 15.3 us
    ppermute x3, waiting for transfers between devices: 7.29 us -> 1.72 us  [swapped(): lax.ppermute(x, axis, [(i, i ^ bit) for i in range(lax.axis_size(axis))])]
    unnamed x18 -> x14, local copies, waits for them, and re-layouts: 4.53 us -> 0.04 us
    all_to_all x1, waiting for transfers between devices: 6.7 us -> 3.2 us  [on_device(): lax.all_to_all(chip, 'tm', 0, 0, tiled=True, axis_index_groups=same_core)]
    ppermute x6, waiting for transfers between devices: 7.62 us -> 4.12 us  [shifted(): return lax.ppermute(x, axis, [(i, (i + by) % size) for i in range(size)])]
    pallas_call x1, Pallas kernels: 3.65 us -> 5.44 us  [project(): pl.pallas_call(project_body, grid=(count // rows,), in_specs=[pl.BlockSpe...]
    ppermute x6, starting transfers between devices: 9.76 us -> 8.61 us  [shifted(): return lax.ppermute(x, axis, [(i, (i + by) % size) for i in range(size)])]
    add x1, other arithmetic: 0.07 us -> 1.04 us  [total(): summed = summed + part.astype(F32)]
    convert_element_type x1, other arithmetic: 0.1 us -> 1.06 us  [on_device(): total(total(ring[0][0], *[r[0] for r in ring_in]), theirs).astype(BF16)]
  transfers between devices with their start and end apart: 12 -> 12, of which waited for: 7 -> 5; matrix products, arithmetic and copies ran while one was open for 2% -> 7% of each run, Pallas kernels for 5% -> 9%
where the time goes in v7:
time: 59.5 us; the launch traced here: 59.2 us
  starting transfers between devices  27.4 us (46%)
  Pallas kernels  15.3 us (26%)
  waiting for transfers between devices  9.04 us (15%)
  other arithmetic  5.43 us (9%)
  local copies, waits for them, and re-layouts  1.25 us (2%)
  between operations  0.85 us (1%)
    pallas_call x1, Pallas kernels, backward(): pl.pallas_call(backward_body, in_specs=[pl.BlockSpec(memory_space=pltpu.S...  9.86 us
    ppermute x6, starting transfers between devices, shifted(): return lax.ppermute(x, axis, [(i, (i + by) % size) for i in range(size)])  8.61 us
    all_to_all x1, starting transfers between devices, on_device(): lax.all_to_all(chip, 'tm', 0, 0, tiled=True, axis_index_groups=same_core)  7.99 us
    pallas_call x1, Pallas kernels, project(): pl.pallas_call(project_body, grid=(count // rows,), in_specs=[pl.BlockSpe...  5.44 us
    ppermute x1, starting transfers between devices, on_device(): lax.ppermute(starts, 'tm', down)  5.15 us
    ppermute x6, waiting for transfers between devices, shifted(): return lax.ppermute(x, axis, [(i, (i + by) % size) for i in range(size)])  4.12 us
    ppermute x3, starting transfers between devices, swapped(): lax.ppermute(x, axis, [(i, i ^ bit) for i in range(lax.axis_size(axis))])  3.68 us
    all_to_all x1, waiting for transfers between devices, on_device(): lax.all_to_all(chip, 'tm', 0, 0, tiled=True, axis_index_groups=same_core)  3.2 us
  transfers between devices with their start and end apart: 12, of which 5 were waited for; matrix products, arithmetic and copies ran while one was open for 7% of the time, Pallas kernels for 9%

profile of v7, /device:TPU:1, one launch (start us, length us, event | category | flops | bytes accessed | tf_op | source)
XLA Modules:
  0.0 59.2 jit_solution(1949011403758451576)
XLA Ops:
  0.6 0.0 copy-start.3
  0.6 0.0 copy-start.2
  0.7 0.0 copy-start.4
  0.7 0.0 copy-start.5
  0.7 1.2 %slice_bitcast_fusion.2 = (bf16[1,64,1024]{2,1,0:T(8,128)(2,1)S(1)}, bf16[1,64,1024]{2,1,0:T(8,128)(2,1)S(1)}, bf16[1,64,1024]{2,1,0:T(8,128)(2,1)S(1)}, bf16[1,64,1024]{2,1,0:T(8,128)(2,1)S(1)}) fusion(bf16[1024,1024]{1,0:T(8,128)(2,1)} %cot_hbm.1, bf16[1024,1024]{1,0:T(8,128)(2,1)} %frames_hbm.1), kind=kLoop, calls=%fused_computation.23 | loop fusion | bytes 1048576 | tf_op jit(solution)/shard_map/stack | solution.py:289
  1.9 5.1 %collective-permute-start.1 = (bf16[2,64,1024]{2,1,0:T(8,128)(2,1)S(1)}, bf16[2,64,1024]{2,1,0:T(8,128)(2,1)S(1)}, u32[]{:S(2)}, u32[]{:S(2)}) collective-permute-start(bf16[2,64,1024]{2,1,0:T(8,128)(2,1)S(1)} %pad_maximum_fusion.2), channel_id=1, source_target_pairs={{16,0},{32,16},{48,32},{64,48},{80,64},{96,80},{112,96},{128,112},... | collective-permute-start | bytes 786440 | tf_op jit(solution)/shard_map/ppermute | solution.py:291
  7.1 1.9 %collective-permute-start = (bf16[2,64,1024]{2,1,0:T(8,128)(2,1)S(1)}, bf16[2,64,1024]{2,1,0:T(8,128)(2,1)S(1)}, u32[]{:S(2)}, u32[]{:S(2)}) collective-permute-start(bf16[2,64,1024]{2,1,0:T(8,128)(2,1)S(1)} %pad_maximum_fusion.1), channel_id=1, source_target_pairs={{0,16},{16,32},{32,48},{48,64},{64,80},{80,96},{96,112},{112,128},... | collective-permute-start | bytes 786440 | tf_op jit(solution)/shard_map/ppermute | solution.py:291
  9.0 0.0 copy-done.3
  9.1 0.0 copy-done.2
  9.1 0.0 copy-done.4
  9.1 0.0 copy-done.5
  9.1 0.0 copy-start
  9.1 0.0 copy-start.1
  9.1 0.0 copy-start.6
  9.1 5.4 %project.1 = (bf16[4,1024,128]{2,1,0:T(8,128)(2,1)S(1)}, bf16[1024,1024]{1,0:T(8,128)(2,1)S(1)}) custom-call(bf16[1024,1024]{1,0:T(8,128)(2,1)} %frames_hbm.1, f32[1,1024]{1,0:T(1,128)S(1)} %bitcast.33, bf16[3,1024,128]{2,1,0:T(8,128)(2,1)S(1)} %copy-done.2, bf16[128,1024]{1,0:T(8,128)(2,1)S(1)} %copy-done.3, bf16[1024,1024]{1,0:T(8,128)(2,1)} %cot_hbm.1, ...), custom_call_target="tpu_custom_call" | custom-call | tf_op jit(solution)/shard_map/project/pallas_call | solution.py:74
  14.6 0.0 collective-permute-done.1
  14.6 0.0 collective-permute-done
  14.6 0.0 copy-done
  14.7 0.0 copy-done.1
  14.7 0.0 copy-done.6
  14.7 9.9 %backward.1 = (bf16[4,512,128]{2,1,0:T(8,128)(2,1)S(1)}, bf16[4,512,128]{2,1,0:T(8,128)(2,1)S(1)}, bf16[2,512,128]{2,1,0:T(8,128)(2,1)S(1)}, bf16[2,512,128]{2,1...) custom-call(s32[8]{0:T(128)S(1)} %copy-done.6, ...), custom_call_target="tpu_custom_call" | custom-call | tf_op jit(solution)/shard_map/backward/pallas_call | solution.py:249
  24.5 0.6 %collective-permute-start.6 = (bf16[8,4,64,128]{3,2,1,0:T(8,128)(2,1)S(1)}, bf16[8,4,64,128]{3,2,1,0:T(8,128)(2,1)S(1)}, u32[]{:S(2)}, u32[]{:S(2)}) collective-permute-start(bf16[8,4,64,128]{3,2,1,0:T(8,128)(2,1)S(1)} %get-tuple-element.30), channel_id=1, source_target_pairs={{0,16},{16,0},{32,48},{48,32},{64,80},{80,64},{96,112},{112,96},{1... | collective-permute-start | bytes 1572872 | tf_op jit(solution)/shard_map/ppermute | solution.py:275
  25.1 2.1 %collective-permute-start.2 = (bf16[4,512,128]{2,1,0:T(8,128)(2,1)S(1)}, bf16[4,512,128]{2,1,0:T(8,128)(2,1)S(1)}, u32[]{:S(2)}, u32[]{:S(2)}) collective-permute-start(bf16[4,512,128]{2,1,0:T(8,128)(2,1)S(1)} %get-tuple-element.25), channel_id=1, source_target_pairs={{0,2},{2,0},{4,6},{6,4},{8,10},{10,8},{12,14},{14,12},{1,3},{3,1},... | collective-permute-start | bytes 1572872 | tf_op jit(solution)/shard_map/ppermute | solution.py:275
  27.3 2.9 %collective-permute-start.3 = (bf16[2,512,128]{2,1,0:T(8,128)(2,1)S(1)}, bf16[2,512,128]{2,1,0:T(8,128)(2,1)S(1)}, u32[]{:S(2)}, u32[]{:S(2)}) collective-permute-start(bf16[2,512,128]{2,1,0:T(8,128)(2,1)S(1)} %get-tuple-element.26), channel_id=1, source_target_pairs={{0,8},{2,10},{4,12},{6,14},{8,0},{10,2},{12,4},{14,6},{1,9},{3,11}... | collective-permute-start | bytes 786440 | tf_op jit(solution)/shard_map/ppermute | solution.py:271
  30.2 0.4 collective-permute-start.4
  30.6 2.3 %collective-permute-start.5 = (bf16[2,512,128]{2,1,0:T(8,128)(2,1)S(1)}, bf16[2,512,128]{2,1,0:T(8,128)(2,1)}, u32[]{:S(2)}, u32[]{:S(2)}) collective-permute-start(bf16[2,512,128]{2,1,0:T(8,128)(2,1)S(1)} %get-tuple-element.28), channel_id=1, source_target_pairs={{0,12},{2,14},{4,0},{6,2},{8,4},{10,6},{12,8},{14,10},{1,13},{3,15... | collective-permute-start | bytes 786440 | tf_op jit(solution)/shard_map/ppermute | solution.py:271
  32.8 0.0 collective-permute-done.6
  32.8 1.0 %add_convert_fusion = bf16[8,4,64,128]{3,2,1,0:T(8,128)(2,1)} fusion(bf16[8,4,64,128]{3,2,1,0:T(8,128)(2,1)S(1)} %collective-permute-done.6, bf16[8,4,64,128]{3,2,1,0:T(8,128)(2,1)S(1)} %get-tuple-element.29), kind=kLoop, calls=%fused_computation | loop fusion | flops 1048576 | bytes 1572864 | tf_op jit(solution)/shard_map/convert_element_type | solution.py:301
  33.8 8.0 %all-to-all-start = ((bf16[8,4,64,128]{3,2,1,0:T(8,128)(2,1)}), bf16[8,4,64,128]{3,2,1,0:T(8,128)(2,1)S(1)}, u32[]{:S(2)}, u32[]{:S(2)}) async-start(bf16[8,4,64,128]{3,2,1,0:T(8,128)(2,1)} %add_convert_fusion), calls=%async_computation | async-start | bytes 1048576 | tf_op jit(solution)/shard_map/all_to_all | solution.py:303
  41.8 0.0 collective-permute-done.3
  41.8 0.9 %collective-permute-done.4 = bf16[2,512,128]{2,1,0:T(8,128)(2,1)} collective-permute-done((bf16[2,512,128]{2,1,0:T(8,128)(2,1)S(1)}, bf16[2,512,128]{2,1,0:T(8,128)(2,1)}, u32[]{:S(2)}, u32[]{:S(2)}) %collective-permute-start.4) | collective-permute-done | bytes 262176 | tf_op jit(solution)/shard_map/ppermute | solution.py:271
  42.7 0.0 collective-permute-done.5
  42.7 0.0 collective-permute-done.2
  42.7 0.1 fusion.5
  42.8 1.0 %fusion.7 = bf16[512,128]{1,0:T(8,128)(2,1)S(1)} fusion(bf16[2,512,128]{2,1,0:T(8,128)(2,1)} %collective-permute-done.5, bf16[2,512,128]{2,1,0:T(8,128)(2,1)} %collective-permute-done.4, bf16[2,512,128]{2,1,0:T(8,128)(2,1)S(1)} %collective-permute-done.3, bf16[2,512,128]{2,1,0:T(8,128)(2,1)S(1)} %get-tuple-element.23), kind=kLoop, calls=%fused_computation.20 | loop fusion | flops 524288 | bytes 655360 | tf_op jit(solution)/shard_map/add | solution.py:281
  43.9 1.0 %collective-permute-start.7 = (bf16[512,128]{1,0:T(8,128)(2,1)S(1)}, bf16[512,128]{1,0:T(8,128)(2,1)S(1)}, u32[]{:S(2)}, u32[]{:S(2)}) collective-permute-start(bf16[512,128]{1,0:T(8,128)(2,1)S(1)} %fusion.7), channel_id=1, source_target_pairs={{0,2},{2,0},{4,6},{6,4},{8,10},{10,8},{12,14},{14,12},{1,3},{3,1},... | collective-permute-start | bytes 393224 | tf_op jit(solution)/shard_map/ppermute | solution.py:275
  44.8 1.2 %collective-permute-start.8 = (bf16[512,128]{1,0:T(8,128)(2,1)S(1)}, bf16[512,128]{1,0:T(8,128)(2,1)S(1)}, u32[]{:S(2)}, u32[]{:S(2)}) collective-permute-start(bf16[512,128]{1,0:T(8,128)(2,1)S(1)} %get-tuple-element.43), channel_id=1, source_target_pairs={{0,8},{2,10},{4,12},{6,14},{8,0},{10,2},{12,4},{14,6},{1,9},{3,11}... | collective-permute-start | bytes 393224 | tf_op jit(solution)/shard_map/ppermute | solution.py:271
  46.0 1.9 %collective-permute-start.10 = (bf16[512,128]{1,0:T(8,128)(2,1)S(1)}, bf16[512,128]{1,0:T(8,128)(2,1)S(1)}, u32[]{:S(2)}, u32[]{:S(2)}) collective-permute-start(bf16[512,128]{1,0:T(8,128)(2,1)S(1)} %get-tuple-element.44), channel_id=1, source_target_pairs={{0,12},{2,14},{4,0},{6,2},{8,4},{10,6},{12,8},{14,10},{1,13},{3,15... | collective-permute-start | bytes 393224 | tf_op jit(solution)/shard_map/ppermute | solution.py:271
  47.9 0.0 collective-permute-start.9
  47.9 1.7 %collective-permute-done.7 = bf16[512,128]{1,0:T(8,128)(2,1)S(1)} collective-permute-done((bf16[512,128]{1,0:T(8,128)(2,1)S(1)}, bf16[512,128]{1,0:T(8,128)(2,1)S(1)}, u32[]{:S(2)}, u32[]{:S(2)}) %collective-permute-start.7) | collective-permute-done | bytes 131104 | tf_op jit(solution)/shard_map/ppermute | solution.py:275
  49.6 1.1 %fusion.3 = bf16[512,128]{1,0:T(8,128)(2,1)S(1)} fusion(bf16[512,128]{1,0:T(8,128)(2,1)S(1)} %collective-permute-done.7, bf16[2,512,128]{2,1,0:T(8,128)(2,1)} %collective-permute-done.5, bf16[2,512,128]{2,1,0:T(8,128)(2,1)} %collective-permute-done.4, bf16[2,512,128]{2,1,0:T(8,128)(2,1)S(1)} %collective-permute-done.3, ...), kind=kLoop, calls=%fused_computation.11 | loop fusion | flops 655360 | bytes 786432 | tf_op jit(solution)/shard_map/convert_element_type | solution.py:309
  50.6 0.0 collective-permute-done.8
  50.7 2.5 %collective-permute-done.10 = bf16[512,128]{1,0:T(8,128)(2,1)S(1)} collective-permute-done((bf16[512,128]{1,0:T(8,128)(2,1)S(1)}, bf16[512,128]{1,0:T(8,128)(2,1)S(1)}, u32[]{:S(2)}, u32[]{:S(2)}) %collective-permute-start.10) | collective-permute-done | bytes 131104 | tf_op jit(solution)/shard_map/ppermute | solution.py:271
  53.1 0.8 %collective-permute-done.9 = bf16[512,128]{1,0:T(8,128)(2,1)S(1)} collective-permute-done((bf16[512,128]{1,0:T(8,128)(2,1)S(1)}, bf16[512,128]{1,0:T(8,128)(2,1)S(1)}, u32[]{:S(2)}, u32[]{:S(2)}) %collective-permute-start.9) | collective-permute-done | bytes 131104 | tf_op jit(solution)/shard_map/ppermute | solution.py:271
  53.9 0.1 fusion.2
  54.0 0.7 %pad_maximum_fusion.3 = bf16[1024,128]{1,0:T(8,128)(2,1)} fusion(bf16[512,128]{1,0:T(8,128)(2,1)S(1)} %fusion.2, bf16[512,128]{1,0:T(8,128)(2,1)S(1)} %fusion.3), kind=kLoop, calls=%fused_computation.5 | loop fusion | flops 524288 | bytes 524288 | tf_op jit(solution)/shard_map/concatenate | solution.py:311
  54.7 3.2 %all-to-all-done = bf16[8,4,64,128]{3,2,1,0:T(8,128)(2,1)S(1)} async-done(((bf16[8,4,64,128]{3,2,1,0:T(8,128)(2,1)}), bf16[8,4,64,128]{3,2,1,0:T(8,128)(2,1)S(1)}, u32[]{:S(2)}, u32[]{:S(2)}) %all-to-all-start) | async-done | bytes 524320 | tf_op jit(solution)/shard_map/all_to_all | solution.py:303
  57.9 0.6 %convert_reduce_fusion.1 = f32[64,128]{1,0:T(8,128)} fusion(bf16[8,4,64,128]{3,2,1,0:T(8,128)(2,1)S(1)} %all-to-all-done), kind=kLoop, calls=%fused_computation.12 | loop fusion | flops 122880 | bytes 163840 | tf_op jit(solution)/shard_map/reduce_sum | solution.py:313
  58.5 0.7 %convert_reduce_fusion = f32[3,64,128]{2,1,0:T(8,128)} fusion(bf16[8,4,64,128]{3,2,1,0:T(8,128)(2,1)S(1)} %all-to-all-done), kind=kLoop, calls=%fused_computation.1 | loop fusion | flops 368640 | bytes 491520 | tf_op jit(solution)/shard_map/reduce_sum | solution.py:312
  (3 shorter events, 0.1 us)
Async XLA Ops:
  0.6 8.4 %copy-start.3 = (bf16[128,1024]{1,0:T(8,128)(2,1)S(1)}, bf16[128,1024]{1,0:T(8,128)(2,1)}, u32[]{:S(2)}) copy-start(bf16[128,1024]{1,0:T(8,128)(2,1)} %out_ref.3) | copy-start | bytes 786436
  0.6 8.4 %copy-start.2 = (bf16[3,1024,128]{2,1,0:T(8,128)(2,1)S(1)}, bf16[3,1024,128]{2,1,0:T(8,128)(2,1)}, u32[]{:S(2)}) copy-start(bf16[3,1024,128]{2,1,0:T(8,128)(2,1)} %qkv_ref.3) | copy-start | bytes 2359300
  0.7 8.4 %copy-start.4 = (s32[16384]{0:T(1024)S(1)}, s32[16384]{0:T(1024)}, u32[]{:S(2)}) copy-start(s32[16384]{0:T(1024)} %param.12) | copy-start | bytes 196612
  0.7 8.4 %copy-start.5 = (f32[1024]{0:T(1024)S(1)}, f32[1024]{0:T(1024)}, u32[]{:S(2)}) copy-start(f32[1024]{0:T(1024)} %param.8) | copy-start | bytes 12292
  1.9 12.7 %collective-permute-start.1 = (bf16[2,64,1024]{2,1,0:T(8,128)(2,1)S(1)}, bf16[2,64,1024]{2,1,0:T(8,128)(2,1)S(1)}, u32[]{:S(2)}, u32[]{:S(2)}) collective-permute-start(bf16[2,64,1024]{2,1,0:T(8,128)(2,1)S(1)} %pad_maximum_fusion.2), channel_id=1, source_target_pairs={{16,0},{32,16},{48,32},{64,48},{80,64},{96,80},{112,96},{128,112},... | collective-permute-start | bytes 786440 | tf_op jit(solution)/shard_map/ppermute | solution.py:291
  7.1 7.5 %collective-permute-start = (bf16[2,64,1024]{2,1,0:T(8,128)(2,1)S(1)}, bf16[2,64,1024]{2,1,0:T(8,128)(2,1)S(1)}, u32[]{:S(2)}, u32[]{:S(2)}) collective-permute-start(bf16[2,64,1024]{2,1,0:T(8,128)(2,1)S(1)} %pad_maximum_fusion.1), channel_id=1, source_target_pairs={{0,16},{16,32},{32,48},{48,64},{64,80},{80,96},{96,112},{112,128},... | collective-permute-start | bytes 786440 | tf_op jit(solution)/shard_map/ppermute | solution.py:291
  9.1 5.6 %copy-start = (bf16[1024,1024]{1,0:T(8,128)(2,1)S(1)}, bf16[1024,1024]{1,0:T(8,128)(2,1)}, u32[]{:S(2)}) copy-start(bf16[1024,1024]{1,0:T(8,128)(2,1)} %frames_hbm.1) | copy-start | bytes 6291460
  9.1 5.6 %copy-start.1 = (bf16[1024,1024]{1,0:T(8,128)(2,1)S(1)}, bf16[1024,1024]{1,0:T(8,128)(2,1)}, u32[]{:S(2)}) copy-start(bf16[1024,1024]{1,0:T(8,128)(2,1)} %cot_hbm.1) | copy-start | bytes 6291460
  9.1 5.6 %copy-start.6 = (s32[8]{0:T(128)S(1)}, s32[8]{0:T(128)}, u32[]{:S(2)}) copy-start(s32[8]{0:T(128)} %len_ref.1) | copy-start | bytes 100
  24.5 8.3 %collective-permute-start.6 = (bf16[8,4,64,128]{3,2,1,0:T(8,128)(2,1)S(1)}, bf16[8,4,64,128]{3,2,1,0:T(8,128)(2,1)S(1)}, u32[]{:S(2)}, u32[]{:S(2)}) collective-permute-start(bf16[8,4,64,128]{3,2,1,0:T(8,128)(2,1)S(1)} %get-tuple-element.30), channel_id=1, source_target_pairs={{0,16},{16,0},{32,48},{48,32},{64,80},{80,64},{96,112},{112,96},{1... | collective-permute-start | bytes 1572872 | tf_op jit(solution)/shard_map/ppermute | solution.py:275
  25.1 17.6 %collective-permute-start.2 = (bf16[4,512,128]{2,1,0:T(8,128)(2,1)S(1)}, bf16[4,512,128]{2,1,0:T(8,128)(2,1)S(1)}, u32[]{:S(2)}, u32[]{:S(2)}) collective-permute-start(bf16[4,512,128]{2,1,0:T(8,128)(2,1)S(1)} %get-tuple-element.25), channel_id=1, source_target_pairs={{0,2},{2,0},{4,6},{6,4},{8,10},{10,8},{12,14},{14,12},{1,3},{3,1},... | collective-permute-start | bytes 1572872 | tf_op jit(solution)/shard_map/ppermute | solution.py:275
  27.3 14.6 %collective-permute-start.3 = (bf16[2,512,128]{2,1,0:T(8,128)(2,1)S(1)}, bf16[2,512,128]{2,1,0:T(8,128)(2,1)S(1)}, u32[]{:S(2)}, u32[]{:S(2)}) collective-permute-start(bf16[2,512,128]{2,1,0:T(8,128)(2,1)S(1)} %get-tuple-element.26), channel_id=1, source_target_pairs={{0,8},{2,10},{4,12},{6,14},{8,0},{10,2},{12,4},{14,6},{1,9},{3,11}... | collective-permute-start | bytes 786440 | tf_op jit(solution)/shard_map/ppermute | solution.py:271
  30.2 12.6 %collective-permute-start.4 = (bf16[2,512,128]{2,1,0:T(8,128)(2,1)S(1)}, bf16[2,512,128]{2,1,0:T(8,128)(2,1)}, u32[]{:S(2)}, u32[]{:S(2)}) collective-permute-start(bf16[2,512,128]{2,1,0:T(8,128)(2,1)S(1)} %get-tuple-element.27), channel_id=1, source_target_pairs={{0,4},{2,6},{4,8},{6,10},{8,12},{10,14},{12,0},{14,2},{1,5},{3,7},... | collective-permute-start | bytes 786440 | tf_op jit(solution)/shard_map/ppermute | solution.py:271
  30.6 12.1 %collective-permute-start.5 = (bf16[2,512,128]{2,1,0:T(8,128)(2,1)S(1)}, bf16[2,512,128]{2,1,0:T(8,128)(2,1)}, u32[]{:S(2)}, u32[]{:S(2)}) collective-permute-start(bf16[2,512,128]{2,1,0:T(8,128)(2,1)S(1)} %get-tuple-element.28), channel_id=1, source_target_pairs={{0,12},{2,14},{4,0},{6,2},{8,4},{10,6},{12,8},{14,10},{1,13},{3,15... | collective-permute-start | bytes 786440 | tf_op jit(solution)/shard_map/ppermute | solution.py:271
  33.8 24.1 %all-to-all-start = ((bf16[8,4,64,128]{3,2,1,0:T(8,128)(2,1)}), bf16[8,4,64,128]{3,2,1,0:T(8,128)(2,1)S(1)}, u32[]{:S(2)}, u32[]{:S(2)}) async-start(bf16[8,4,64,128]{3,2,1,0:T(8,128)(2,1)} %add_convert_fusion), calls=%async_computation | async-start | bytes 1048576 | tf_op jit(solution)/shard_map/all_to_all | solution.py:303
  43.9 5.7 %collective-permute-start.7 = (bf16[512,128]{1,0:T(8,128)(2,1)S(1)}, bf16[512,128]{1,0:T(8,128)(2,1)S(1)}, u32[]{:S(2)}, u32[]{:S(2)}) collective-permute-start(bf16[512,128]{1,0:T(8,128)(2,1)S(1)} %fusion.7), channel_id=1, source_target_pairs={{0,2},{2,0},{4,6},{6,4},{8,10},{10,8},{12,14},{14,12},{1,3},{3,1},... | collective-permute-start | bytes 393224 | tf_op jit(solution)/shard_map/ppermute | solution.py:275
  44.8 5.8 %collective-permute-start.8 = (bf16[512,128]{1,0:T(8,128)(2,1)S(1)}, bf16[512,128]{1,0:T(8,128)(2,1)S(1)}, u32[]{:S(2)}, u32[]{:S(2)}) collective-permute-start(bf16[512,128]{1,0:T(8,128)(2,1)S(1)} %get-tuple-element.43), channel_id=1, source_target_pairs={{0,8},{2,10},{4,12},{6,14},{8,0},{10,2},{12,4},{14,6},{1,9},{3,11}... | collective-permute-start | bytes 393224 | tf_op jit(solution)/shard_map/ppermute | solution.py:271
  46.0 7.1 %collective-permute-start.10 = (bf16[512,128]{1,0:T(8,128)(2,1)S(1)}, bf16[512,128]{1,0:T(8,128)(2,1)S(1)}, u32[]{:S(2)}, u32[]{:S(2)}) collective-permute-start(bf16[512,128]{1,0:T(8,128)(2,1)S(1)} %get-tuple-element.44), channel_id=1, source_target_pairs={{0,12},{2,14},{4,0},{6,2},{8,4},{10,6},{12,8},{14,10},{1,13},{3,15... | collective-permute-start | bytes 393224 | tf_op jit(solution)/shard_map/ppermute | solution.py:271
  47.9 6.0 %collective-permute-start.9 = (bf16[512,128]{1,0:T(8,128)(2,1)S(1)}, bf16[512,128]{1,0:T(8,128)(2,1)S(1)}, u32[]{:S(2)}, u32[]{:S(2)}) collective-permute-start(bf16[512,128]{1,0:T(8,128)(2,1)S(1)} %get-tuple-element.45), channel_id=1, source_target_pairs={{0,4},{2,6},{4,8},{6,10},{8,12},{10,14},{12,0},{14,2},{1,5},{3,7},... | collective-permute-start | bytes 393224 | tf_op jit(solution)/shard_map/ppermute | solution.py:271

commit v8 on v7

v8 whole, which is shorter than its diff:
```python
import jax
import jax.numpy as jnp
from jax import lax
from jax.experimental import pallas as pl
from jax.experimental.pallas import tpu as pltpu
from jax.sharding import PartitionSpec as P

HS = 128
CH = 32
HALO = 64
EPSILON = 1e-05
SCALE = HS ** (-0.5)
F32 = jnp.float32
BF16 = jnp.bfloat16


def rows_by_rows(left, right):
    return lax.dot_general(left, right, (((1,), (1,)), ((), ())), preferred_element_type=F32)


def cols_by_cols(left, right):
    return lax.dot_general(left, right, (((0,), (0,)), ((), ())), preferred_element_type=F32)


def plain(left, right):
    return jnp.dot(left, right, preferred_element_type=F32)


def normalised(values):
    values = values.astype(F32)
    mean = jnp.mean(values, axis=-1, keepdims=True)
    center = values - mean
    inverse = lax.rsqrt(jnp.mean(center * center, axis=-1, keepdims=True) + EPSILON)
    return center * inverse, inverse, mean


def pad_rows(pad_ref, first, count):
    total = pad_ref.shape[0]
    return [pad_ref[pl.ds(jnp.clip(first + i, 0, total - 1), 1), :] for i in range(count)]


def as_columns(rows):
    height = -(-len(rows) // 8) * 8
    full = jnp.concatenate(rows + [jnp.zeros_like(rows[0])] * (height - len(rows)), axis=0)
    return full.T


def project_body(
    frames_hbm, gain_ref, qkv_hbm, out_hbm, cot_hbm, pad_ref, proj_ref, stats_ref, normed_hbm,
    frames_ref, w_scr, out_ref, cot_ref, normed_ref, sems,
):
    count = frames_ref.shape[0]
    rows = count // 2
    halves = [pl.ds(0, rows), pl.ds(rows, rows)]
    moves = [(frames_hbm.at[span], frames_ref.at[span]) for span in halves]
    moves += [(qkv_hbm.at[m], w_scr.at[:, m * HS : (m + 1) * HS]) for m in range(3)]
    moves += [(out_hbm, out_ref), (cot_hbm, cot_ref)]
    moves += [(normed_ref.at[span], normed_hbm.at[span]) for span in halves]
    copies = [pltpu.make_async_copy(source, target, sems.at[i]) for i, (source, target) in enumerate(moves)]
    for i in (0, 2, 3, 4, 1, 5, 6):
        copies[i].start()
    lane = lax.broadcasted_iota(jnp.int32, (rows, 128), 1)

    def norm_rows(half):
        normal_form, inverse, mean = normalised(frames_ref[halves[half], :])
        stats_ref[halves[half], :] = jnp.where(lane == 0, mean, inverse)
        normed = (normal_form * gain_ref[...]).astype(BF16)
        normed_ref[halves[half], :] = normed
        return normed

    def project_rows(half, normed):
        qkv = plain(normed, w_scr[...]).astype(BF16)
        for m in range(3):
            proj_ref[m, halves[half], :] = qkv[:, m * HS : (m + 1) * HS]

    copies[0].wait()
    first = norm_rows(0)
    copies[7].start()
    for i in (2, 3, 4, 1):
        copies[i].wait()
    project_rows(0, first)
    second = norm_rows(1)
    for i in (5, 6):
        copies[i].wait()
    copies[8].start()
    blocks = count // 128
    live = as_columns([r.astype(F32) for r in pad_rows(pad_ref, lax.axis_index("tm") * blocks, blocks)])
    live = jnp.concatenate([live[:, i : i + 1] for i in range(blocks)], axis=0)
    project_rows(1, second)
    grads = rows_by_rows(cot_ref[...], out_ref[...])
    proj_ref[3] = jnp.where(live == 1.0, grads, 0.0).astype(BF16)
    copies[7].wait()
    copies[8].wait()


def project(frames, gain, qkv_weight, out_weight, cotangent, pad2d):
    count, width = frames.shape
    vmem = pl.BlockSpec(memory_space=pltpu.VMEM)
    hbm = pl.BlockSpec(memory_space=pl.ANY)
    return pl.pallas_call(
        project_body,
        in_specs=[hbm, vmem, hbm, hbm, hbm, vmem],
        out_specs=[vmem, vmem, hbm],
        out_shape=[
            jax.ShapeDtypeStruct((4, count, HS), BF16),
            jax.ShapeDtypeStruct((count, 128), F32),
            jax.ShapeDtypeStruct((count, width), BF16),
        ],
        scratch_shapes=[
            pltpu.VMEM((count, width), BF16),
            pltpu.VMEM((width, 3 * HS), BF16),
            pltpu.VMEM(out_weight.shape, BF16),
            pltpu.VMEM((count, width), BF16),
            pltpu.VMEM((count, width), BF16),
            pltpu.SemaphoreType.DMA((9,)),
        ],
        compiler_params=pltpu.CompilerParams(vmem_limit_bytes=48 << 20),
        name="project",
    )(frames, gain, qkv_weight, out_weight, cotangent, pad2d)


def backward_body(
    len_ref, proj_ref, stats_ref, halo_ref, gain_ref, qkv_ref, out_ref, pad_ref, frames_hbm, normed_hbm, cot_hbm,
    near_ref, across_ref, ring0_ref, ring1_ref, ring2_ref, ring3_ref, keep_ref, send_ref,
    x_scr, grads_ref, mixed_ref, w_scr, frames_ref, normed_ref, cot_ref, sems,
):
    fetches = [
        pltpu.make_async_copy(source, target, sems.at[i])
        for i, (source, target) in enumerate(
            [(frames_hbm, frames_ref), (normed_hbm, normed_ref), (cot_hbm, cot_ref)]
        )
    ]
    for fetch in fetches:
        fetch.start()
    count = proj_ref.shape[1]
    tiles = count // 128 + 1
    shard = lax.axis_index("tm")
    first_block = shard * (count // 128) - 1
    normal_form, _, _ = normalised(halo_ref[0])
    normed = (normal_form * gain_ref[...]).astype(BF16)
    blocks = tiles + 1
    live_rows = [r.astype(F32) for r in pad_rows(pad_ref, first_block, blocks)]
    live_cols = as_columns(live_rows)
    halo_live = jnp.concatenate([live_cols[HALO:, 0:1], live_cols[:HALO, blocks - 1 : blocks]], axis=0)
    zeros = jnp.zeros((HALO, HS), BF16)
    for m in range(4):
        if m < 3:
            part = plain(normed, qkv_ref[m])
        else:
            part = jnp.where(halo_live == 1.0, rows_by_rows(halo_ref[1], out_ref[...]), 0.0)
        part = part.astype(BF16)
        x_scr[m, 0:HALO, :] = zeros
        x_scr[m, HALO : 2 * HALO, :] = part[:HALO]
        x_scr[m, 2 * HALO : 2 * HALO + count, :] = proj_ref[m]
        x_scr[m, 2 * HALO + count : 3 * HALO + count, :] = part[HALO:]
        x_scr[m, 3 * HALO + count :, :] = zeros

    ends = []
    total = 0
    for u in range(len_ref.shape[0]):
        total = total + len_ref[u]
        ends.append(total)

    def segment(positions):
        found = jnp.zeros(positions.shape, jnp.int32)
        for end in ends:
            found = found + jnp.where(positions >= end, 1, 0)
        return found.astype(F32)

    lane = lax.broadcasted_iota(jnp.int32, (1, 128), 1)
    codes = []
    for b in range(blocks):
        at = (first_block + b) * 128 + lane
        codes.append(jnp.where((live_rows[b] == 1.0) & (at >= 0), segment(at), -1.0))
    code_cols = as_columns(codes)

    keys = 192
    key_at = lax.broadcasted_iota(jnp.int32, (keys, 128), 0)
    query_at = lax.broadcasted_iota(jnp.int32, (keys, 128), 1)
    apart = key_at // CH - query_at // CH
    in_band = (apart >= 0) & (apart <= 2)
    same = key_at == query_at + CH

    place = lax.axis_index("mp")
    owners = [jnp.bitwise_xor(place, j) for j in range(8)]
    spans = [pl.ds(pl.multiple_of(owner * 128, 128), 128) for owner in owners]
    for m in range(3):
        for j, span in enumerate(spans):
            w_scr[j * 128 : (j + 1) * 128, m * HS : (m + 1) * HS] = qkv_ref[m, span, :]
    gain = jnp.concatenate([gain_ref[:, span] for span in spans], axis=1)
    ring_refs = (ring0_ref, ring1_ref, ring2_ref, ring3_ref)

    def input_rows(at, rows):
        incoming = rows_by_rows(grads_ref[at : at + rows, :], w_scr[...])
        frames = jnp.concatenate([frames_ref[at : at + rows, span] for span in spans], axis=1)
        center = frames.astype(F32) - stats_ref[at : at + rows, 0:1]
        inverse = stats_ref[at : at + rows, 1:2]
        scaled = incoming * gain
        mean_grad = jnp.mean(scaled, axis=-1, keepdims=True)
        slope = jnp.mean(scaled * center, axis=-1, keepdims=True) * (inverse * inverse)
        result = (inverse * (scaled - mean_grad - center * slope)).astype(BF16)
        to = at % (count // 2)
        for j in range(8):
            part = result[:, j * 128 : (j + 1) * 128]
            if at < count // 2:
                ring_refs[j // 2][j % 2, to : to + rows, :] = part
            else:
                (near_ref, across_ref)[j % 2][j // 2, to : to + rows, :] = part

    carry = [None, None]

    def attention(tiles_now):
        q = [x_scr[0, 128 * t + HALO : 128 * t + HALO + 128, :] for t in tiles_now]
        g = [x_scr[3, 128 * t + HALO : 128 * t + HALO + 128, :] for t in tiles_now]
        k = [x_scr[1, 128 * t + CH : 128 * t + CH + keys, :] for t in tiles_now]
        v = [x_scr[2, 128 * t + CH : 128 * t + CH + keys, :] for t in tiles_now]
        n = range(len(tiles_now))
        scores = [rows_by_rows(k[i], q[i]) for i in n]
        prob_grad = [rows_by_rows(v[i], g[i]) for i in n]
        probs = []
        for i in n:
            t = tiles_now[i]
            query_seg = segment((first_block + t) * 128 + HALO + lane)
            code = jnp.concatenate([code_cols[CH:, t : t + 1], code_cols[: keys - 96, t + 1 : t + 2]], axis=0)
            allowed = in_band & ((code == query_seg) | same)
            masked = jnp.where(allowed, scores[i] * SCALE, -1e30)
            weights = jnp.exp(masked - jnp.max(masked, axis=0, keepdims=True))
            probs.append(weights * (1.0 / jnp.sum(weights, axis=0, keepdims=True)))
        rounded = [p.astype(BF16) for p in probs]
        score_grad = []
        for i in n:
            centre = jnp.sum(probs[i] * prob_grad[i], axis=0, keepdims=True)
            score_grad.append((probs[i] * (prob_grad[i] - centre) * SCALE).astype(BF16))
        value_grad = [plain(rounded[i], g[i]) for i in n]
        key_grad = [plain(score_grad[i], q[i]) for i in n]
        mixed = [cols_by_cols(rounded[i], v[i]).astype(BF16) for i in n]
        query_grad = [cols_by_cols(score_grad[i], k[i]).astype(BF16) for i in n]
        for i in n:
            t = tiles_now[i]
            base = 128 * t
            live = jnp.concatenate([live_cols[HALO:, t : t + 1], live_cols[:HALO, t + 1 : t + 2]], axis=0)
            shown = jnp.where(live == 1.0, mixed[i], jnp.zeros_like(mixed[i]))
            lo, hi = (HALO if t == 0 else 0), (HALO if t == tiles - 1 else 128)
            at = base - HALO
            mixed_ref[at + lo : at + hi, :] = shown[lo:hi]
            grads_ref[at + lo : at + hi, 0:HS] = query_grad[i][lo:hi]
            lo, hi = (96 if t == 0 else 0), (96 if t == tiles - 1 else 128)
            at = base - 96
            for m, grad in enumerate((key_grad[i], value_grad[i])):
                left = carry[m]
                carry[m] = grad[128:]
                if t > 0:
                    grad = jnp.concatenate([grad[:64] + left, grad[64:]], axis=0)
                grads_ref[at + lo : at + hi, (m + 1) * HS : (m + 2) * HS] = grad[lo:hi].astype(BF16)

    attention([0, 1, 2, 3, 4, 5, 6, 7, 8])
    fetches[0].wait()
    input_rows(0, 512)
    input_rows(512, 512)

    fetches[1].wait()
    fetches[2].wait()
    core = shard % 2
    qkv = cols_by_cols(grads_ref[...], normed_ref[...]).astype(BF16)
    out = cols_by_cols(mixed_ref[...], cot_ref[...]).astype(BF16)
    full = jnp.concatenate([qkv, out], axis=0)
    for z in range(8):
        both = full[:, z * 128 : (z + 1) * 128].T
        low, high = both[:64], both[64:]
        keep = jnp.where(core == 0, low, high)
        send = jnp.where(core == 0, high, low)
        for m in range(4):
            keep_ref[z, m] = keep[:, m * HS : (m + 1) * HS]
            send_ref[z, m] = send[:, m * HS : (m + 1) * HS]


def backward(lengths, proj, stats, halo, gain, qkv_weight, out_weight, pad2d, frames, normed, cotangent):
    count, width = frames.shape
    vmem = pl.BlockSpec(memory_space=pltpu.VMEM)
    half = count // 2
    shapes = [(4, half, 128)] * 2 + [(2, half, 128)] * 4 + [(8, 4, width // 16, HS)] * 2
    return pl.pallas_call(
        backward_body,
        in_specs=[pl.BlockSpec(memory_space=pltpu.SMEM)] + [vmem] * 7 + [pl.BlockSpec(memory_space=pl.ANY)] * 3,
        out_specs=[vmem] * len(shapes),
        out_shape=[jax.ShapeDtypeStruct(shape, BF16) for shape in shapes],
        scratch_shapes=[
            pltpu.VMEM((4, count + 4 * HALO, HS), BF16),
            pltpu.VMEM((count, 3 * HS), BF16),
            pltpu.VMEM((count, HS), BF16),
            pltpu.VMEM((width, 3 * HS), BF16),
            pltpu.VMEM((count, width), BF16),
            pltpu.VMEM((count, width), BF16),
            pltpu.VMEM((count, width), BF16),
            pltpu.SemaphoreType.DMA((3,)),
        ],
        compiler_params=pltpu.CompilerParams(vmem_limit_bytes=40 << 20),
        name="backward",
    )(lengths, proj, stats, halo, gain, qkv_weight, out_weight, pad2d, frames, normed, cotangent)


def swapped(x, axis, bit):
    return lax.ppermute(x, axis, [(i, i ^ bit) for i in range(lax.axis_size(axis))])


def total(*parts):
    summed = parts[0].astype(F32)
    for part in parts[1:]:
        summed = summed + part.astype(F32)
    return summed


def on_device(frames, norm_gain, qkv_weight, out_weight, cotangent, pad_mask, utt_lengths):
    shards = lax.axis_size("tm")
    up = [(i, i + 1) for i in range(shards - 1)]
    down = [(i + 1, i) for i in range(shards - 1)]
    ends = jnp.stack([frames[-HALO:], cotangent[-HALO:]])
    starts = jnp.stack([frames[:HALO], cotangent[:HALO]])
    halo = jnp.concatenate([lax.ppermute(ends, "tm", up), lax.ppermute(starts, "tm", down)], axis=1)
    gain = norm_gain[None, :]
    pad2d = pad_mask.reshape(-1, 128)
    proj, stats, normed = project(frames, gain, qkv_weight, out_weight, cotangent, pad2d)
    near, across, *ring, keep, send = backward(
        utt_lengths, proj, stats, halo, gain, qkv_weight, out_weight, pad2d, frames, normed, cotangent
    )
    other = swapped(send, "tm", 1)
    across = swapped(across, "mp", 1)
    ring_in = [swapped(ring[k], "mp", 2 * k) for k in (2, 1, 3)]
    chip = total(keep, other).astype(BF16)
    same_core = [[c + 2 * z for z in range(shards // 2)] for c in range(2)]
    weights = lax.all_to_all(chip, "tm", 0, 0, tiled=True, axis_index_groups=same_core)
    (near, across, ring_in), _ = lax.optimization_barrier(((near, across, ring_in), chip))
    col = [total(near[k], across[k]) for k in range(4)]
    col_in = [swapped(col[k].astype(BF16), "mp", 2 * k) for k in (2, 1, 3)]
    ring_in, _ = lax.optimization_barrier((ring_in, [c.astype(BF16) for c in col[1:]]))
    theirs = swapped(total(ring[0][1], *[r[1] for r in ring_in]).astype(BF16), "mp", 1)
    qkv_grad = weights[:, :3].astype(F32).sum(axis=0)
    out_grad = weights[:, 3].astype(F32).sum(axis=0)
    (theirs, col_in), _ = lax.optimization_barrier(((theirs, col_in), (qkv_grad, out_grad)))
    first_half = total(total(ring[0][0], *[r[0] for r in ring_in]), theirs).astype(BF16)
    second_half = total(col[0], *col_in).astype(BF16)
    frame_grad = jnp.concatenate([first_half, second_half], axis=0)
    return frame_grad, qkv_grad, out_grad.T


def solution(mesh):
    placed = (
        P(("batch", "tm"), None),
        P(),
        P(None, None, "mp"),
        P("mp", None),
        P(("batch", "tm"), None),
        P("batch"),
        P("batch"),
    )
    return jax.shard_map(
        on_device,
        mesh=mesh,
        in_specs=placed,
        out_specs=(P(("batch", "tm"), "mp"), P("batch", "tm", "mp"), P(("batch", "mp"), "tm")),
        check_vma=False,
    )
```

time: 59.5 us -> 61 us (1.025); the launches traced: 59.2 us -> 60 us
  waiting for transfers between devices: 9.04 us -> 14.4 us
  Pallas kernels: 15.3 us -> 11.6 us
  other arithmetic: 5.43 us -> 4.46 us
    ppermute x3 -> x9, waiting for transfers between devices: 1.72 us -> 14.4 us  [swapped(): lax.ppermute(x, axis, [(i, i ^ bit) for i in range(lax.axis_size(axis))])]
    ppermute x6 -> x0, starting transfers between devices: 8.61 us -> none  [shifted(): return lax.ppermute(x, axis, [(i, (i + by) % size) for i in range(size)])]
    ppermute x3 -> x9, starting transfers between devices: 3.68 us -> 11.5 us  [swapped(): lax.ppermute(x, axis, [(i, i ^ bit) for i in range(lax.axis_size(axis))])]
    ppermute x6 -> x0, waiting for transfers between devices: 4.12 us -> none  [shifted(): return lax.ppermute(x, axis, [(i, (i + by) % size) for i in range(size)])]
    all_to_all x1, waiting for transfers between devices: 3.2 us -> 0.01 us  [on_device(): lax.all_to_all(chip, 'tm', 0, 0, tiled=True, axis_index_groups=same_core)]
    pallas_call x1, Pallas kernels: 9.86 us -> 6.96 us  [backward(): pl.pallas_call(backward_body, in_specs=[pl.BlockSpec(memory_space=pltpu.S...]
    add x1, other arithmetic: 1.04 us -> 0.08 us  [total(): summed = summed + part.astype(F32)]
    all_to_all x1, starting transfers between devices: 7.99 us -> 8.83 us  [on_device(): lax.all_to_all(chip, 'tm', 0, 0, tiled=True, axis_index_groups=same_core)]
  transfers between devices with their start and end apart: 12 -> 12, of which waited for: 5 -> 4; matrix products, arithmetic and copies ran while one was open for 7% -> 4% of each run, Pallas kernels for 9% -> 8%
where the time goes in v8:
time: 61 us; the launch traced here: 60 us
  starting transfers between devices  27.4 us (45%)
  waiting for transfers between devices  14.4 us (24%)
  Pallas kernels  11.6 us (19%)
  other arithmetic  4.46 us (7%)
  local copies, waits for them, and re-layouts  1.26 us (2%)
  between operations  0.86 us (1%)
    ppermute x9, waiting for transfers between devices, swapped(): lax.ppermute(x, axis, [(i, i ^ bit) for i in range(lax.axis_size(axis))])  14.4 us
    ppermute x9, starting transfers between devices, swapped(): lax.ppermute(x, axis, [(i, i ^ bit) for i in range(lax.axis_size(axis))])  11.5 us
    all_to_all x1, starting transfers between devices, on_device(): lax.all_to_all(chip, 'tm', 0, 0, tiled=True, axis_index_groups=same_core)  8.83 us
    pallas_call x1, Pallas kernels, backward(): pl.pallas_call(backward_body, in_specs=[pl.BlockSpec(memory_space=pltpu.S...  6.96 us
    ppermute x1, starting transfers between devices, on_device(): lax.ppermute(starts, 'tm', down)  5.15 us
    pallas_call x1, Pallas kernels, project(): pl.pallas_call(project_body, in_specs=[hbm, vmem, hbm, hbm, hbm, vmem], o...  4.64 us
    ppermute x1, starting transfers between devices, on_device(): lax.ppermute(ends, 'tm', up)  1.92 us
  transfers between devices with their start and end apart: 12, of which 4 were waited for; matrix products, arithmetic and copies ran while one was open for 4% of the time, Pallas kernels for 8%

profile of v8, /device:TPU:1, one launch (start us, length us, event | category | flops | bytes accessed | tf_op | source)
XLA Modules:
  0.0 60.0 jit_solution(14995722988191699782)
XLA Ops:
  0.6 0.0 copy-start.3
  0.6 0.0 copy-start.2
  0.7 0.0 copy-start.4
  0.7 0.0 copy-start.5
  0.7 1.2 %slice_bitcast_fusion.2 = (bf16[1,64,1024]{2,1,0:T(8,128)(2,1)S(1)}, bf16[1,64,1024]{2,1,0:T(8,128)(2,1)S(1)}, bf16[1,64,1024]{2,1,0:T(8,128)(2,1)S(1)}, bf16[1,64,1024]{2,1,0:T(8,128)(2,1)S(1)}) fusion(bf16[1024,1024]{1,0:T(8,128)(2,1)} %cot_hbm.3, bf16[1024,1024]{1,0:T(8,128)(2,1)} %frames_hbm.3), kind=kLoop, calls=%fused_computation.23 | loop fusion | bytes 1048576 | tf_op jit(solution)/shard_map/stack | solution.py:317
  1.9 5.1 %collective-permute-start.1 = (bf16[2,64,1024]{2,1,0:T(8,128)(2,1)S(1)}, bf16[2,64,1024]{2,1,0:T(8,128)(2,1)S(1)}, u32[]{:S(2)}, u32[]{:S(2)}) collective-permute-start(bf16[2,64,1024]{2,1,0:T(8,128)(2,1)S(1)} %pad_maximum_fusion.2), channel_id=1, source_target_pairs={{16,0},{32,16},{48,32},{64,48},{80,64},{96,80},{112,96},{128,112},... | collective-permute-start | bytes 786440 | tf_op jit(solution)/shard_map/ppermute | solution.py:319
  7.1 1.9 %collective-permute-start = (bf16[2,64,1024]{2,1,0:T(8,128)(2,1)S(1)}, bf16[2,64,1024]{2,1,0:T(8,128)(2,1)S(1)}, u32[]{:S(2)}, u32[]{:S(2)}) collective-permute-start(bf16[2,64,1024]{2,1,0:T(8,128)(2,1)S(1)} %pad_maximum_fusion.1), channel_id=1, source_target_pairs={{0,16},{16,32},{32,48},{48,64},{64,80},{80,96},{96,112},{112,128},... | collective-permute-start | bytes 786440 | tf_op jit(solution)/shard_map/ppermute | solution.py:319
  9.0 0.0 copy-done.3
  9.1 0.0 copy-done.2
  9.1 0.0 copy-done.4
  9.1 0.0 copy-done.5
  9.1 0.0 copy-start
  9.1 0.0 copy-start.1
  9.1 0.0 copy-start.6
  9.1 4.6 %project.1 = (bf16[4,1024,128]{2,1,0:T(8,128)(2,1)S(1)}, f32[1024,128]{1,0:T(8,128)S(1)}, bf16[1024,1024]{1,0:T(8,128)(2,1)S(1)}) custom-call(bf16[1024,1024]{1,0:T(8,128)(2,1)} %frames_hbm.3, f32[1,1024]{1,0:T(1,128)S(1)} %bitcast.33, bf16[3,1024,128]{2,1,0:T(8,128)(2,1)S(1)} %copy-done.2, bf16[128,1024]{1,0:T(8,128)(2,1)S(1)} %copy-done.3, ...), custom_call_target="tpu_custom_call" | custom-call | tf_op jit(solution)/shard_map/project/pallas_call | solution.py:100
  13.8 0.0 collective-permute-done.1
  13.8 0.0 collective-permute-done
  13.8 0.0 copy-done
  13.8 0.0 copy-done.1
  13.9 0.0 copy-done.6
  13.9 7.0 %backward.1 = (bf16[4,512,128]{2,1,0:T(8,128)(2,1)S(1)}, bf16[4,512,128]{2,1,0:T(8,128)(2,1)S(1)}, bf16[2,512,128]{2,1,0:T(8,128)(2,1)S(1)}, bf16[2,512,128]{2,1...) custom-call(s32[8]{0:T(128)S(1)} %copy-done.6, ...), custom_call_target="tpu_custom_call" | custom-call | tf_op jit(solution)/shard_map/backward/pallas_call | solution.py:282
  20.8 0.6 %collective-permute-start.6 = (bf16[8,4,64,128]{3,2,1,0:T(8,128)(2,1)S(1)}, bf16[8,4,64,128]{3,2,1,0:T(8,128)(2,1)S(1)}, u32[]{:S(2)}, u32[]{:S(2)}) collective-permute-start(bf16[8,4,64,128]{3,2,1,0:T(8,128)(2,1)S(1)} %get-tuple-element.36), channel_id=1, source_target_pairs={{0,16},{16,0},{32,48},{48,32},{64,80},{80,64},{96,112},{112,96},{1... | collective-permute-start | bytes 1572872 | tf_op jit(solution)/shard_map/ppermute | solution.py:303
  21.4 2.1 %collective-permute-start.2 = (bf16[4,512,128]{2,1,0:T(8,128)(2,1)S(1)}, bf16[4,512,128]{2,1,0:T(8,128)(2,1)S(1)}, u32[]{:S(2)}, u32[]{:S(2)}) collective-permute-start(bf16[4,512,128]{2,1,0:T(8,128)(2,1)S(1)} %get-tuple-element.31), channel_id=1, source_target_pairs={{0,2},{2,0},{4,6},{6,4},{8,10},{10,8},{12,14},{14,12},{1,3},{3,1},... | collective-permute-start | bytes 1572872 | tf_op jit(solution)/shard_map/ppermute | solution.py:303
  23.5 0.0 collective-permute-done.6
  23.5 1.0 %add_convert_fusion = bf16[8,4,64,128]{3,2,1,0:T(8,128)(2,1)} fusion(bf16[8,4,64,128]{3,2,1,0:T(8,128)(2,1)S(1)} %collective-permute-done.6, bf16[8,4,64,128]{3,2,1,0:T(8,128)(2,1)S(1)} %get-tuple-element.35), kind=kLoop, calls=%fused_computation | loop fusion | flops 1048576 | bytes 1572864 | tf_op jit(solution)/shard_map/convert_element_type | solution.py:329
  24.5 8.8 %all-to-all-start = ((bf16[8,4,64,128]{3,2,1,0:T(8,128)(2,1)}), bf16[8,4,64,128]{3,2,1,0:T(8,128)(2,1)S(1)}, u32[]{:S(2)}, u32[]{:S(2)}) async-start(bf16[8,4,64,128]{3,2,1,0:T(8,128)(2,1)} %add_convert_fusion), calls=%async_computation | async-start | bytes 1048576 | tf_op jit(solution)/shard_map/all_to_all | solution.py:331
  33.3 2.9 %collective-permute-start.3 = (bf16[2,512,128]{2,1,0:T(8,128)(2,1)S(1)}, bf16[2,512,128]{2,1,0:T(8,128)(2,1)S(1)}, u32[]{:S(2)}, u32[]{:S(2)}) collective-permute-start(bf16[2,512,128]{2,1,0:T(8,128)(2,1)S(1)} %get-tuple-element.32), channel_id=1, source_target_pairs={{0,8},{2,10},{4,12},{6,14},{8,0},{10,2},{12,4},{14,6},{1,9},{3,11}... | collective-permute-start | bytes 786440 | tf_op jit(solution)/shard_map/ppermute | solution.py:303
  36.3 0.4 collective-permute-start.4
  36.7 0.4 collective-permute-start.5
  37.1 5.0 %collective-permute-done.3 = bf16[2,512,128]{2,1,0:T(8,128)(2,1)S(1)} collective-permute-done((bf16[2,512,128]{2,1,0:T(8,128)(2,1)S(1)}, bf16[2,512,128]{2,1,0:T(8,128)(2,1)S(1)}, u32[]{:S(2)}, u32[]{:S(2)}) %collective-permute-start.3) | collective-permute-done | bytes 262176 | tf_op jit(solution)/shard_map/ppermute | solution.py:303
  42.1 6.0 %collective-permute-done.4 = bf16[2,512,128]{2,1,0:T(8,128)(2,1)S(1)} collective-permute-done((bf16[2,512,128]{2,1,0:T(8,128)(2,1)S(1)}, bf16[2,512,128]{2,1,0:T(8,128)(2,1)S(1)}, u32[]{:S(2)}, u32[]{:S(2)}) %collective-permute-start.4) | collective-permute-done | bytes 262176 | tf_op jit(solution)/shard_map/ppermute | solution.py:303
  48.1 0.0 copy-start.7
  48.1 0.6 %collective-permute-done.5 = bf16[2,512,128]{2,1,0:T(8,128)(2,1)S(1)} collective-permute-done((bf16[2,512,128]{2,1,0:T(8,128)(2,1)S(1)}, bf16[2,512,128]{2,1,0:T(8,128)(2,1)S(1)}, u32[]{:S(2)}, u32[]{:S(2)}) %collective-permute-start.5) | collective-permute-done | bytes 262176 | tf_op jit(solution)/shard_map/ppermute | solution.py:303
  48.7 0.0 copy-start.8
  48.7 0.0 collective-permute-done.2
  48.7 0.1 fusion.6
  48.8 2.8 %collective-permute-start.10 = (bf16[512,128]{1,0:T(8,128)(2,1)S(1)}, bf16[512,128]{1,0:T(8,128)(2,1)S(1)}, u32[]{:S(2)}, u32[]{:S(2)}) collective-permute-start(bf16[512,128]{1,0:T(8,128)(2,1)S(1)} %get-tuple-element.53), channel_id=1, source_target_pairs={{0,12},{2,14},{4,8},{6,10},{8,4},{10,6},{12,0},{14,2},{1,13},{3,15... | collective-permute-start | bytes 393224 | tf_op jit(solution)/shard_map/ppermute | solution.py:303
  51.6 0.4 collective-permute-start.8
  52.0 0.3 collective-permute-start.9
  52.3 0.1 fusion.7
  52.4 0.0 copy-done.7
  52.4 0.0 copy-done.8
  52.4 1.6 %collective-permute-start.7 = (bf16[512,128]{1,0:T(8,128)(2,1)S(1)}, bf16[512,128]{1,0:T(8,128)(2,1)S(1)}, u32[]{:S(2)}, u32[]{:S(2)}) collective-permute-start(bf16[512,128]{1,0:T(8,128)(2,1)S(1)} %fusion.7), channel_id=1, source_target_pairs={{0,2},{2,0},{4,6},{6,4},{8,10},{10,8},{12,14},{14,12},{1,3},{3,1},... | collective-permute-start | bytes 393224 | tf_op jit(solution)/shard_map/ppermute | solution.py:303
  54.0 0.0 all-to-all-done
  54.0 0.6 %convert_reduce_fusion.1 = f32[64,128]{1,0:T(8,128)} fusion(bf16[8,4,64,128]{3,2,1,0:T(8,128)(2,1)S(1)} %all-to-all-done), kind=kLoop, calls=%fused_computation.12 | loop fusion | flops 122880 | bytes 163840 | tf_op jit(solution)/shard_map/reduce_sum | solution.py:338
  54.7 0.7 %convert_reduce_fusion = f32[3,64,128]{2,1,0:T(8,128)} fusion(bf16[8,4,64,128]{3,2,1,0:T(8,128)(2,1)S(1)} %all-to-all-done), kind=kLoop, calls=%fused_computation.1 | loop fusion | flops 368640 | bytes 491520 | tf_op jit(solution)/shard_map/reduce_sum | solution.py:337
  55.4 2.8 %collective-permute-done.7 = bf16[512,128]{1,0:T(8,128)(2,1)S(1)} collective-permute-done((bf16[512,128]{1,0:T(8,128)(2,1)S(1)}, bf16[512,128]{1,0:T(8,128)(2,1)S(1)}, u32[]{:S(2)}, u32[]{:S(2)}) %collective-permute-start.7) | collective-permute-done | bytes 131104 | tf_op jit(solution)/shard_map/ppermute | solution.py:303
  58.1 0.0 collective-permute-done.10
  58.1 0.0 collective-permute-done.8
  58.1 0.0 collective-permute-done.9
  58.1 1.1 %fusion.3 = bf16[512,128]{1,0:T(8,128)(2,1)S(1)} fusion(bf16[512,128]{1,0:T(8,128)(2,1)S(1)} %collective-permute-done.7, bf16[2,512,128]{2,1,0:T(8,128)(2,1)} %copy-done.8, bf16[2,512,128]{2,1,0:T(8,128)(2,1)} %copy-done.7, bf16[2,512,128]{2,1,0:T(8,128)(2,1)S(1)} %collective-permute-done.3, bf16[2,512,128]{2,1,0:T(8,128)(2,1)S(1)} %get-tuple-element.29), kind=kLoop, calls=%fused_computation.11 | loop fusion | flops 655360 | bytes 786432 | tf_op jit(solution)/shard_map/convert_element_type | solution.py:340
  59.2 0.1 fusion.2
  59.3 0.7 %pad_maximum_fusion.3 = bf16[1024,128]{1,0:T(8,128)(2,1)} fusion(bf16[512,128]{1,0:T(8,128)(2,1)S(1)} %fusion.2, bf16[512,128]{1,0:T(8,128)(2,1)S(1)} %fusion.3), kind=kLoop, calls=%fused_computation.5 | loop fusion | flops 524288 | bytes 524288 | tf_op jit(solution)/shard_map/concatenate | solution.py:342
  (3 shorter events, 0.1 us)
Async XLA Ops:
  0.6 8.4 %copy-start.3 = (bf16[128,1024]{1,0:T(8,128)(2,1)S(1)}, bf16[128,1024]{1,0:T(8,128)(2,1)}, u32[]{:S(2)}) copy-start(bf16[128,1024]{1,0:T(8,128)(2,1)} %out_ref.1) | copy-start | bytes 786436
  0.6 8.4 %copy-start.2 = (bf16[3,1024,128]{2,1,0:T(8,128)(2,1)S(1)}, bf16[3,1024,128]{2,1,0:T(8,128)(2,1)}, u32[]{:S(2)}) copy-start(bf16[3,1024,128]{2,1,0:T(8,128)(2,1)} %qkv_ref.1) | copy-start | bytes 2359300
  0.7 8.4 %copy-start.4 = (s32[16384]{0:T(1024)S(1)}, s32[16384]{0:T(1024)}, u32[]{:S(2)}) copy-start(s32[16384]{0:T(1024)} %param.12) | copy-start | bytes 196612
  0.7 8.4 %copy-start.5 = (f32[1024]{0:T(1024)S(1)}, f32[1024]{0:T(1024)}, u32[]{:S(2)}) copy-start(f32[1024]{0:T(1024)} %param.8) | copy-start | bytes 12292
  1.9 11.8 %collective-permute-start.1 = (bf16[2,64,1024]{2,1,0:T(8,128)(2,1)S(1)}, bf16[2,64,1024]{2,1,0:T(8,128)(2,1)S(1)}, u32[]{:S(2)}, u32[]{:S(2)}) collective-permute-start(bf16[2,64,1024]{2,1,0:T(8,128)(2,1)S(1)} %pad_maximum_fusion.2), channel_id=1, source_target_pairs={{16,0},{32,16},{48,32},{64,48},{80,64},{96,80},{112,96},{128,112},... | collective-permute-start | bytes 786440 | tf_op jit(solution)/shard_map/ppermute | solution.py:319
  7.1 6.7 %collective-permute-start = (bf16[2,64,1024]{2,1,0:T(8,128)(2,1)S(1)}, bf16[2,64,1024]{2,1,0:T(8,128)(2,1)S(1)}, u32[]{:S(2)}, u32[]{:S(2)}) collective-permute-start(bf16[2,64,1024]{2,1,0:T(8,128)(2,1)S(1)} %pad_maximum_fusion.1), channel_id=1, source_target_pairs={{0,16},{16,32},{32,48},{48,64},{64,80},{80,96},{96,112},{112,128},... | collective-permute-start | bytes 786440 | tf_op jit(solution)/shard_map/ppermute | solution.py:319
  9.1 4.7 %copy-start = (bf16[1024,1024]{1,0:T(8,128)(2,1)S(1)}, bf16[1024,1024]{1,0:T(8,128)(2,1)}, u32[]{:S(2)}) copy-start(bf16[1024,1024]{1,0:T(8,128)(2,1)} %frames_hbm.3) | copy-start | bytes 6291460
  9.1 4.7 %copy-start.1 = (bf16[1024,1024]{1,0:T(8,128)(2,1)S(1)}, bf16[1024,1024]{1,0:T(8,128)(2,1)}, u32[]{:S(2)}) copy-start(bf16[1024,1024]{1,0:T(8,128)(2,1)} %cot_hbm.3) | copy-start | bytes 6291460
  9.1 4.7 %copy-start.6 = (s32[8]{0:T(128)S(1)}, s32[8]{0:T(128)}, u32[]{:S(2)}) copy-start(s32[8]{0:T(128)} %len_ref.1) | copy-start | bytes 100
  20.8 2.7 %collective-permute-start.6 = (bf16[8,4,64,128]{3,2,1,0:T(8,128)(2,1)S(1)}, bf16[8,4,64,128]{3,2,1,0:T(8,128)(2,1)S(1)}, u32[]{:S(2)}, u32[]{:S(2)}) collective-permute-start(bf16[8,4,64,128]{3,2,1,0:T(8,128)(2,1)S(1)} %get-tuple-element.36), channel_id=1, source_target_pairs={{0,16},{16,0},{32,48},{48,32},{64,80},{80,64},{96,112},{112,96},{1... | collective-permute-start | bytes 1572872 | tf_op jit(solution)/shard_map/ppermute | solution.py:303
  21.4 27.3 %collective-permute-start.2 = (bf16[4,512,128]{2,1,0:T(8,128)(2,1)S(1)}, bf16[4,512,128]{2,1,0:T(8,128)(2,1)S(1)}, u32[]{:S(2)}, u32[]{:S(2)}) collective-permute-start(bf16[4,512,128]{2,1,0:T(8,128)(2,1)S(1)} %get-tuple-element.31), channel_id=1, source_target_pairs={{0,2},{2,0},{4,6},{6,4},{8,10},{10,8},{12,14},{14,12},{1,3},{3,1},... | collective-permute-start | bytes 1572872 | tf_op jit(solution)/shard_map/ppermute | solution.py:303
  24.5 29.5 %all-to-all-start = ((bf16[8,4,64,128]{3,2,1,0:T(8,128)(2,1)}), bf16[8,4,64,128]{3,2,1,0:T(8,128)(2,1)S(1)}, u32[]{:S(2)}, u32[]{:S(2)}) async-start(bf16[8,4,64,128]{3,2,1,0:T(8,128)(2,1)} %add_convert_fusion), calls=%async_computation | async-start | bytes 1048576 | tf_op jit(solution)/shard_map/all_to_all | solution.py:331
  33.3 8.7 %collective-permute-start.3 = (bf16[2,512,128]{2,1,0:T(8,128)(2,1)S(1)}, bf16[2,512,128]{2,1,0:T(8,128)(2,1)S(1)}, u32[]{:S(2)}, u32[]{:S(2)}) collective-permute-start(bf16[2,512,128]{2,1,0:T(8,128)(2,1)S(1)} %get-tuple-element.32), channel_id=1, source_target_pairs={{0,8},{2,10},{4,12},{6,14},{8,0},{10,2},{12,4},{14,6},{1,9},{3,11}... | collective-permute-start | bytes 786440 | tf_op jit(solution)/shard_map/ppermute | solution.py:303
  36.3 11.8 %collective-permute-start.4 = (bf16[2,512,128]{2,1,0:T(8,128)(2,1)S(1)}, bf16[2,512,128]{2,1,0:T(8,128)(2,1)S(1)}, u32[]{:S(2)}, u32[]{:S(2)}) collective-permute-start(bf16[2,512,128]{2,1,0:T(8,128)(2,1)S(1)} %get-tuple-element.33), channel_id=1, source_target_pairs={{0,4},{2,6},{4,0},{6,2},{8,12},{10,14},{12,8},{14,10},{1,5},{3,7},... | collective-permute-start | bytes 786440 | tf_op jit(solution)/shard_map/ppermute | solution.py:303
  36.7 12.0 %collective-permute-start.5 = (bf16[2,512,128]{2,1,0:T(8,128)(2,1)S(1)}, bf16[2,512,128]{2,1,0:T(8,128)(2,1)S(1)}, u32[]{:S(2)}, u32[]{:S(2)}) collective-permute-start(bf16[2,512,128]{2,1,0:T(8,128)(2,1)S(1)} %get-tuple-element.34), channel_id=1, source_target_pairs={{0,12},{2,14},{4,8},{6,10},{8,4},{10,6},{12,0},{14,2},{1,13},{3,15... | collective-permute-start | bytes 786440 | tf_op jit(solution)/shard_map/ppermute | solution.py:303
  48.1 4.3 %copy-start.7 = (bf16[2,512,128]{2,1,0:T(8,128)(2,1)}, bf16[2,512,128]{2,1,0:T(8,128)(2,1)S(1)}, u32[]{:S(2)}) copy-start(bf16[2,512,128]{2,1,0:T(8,128)(2,1)S(1)} %collective-permute-done.4) | copy-start | bytes 786436
  48.7 3.7 %copy-start.8 = (bf16[2,512,128]{2,1,0:T(8,128)(2,1)}, bf16[2,512,128]{2,1,0:T(8,128)(2,1)S(1)}, u32[]{:S(2)}) copy-start(bf16[2,512,128]{2,1,0:T(8,128)(2,1)S(1)} %collective-permute-done.5) | copy-start | bytes 786436
  48.8 9.3 %collective-permute-start.10 = (bf16[512,128]{1,0:T(8,128)(2,1)S(1)}, bf16[512,128]{1,0:T(8,128)(2,1)S(1)}, u32[]{:S(2)}, u32[]{:S(2)}) collective-permute-start(bf16[512,128]{1,0:T(8,128)(2,1)S(1)} %get-tuple-element.53), channel_id=1, source_target_pairs={{0,12},{2,14},{4,8},{6,10},{8,4},{10,6},{12,0},{14,2},{1,13},{3,15... | collective-permute-start | bytes 393224 | tf_op jit(solution)/shard_map/ppermute | solution.py:303
  51.6 6.5 %collective-permute-start.8 = (bf16[512,128]{1,0:T(8,128)(2,1)S(1)}, bf16[512,128]{1,0:T(8,128)(2,1)S(1)}, u32[]{:S(2)}, u32[]{:S(2)}) collective-permute-start(bf16[512,128]{1,0:T(8,128)(2,1)S(1)} %get-tuple-element.54), channel_id=1, source_target_pairs={{0,8},{2,10},{4,12},{6,14},{8,0},{10,2},{12,4},{14,6},{1,9},{3,11}... | collective-permute-start | bytes 393224 | tf_op jit(solution)/shard_map/ppermute | solution.py:303
  52.0 6.1 %collective-permute-start.9 = (bf16[512,128]{1,0:T(8,128)(2,1)S(1)}, bf16[512,128]{1,0:T(8,128)(2,1)S(1)}, u32[]{:S(2)}, u32[]{:S(2)}) collective-permute-start(bf16[512,128]{1,0:T(8,128)(2,1)S(1)} %get-tuple-element.55), channel_id=1, source_target_pairs={{0,4},{2,6},{4,0},{6,2},{8,12},{10,14},{12,8},{14,10},{1,5},{3,7},... | collective-permute-start | bytes 393224 | tf_op jit(solution)/shard_map/ppermute | solution.py:303
  52.4 5.7 %collective-permute-start.7 = (bf16[512,128]{1,0:T(8,128)(2,1)S(1)}, bf16[512,128]{1,0:T(8,128)(2,1)S(1)}, u32[]{:S(2)}, u32[]{:S(2)}) collective-permute-start(bf16[512,128]{1,0:T(8,128)(2,1)S(1)} %fusion.7), channel_id=1, source_target_pairs={{0,2},{2,0},{4,6},{6,4},{8,10},{10,8},{12,14},{14,12},{1,3},{3,1},... | collective-permute-start | bytes 393224 | tf_op jit(solution)/shard_map/ppermute | solution.py:303

commit v9 on v8

--- a/solution.py
+++ b/solution.py
@@ -336,7 +336,6 @@
     theirs = swapped(total(ring[0][1], *[r[1] for r in ring_in]).astype(BF16), "mp", 1)
     qkv_grad = weights[:, :3].astype(F32).sum(axis=0)
     out_grad = weights[:, 3].astype(F32).sum(axis=0)
-    (theirs, col_in), _ = lax.optimization_barrier(((theirs, col_in), (qkv_grad, out_grad)))
     first_half = total(total(ring[0][0], *[r[0] for r in ring_in]), theirs).astype(BF16)
     second_half = total(col[0], *col_in).astype(BF16)
     frame_grad = jnp.concatenate([first_half, second_half], axis=0)

time: 61 us -> 55.8 us (0.915); the launches traced: 60 us -> 55.5 us
  waiting for transfers between devices: 14.4 us -> 9.97 us
  starting transfers between devices: 27.4 us -> 26.4 us
  other arithmetic: 4.46 us -> 5.43 us
    ppermute x9, waiting for transfers between devices: 14.4 us -> 6.85 us  [swapped(): lax.ppermute(x, axis, [(i, i ^ bit) for i in range(lax.axis_size(axis))])]
    all_to_all x1, waiting for transfers between devices: 0.01 us -> 3.12 us  [on_device(): lax.all_to_all(chip, 'tm', 0, 0, tiled=True, axis_index_groups=same_core)]
    ppermute x9, starting transfers between devices: 11.5 us -> 10.5 us  [swapped(): lax.ppermute(x, axis, [(i, i ^ bit) for i in range(lax.axis_size(axis))])]
    add x1, other arithmetic: 0.08 us -> 1.04 us  [total(): summed = summed + part.astype(F32)]
  transfers between devices with their start and end apart: 12 -> 12, of which waited for: 4 -> 5; matrix products, arithmetic and copies ran while one was open for 4% -> 7% of each run, Pallas kernels for 8% -> 8%
where the time goes in v9:
time: 55.8 us; the launch traced here: 55.5 us
  starting transfers between devices  26.4 us (47%)
  Pallas kernels  11.7 us (21%)
  waiting for transfers between devices  9.97 us (18%)
  other arithmetic  5.43 us (10%)
  local copies, waits for them, and re-layouts  1.25 us (2%)
  between operations  0.85 us (2%)
    ppermute x9, starting transfers between devices, swapped(): lax.ppermute(x, axis, [(i, i ^ bit) for i in range(lax.axis_size(axis))])  10.5 us
    all_to_all x1, starting transfers between devices, on_device(): lax.all_to_all(chip, 'tm', 0, 0, tiled=True, axis_index_groups=same_core)  8.81 us
    pallas_call x1, Pallas kernels, backward(): pl.pallas_call(backward_body, in_specs=[pl.BlockSpec(memory_space=pltpu.S...  7.02 us
    ppermute x9, waiting for transfers between devices, swapped(): lax.ppermute(x, axis, [(i, i ^ bit) for i in range(lax.axis_size(axis))])  6.85 us
    ppermute x1, starting transfers between devices, on_device(): lax.ppermute(starts, 'tm', down)  5.15 us
    pallas_call x1, Pallas kernels, project(): pl.pallas_call(project_body, in_specs=[hbm, vmem, hbm, hbm, hbm, vmem], o...  4.64 us
    all_to_all x1, waiting for transfers between devices, on_device(): lax.all_to_all(chip, 'tm', 0, 0, tiled=True, axis_index_groups=same_core)  3.12 us
    ppermute x1, starting transfers between devices, on_device(): lax.ppermute(ends, 'tm', up)  1.92 us
  transfers between devices with their start and end apart: 12, of which 5 were waited for; matrix products, arithmetic and copies ran while one was open for 7% of the time, Pallas kernels for 8%

profile of v9, /device:TPU:1, one launch (start us, length us, event | category | flops | bytes accessed | tf_op | source)
XLA Modules:
  0.0 55.5 jit_solution(4693084809030147625)
XLA Ops:
  0.6 0.0 copy-start.3
  0.6 0.0 copy-start.2
  0.7 0.0 copy-start.4
  0.7 0.0 copy-start.5
  0.7 1.2 %slice_bitcast_fusion.2 = (bf16[1,64,1024]{2,1,0:T(8,128)(2,1)S(1)}, bf16[1,64,1024]{2,1,0:T(8,128)(2,1)S(1)}, bf16[1,64,1024]{2,1,0:T(8,128)(2,1)S(1)}, bf16[1,64,1024]{2,1,0:T(8,128)(2,1)S(1)}) fusion(bf16[1024,1024]{1,0:T(8,128)(2,1)} %cot_hbm.3, bf16[1024,1024]{1,0:T(8,128)(2,1)} %frames_hbm.3), kind=kLoop, calls=%fused_computation.23 | loop fusion | bytes 1048576 | tf_op jit(solution)/shard_map/stack | solution.py:317
  1.9 5.1 %collective-permute-start.1 = (bf16[2,64,1024]{2,1,0:T(8,128)(2,1)S(1)}, bf16[2,64,1024]{2,1,0:T(8,128)(2,1)S(1)}, u32[]{:S(2)}, u32[]{:S(2)}) collective-permute-start(bf16[2,64,1024]{2,1,0:T(8,128)(2,1)S(1)} %pad_maximum_fusion.2), channel_id=1, source_target_pairs={{16,0},{32,16},{48,32},{64,48},{80,64},{96,80},{112,96},{128,112},... | collective-permute-start | bytes 786440 | tf_op jit(solution)/shard_map/ppermute | solution.py:319
  7.1 1.9 %collective-permute-start = (bf16[2,64,1024]{2,1,0:T(8,128)(2,1)S(1)}, bf16[2,64,1024]{2,1,0:T(8,128)(2,1)S(1)}, u32[]{:S(2)}, u32[]{:S(2)}) collective-permute-start(bf16[2,64,1024]{2,1,0:T(8,128)(2,1)S(1)} %pad_maximum_fusion.1), channel_id=1, source_target_pairs={{0,16},{16,32},{32,48},{48,64},{64,80},{80,96},{96,112},{112,128},... | collective-permute-start | bytes 786440 | tf_op jit(solution)/shard_map/ppermute | solution.py:319
  9.0 0.0 copy-done.3
  9.1 0.0 copy-done.2
  9.1 0.0 copy-done.4
  9.1 0.0 copy-done.5
  9.1 0.0 copy-start
  9.1 0.0 copy-start.1
  9.1 0.0 copy-start.6
  9.1 4.6 %project.1 = (bf16[4,1024,128]{2,1,0:T(8,128)(2,1)S(1)}, f32[1024,128]{1,0:T(8,128)S(1)}, bf16[1024,1024]{1,0:T(8,128)(2,1)S(1)}) custom-call(bf16[1024,1024]{1,0:T(8,128)(2,1)} %frames_hbm.3, f32[1,1024]{1,0:T(1,128)S(1)} %bitcast.33, bf16[3,1024,128]{2,1,0:T(8,128)(2,1)S(1)} %copy-done.2, bf16[128,1024]{1,0:T(8,128)(2,1)S(1)} %copy-done.3, ...), custom_call_target="tpu_custom_call" | custom-call | tf_op jit(solution)/shard_map/project/pallas_call | solution.py:100
  13.8 0.0 collective-permute-done.1
  13.8 0.0 collective-permute-done
  13.8 0.0 copy-done
  13.8 0.0 copy-done.1
  13.9 0.0 copy-done.6
  13.9 7.0 %backward.1 = (bf16[4,512,128]{2,1,0:T(8,128)(2,1)S(1)}, bf16[4,512,128]{2,1,0:T(8,128)(2,1)S(1)}, bf16[2,512,128]{2,1,0:T(8,128)(2,1)S(1)}, bf16[2,512,128]{2,1...) custom-call(s32[8]{0:T(128)S(1)} %copy-done.6, ...), custom_call_target="tpu_custom_call" | custom-call | tf_op jit(solution)/shard_map/backward/pallas_call | solution.py:282
  20.9 0.6 %collective-permute-start.6 = (bf16[8,4,64,128]{3,2,1,0:T(8,128)(2,1)S(1)}, bf16[8,4,64,128]{3,2,1,0:T(8,128)(2,1)S(1)}, u32[]{:S(2)}, u32[]{:S(2)}) collective-permute-start(bf16[8,4,64,128]{3,2,1,0:T(8,128)(2,1)S(1)} %get-tuple-element.32), channel_id=1, source_target_pairs={{0,16},{16,0},{32,48},{48,32},{64,80},{80,64},{96,112},{112,96},{1... | collective-permute-start | bytes 1572872 | tf_op jit(solution)/shard_map/ppermute | solution.py:303
  21.5 2.1 %collective-permute-start.2 = (bf16[4,512,128]{2,1,0:T(8,128)(2,1)S(1)}, bf16[4,512,128]{2,1,0:T(8,128)(2,1)S(1)}, u32[]{:S(2)}, u32[]{:S(2)}) collective-permute-start(bf16[4,512,128]{2,1,0:T(8,128)(2,1)S(1)} %get-tuple-element.27), channel_id=1, source_target_pairs={{0,2},{2,0},{4,6},{6,4},{8,10},{10,8},{12,14},{14,12},{1,3},{3,1},... | collective-permute-start | bytes 1572872 | tf_op jit(solution)/shard_map/ppermute | solution.py:303
  23.6 2.9 %collective-permute-start.3 = (bf16[2,512,128]{2,1,0:T(8,128)(2,1)S(1)}, bf16[2,512,128]{2,1,0:T(8,128)(2,1)S(1)}, u32[]{:S(2)}, u32[]{:S(2)}) collective-permute-start(bf16[2,512,128]{2,1,0:T(8,128)(2,1)S(1)} %get-tuple-element.28), channel_id=1, source_target_pairs={{0,8},{2,10},{4,12},{6,14},{8,0},{10,2},{12,4},{14,6},{1,9},{3,11}... | collective-permute-start | bytes 786440 | tf_op jit(solution)/shard_map/ppermute | solution.py:303
  26.5 0.4 collective-permute-start.4
  26.9 0.4 collective-permute-start.5
  27.3 0.0 collective-permute-done.6
  27.3 1.0 %add_convert_fusion = bf16[8,4,64,128]{3,2,1,0:T(8,128)(2,1)} fusion(bf16[8,4,64,128]{3,2,1,0:T(8,128)(2,1)S(1)} %collective-permute-done.6, bf16[8,4,64,128]{3,2,1,0:T(8,128)(2,1)S(1)} %get-tuple-element.31), kind=kLoop, calls=%fused_computation | loop fusion | flops 1048576 | bytes 1572864 | tf_op jit(solution)/shard_map/convert_element_type | solution.py:329
  28.3 8.8 %all-to-all-start = ((bf16[8,4,64,128]{3,2,1,0:T(8,128)(2,1)}), bf16[8,4,64,128]{3,2,1,0:T(8,128)(2,1)S(1)}, u32[]{:S(2)}, u32[]{:S(2)}) async-start(bf16[8,4,64,128]{3,2,1,0:T(8,128)(2,1)} %add_convert_fusion), calls=%async_computation | async-start | bytes 1048576 | tf_op jit(solution)/shard_map/all_to_all | solution.py:331
  37.1 0.0 collective-permute-done.3
  37.1 1.2 %collective-permute-done.4 = bf16[2,512,128]{2,1,0:T(8,128)(2,1)} collective-permute-done((bf16[2,512,128]{2,1,0:T(8,128)(2,1)S(1)}, bf16[2,512,128]{2,1,0:T(8,128)(2,1)}, u32[]{:S(2)}, u32[]{:S(2)}) %collective-permute-start.4) | collective-permute-done | bytes 262176 | tf_op jit(solution)/shard_map/ppermute | solution.py:303
  38.4 0.6 %collective-permute-done.5 = bf16[2,512,128]{2,1,0:T(8,128)(2,1)} collective-permute-done((bf16[2,512,128]{2,1,0:T(8,128)(2,1)S(1)}, bf16[2,512,128]{2,1,0:T(8,128)(2,1)}, u32[]{:S(2)}, u32[]{:S(2)}) %collective-permute-start.5) | collective-permute-done | bytes 262176 | tf_op jit(solution)/shard_map/ppermute | solution.py:303
  39.0 0.0 collective-permute-done.2
  39.0 0.1 fusion.5
  39.1 1.0 %fusion.7 = bf16[512,128]{1,0:T(8,128)(2,1)S(1)} fusion(bf16[2,512,128]{2,1,0:T(8,128)(2,1)} %collective-permute-done.5, bf16[2,512,128]{2,1,0:T(8,128)(2,1)} %collective-permute-done.4, bf16[2,512,128]{2,1,0:T(8,128)(2,1)S(1)} %collective-permute-done.3, bf16[2,512,128]{2,1,0:T(8,128)(2,1)S(1)} %get-tuple-element.25), kind=kLoop, calls=%fused_computation.20 | loop fusion | flops 524288 | bytes 655360 | tf_op jit(solution)/shard_map/add | solution.py:309
  40.2 1.0 %collective-permute-start.7 = (bf16[512,128]{1,0:T(8,128)(2,1)S(1)}, bf16[512,128]{1,0:T(8,128)(2,1)S(1)}, u32[]{:S(2)}, u32[]{:S(2)}) collective-permute-start(bf16[512,128]{1,0:T(8,128)(2,1)S(1)} %fusion.7), channel_id=1, source_target_pairs={{0,2},{2,0},{4,6},{6,4},{8,10},{10,8},{12,14},{14,12},{1,3},{3,1},... | collective-permute-start | bytes 393224 | tf_op jit(solution)/shard_map/ppermute | solution.py:303
  41.2 2.3 %collective-permute-start.8 = (bf16[512,128]{1,0:T(8,128)(2,1)S(1)}, bf16[512,128]{1,0:T(8,128)(2,1)S(1)}, u32[]{:S(2)}, u32[]{:S(2)}) collective-permute-start(bf16[512,128]{1,0:T(8,128)(2,1)S(1)} %get-tuple-element.45), channel_id=1, source_target_pairs={{0,8},{2,10},{4,12},{6,14},{8,0},{10,2},{12,4},{14,6},{1,9},{3,11}... | collective-permute-start | bytes 393224 | tf_op jit(solution)/shard_map/ppermute | solution.py:303
  43.4 0.8 %collective-permute-start.10 = (bf16[512,128]{1,0:T(8,128)(2,1)S(1)}, bf16[512,128]{1,0:T(8,128)(2,1)S(1)}, u32[]{:S(2)}, u32[]{:S(2)}) collective-permute-start(bf16[512,128]{1,0:T(8,128)(2,1)S(1)} %get-tuple-element.46), channel_id=1, source_target_pairs={{0,12},{2,14},{4,8},{6,10},{8,4},{10,6},{12,0},{14,2},{1,13},{3,15... | collective-permute-start | bytes 393224 | tf_op jit(solution)/shard_map/ppermute | solution.py:303
  44.2 0.0 collective-permute-start.9
  44.2 1.6 %collective-permute-done.7 = bf16[512,128]{1,0:T(8,128)(2,1)S(1)} collective-permute-done((bf16[512,128]{1,0:T(8,128)(2,1)S(1)}, bf16[512,128]{1,0:T(8,128)(2,1)S(1)}, u32[]{:S(2)}, u32[]{:S(2)}) %collective-permute-start.7) | collective-permute-done | bytes 131104 | tf_op jit(solution)/shard_map/ppermute | solution.py:303
  45.9 1.1 %fusion.3 = bf16[512,128]{1,0:T(8,128)(2,1)S(1)} fusion(bf16[512,128]{1,0:T(8,128)(2,1)S(1)} %collective-permute-done.7, bf16[2,512,128]{2,1,0:T(8,128)(2,1)} %collective-permute-done.5, bf16[2,512,128]{2,1,0:T(8,128)(2,1)} %collective-permute-done.4, bf16[2,512,128]{2,1,0:T(8,128)(2,1)S(1)} %collective-permute-done.3, ...), kind=kLoop, calls=%fused_computation.11 | loop fusion | flops 655360 | bytes 786432 | tf_op jit(solution)/shard_map/convert_element_type | solution.py:339
  46.9 0.0 collective-permute-done.8
  47.0 3.3 %collective-permute-done.10 = bf16[512,128]{1,0:T(8,128)(2,1)S(1)} collective-permute-done((bf16[512,128]{1,0:T(8,128)(2,1)S(1)}, bf16[512,128]{1,0:T(8,128)(2,1)S(1)}, u32[]{:S(2)}, u32[]{:S(2)}) %collective-permute-start.10) | collective-permute-done | bytes 131104 | tf_op jit(solution)/shard_map/ppermute | solution.py:303
  50.3 0.0 collective-permute-done.9
  50.3 0.1 fusion.2
  50.4 0.7 %pad_maximum_fusion.3 = bf16[1024,128]{1,0:T(8,128)(2,1)} fusion(bf16[512,128]{1,0:T(8,128)(2,1)S(1)} %fusion.2, bf16[512,128]{1,0:T(8,128)(2,1)S(1)} %fusion.3), kind=kLoop, calls=%fused_computation.5 | loop fusion | flops 524288 | bytes 524288 | tf_op jit(solution)/shard_map/concatenate | solution.py:341
  51.1 3.1 %all-to-all-done = bf16[8,4,64,128]{3,2,1,0:T(8,128)(2,1)S(1)} async-done(((bf16[8,4,64,128]{3,2,1,0:T(8,128)(2,1)}), bf16[8,4,64,128]{3,2,1,0:T(8,128)(2,1)S(1)}, u32[]{:S(2)}, u32[]{:S(2)}) %all-to-all-start) | async-done | bytes 524320 | tf_op jit(solution)/shard_map/all_to_all | solution.py:331
  54.2 0.6 %convert_reduce_fusion.1 = f32[64,128]{1,0:T(8,128)} fusion(bf16[8,4,64,128]{3,2,1,0:T(8,128)(2,1)S(1)} %all-to-all-done), kind=kLoop, calls=%fused_computation.12 | loop fusion | flops 122880 | bytes 163840 | tf_op jit(solution)/shard_map/reduce_sum | solution.py:338
  54.8 0.7 %convert_reduce_fusion = f32[3,64,128]{2,1,0:T(8,128)} fusion(bf16[8,4,64,128]{3,2,1,0:T(8,128)(2,1)S(1)} %all-to-all-done), kind=kLoop, calls=%fused_computation.1 | loop fusion | flops 368640 | bytes 491520 | tf_op jit(solution)/shard_map/reduce_sum | solution.py:337
  (3 shorter events, 0.1 us)
Async XLA Ops:
  0.6 8.4 %copy-start.3 = (bf16[128,1024]{1,0:T(8,128)(2,1)S(1)}, bf16[128,1024]{1,0:T(8,128)(2,1)}, u32[]{:S(2)}) copy-start(bf16[128,1024]{1,0:T(8,128)(2,1)} %out_ref.1) | copy-start | bytes 786436
  0.6 8.4 %copy-start.2 = (bf16[3,1024,128]{2,1,0:T(8,128)(2,1)S(1)}, bf16[3,1024,128]{2,1,0:T(8,128)(2,1)}, u32[]{:S(2)}) copy-start(bf16[3,1024,128]{2,1,0:T(8,128)(2,1)} %qkv_ref.1) | copy-start | bytes 2359300
  0.7 8.4 %copy-start.4 = (s32[16384]{0:T(1024)S(1)}, s32[16384]{0:T(1024)}, u32[]{:S(2)}) copy-start(s32[16384]{0:T(1024)} %param.12) | copy-start | bytes 196612
  0.7 8.4 %copy-start.5 = (f32[1024]{0:T(1024)S(1)}, f32[1024]{0:T(1024)}, u32[]{:S(2)}) copy-start(f32[1024]{0:T(1024)} %param.8) | copy-start | bytes 12292
  1.9 11.8 %collective-permute-start.1 = (bf16[2,64,1024]{2,1,0:T(8,128)(2,1)S(1)}, bf16[2,64,1024]{2,1,0:T(8,128)(2,1)S(1)}, u32[]{:S(2)}, u32[]{:S(2)}) collective-permute-start(bf16[2,64,1024]{2,1,0:T(8,128)(2,1)S(1)} %pad_maximum_fusion.2), channel_id=1, source_target_pairs={{16,0},{32,16},{48,32},{64,48},{80,64},{96,80},{112,96},{128,112},... | collective-permute-start | bytes 786440 | tf_op jit(solution)/shard_map/ppermute | solution.py:319
  7.1 6.7 %collective-permute-start = (bf16[2,64,1024]{2,1,0:T(8,128)(2,1)S(1)}, bf16[2,64,1024]{2,1,0:T(8,128)(2,1)S(1)}, u32[]{:S(2)}, u32[]{:S(2)}) collective-permute-start(bf16[2,64,1024]{2,1,0:T(8,128)(2,1)S(1)} %pad_maximum_fusion.1), channel_id=1, source_target_pairs={{0,16},{16,32},{32,48},{48,64},{64,80},{80,96},{96,112},{112,128},... | collective-permute-start | bytes 786440 | tf_op jit(solution)/shard_map/ppermute | solution.py:319
  9.1 4.7 %copy-start = (bf16[1024,1024]{1,0:T(8,128)(2,1)S(1)}, bf16[1024,1024]{1,0:T(8,128)(2,1)}, u32[]{:S(2)}) copy-start(bf16[1024,1024]{1,0:T(8,128)(2,1)} %frames_hbm.3) | copy-start | bytes 6291460
  9.1 4.7 %copy-start.1 = (bf16[1024,1024]{1,0:T(8,128)(2,1)S(1)}, bf16[1024,1024]{1,0:T(8,128)(2,1)}, u32[]{:S(2)}) copy-start(bf16[1024,1024]{1,0:T(8,128)(2,1)} %cot_hbm.3) | copy-start | bytes 6291460
  9.1 4.7 %copy-start.6 = (s32[8]{0:T(128)S(1)}, s32[8]{0:T(128)}, u32[]{:S(2)}) copy-start(s32[8]{0:T(128)} %len_ref.1) | copy-start | bytes 100
  20.9 6.4 %collective-permute-start.6 = (bf16[8,4,64,128]{3,2,1,0:T(8,128)(2,1)S(1)}, bf16[8,4,64,128]{3,2,1,0:T(8,128)(2,1)S(1)}, u32[]{:S(2)}, u32[]{:S(2)}) collective-permute-start(bf16[8,4,64,128]{3,2,1,0:T(8,128)(2,1)S(1)} %get-tuple-element.32), channel_id=1, source_target_pairs={{0,16},{16,0},{32,48},{48,32},{64,80},{80,64},{96,112},{112,96},{1... | collective-permute-start | bytes 1572872 | tf_op jit(solution)/shard_map/ppermute | solution.py:303
  21.5 17.5 %collective-permute-start.2 = (bf16[4,512,128]{2,1,0:T(8,128)(2,1)S(1)}, bf16[4,512,128]{2,1,0:T(8,128)(2,1)S(1)}, u32[]{:S(2)}, u32[]{:S(2)}) collective-permute-start(bf16[4,512,128]{2,1,0:T(8,128)(2,1)S(1)} %get-tuple-element.27), channel_id=1, source_target_pairs={{0,2},{2,0},{4,6},{6,4},{8,10},{10,8},{12,14},{14,12},{1,3},{3,1},... | collective-permute-start | bytes 1572872 | tf_op jit(solution)/shard_map/ppermute | solution.py:303
  23.6 13.5 %collective-permute-start.3 = (bf16[2,512,128]{2,1,0:T(8,128)(2,1)S(1)}, bf16[2,512,128]{2,1,0:T(8,128)(2,1)S(1)}, u32[]{:S(2)}, u32[]{:S(2)}) collective-permute-start(bf16[2,512,128]{2,1,0:T(8,128)(2,1)S(1)} %get-tuple-element.28), channel_id=1, source_target_pairs={{0,8},{2,10},{4,12},{6,14},{8,0},{10,2},{12,4},{14,6},{1,9},{3,11}... | collective-permute-start | bytes 786440 | tf_op jit(solution)/shard_map/ppermute | solution.py:303
  26.5 11.9 %collective-permute-start.4 = (bf16[2,512,128]{2,1,0:T(8,128)(2,1)S(1)}, bf16[2,512,128]{2,1,0:T(8,128)(2,1)}, u32[]{:S(2)}, u32[]{:S(2)}) collective-permute-start(bf16[2,512,128]{2,1,0:T(8,128)(2,1)S(1)} %get-tuple-element.29), channel_id=1, source_target_pairs={{0,4},{2,6},{4,0},{6,2},{8,12},{10,14},{12,8},{14,10},{1,5},{3,7},... | collective-permute-start | bytes 786440 | tf_op jit(solution)/shard_map/ppermute | solution.py:303
  26.9 12.1 %collective-permute-start.5 = (bf16[2,512,128]{2,1,0:T(8,128)(2,1)S(1)}, bf16[2,512,128]{2,1,0:T(8,128)(2,1)}, u32[]{:S(2)}, u32[]{:S(2)}) collective-permute-start(bf16[2,512,128]{2,1,0:T(8,128)(2,1)S(1)} %get-tuple-element.30), channel_id=1, source_target_pairs={{0,12},{2,14},{4,8},{6,10},{8,4},{10,6},{12,0},{14,2},{1,13},{3,15... | collective-permute-start | bytes 786440 | tf_op jit(solution)/shard_map/ppermute | solution.py:303
  28.3 25.9 %all-to-all-start = ((bf16[8,4,64,128]{3,2,1,0:T(8,128)(2,1)}), bf16[8,4,64,128]{3,2,1,0:T(8,128)(2,1)S(1)}, u32[]{:S(2)}, u32[]{:S(2)}) async-start(bf16[8,4,64,128]{3,2,1,0:T(8,128)(2,1)} %add_convert_fusion), calls=%async_computation | async-start | bytes 1048576 | tf_op jit(solution)/shard_map/all_to_all | solution.py:331
  40.2 5.7 %collective-permute-start.7 = (bf16[512,128]{1,0:T(8,128)(2,1)S(1)}, bf16[512,128]{1,0:T(8,128)(2,1)S(1)}, u32[]{:S(2)}, u32[]{:S(2)}) collective-permute-start(bf16[512,128]{1,0:T(8,128)(2,1)S(1)} %fusion.7), channel_id=1, source_target_pairs={{0,2},{2,0},{4,6},{6,4},{8,10},{10,8},{12,14},{14,12},{1,3},{3,1},... | collective-permute-start | bytes 393224 | tf_op jit(solution)/shard_map/ppermute | solution.py:303
  41.2 5.8 %collective-permute-start.8 = (bf16[512,128]{1,0:T(8,128)(2,1)S(1)}, bf16[512,128]{1,0:T(8,128)(2,1)S(1)}, u32[]{:S(2)}, u32[]{:S(2)}) collective-permute-start(bf16[512,128]{1,0:T(8,128)(2,1)S(1)} %get-tuple-element.45), channel_id=1, source_target_pairs={{0,8},{2,10},{4,12},{6,14},{8,0},{10,2},{12,4},{14,6},{1,9},{3,11}... | collective-permute-start | bytes 393224 | tf_op jit(solution)/shard_map/ppermute | solution.py:303
  43.4 6.8 %collective-permute-start.10 = (bf16[512,128]{1,0:T(8,128)(2,1)S(1)}, bf16[512,128]{1,0:T(8,128)(2,1)S(1)}, u32[]{:S(2)}, u32[]{:S(2)}) collective-permute-start(bf16[512,128]{1,0:T(8,128)(2,1)S(1)} %get-tuple-element.46), channel_id=1, source_target_pairs={{0,12},{2,14},{4,8},{6,10},{8,4},{10,6},{12,0},{14,2},{1,13},{3,15... | collective-permute-start | bytes 393224 | tf_op jit(solution)/shard_map/ppermute | solution.py:303
  44.2 6.0 %collective-permute-start.9 = (bf16[512,128]{1,0:T(8,128)(2,1)S(1)}, bf16[512,128]{1,0:T(8,128)(2,1)S(1)}, u32[]{:S(2)}, u32[]{:S(2)}) collective-permute-start(bf16[512,128]{1,0:T(8,128)(2,1)S(1)} %get-tuple-element.47), channel_id=1, source_target_pairs={{0,4},{2,6},{4,0},{6,2},{8,12},{10,14},{12,8},{14,10},{1,5},{3,7},... | collective-permute-start | bytes 393224 | tf_op jit(solution)/shard_map/ppermute | solution.py:303

commit v10 on v9

--- a/solution.py
+++ b/solution.py
@@ -199,13 +199,13 @@
         mean_grad = jnp.mean(scaled, axis=-1, keepdims=True)
         slope = jnp.mean(scaled * center, axis=-1, keepdims=True) * (inverse * inverse)
         result = (inverse * (scaled - mean_grad - center * slope)).astype(BF16)
-        to = at % (count // 2)
+        split = ring0_ref.shape[1]
         for j in range(8):
             part = result[:, j * 128 : (j + 1) * 128]
-            if at < count // 2:
-                ring_refs[j // 2][j % 2, to : to + rows, :] = part
+            if at < split:
+                ring_refs[j // 2][j % 2, at : at + rows, :] = part
             else:
-                (near_ref, across_ref)[j % 2][j // 2, to : to + rows, :] = part
+                (near_ref, across_ref)[j % 2][j // 2, at - split : at - split + rows, :] = part
 
     carry = [None, None]
 
@@ -255,12 +255,12 @@
 
     attention([0, 1, 2, 3, 4, 5, 6, 7, 8])
     fetches[0].wait()
-    input_rows(0, 512)
-    input_rows(512, 512)
+    input_rows(0, ring0_ref.shape[1])
+    input_rows(ring0_ref.shape[1], near_ref.shape[1])
 
     fetches[1].wait()
     fetches[2].wait()
-    core = shard % 2
+    core, zl = shard % 2, (shard // 2) % 2
     qkv = cols_by_cols(grads_ref[...], normed_ref[...]).astype(BF16)
     out = cols_by_cols(mixed_ref[...], cot_ref[...]).astype(BF16)
     full = jnp.concatenate([qkv, out], axis=0)
@@ -269,16 +269,17 @@
         low, high = both[:64], both[64:]
         keep = jnp.where(core == 0, low, high)
         send = jnp.where(core == 0, high, low)
+        side = jnp.bitwise_xor(zl, z % 2)
         for m in range(4):
-            keep_ref[z, m] = keep[:, m * HS : (m + 1) * HS]
-            send_ref[z, m] = send[:, m * HS : (m + 1) * HS]
+            keep_ref[side, z // 2, m] = keep[:, m * HS : (m + 1) * HS]
+            send_ref[side, z // 2, m] = send[:, m * HS : (m + 1) * HS]
 
 
 def backward(lengths, proj, stats, halo, gain, qkv_weight, out_weight, pad2d, frames, normed, cotangent):
     count, width = frames.shape
     vmem = pl.BlockSpec(memory_space=pltpu.VMEM)
-    half = count // 2
-    shapes = [(4, half, 128)] * 2 + [(2, half, 128)] * 4 + [(8, 4, width // 16, HS)] * 2
+    split = count * 3 // 8
+    shapes = [(4, count - split, 128)] * 2 + [(2, split, 128)] * 4 + [(2, 4, 4, width // 16, HS)] * 2
     return pl.pallas_call(
         backward_body,
         in_specs=[pl.BlockSpec(memory_space=pltpu.SMEM)] + [vmem] * 7 + [pl.BlockSpec(memory_space=pl.ANY)] * 3,
@@ -326,17 +327,20 @@
     other = swapped(send, "tm", 1)
     across = swapped(across, "mp", 1)
     ring_in = [swapped(ring[k], "mp", 2 * k) for k in (2, 1, 3)]
-    chip = total(keep, other).astype(BF16)
-    same_core = [[c + 2 * z for z in range(shards // 2)] for c in range(2)]
-    weights = lax.all_to_all(chip, "tm", 0, 0, tiled=True, axis_index_groups=same_core)
-    (near, across, ring_in), _ = lax.optimization_barrier(((near, across, ring_in), chip))
+    stay, cross = total(keep[0], other[0]).astype(BF16), total(keep[1], other[1]).astype(BF16)
+    pair = total(stay, swapped(cross, "tm", 2)).astype(BF16)
+    groups = [[c + 4 * z for z in range(shards // 4)] for c in range(4)]
+    weights = lax.all_to_all(pair, "tm", 0, 0, tiled=True, axis_index_groups=groups)
+    (near, across, ring_in), _ = lax.optimization_barrier(((near, across, ring_in), pair))
     col = [total(near[k], across[k]) for k in range(4)]
     col_in = [swapped(col[k].astype(BF16), "mp", 2 * k) for k in (2, 1, 3)]
     ring_in, _ = lax.optimization_barrier((ring_in, [c.astype(BF16) for c in col[1:]]))
     theirs = swapped(total(ring[0][1], *[r[1] for r in ring_in]).astype(BF16), "mp", 1)
+    first_half = total(total(ring[0][0], *[r[0] for r in ring_in]), theirs).astype(BF16)
+    weights, _ = lax.optimization_barrier((weights, first_half))
     qkv_grad = weights[:, :3].astype(F32).sum(axis=0)
     out_grad = weights[:, 3].astype(F32).sum(axis=0)
-    first_half = total(total(ring[0][0], *[r[0] for r in ring_in]), theirs).astype(BF16)
+    col_in, _ = lax.optimization_barrier((col_in, (qkv_grad, out_grad)))
     second_half = total(col[0], *col_in).astype(BF16)
     frame_grad = jnp.concatenate([first_half, second_half], axis=0)
     return frame_grad, qkv_grad, out_grad.T

time: 55.8 us -> 55.8 us (level)
  the two profiles are of different devices: /device:TPU:1 before, /device:TPU:96 now
where the time goes in v10:
time: 55.8 us; the launch traced here: 55.5 us
  starting transfers between devices  27.2 us (49%)
  Pallas kernels  11.8 us (21%)
  waiting for transfers between devices  9.3 us (17%)
  other arithmetic  5.14 us (9%)
  local copies, waits for them, and re-layouts  1.25 us (2%)
  between operations  0.85 us (2%)
    ppermute x10, starting transfers between devices, swapped(): lax.ppermute(x, axis, [(i, i ^ bit) for i in range(lax.axis_size(axis))])  16.9 us
    ppermute x10, waiting for transfers between devices, swapped(): lax.ppermute(x, axis, [(i, i ^ bit) for i in range(lax.axis_size(axis))])  8.75 us
    pallas_call x1, Pallas kernels, backward(): pl.pallas_call(backward_body, in_specs=[pl.BlockSpec(memory_space=pltpu.S...  7.12 us
    all_to_all x1, starting transfers between devices, on_device(): lax.all_to_all(pair, 'tm', 0, 0, tiled=True, axis_index_groups=groups)  5.9 us
    pallas_call x1, Pallas kernels, project(): pl.pallas_call(project_body, in_specs=[hbm, vmem, hbm, hbm, hbm, vmem], o...  4.64 us
    ppermute x1, starting transfers between devices, on_device(): lax.ppermute(ends, 'tm', up)  2.41 us
    ppermute x1, starting transfers between devices, on_device(): lax.ppermute(starts, 'tm', down)  1.92 us
    another operation x1, local copies, waits for them, and re-layouts, on_device(): ends = jnp.stack([frames[-HALO:], cotangent[-HALO:]])  1.22 us
  transfers between devices with their start and end apart: 13, of which 5 were waited for; matrix products, arithmetic and copies ran while one was open for 8% of the time, Pallas kernels for 8%

profile of v10, /device:TPU:96, one launch (start us, length us, event | category | flops | bytes accessed | tf_op | source)
XLA Modules:
  0.0 55.5 jit_solution(14122939281636447729)
XLA Ops:
  0.6 0.0 copy-start.3
  0.6 0.0 copy-start.2
  0.7 0.0 copy-start.4
  0.7 0.0 copy-start.5
  0.7 1.2 %slice_bitcast_fusion.2 = (bf16[1,64,1024]{2,1,0:T(8,128)(2,1)S(1)}, bf16[1,64,1024]{2,1,0:T(8,128)(2,1)S(1)}, bf16[1,64,1024]{2,1,0:T(8,128)(2,1)S(1)}, bf16[1,64,1024]{2,1,0:T(8,128)(2,1)S(1)}) fusion(bf16[1024,1024]{1,0:T(8,128)(2,1)} %cot_hbm.3, bf16[1024,1024]{1,0:T(8,128)(2,1)} %frames_hbm.3), kind=kLoop, calls=%fused_computation.27 | loop fusion | bytes 1048576 | tf_op jit(solution)/shard_map/stack | solution.py:318
  1.9 1.9 %collective-permute-start.1 = (bf16[2,64,1024]{2,1,0:T(8,128)(2,1)S(1)}, bf16[2,64,1024]{2,1,0:T(8,128)(2,1)S(1)}, u32[]{:S(2)}, u32[]{:S(2)}) collective-permute-start(bf16[2,64,1024]{2,1,0:T(8,128)(2,1)S(1)} %pad_maximum_fusion.2), channel_id=1, source_target_pairs={{16,0},{32,16},{48,32},{64,48},{80,64},{96,80},{112,96},{128,112},... | collective-permute-start | bytes 786440 | tf_op jit(solution)/shard_map/ppermute | solution.py:320
  3.9 2.4 %collective-permute-start = (bf16[2,64,1024]{2,1,0:T(8,128)(2,1)S(1)}, bf16[2,64,1024]{2,1,0:T(8,128)(2,1)S(1)}, u32[]{:S(2)}, u32[]{:S(2)}) collective-permute-start(bf16[2,64,1024]{2,1,0:T(8,128)(2,1)S(1)} %pad_maximum_fusion.1), channel_id=1, source_target_pairs={{0,16},{16,32},{32,48},{48,64},{64,80},{80,96},{96,112},{112,128},... | collective-permute-start | bytes 786440 | tf_op jit(solution)/shard_map/ppermute | solution.py:320
  6.3 0.0 copy-done.3
  6.3 0.0 copy-done.2
  6.3 0.0 copy-done.4
  6.3 0.0 copy-done.5
  6.3 0.0 copy-start
  6.4 0.0 copy-start.1
  6.4 0.0 copy-start.6
  6.4 4.6 %project.1 = (bf16[4,1024,128]{2,1,0:T(8,128)(2,1)S(1)}, f32[1024,128]{1,0:T(8,128)S(1)}, bf16[1024,1024]{1,0:T(8,128)(2,1)S(1)}) custom-call(bf16[1024,1024]{1,0:T(8,128)(2,1)} %frames_hbm.3, f32[1,1024]{1,0:T(1,128)S(1)} %bitcast.40, bf16[3,1024,128]{2,1,0:T(8,128)(2,1)S(1)} %copy-done.2, bf16[128,1024]{1,0:T(8,128)(2,1)S(1)} %copy-done.3, ...), custom_call_target="tpu_custom_call" | custom-call | tf_op jit(solution)/shard_map/project/pallas_call | solution.py:100
  11.0 0.0 collective-permute-done.1
  11.0 0.5 collective-permute-done
  11.6 0.0 copy-done
  11.6 0.0 copy-done.1
  11.6 0.0 copy-done.6
  11.7 7.1 %backward.1 = (bf16[4,640,128]{2,1,0:T(8,128)(2,1)S(1)}, bf16[4,640,128]{2,1,0:T(8,128)(2,1)S(1)}, bf16[2,384,128]{2,1,0:T(8,128)(2,1)S(1)}, bf16[2,384,128]{2,1...) custom-call(s32[8]{0:T(128)S(1)} %copy-done.6, ...), custom_call_target="tpu_custom_call" | custom-call | tf_op jit(solution)/shard_map/backward/pallas_call | solution.py:283
  18.8 2.3 %collective-permute-start.6 = (bf16[2,4,4,64,128]{4,3,2,1,0:T(8,128)(2,1)S(1)}, bf16[2,4,4,64,128]{4,3,2,1,0:T(8,128)(2,1)S(1)}, u32[]{:S(2)}, u32[]{:S(2)}) collective-permute-start(bf16[2,4,4,64,128]{4,3,2,1,0:T(8,128)(2,1)S(1)} %get-tuple-element.36), channel_id=1, source_target_pairs={{0,16},{16,0},{32,48},{48,32},{64,80},{80,64},{96,112},{112,96},{1... | collective-permute-start | bytes 1572872 | tf_op jit(solution)/shard_map/ppermute | solution.py:304
  21.1 3.0 %collective-permute-start.2 = (bf16[4,640,128]{2,1,0:T(8,128)(2,1)S(1)}, bf16[4,640,128]{2,1,0:T(8,128)(2,1)S(1)}, u32[]{:S(2)}, u32[]{:S(2)}) collective-permute-start(bf16[4,640,128]{2,1,0:T(8,128)(2,1)S(1)} %get-tuple-element.31), channel_id=1, source_target_pairs={{0,2},{2,0},{4,6},{6,4},{8,10},{10,8},{12,14},{14,12},{1,3},{3,1},... | collective-permute-start | bytes 1966088 | tf_op jit(solution)/shard_map/ppermute | solution.py:304
  24.1 0.0 collective-permute-done.6
  24.1 0.1 fusion.5
  24.2 0.1 collective-permute-start.7
  24.3 3.3 %collective-permute-start.3 = (bf16[2,384,128]{2,1,0:T(8,128)(2,1)S(1)}, bf16[2,384,128]{2,1,0:T(8,128)(2,1)S(1)}, u32[]{:S(2)}, u32[]{:S(2)}) collective-permute-start(bf16[2,384,128]{2,1,0:T(8,128)(2,1)S(1)} %get-tuple-element.32), channel_id=1, source_target_pairs={{0,8},{2,10},{4,12},{6,14},{8,0},{10,2},{12,4},{14,6},{1,9},{3,11}... | collective-permute-start | bytes 589832 | tf_op jit(solution)/shard_map/ppermute | solution.py:304
  27.5 0.7 %collective-permute-start.4 = (bf16[2,384,128]{2,1,0:T(8,128)(2,1)S(1)}, bf16[2,384,128]{2,1,0:T(8,128)(2,1)S(1)}, u32[]{:S(2)}, u32[]{:S(2)}) collective-permute-start(bf16[2,384,128]{2,1,0:T(8,128)(2,1)S(1)} %get-tuple-element.33), channel_id=1, source_target_pairs={{0,4},{2,6},{4,0},{6,2},{8,12},{10,14},{12,8},{14,10},{1,5},{3,7},... | collective-permute-start | bytes 589832 | tf_op jit(solution)/shard_map/ppermute | solution.py:304
  28.2 0.4 collective-permute-start.5
  28.6 3.7 %collective-permute-done.7 = bf16[4,4,64,128]{3,2,1,0:T(8,128)(2,1)S(1)} collective-permute-done((bf16[4,4,64,128]{3,2,1,0:T(8,128)(2,1)S(1)}, bf16[4,4,64,128]{3,2,1,0:T(8,128)(2,1)S(1)}, u32[]{:S(2)}, u32[]{:S(2)}) %collective-permute-start.7) | collective-permute-done | bytes 262176 | tf_op jit(solution)/shard_map/ppermute | solution.py:304
  32.3 0.8 %fusion = bf16[4,4,64,128]{3,2,1,0:T(8,128)(2,1)} fusion(bf16[4,4,64,128]{3,2,1,0:T(8,128)(2,1)S(1)} %collective-permute-done.7, bf16[2,4,4,64,128]{4,3,2,1,0:T(8,128)(2,1)S(1)} %collective-permute-done.6, bf16[2,4,4,64,128]{4,3,2,1,0:T(8,128)(2,1)S(1)} %get-tuple-element.35), kind=kLoop, calls=%fused_computation.2 | loop fusion | flops 1048576 | bytes 1048576 | tf_op jit(solution)/shard_map/convert_element_type | solution.py:331
  33.1 5.9 %all-to-all-start = ((bf16[4,4,64,128]{3,2,1,0:T(8,128)(2,1)}), bf16[4,4,64,128]{3,2,1,0:T(8,128)(2,1)S(1)}, u32[]{:S(2)}, u32[]{:S(2)}) async-start(bf16[4,4,64,128]{3,2,1,0:T(8,128)(2,1)} %fusion), calls=%async_computation | async-start | bytes 524288 | tf_op jit(solution)/shard_map/all_to_all | solution.py:333
  39.0 0.0 collective-permute-done.3
  39.0 0.0 collective-permute-done.4
  39.0 0.0 collective-permute-done.5
  39.0 0.3 collective-permute-done.2
  39.3 0.1 fusion.9
  39.4 0.9 %fusion.10 = bf16[384,128]{1,0:T(8,128)(2,1)S(1)} fusion(bf16[2,384,128]{2,1,0:T(8,128)(2,1)} %collective-permute-done.5, bf16[2,384,128]{2,1,0:T(8,128)(2,1)S(1)} %collective-permute-done.4, bf16[2,384,128]{2,1,0:T(8,128)(2,1)S(1)} %collective-permute-done.3, bf16[2,384,128]{2,1,0:T(8,128)(2,1)S(1)} %get-tuple-element.29), kind=kLoop, calls=%fused_computation.29 | loop fusion | flops 393216 | bytes 491520 | tf_op jit(solution)/shard_map/add | solution.py:310
  40.4 3.1 %collective-permute-start.8 = (bf16[384,128]{1,0:T(8,128)(2,1)S(1)}, bf16[384,128]{1,0:T(8,128)(2,1)S(1)}, u32[]{:S(2)}, u32[]{:S(2)}) collective-permute-start(bf16[384,128]{1,0:T(8,128)(2,1)S(1)} %fusion.10), channel_id=1, source_target_pairs={{0,2},{2,0},{4,6},{6,4},{8,10},{10,8},{12,14},{14,12},{1,3},{3,1},... | collective-permute-start | bytes 294920 | tf_op jit(solution)/shard_map/ppermute | solution.py:304
  43.5 3.0 %collective-permute-start.11 = (bf16[640,128]{1,0:T(8,128)(2,1)S(1)}, bf16[640,128]{1,0:T(8,128)(2,1)S(1)}, u32[]{:S(2)}, u32[]{:S(2)}) collective-permute-start(bf16[640,128]{1,0:T(8,128)(2,1)S(1)} %get-tuple-element.53), channel_id=1, source_target_pairs={{0,12},{2,14},{4,8},{6,10},{8,4},{10,6},{12,0},{14,2},{1,13},{3,15... | collective-permute-start | bytes 491528 | tf_op jit(solution)/shard_map/ppermute | solution.py:304
  46.5 0.6 %collective-permute-start.9 = (bf16[640,128]{1,0:T(8,128)(2,1)S(1)}, bf16[640,128]{1,0:T(8,128)(2,1)S(1)}, u32[]{:S(2)}, u32[]{:S(2)}) collective-permute-start(bf16[640,128]{1,0:T(8,128)(2,1)S(1)} %get-tuple-element.54), channel_id=1, source_target_pairs={{0,8},{2,10},{4,12},{6,14},{8,0},{10,2},{12,4},{14,6},{1,9},{3,11}... | collective-permute-start | bytes 491528 | tf_op jit(solution)/shard_map/ppermute | solution.py:304
  47.2 0.5 collective-permute-start.10
  47.6 0.0 collective-permute-done.8
  47.6 1.0 %fusion.6 = bf16[384,128]{1,0:T(8,128)(2,1)S(1)} fusion(bf16[384,128]{1,0:T(8,128)(2,1)S(1)} %collective-permute-done.8, bf16[2,384,128]{2,1,0:T(8,128)(2,1)} %collective-permute-done.5, bf16[2,384,128]{2,1,0:T(8,128)(2,1)S(1)} %collective-permute-done.4, bf16[2,384,128]{2,1,0:T(8,128)(2,1)S(1)} %collective-permute-done.3, ...), kind=kLoop, calls=%fused_computation.19 | loop fusion | flops 491520 | bytes 589824 | tf_op jit(solution)/shard_map/convert_element_type | solution.py:339
  48.6 0.0 all-to-all-done
  48.6 0.6 %convert_reduce_fusion.1 = f32[64,128]{1,0:T(8,128)} fusion(bf16[4,4,64,128]{3,2,1,0:T(8,128)(2,1)S(1)} %all-to-all-done), kind=kLoop, calls=%fused_computation.24 | loop fusion | flops 57344 | bytes 98304 | tf_op jit(solution)/shard_map/reduce_sum | solution.py:342
  49.2 0.7 %convert_reduce_fusion = f32[3,64,128]{2,1,0:T(8,128)} fusion(bf16[4,4,64,128]{3,2,1,0:T(8,128)(2,1)S(1)} %all-to-all-done), kind=kLoop, calls=%fused_computation.5 | loop fusion | flops 172032 | bytes 294912 | tf_op jit(solution)/shard_map/reduce_sum | solution.py:341
  49.9 2.8 %collective-permute-done.11 = bf16[640,128]{1,0:T(8,128)(2,1)S(1)} collective-permute-done((bf16[640,128]{1,0:T(8,128)(2,1)S(1)}, bf16[640,128]{1,0:T(8,128)(2,1)S(1)}, u32[]{:S(2)}, u32[]{:S(2)}) %collective-permute-start.11) | collective-permute-done | bytes 163872 | tf_op jit(solution)/shard_map/ppermute | solution.py:304
  52.6 2.0 %collective-permute-done.9 = bf16[640,128]{1,0:T(8,128)(2,1)S(1)} collective-permute-done((bf16[640,128]{1,0:T(8,128)(2,1)S(1)}, bf16[640,128]{1,0:T(8,128)(2,1)S(1)}, u32[]{:S(2)}, u32[]{:S(2)}) %collective-permute-start.9) | collective-permute-done | bytes 163872 | tf_op jit(solution)/shard_map/ppermute | solution.py:304
  54.6 0.0 collective-permute-done.10
  54.6 0.1 fusion.3
  54.8 0.7 %pad_maximum_fusion.3 = bf16[1024,128]{1,0:T(8,128)(2,1)} fusion(bf16[640,128]{1,0:T(8,128)(2,1)S(1)} %fusion.3, bf16[384,128]{1,0:T(8,128)(2,1)S(1)} %fusion.6), kind=kLoop, calls=%fused_computation.17 | loop fusion | flops 524288 | bytes 524288 | tf_op jit(solution)/shard_map/concatenate | solution.py:345
  (3 shorter events, 0.1 us)
Async XLA Ops:
  0.6 5.7 %copy-start.3 = (bf16[128,1024]{1,0:T(8,128)(2,1)S(1)}, bf16[128,1024]{1,0:T(8,128)(2,1)}, u32[]{:S(2)}) copy-start(bf16[128,1024]{1,0:T(8,128)(2,1)} %out_ref.1) | copy-start | bytes 786436
  0.6 5.7 %copy-start.2 = (bf16[3,1024,128]{2,1,0:T(8,128)(2,1)S(1)}, bf16[3,1024,128]{2,1,0:T(8,128)(2,1)}, u32[]{:S(2)}) copy-start(bf16[3,1024,128]{2,1,0:T(8,128)(2,1)} %qkv_ref.1) | copy-start | bytes 2359300
  0.7 5.7 %copy-start.4 = (s32[16384]{0:T(1024)S(1)}, s32[16384]{0:T(1024)}, u32[]{:S(2)}) copy-start(s32[16384]{0:T(1024)} %param.12) | copy-start | bytes 196612
  0.7 5.7 %copy-start.5 = (f32[1024]{0:T(1024)S(1)}, f32[1024]{0:T(1024)}, u32[]{:S(2)}) copy-start(f32[1024]{0:T(1024)} %param.8) | copy-start | bytes 12292
  1.9 9.1 %collective-permute-start.1 = (bf16[2,64,1024]{2,1,0:T(8,128)(2,1)S(1)}, bf16[2,64,1024]{2,1,0:T(8,128)(2,1)S(1)}, u32[]{:S(2)}, u32[]{:S(2)}) collective-permute-start(bf16[2,64,1024]{2,1,0:T(8,128)(2,1)S(1)} %pad_maximum_fusion.2), channel_id=1, source_target_pairs={{16,0},{32,16},{48,32},{64,48},{80,64},{96,80},{112,96},{128,112},... | collective-permute-start | bytes 786440 | tf_op jit(solution)/shard_map/ppermute | solution.py:320
  3.9 7.7 %collective-permute-start = (bf16[2,64,1024]{2,1,0:T(8,128)(2,1)S(1)}, bf16[2,64,1024]{2,1,0:T(8,128)(2,1)S(1)}, u32[]{:S(2)}, u32[]{:S(2)}) collective-permute-start(bf16[2,64,1024]{2,1,0:T(8,128)(2,1)S(1)} %pad_maximum_fusion.1), channel_id=1, source_target_pairs={{0,16},{16,32},{32,48},{48,64},{64,80},{80,96},{96,112},{112,128},... | collective-permute-start | bytes 786440 | tf_op jit(solution)/shard_map/ppermute | solution.py:320
  6.3 5.3 %copy-start = (bf16[1024,1024]{1,0:T(8,128)(2,1)S(1)}, bf16[1024,1024]{1,0:T(8,128)(2,1)}, u32[]{:S(2)}) copy-start(bf16[1024,1024]{1,0:T(8,128)(2,1)} %frames_hbm.3) | copy-start | bytes 6291460
  6.4 5.3 %copy-start.1 = (bf16[1024,1024]{1,0:T(8,128)(2,1)S(1)}, bf16[1024,1024]{1,0:T(8,128)(2,1)}, u32[]{:S(2)}) copy-start(bf16[1024,1024]{1,0:T(8,128)(2,1)} %cot_hbm.3) | copy-start | bytes 6291460
  6.4 5.3 %copy-start.6 = (s32[8]{0:T(128)S(1)}, s32[8]{0:T(128)}, u32[]{:S(2)}) copy-start(s32[8]{0:T(128)} %len_ref.1) | copy-start | bytes 100
  18.8 5.3 %collective-permute-start.6 = (bf16[2,4,4,64,128]{4,3,2,1,0:T(8,128)(2,1)S(1)}, bf16[2,4,4,64,128]{4,3,2,1,0:T(8,128)(2,1)S(1)}, u32[]{:S(2)}, u32[]{:S(2)}) collective-permute-start(bf16[2,4,4,64,128]{4,3,2,1,0:T(8,128)(2,1)S(1)} %get-tuple-element.36), channel_id=1, source_target_pairs={{0,16},{16,0},{32,48},{48,32},{64,80},{80,64},{96,112},{112,96},{1... | collective-permute-start | bytes 1572872 | tf_op jit(solution)/shard_map/ppermute | solution.py:304
  21.1 18.2 %collective-permute-start.2 = (bf16[4,640,128]{2,1,0:T(8,128)(2,1)S(1)}, bf16[4,640,128]{2,1,0:T(8,128)(2,1)S(1)}, u32[]{:S(2)}, u32[]{:S(2)}) collective-permute-start(bf16[4,640,128]{2,1,0:T(8,128)(2,1)S(1)} %get-tuple-element.31), channel_id=1, source_target_pairs={{0,2},{2,0},{4,6},{6,4},{8,10},{10,8},{12,14},{14,12},{1,3},{3,1},... | collective-permute-start | bytes 1966088 | tf_op jit(solution)/shard_map/ppermute | solution.py:304
  24.2 8.1 %collective-permute-start.7 = (bf16[4,4,64,128]{3,2,1,0:T(8,128)(2,1)S(1)}, bf16[4,4,64,128]{3,2,1,0:T(8,128)(2,1)S(1)}, u32[]{:S(2)}, u32[]{:S(2)}) collective-permute-start(bf16[4,4,64,128]{3,2,1,0:T(8,128)(2,1)S(1)} %fusion.5), channel_id=1, source_target_pairs={{0,32},{16,48},{32,0},{48,16},{64,96},{80,112},{96,64},{112,80},{1... | collective-permute-start | bytes 786440 | tf_op jit(solution)/shard_map/ppermute | solution.py:304
  24.3 14.7 %collective-permute-start.3 = (bf16[2,384,128]{2,1,0:T(8,128)(2,1)S(1)}, bf16[2,384,128]{2,1,0:T(8,128)(2,1)S(1)}, u32[]{:S(2)}, u32[]{:S(2)}) collective-permute-start(bf16[2,384,128]{2,1,0:T(8,128)(2,1)S(1)} %get-tuple-element.32), channel_id=1, source_target_pairs={{0,8},{2,10},{4,12},{6,14},{8,0},{10,2},{12,4},{14,6},{1,9},{3,11}... | collective-permute-start | bytes 589832 | tf_op jit(solution)/shard_map/ppermute | solution.py:304
  27.5 11.5 %collective-permute-start.4 = (bf16[2,384,128]{2,1,0:T(8,128)(2,1)S(1)}, bf16[2,384,128]{2,1,0:T(8,128)(2,1)S(1)}, u32[]{:S(2)}, u32[]{:S(2)}) collective-permute-start(bf16[2,384,128]{2,1,0:T(8,128)(2,1)S(1)} %get-tuple-element.33), channel_id=1, source_target_pairs={{0,4},{2,6},{4,0},{6,2},{8,12},{10,14},{12,8},{14,10},{1,5},{3,7},... | collective-permute-start | bytes 589832 | tf_op jit(solution)/shard_map/ppermute | solution.py:304
  28.2 10.8 %collective-permute-start.5 = (bf16[2,384,128]{2,1,0:T(8,128)(2,1)S(1)}, bf16[2,384,128]{2,1,0:T(8,128)(2,1)}, u32[]{:S(2)}, u32[]{:S(2)}) collective-permute-start(bf16[2,384,128]{2,1,0:T(8,128)(2,1)S(1)} %get-tuple-element.34), channel_id=1, source_target_pairs={{0,12},{2,14},{4,8},{6,10},{8,4},{10,6},{12,0},{14,2},{1,13},{3,15... | collective-permute-start | bytes 589832 | tf_op jit(solution)/shard_map/ppermute | solution.py:304
  33.1 15.5 %all-to-all-start = ((bf16[4,4,64,128]{3,2,1,0:T(8,128)(2,1)}), bf16[4,4,64,128]{3,2,1,0:T(8,128)(2,1)S(1)}, u32[]{:S(2)}, u32[]{:S(2)}) async-start(bf16[4,4,64,128]{3,2,1,0:T(8,128)(2,1)} %fusion), calls=%async_computation | async-start | bytes 524288 | tf_op jit(solution)/shard_map/all_to_all | solution.py:333
  40.4 7.2 %collective-permute-start.8 = (bf16[384,128]{1,0:T(8,128)(2,1)S(1)}, bf16[384,128]{1,0:T(8,128)(2,1)S(1)}, u32[]{:S(2)}, u32[]{:S(2)}) collective-permute-start(bf16[384,128]{1,0:T(8,128)(2,1)S(1)} %fusion.10), channel_id=1, source_target_pairs={{0,2},{2,0},{4,6},{6,4},{8,10},{10,8},{12,14},{14,12},{1,3},{3,1},... | collective-permute-start | bytes 294920 | tf_op jit(solution)/shard_map/ppermute | solution.py:304
  43.5 9.1 %collective-permute-start.11 = (bf16[640,128]{1,0:T(8,128)(2,1)S(1)}, bf16[640,128]{1,0:T(8,128)(2,1)S(1)}, u32[]{:S(2)}, u32[]{:S(2)}) collective-permute-start(bf16[640,128]{1,0:T(8,128)(2,1)S(1)} %get-tuple-element.53), channel_id=1, source_target_pairs={{0,12},{2,14},{4,8},{6,10},{8,4},{10,6},{12,0},{14,2},{1,13},{3,15... | collective-permute-start | bytes 491528 | tf_op jit(solution)/shard_map/ppermute | solution.py:304
  46.5 8.1 %collective-permute-start.9 = (bf16[640,128]{1,0:T(8,128)(2,1)S(1)}, bf16[640,128]{1,0:T(8,128)(2,1)S(1)}, u32[]{:S(2)}, u32[]{:S(2)}) collective-permute-start(bf16[640,128]{1,0:T(8,128)(2,1)S(1)} %get-tuple-element.54), channel_id=1, source_target_pairs={{0,8},{2,10},{4,12},{6,14},{8,0},{10,2},{12,4},{14,6},{1,9},{3,11}... | collective-permute-start | bytes 491528 | tf_op jit(solution)/shard_map/ppermute | solution.py:304
  47.2 7.5 %collective-permute-start.10 = (bf16[640,128]{1,0:T(8,128)(2,1)S(1)}, bf16[640,128]{1,0:T(8,128)(2,1)S(1)}, u32[]{:S(2)}, u32[]{:S(2)}) collective-permute-start(bf16[640,128]{1,0:T(8,128)(2,1)S(1)} %get-tuple-element.55), channel_id=1, source_target_pairs={{0,4},{2,6},{4,0},{6,2},{8,12},{10,14},{12,8},{14,10},{1,5},{3,7},... | collective-permute-start | bytes 491528 | tf_op jit(solution)/shard_map/ppermute | solution.py:304

commit v11 on v8

--- a/solution.py
+++ b/solution.py
@@ -260,7 +260,7 @@
 
     fetches[1].wait()
     fetches[2].wait()
-    core = shard % 2
+    core, zl = shard % 2, (shard // 2) % 2
     qkv = cols_by_cols(grads_ref[...], normed_ref[...]).astype(BF16)
     out = cols_by_cols(mixed_ref[...], cot_ref[...]).astype(BF16)
     full = jnp.concatenate([qkv, out], axis=0)
@@ -269,16 +269,17 @@
         low, high = both[:64], both[64:]
         keep = jnp.where(core == 0, low, high)
         send = jnp.where(core == 0, high, low)
+        side = jnp.bitwise_xor(zl, z % 2)
         for m in range(4):
-            keep_ref[z, m] = keep[:, m * HS : (m + 1) * HS]
-            send_ref[z, m] = send[:, m * HS : (m + 1) * HS]
+            keep_ref[side, z // 2, m] = keep[:, m * HS : (m + 1) * HS]
+            send_ref[side, z // 2, m] = send[:, m * HS : (m + 1) * HS]
 
 
 def backward(lengths, proj, stats, halo, gain, qkv_weight, out_weight, pad2d, frames, normed, cotangent):
     count, width = frames.shape
     vmem = pl.BlockSpec(memory_space=pltpu.VMEM)
     half = count // 2
-    shapes = [(4, half, 128)] * 2 + [(2, half, 128)] * 4 + [(8, 4, width // 16, HS)] * 2
+    shapes = [(4, half, 128)] * 2 + [(2, half, 128)] * 4 + [(2, 4, 4, width // 16, HS)] * 2
     return pl.pallas_call(
         backward_body,
         in_specs=[pl.BlockSpec(memory_space=pltpu.SMEM)] + [vmem] * 7 + [pl.BlockSpec(memory_space=pl.ANY)] * 3,
@@ -326,18 +327,20 @@
     other = swapped(send, "tm", 1)
     across = swapped(across, "mp", 1)
     ring_in = [swapped(ring[k], "mp", 2 * k) for k in (2, 1, 3)]
-    chip = total(keep, other).astype(BF16)
-    same_core = [[c + 2 * z for z in range(shards // 2)] for c in range(2)]
-    weights = lax.all_to_all(chip, "tm", 0, 0, tiled=True, axis_index_groups=same_core)
-    (near, across, ring_in), _ = lax.optimization_barrier(((near, across, ring_in), chip))
+    stay, cross = total(keep[0], other[0]).astype(BF16), total(keep[1], other[1]).astype(BF16)
+    pair = total(stay, swapped(cross, "tm", 2)).astype(BF16)
+    groups = [[c + 4 * z for z in range(shards // 4)] for c in range(4)]
+    weights = lax.all_to_all(pair, "tm", 0, 0, tiled=True, axis_index_groups=groups)
+    (near, across, ring_in), _ = lax.optimization_barrier(((near, across, ring_in), pair))
     col = [total(near[k], across[k]) for k in range(4)]
     col_in = [swapped(col[k].astype(BF16), "mp", 2 * k) for k in (2, 1, 3)]
     ring_in, _ = lax.optimization_barrier((ring_in, [c.astype(BF16) for c in col[1:]]))
-    theirs = swapped(total(ring[0][1], *[r[1] for r in ring_in]).astype(BF16), "mp", 1)
+    both = lax.optimization_barrier(total(ring[0], *ring_in))
+    theirs = swapped(both[1].astype(BF16), "mp", 1)
     qkv_grad = weights[:, :3].astype(F32).sum(axis=0)
     out_grad = weights[:, 3].astype(F32).sum(axis=0)
     (theirs, col_in), _ = lax.optimization_barrier(((theirs, col_in), (qkv_grad, out_grad)))
-    first_half = total(total(ring[0][0], *[r[0] for r in ring_in]), theirs).astype(BF16)
+    first_half = total(both[0], theirs).astype(BF16)
     second_half = total(col[0], *col_in).astype(BF16)
     frame_grad = jnp.concatenate([first_half, second_half], axis=0)
     return frame_grad, qkv_grad, out_grad.T

time: 61 us -> 54.5 us (0.89)
  the two profiles are of different devices: /device:TPU:1 before, /device:TPU:64 now
where the time goes in v11:
time: 54.5 us; the launch traced here: 54.2 us
  starting transfers between devices  29.6 us (54%)
  Pallas kernels  11.7 us (21%)
  waiting for transfers between devices  6.5 us (12%)
  other arithmetic  4.29 us (8%)
  local copies, waits for them, and re-layouts  1.27 us (2%)
  between operations  0.86 us (2%)
    ppermute x10, starting transfers between devices, swapped(): lax.ppermute(x, axis, [(i, i ^ bit) for i in range(lax.axis_size(axis))])  18 us
    all_to_all x1, starting transfers between devices, on_device(): lax.all_to_all(pair, 'tm', 0, 0, tiled=True, axis_index_groups=groups)  7.34 us
    pallas_call x1, Pallas kernels, backward(): pl.pallas_call(backward_body, in_specs=[pl.BlockSpec(memory_space=pltpu.S...  7.04 us
    ppermute x10, waiting for transfers between devices, swapped(): lax.ppermute(x, axis, [(i, i ^ bit) for i in range(lax.axis_size(axis))])  5.81 us
    pallas_call x1, Pallas kernels, project(): pl.pallas_call(project_body, in_specs=[hbm, vmem, hbm, hbm, hbm, vmem], o...  4.64 us
    ppermute x1, starting transfers between devices, on_device(): lax.ppermute(ends, 'tm', up)  2.41 us
    ppermute x1, starting transfers between devices, on_device(): lax.ppermute(starts, 'tm', down)  1.92 us
    another operation x1, local copies, waits for them, and re-layouts, on_device(): ends = jnp.stack([frames[-HALO:], cotangent[-HALO:]])  1.22 us
  transfers between devices with their start and end apart: 13, of which 5 were waited for; matrix products, arithmetic and copies ran while one was open for 6% of the time, Pallas kernels for 9%

profile of v11, /device:TPU:64, one launch (start us, length us, event | category | flops | bytes accessed | tf_op | source)
XLA Modules:
  0.0 54.2 jit_solution(6589701438962791519)
XLA Ops:
  0.6 0.0 copy-start.3
  0.6 0.0 copy-start.2
  0.7 0.0 copy-start.4
  0.7 0.0 copy-start.5
  0.7 1.2 %slice_bitcast_fusion.3 = (bf16[1,64,1024]{2,1,0:T(8,128)(2,1)S(1)}, bf16[1,64,1024]{2,1,0:T(8,128)(2,1)S(1)}, bf16[1,64,1024]{2,1,0:T(8,128)(2,1)S(1)}, bf16[1,64,1024]{2,1,0:T(8,128)(2,1)S(1)}) fusion(bf16[1024,1024]{1,0:T(8,128)(2,1)} %cot_hbm.3, bf16[1024,1024]{1,0:T(8,128)(2,1)} %frames_hbm.3), kind=kLoop, calls=%fused_computation.30 | loop fusion | bytes 1048576 | tf_op jit(solution)/shard_map/stack | solution.py:318
  1.9 1.9 %collective-permute-start.1 = (bf16[2,64,1024]{2,1,0:T(8,128)(2,1)S(1)}, bf16[2,64,1024]{2,1,0:T(8,128)(2,1)S(1)}, u32[]{:S(2)}, u32[]{:S(2)}) collective-permute-start(bf16[2,64,1024]{2,1,0:T(8,128)(2,1)S(1)} %pad_maximum_fusion.2), channel_id=1, source_target_pairs={{16,0},{32,16},{48,32},{64,48},{80,64},{96,80},{112,96},{128,112},... | collective-permute-start | bytes 786440 | tf_op jit(solution)/shard_map/ppermute | solution.py:320
  3.9 2.4 %collective-permute-start = (bf16[2,64,1024]{2,1,0:T(8,128)(2,1)S(1)}, bf16[2,64,1024]{2,1,0:T(8,128)(2,1)S(1)}, u32[]{:S(2)}, u32[]{:S(2)}) collective-permute-start(bf16[2,64,1024]{2,1,0:T(8,128)(2,1)S(1)} %pad_maximum_fusion.1), channel_id=1, source_target_pairs={{0,16},{16,32},{32,48},{48,64},{64,80},{80,96},{96,112},{112,128},... | collective-permute-start | bytes 786440 | tf_op jit(solution)/shard_map/ppermute | solution.py:320
  6.3 0.0 copy-done.3
  6.3 0.0 copy-done.2
  6.3 0.0 copy-done.4
  6.3 0.0 copy-done.5
  6.3 0.0 copy-start
  6.4 0.0 copy-start.1
  6.4 0.0 copy-start.6
  6.4 4.6 %project.1 = (bf16[4,1024,128]{2,1,0:T(8,128)(2,1)S(1)}, f32[1024,128]{1,0:T(8,128)S(1)}, bf16[1024,1024]{1,0:T(8,128)(2,1)S(1)}) custom-call(bf16[1024,1024]{1,0:T(8,128)(2,1)} %frames_hbm.3, f32[1,1024]{1,0:T(1,128)S(1)} %bitcast.42, bf16[3,1024,128]{2,1,0:T(8,128)(2,1)S(1)} %copy-done.2, bf16[128,1024]{1,0:T(8,128)(2,1)S(1)} %copy-done.3, ...), custom_call_target="tpu_custom_call" | custom-call | tf_op jit(solution)/shard_map/project/pallas_call | solution.py:100
  11.0 0.0 collective-permute-done.1
  11.0 0.5 %collective-permute-done = bf16[2,64,1024]{2,1,0:T(8,128)(2,1)S(1)} collective-permute-done((bf16[2,64,1024]{2,1,0:T(8,128)(2,1)S(1)}, bf16[2,64,1024]{2,1,0:T(8,128)(2,1)S(1)}, u32[]{:S(2)}, u32[]{:S(2)}) %collective-permute-start) | collective-permute-done | bytes 262176 | tf_op jit(solution)/shard_map/ppermute | solution.py:320
  11.6 0.0 copy-done
  11.6 0.0 copy-done.1
  11.6 0.0 copy-done.6
  11.7 7.0 %backward.1 = (bf16[4,512,128]{2,1,0:T(8,128)(2,1)S(1)}, bf16[4,512,128]{2,1,0:T(8,128)(2,1)S(1)}, bf16[2,512,128]{2,1,0:T(8,128)(2,1)S(1)}, bf16[2,512,128]{2,1...) custom-call(s32[8]{0:T(128)S(1)} %copy-done.6, ...), custom_call_target="tpu_custom_call" | custom-call | tf_op jit(solution)/shard_map/backward/pallas_call | solution.py:283
  18.7 1.1 %collective-permute-start.6 = (bf16[2,4,4,64,128]{4,3,2,1,0:T(8,128)(2,1)S(1)}, bf16[2,4,4,64,128]{4,3,2,1,0:T(8,128)(2,1)S(1)}, u32[]{:S(2)}, u32[]{:S(2)}) collective-permute-start(bf16[2,4,4,64,128]{4,3,2,1,0:T(8,128)(2,1)S(1)} %get-tuple-element.36), channel_id=1, source_target_pairs={{0,16},{16,0},{32,48},{48,32},{64,80},{80,64},{96,112},{112,96},{1... | collective-permute-start | bytes 1572872 | tf_op jit(solution)/shard_map/ppermute | solution.py:304
  19.8 3.0 %collective-permute-start.2 = (bf16[4,512,128]{2,1,0:T(8,128)(2,1)S(1)}, bf16[4,512,128]{2,1,0:T(8,128)(2,1)S(1)}, u32[]{:S(2)}, u32[]{:S(2)}) collective-permute-start(bf16[4,512,128]{2,1,0:T(8,128)(2,1)S(1)} %get-tuple-element.31), channel_id=1, source_target_pairs={{0,2},{2,0},{4,6},{6,4},{8,10},{10,8},{12,14},{14,12},{1,3},{3,1},... | collective-permute-start | bytes 1572872 | tf_op jit(solution)/shard_map/ppermute | solution.py:304
  22.8 0.0 collective-permute-done.6
  22.8 0.1 fusion.2
  22.9 3.2 %collective-permute-start.7 = (bf16[4,4,64,128]{3,2,1,0:T(8,128)(2,1)S(1)}, bf16[4,4,64,128]{3,2,1,0:T(8,128)(2,1)S(1)}, u32[]{:S(2)}, u32[]{:S(2)}) collective-permute-start(bf16[4,4,64,128]{3,2,1,0:T(8,128)(2,1)S(1)} %fusion.2), channel_id=1, source_target_pairs={{0,32},{16,48},{32,0},{48,16},{64,96},{80,112},{96,64},{112,80},{1... | collective-permute-start | bytes 786440 | tf_op jit(solution)/shard_map/ppermute | solution.py:304
  26.1 3.2 %collective-permute-start.3 = (bf16[2,512,128]{2,1,0:T(8,128)(2,1)S(1)}, bf16[2,512,128]{2,1,0:T(8,128)(2,1)S(1)}, u32[]{:S(2)}, u32[]{:S(2)}) collective-permute-start(bf16[2,512,128]{2,1,0:T(8,128)(2,1)S(1)} %get-tuple-element.32), channel_id=1, source_target_pairs={{0,8},{2,10},{4,12},{6,14},{8,0},{10,2},{12,4},{14,6},{1,9},{3,11}... | collective-permute-start | bytes 786440 | tf_op jit(solution)/shard_map/ppermute | solution.py:304
  29.3 0.7 %collective-permute-start.4 = (bf16[2,512,128]{2,1,0:T(8,128)(2,1)S(1)}, bf16[2,512,128]{2,1,0:T(8,128)(2,1)S(1)}, u32[]{:S(2)}, u32[]{:S(2)}) collective-permute-start(bf16[2,512,128]{2,1,0:T(8,128)(2,1)S(1)} %get-tuple-element.33), channel_id=1, source_target_pairs={{0,4},{2,6},{4,0},{6,2},{8,12},{10,14},{12,8},{14,10},{1,5},{3,7},... | collective-permute-start | bytes 786440 | tf_op jit(solution)/shard_map/ppermute | solution.py:304
  30.0 0.4 collective-permute-start.5
  30.4 2.0 %collective-permute-done.7 = bf16[4,4,64,128]{3,2,1,0:T(8,128)(2,1)S(1)} collective-permute-done((bf16[4,4,64,128]{3,2,1,0:T(8,128)(2,1)S(1)}, bf16[4,4,64,128]{3,2,1,0:T(8,128)(2,1)S(1)}, u32[]{:S(2)}, u32[]{:S(2)}) %collective-permute-start.7) | collective-permute-done | bytes 262176 | tf_op jit(solution)/shard_map/ppermute | solution.py:304
  32.4 0.8 %fusion = bf16[4,4,64,128]{3,2,1,0:T(8,128)(2,1)} fusion(bf16[4,4,64,128]{3,2,1,0:T(8,128)(2,1)S(1)} %collective-permute-done.7, bf16[2,4,4,64,128]{4,3,2,1,0:T(8,128)(2,1)S(1)} %collective-permute-done.6, bf16[2,4,4,64,128]{4,3,2,1,0:T(8,128)(2,1)S(1)} %get-tuple-element.35), kind=kLoop, calls=%fused_computation.2 | loop fusion | flops 1048576 | bytes 1048576 | tf_op jit(solution)/shard_map/convert_element_type | solution.py:331
  33.2 7.3 %all-to-all-start = ((bf16[4,4,64,128]{3,2,1,0:T(8,128)(2,1)}), bf16[4,4,64,128]{3,2,1,0:T(8,128)(2,1)S(1)}, u32[]{:S(2)}, u32[]{:S(2)}) async-start(bf16[4,4,64,128]{3,2,1,0:T(8,128)(2,1)} %fusion), calls=%async_computation | async-start | bytes 524288 | tf_op jit(solution)/shard_map/all_to_all | solution.py:333
  40.6 0.0 collective-permute-done.3
  40.6 0.8 %collective-permute-done.4 = bf16[2,512,128]{2,1,0:T(8,128)(2,1)S(1)} collective-permute-done((bf16[2,512,128]{2,1,0:T(8,128)(2,1)S(1)}, bf16[2,512,128]{2,1,0:T(8,128)(2,1)S(1)}, u32[]{:S(2)}, u32[]{:S(2)}) %collective-permute-start.4) | collective-permute-done | bytes 262176 | tf_op jit(solution)/shard_map/ppermute | solution.py:304
  41.4 0.0 collective-permute-done.5
  41.4 0.0 collective-permute-done.2
  41.4 0.1 fusion.10
  41.5 2.8 %collective-permute-start.11 = (bf16[512,128]{1,0:T(8,128)(2,1)S(1)}, bf16[512,128]{1,0:T(8,128)(2,1)S(1)}, u32[]{:S(2)}, u32[]{:S(2)}) collective-permute-start(bf16[512,128]{1,0:T(8,128)(2,1)S(1)} %get-tuple-element.53), channel_id=1, source_target_pairs={{0,12},{2,14},{4,8},{6,10},{8,4},{10,6},{12,0},{14,2},{1,13},{3,15... | collective-permute-start | bytes 393224 | tf_op jit(solution)/shard_map/ppermute | solution.py:304
  44.3 0.7 %collective-permute-start.9 = (bf16[512,128]{1,0:T(8,128)(2,1)S(1)}, bf16[512,128]{1,0:T(8,128)(2,1)S(1)}, u32[]{:S(2)}, u32[]{:S(2)}) collective-permute-start(bf16[512,128]{1,0:T(8,128)(2,1)S(1)} %get-tuple-element.54), channel_id=1, source_target_pairs={{0,8},{2,10},{4,12},{6,14},{8,0},{10,2},{12,4},{14,6},{1,9},{3,11}... | collective-permute-start | bytes 393224 | tf_op jit(solution)/shard_map/ppermute | solution.py:304
  45.0 0.7 %collective-permute-start.10 = (bf16[512,128]{1,0:T(8,128)(2,1)S(1)}, bf16[512,128]{1,0:T(8,128)(2,1)S(1)}, u32[]{:S(2)}, u32[]{:S(2)}) collective-permute-start(bf16[512,128]{1,0:T(8,128)(2,1)S(1)} %get-tuple-element.55), channel_id=1, source_target_pairs={{0,4},{2,6},{4,0},{6,2},{8,12},{10,14},{12,8},{14,10},{1,5},{3,7},... | collective-permute-start | bytes 393224 | tf_op jit(solution)/shard_map/ppermute | solution.py:304
  45.7 1.1 %convert_add_fusion.1 = f32[2,512,128]{2,1,0:T(8,128)S(1)} fusion(bf16[2,512,128]{2,1,0:T(8,128)(2,1)} %collective-permute-done.5, bf16[2,512,128]{2,1,0:T(8,128)(2,1)S(1)} %collective-permute-done.4, bf16[2,512,128]{2,1,0:T(8,128)(2,1)S(1)} %collective-permute-done.3, bf16[2,512,128]{2,1,0:T(8,128)(2,1)S(1)} %get-tuple-element.29), kind=kLoop, calls=%fused_computation.3 | loop fusion | flops 917504 | bytes 1572864 | tf_op jit(solution)/shard_map/add | solution.py:310
  46.8 2.2 %collective-permute-start.8 = (bf16[512,128]{1,0:T(8,128)(2,1)S(1)}, bf16[512,128]{1,0:T(8,128)(2,1)S(1)}, u32[]{:S(2)}, u32[]{:S(2)}) collective-permute-start(bf16[512,128]{1,0:T(8,128)(2,1)S(1)} %fusion.11), channel_id=1, source_target_pairs={{0,2},{2,0},{4,6},{6,4},{8,10},{10,8},{12,14},{14,12},{1,3},{3,1},... | collective-permute-start | bytes 393224 | tf_op jit(solution)/shard_map/ppermute | solution.py:304
  49.0 0.1 all-to-all-done
  49.1 0.6 %convert_reduce_fusion.1 = f32[64,128]{1,0:T(8,128)} fusion(bf16[4,4,64,128]{3,2,1,0:T(8,128)(2,1)S(1)} %all-to-all-done), kind=kLoop, calls=%fused_computation.27 | loop fusion | flops 57344 | bytes 98304 | tf_op jit(solution)/shard_map/reduce_sum | solution.py:341
  49.7 0.7 %convert_reduce_fusion = f32[3,64,128]{2,1,0:T(8,128)} fusion(bf16[4,4,64,128]{3,2,1,0:T(8,128)(2,1)S(1)} %all-to-all-done), kind=kLoop, calls=%fused_computation.6 | loop fusion | flops 172032 | bytes 294912 | tf_op jit(solution)/shard_map/reduce_sum | solution.py:340
  50.4 3.0 %collective-permute-done.8 = bf16[512,128]{1,0:T(8,128)(2,1)S(1)} collective-permute-done((bf16[512,128]{1,0:T(8,128)(2,1)S(1)}, bf16[512,128]{1,0:T(8,128)(2,1)S(1)}, u32[]{:S(2)}, u32[]{:S(2)}) %collective-permute-start.8) | collective-permute-done | bytes 131104 | tf_op jit(solution)/shard_map/ppermute | solution.py:304
  53.3 0.0 collective-permute-done.11
  53.4 0.0 collective-permute-done.9
  53.4 0.0 collective-permute-done.10
  53.4 0.1 fusion.7
  53.5 0.7 %pad_maximum_fusion.3 = bf16[1024,128]{1,0:T(8,128)(2,1)} fusion(bf16[512,128]{1,0:T(8,128)(2,1)S(1)} %fusion.7, bf16[512,128]{1,0:T(8,128)(2,1)S(1)} %fusion.4), kind=kLoop, calls=%fused_computation.15 | loop fusion | flops 524288 | bytes 524288 | tf_op jit(solution)/shard_map/concatenate | solution.py:345
  (5 shorter events, 0.1 us)
Async XLA Ops:
  0.6 5.7 %copy-start.3 = (bf16[128,1024]{1,0:T(8,128)(2,1)S(1)}, bf16[128,1024]{1,0:T(8,128)(2,1)}, u32[]{:S(2)}) copy-start(bf16[128,1024]{1,0:T(8,128)(2,1)} %out_ref.1) | copy-start | bytes 786436
  0.6 5.7 %copy-start.2 = (bf16[3,1024,128]{2,1,0:T(8,128)(2,1)S(1)}, bf16[3,1024,128]{2,1,0:T(8,128)(2,1)}, u32[]{:S(2)}) copy-start(bf16[3,1024,128]{2,1,0:T(8,128)(2,1)} %qkv_ref.1) | copy-start | bytes 2359300
  0.7 5.7 %copy-start.4 = (s32[16384]{0:T(1024)S(1)}, s32[16384]{0:T(1024)}, u32[]{:S(2)}) copy-start(s32[16384]{0:T(1024)} %param.12) | copy-start | bytes 196612
  0.7 5.7 %copy-start.5 = (f32[1024]{0:T(1024)S(1)}, f32[1024]{0:T(1024)}, u32[]{:S(2)}) copy-start(f32[1024]{0:T(1024)} %param.8) | copy-start | bytes 12292
  1.9 9.1 %collective-permute-start.1 = (bf16[2,64,1024]{2,1,0:T(8,128)(2,1)S(1)}, bf16[2,64,1024]{2,1,0:T(8,128)(2,1)S(1)}, u32[]{:S(2)}, u32[]{:S(2)}) collective-permute-start(bf16[2,64,1024]{2,1,0:T(8,128)(2,1)S(1)} %pad_maximum_fusion.2), channel_id=1, source_target_pairs={{16,0},{32,16},{48,32},{64,48},{80,64},{96,80},{112,96},{128,112},... | collective-permute-start | bytes 786440 | tf_op jit(solution)/shard_map/ppermute | solution.py:320
  3.9 7.7 %collective-permute-start = (bf16[2,64,1024]{2,1,0:T(8,128)(2,1)S(1)}, bf16[2,64,1024]{2,1,0:T(8,128)(2,1)S(1)}, u32[]{:S(2)}, u32[]{:S(2)}) collective-permute-start(bf16[2,64,1024]{2,1,0:T(8,128)(2,1)S(1)} %pad_maximum_fusion.1), channel_id=1, source_target_pairs={{0,16},{16,32},{32,48},{48,64},{64,80},{80,96},{96,112},{112,128},... | collective-permute-start | bytes 786440 | tf_op jit(solution)/shard_map/ppermute | solution.py:320
  6.3 5.3 %copy-start = (bf16[1024,1024]{1,0:T(8,128)(2,1)S(1)}, bf16[1024,1024]{1,0:T(8,128)(2,1)}, u32[]{:S(2)}) copy-start(bf16[1024,1024]{1,0:T(8,128)(2,1)} %frames_hbm.3) | copy-start | bytes 6291460
  6.4 5.3 %copy-start.1 = (bf16[1024,1024]{1,0:T(8,128)(2,1)S(1)}, bf16[1024,1024]{1,0:T(8,128)(2,1)}, u32[]{:S(2)}) copy-start(bf16[1024,1024]{1,0:T(8,128)(2,1)} %cot_hbm.3) | copy-start | bytes 6291460
  6.4 5.3 %copy-start.6 = (s32[8]{0:T(128)S(1)}, s32[8]{0:T(128)}, u32[]{:S(2)}) copy-start(s32[8]{0:T(128)} %len_ref.1) | copy-start | bytes 100
  18.7 4.1 %collective-permute-start.6 = (bf16[2,4,4,64,128]{4,3,2,1,0:T(8,128)(2,1)S(1)}, bf16[2,4,4,64,128]{4,3,2,1,0:T(8,128)(2,1)S(1)}, u32[]{:S(2)}, u32[]{:S(2)}) collective-permute-start(bf16[2,4,4,64,128]{4,3,2,1,0:T(8,128)(2,1)S(1)} %get-tuple-element.36), channel_id=1, source_target_pairs={{0,16},{16,0},{32,48},{48,32},{64,80},{80,64},{96,112},{112,96},{1... | collective-permute-start | bytes 1572872 | tf_op jit(solution)/shard_map/ppermute | solution.py:304
  19.8 21.6 %collective-permute-start.2 = (bf16[4,512,128]{2,1,0:T(8,128)(2,1)S(1)}, bf16[4,512,128]{2,1,0:T(8,128)(2,1)S(1)}, u32[]{:S(2)}, u32[]{:S(2)}) collective-permute-start(bf16[4,512,128]{2,1,0:T(8,128)(2,1)S(1)} %get-tuple-element.31), channel_id=1, source_target_pairs={{0,2},{2,0},{4,6},{6,4},{8,10},{10,8},{12,14},{14,12},{1,3},{3,1},... | collective-permute-start | bytes 1572872 | tf_op jit(solution)/shard_map/ppermute | solution.py:304
  22.9 9.5 %collective-permute-start.7 = (bf16[4,4,64,128]{3,2,1,0:T(8,128)(2,1)S(1)}, bf16[4,4,64,128]{3,2,1,0:T(8,128)(2,1)S(1)}, u32[]{:S(2)}, u32[]{:S(2)}) collective-permute-start(bf16[4,4,64,128]{3,2,1,0:T(8,128)(2,1)S(1)} %fusion.2), channel_id=1, source_target_pairs={{0,32},{16,48},{32,0},{48,16},{64,96},{80,112},{96,64},{112,80},{1... | collective-permute-start | bytes 786440 | tf_op jit(solution)/shard_map/ppermute | solution.py:304
  26.1 14.4 %collective-permute-start.3 = (bf16[2,512,128]{2,1,0:T(8,128)(2,1)S(1)}, bf16[2,512,128]{2,1,0:T(8,128)(2,1)S(1)}, u32[]{:S(2)}, u32[]{:S(2)}) collective-permute-start(bf16[2,512,128]{2,1,0:T(8,128)(2,1)S(1)} %get-tuple-element.32), channel_id=1, source_target_pairs={{0,8},{2,10},{4,12},{6,14},{8,0},{10,2},{12,4},{14,6},{1,9},{3,11}... | collective-permute-start | bytes 786440 | tf_op jit(solution)/shard_map/ppermute | solution.py:304
  29.3 12.1 %collective-permute-start.4 = (bf16[2,512,128]{2,1,0:T(8,128)(2,1)S(1)}, bf16[2,512,128]{2,1,0:T(8,128)(2,1)S(1)}, u32[]{:S(2)}, u32[]{:S(2)}) collective-permute-start(bf16[2,512,128]{2,1,0:T(8,128)(2,1)S(1)} %get-tuple-element.33), channel_id=1, source_target_pairs={{0,4},{2,6},{4,0},{6,2},{8,12},{10,14},{12,8},{14,10},{1,5},{3,7},... | collective-permute-start | bytes 786440 | tf_op jit(solution)/shard_map/ppermute | solution.py:304
  30.0 11.4 %collective-permute-start.5 = (bf16[2,512,128]{2,1,0:T(8,128)(2,1)S(1)}, bf16[2,512,128]{2,1,0:T(8,128)(2,1)}, u32[]{:S(2)}, u32[]{:S(2)}) collective-permute-start(bf16[2,512,128]{2,1,0:T(8,128)(2,1)S(1)} %get-tuple-element.34), channel_id=1, source_target_pairs={{0,12},{2,14},{4,8},{6,10},{8,4},{10,6},{12,0},{14,2},{1,13},{3,15... | collective-permute-start | bytes 786440 | tf_op jit(solution)/shard_map/ppermute | solution.py:304
  33.2 15.9 %all-to-all-start = ((bf16[4,4,64,128]{3,2,1,0:T(8,128)(2,1)}), bf16[4,4,64,128]{3,2,1,0:T(8,128)(2,1)S(1)}, u32[]{:S(2)}, u32[]{:S(2)}) async-start(bf16[4,4,64,128]{3,2,1,0:T(8,128)(2,1)} %fusion), calls=%async_computation | async-start | bytes 524288 | tf_op jit(solution)/shard_map/all_to_all | solution.py:333
  41.5 11.8 %collective-permute-start.11 = (bf16[512,128]{1,0:T(8,128)(2,1)S(1)}, bf16[512,128]{1,0:T(8,128)(2,1)S(1)}, u32[]{:S(2)}, u32[]{:S(2)}) collective-permute-start(bf16[512,128]{1,0:T(8,128)(2,1)S(1)} %get-tuple-element.53), channel_id=1, source_target_pairs={{0,12},{2,14},{4,8},{6,10},{8,4},{10,6},{12,0},{14,2},{1,13},{3,15... | collective-permute-start | bytes 393224 | tf_op jit(solution)/shard_map/ppermute | solution.py:304
  44.3 9.0 %collective-permute-start.9 = (bf16[512,128]{1,0:T(8,128)(2,1)S(1)}, bf16[512,128]{1,0:T(8,128)(2,1)S(1)}, u32[]{:S(2)}, u32[]{:S(2)}) collective-permute-start(bf16[512,128]{1,0:T(8,128)(2,1)S(1)} %get-tuple-element.54), channel_id=1, source_target_pairs={{0,8},{2,10},{4,12},{6,14},{8,0},{10,2},{12,4},{14,6},{1,9},{3,11}... | collective-permute-start | bytes 393224 | tf_op jit(solution)/shard_map/ppermute | solution.py:304
  45.0 8.4 %collective-permute-start.10 = (bf16[512,128]{1,0:T(8,128)(2,1)S(1)}, bf16[512,128]{1,0:T(8,128)(2,1)S(1)}, u32[]{:S(2)}, u32[]{:S(2)}) collective-permute-start(bf16[512,128]{1,0:T(8,128)(2,1)S(1)} %get-tuple-element.55), channel_id=1, source_target_pairs={{0,4},{2,6},{4,0},{6,2},{8,12},{10,14},{12,8},{14,10},{1,5},{3,7},... | collective-permute-start | bytes 393224 | tf_op jit(solution)/shard_map/ppermute | solution.py:304
  46.8 6.6 %collective-permute-start.8 = (bf16[512,128]{1,0:T(8,128)(2,1)S(1)}, bf16[512,128]{1,0:T(8,128)(2,1)S(1)}, u32[]{:S(2)}, u32[]{:S(2)}) collective-permute-start(bf16[512,128]{1,0:T(8,128)(2,1)S(1)} %fusion.11), channel_id=1, source_target_pairs={{0,2},{2,0},{4,6},{6,4},{8,10},{10,8},{12,14},{14,12},{1,3},{3,1},... | collective-permute-start | bytes 393224 | tf_op jit(solution)/shard_map/ppermute | solution.py:304

commit v12 on v11

--- a/solution.py
+++ b/solution.py
@@ -46,8 +46,9 @@
 
 
 def project_body(
-    frames_hbm, gain_ref, qkv_hbm, out_hbm, cot_hbm, pad_ref, proj_ref, stats_ref, normed_hbm,
-    frames_ref, w_scr, out_ref, cot_ref, normed_ref, sems,
+    frames_hbm, gain_hbm, qkv_hbm, out_hbm, cot_hbm, pad_hbm,
+    proj_ref, stats_ref, first_ref, last_ref, normed_hbm,
+    frames_ref, w_scr, out_ref, cot_ref, normed_ref, gain_ref, pad_ref, sems,
 ):
     count = frames_ref.shape[0]
     rows = count // 2
@@ -56,8 +57,9 @@
     moves += [(qkv_hbm.at[m], w_scr.at[:, m * HS : (m + 1) * HS]) for m in range(3)]
     moves += [(out_hbm, out_ref), (cot_hbm, cot_ref)]
     moves += [(normed_ref.at[span], normed_hbm.at[span]) for span in halves]
+    moves += [(gain_hbm, gain_ref), (pad_hbm, pad_ref)]
     copies = [pltpu.make_async_copy(source, target, sems.at[i]) for i, (source, target) in enumerate(moves)]
-    for i in (0, 2, 3, 4, 1, 5, 6):
+    for i in (9, 0, 2, 3, 4, 1, 5, 10, 6):
         copies[i].start()
     lane = lax.broadcasted_iota(jnp.int32, (rows, 128), 1)
 
@@ -73,6 +75,7 @@
         for m in range(3):
             proj_ref[m, halves[half], :] = qkv[:, m * HS : (m + 1) * HS]
 
+    copies[9].wait()
     copies[0].wait()
     first = norm_rows(0)
     copies[7].start()
@@ -80,7 +83,7 @@
         copies[i].wait()
     project_rows(0, first)
     second = norm_rows(1)
-    for i in (5, 6):
+    for i in (5, 10, 6):
         copies[i].wait()
     copies[8].start()
     blocks = count // 128
@@ -89,6 +92,8 @@
     project_rows(1, second)
     grads = rows_by_rows(cot_ref[...], out_ref[...])
     proj_ref[3] = jnp.where(live == 1.0, grads, 0.0).astype(BF16)
+    first_ref[...] = proj_ref[:, :HALO, :]
+    last_ref[...] = proj_ref[:, count - HALO :, :]
     copies[7].wait()
     copies[8].wait()
 
@@ -99,11 +104,13 @@
     hbm = pl.BlockSpec(memory_space=pl.ANY)
     return pl.pallas_call(
         project_body,
-        in_specs=[hbm, vmem, hbm, hbm, hbm, vmem],
-        out_specs=[vmem, vmem, hbm],
+        in_specs=[hbm] * 6,
+        out_specs=[vmem, vmem, vmem, vmem, hbm],
         out_shape=[
             jax.ShapeDtypeStruct((4, count, HS), BF16),
             jax.ShapeDtypeStruct((count, 128), F32),
+            jax.ShapeDtypeStruct((4, HALO, HS), BF16),
+            jax.ShapeDtypeStruct((4, HALO, HS), BF16),
             jax.ShapeDtypeStruct((count, width), BF16),
         ],
         scratch_shapes=[
@@ -112,15 +119,17 @@
             pltpu.VMEM(out_weight.shape, BF16),
             pltpu.VMEM((count, width), BF16),
             pltpu.VMEM((count, width), BF16),
-            pltpu.SemaphoreType.DMA((9,)),
+            pltpu.VMEM(gain.shape, F32),
+            pltpu.VMEM(pad2d.shape, jnp.int32),
+            pltpu.SemaphoreType.DMA((11,)),
         ],
-        compiler_params=pltpu.CompilerParams(vmem_limit_bytes=48 << 20),
+        compiler_params=pltpu.CompilerParams(vmem_limit_bytes=54 << 20),
         name="project",
     )(frames, gain, qkv_weight, out_weight, cotangent, pad2d)
 
 
 def backward_body(
-    len_ref, proj_ref, stats_ref, halo_ref, gain_ref, qkv_ref, out_ref, pad_ref, frames_hbm, normed_hbm, cot_hbm,
+    len_ref, proj_ref, stats_ref, below_ref, above_ref, gain_ref, qkv_ref, pad_ref, frames_hbm, normed_hbm, cot_hbm,
     near_ref, across_ref, ring0_ref, ring1_ref, ring2_ref, ring3_ref, keep_ref, send_ref,
     x_scr, grads_ref, mixed_ref, w_scr, frames_ref, normed_ref, cot_ref, sems,
 ):
@@ -136,23 +145,15 @@
     tiles = count // 128 + 1
     shard = lax.axis_index("tm")
     first_block = shard * (count // 128) - 1
-    normal_form, _, _ = normalised(halo_ref[0])
-    normed = (normal_form * gain_ref[...]).astype(BF16)
     blocks = tiles + 1
     live_rows = [r.astype(F32) for r in pad_rows(pad_ref, first_block, blocks)]
     live_cols = as_columns(live_rows)
-    halo_live = jnp.concatenate([live_cols[HALO:, 0:1], live_cols[:HALO, blocks - 1 : blocks]], axis=0)
     zeros = jnp.zeros((HALO, HS), BF16)
     for m in range(4):
-        if m < 3:
-            part = plain(normed, qkv_ref[m])
-        else:
-            part = jnp.where(halo_live == 1.0, rows_by_rows(halo_ref[1], out_ref[...]), 0.0)
-        part = part.astype(BF16)
         x_scr[m, 0:HALO, :] = zeros
-        x_scr[m, HALO : 2 * HALO, :] = part[:HALO]
+        x_scr[m, HALO : 2 * HALO, :] = below_ref[m]
         x_scr[m, 2 * HALO : 2 * HALO + count, :] = proj_ref[m]
-        x_scr[m, 2 * HALO + count : 3 * HALO + count, :] = part[HALO:]
+        x_scr[m, 2 * HALO + count : 3 * HALO + count, :] = above_ref[m]
         x_scr[m, 3 * HALO + count :, :] = zeros
 
     ends = []
@@ -275,7 +276,7 @@
             send_ref[side, z // 2, m] = send[:, m * HS : (m + 1) * HS]
 
 
-def backward(lengths, proj, stats, halo, gain, qkv_weight, out_weight, pad2d, frames, normed, cotangent):
+def backward(lengths, proj, stats, below, above, gain, qkv_weight, pad2d, frames, normed, cotangent):
     count, width = frames.shape
     vmem = pl.BlockSpec(memory_space=pltpu.VMEM)
     half = count // 2
@@ -297,7 +298,7 @@
         ],
         compiler_params=pltpu.CompilerParams(vmem_limit_bytes=40 << 20),
         name="backward",
-    )(lengths, proj, stats, halo, gain, qkv_weight, out_weight, pad2d, frames, normed, cotangent)
+    )(lengths, proj, stats, below, above, gain, qkv_weight, pad2d, frames, normed, cotangent)
 
 
 def swapped(x, axis, bit):
@@ -315,14 +316,12 @@
     shards = lax.axis_size("tm")
     up = [(i, i + 1) for i in range(shards - 1)]
     down = [(i + 1, i) for i in range(shards - 1)]
-    ends = jnp.stack([frames[-HALO:], cotangent[-HALO:]])
-    starts = jnp.stack([frames[:HALO], cotangent[:HALO]])
-    halo = jnp.concatenate([lax.ppermute(ends, "tm", up), lax.ppermute(starts, "tm", down)], axis=1)
     gain = norm_gain[None, :]
     pad2d = pad_mask.reshape(-1, 128)
-    proj, stats, normed = project(frames, gain, qkv_weight, out_weight, cotangent, pad2d)
+    proj, stats, first, last, normed = project(frames, gain, qkv_weight, out_weight, cotangent, pad2d)
+    below, above = lax.ppermute(last, "tm", up), lax.ppermute(first, "tm", down)
     near, across, *ring, keep, send = backward(
-        utt_lengths, proj, stats, halo, gain, qkv_weight, out_weight, pad2d, frames, normed, cotangent
+        utt_lengths, proj, stats, below, above, gain, qkv_weight, pad2d, frames, normed, cotangent
     )
     other = swapped(send, "tm", 1)
     across = swapped(across, "mp", 1)

time: 54.5 us -> 63.1 us (1.16)
  waiting for transfers between devices: 6.5 us -> 10.3 us
  local copies, waits for them, and re-layouts: 1.27 us -> 3.89 us
  starting transfers between devices: 29.6 us -> 30.9 us
  Pallas kernels: 11.7 us -> 12.7 us
    unnamed x14 -> x18, local copies, waits for them, and re-layouts: 0.04 us -> 3.87 us
    ppermute x10, waiting for transfers between devices: 5.81 us -> 8.1 us  [swapped(): lax.ppermute(x, axis, [(i, i ^ bit) for i in range(lax.axis_size(axis))])]
    all_to_all x1, starting transfers between devices: 7.34 us -> 5.18 us  [on_device(): lax.all_to_all(pair, 'tm', 0, 0, tiled=True, axis_index_groups=groups)]
    ppermute x10, starting transfers between devices: 18 us -> 20.1 us  [swapped(): lax.ppermute(x, axis, [(i, i ^ bit) for i in range(lax.axis_size(axis))])]
    ppermute x2, waiting for transfers between devices: 0.55 us -> 2.2 us  [the longest x1 1.98 us: on_device(): lax.ppermute(first, 'tm', down)]
    pallas_call x1, Pallas kernels: 4.64 us -> 5.96 us  [project(): pl.pallas_call(project_body, in_specs=[hbm] * 6, out_specs=[vmem, vmem, v...]
    ppermute x2, starting transfers between devices: 4.33 us -> 5.56 us  [the longest x1 3.64 us: on_device(): lax.ppermute(first, 'tm', down)]
    another operation x1 -> x0, local copies, waits for them, and re-layouts: 1.22 us -> none  [on_device(): ends = jnp.stack([frames[-HALO:], cotangent[-HALO:]])]
  transfers between devices with their start and end apart: 13 -> 13, of which waited for: 5 -> 5; matrix products, arithmetic and copies ran while one was open for 6% -> 5% of each run, Pallas kernels for 9% -> 0%
where the time goes in v12:
time: 63.1 us; the launch traced here: 62.8 us
  starting transfers between devices  30.9 us (49%)
  Pallas kernels  12.7 us (20%)
  waiting for transfers between devices  10.3 us (16%)
  other arithmetic  4.19 us (7%)
  local copies, waits for them, and re-layouts  3.89 us (6%)
  between operations  0.79 us (1%)
    ppermute x10, starting transfers between devices, swapped(): lax.ppermute(x, axis, [(i, i ^ bit) for i in range(lax.axis_size(axis))])  20.1 us
    ppermute x10, waiting for transfers between devices, swapped(): lax.ppermute(x, axis, [(i, i ^ bit) for i in range(lax.axis_size(axis))])  8.1 us
    pallas_call x1, Pallas kernels, backward(): pl.pallas_call(backward_body, in_specs=[pl.BlockSpec(memory_space=pltpu.S...  6.77 us
    pallas_call x1, Pallas kernels, project(): pl.pallas_call(project_body, in_specs=[hbm] * 6, out_specs=[vmem, vmem, v...  5.96 us
    all_to_all x1, starting transfers between devices, on_device(): lax.all_to_all(pair, 'tm', 0, 0, tiled=True, axis_index_groups=groups)  5.18 us
    unnamed x18, local copies, waits for them, and re-layouts  3.87 us
    ppermute x1, starting transfers between devices, on_device(): lax.ppermute(first, 'tm', down)  3.64 us
    ppermute x1, waiting for transfers between devices, on_device(): lax.ppermute(first, 'tm', down)  1.98 us
  transfers between devices with their start and end apart: 13, of which 5 were waited for; matrix products, arithmetic and copies ran while one was open for 5% of the time, Pallas kernels for 0%

profile of v12, /device:TPU:64, one launch (start us, length us, event | category | flops | bytes accessed | tf_op | source)
XLA Modules:
  0.0 62.8 jit_solution(12883396433013112381)
XLA Ops:
  0.6 0.0 copy-start
  0.6 0.0 copy-start.1
  0.7 0.0 copy-start.2
  0.7 0.0 copy-start.6
  0.7 0.0 copy-start.7
  0.7 0.0 copy-start.8
  0.7 6.0 %project.1 = (bf16[4,1024,128]{2,1,0:T(8,128)(2,1)}, f32[1024,128]{1,0:T(8,128)}, bf16[4,64,128]{2,1,0:T(8,128)(2,1)}, bf16[4,64,128]{2,1,0:T(8,128)(2,1)}, bf16[1024,1024]{1,0:T(8,128)(2,1)}) custom-call(bf16[1024,1024]{1,0:T(8,128)(2,1)} %frames_hbm.3, f32[1,1024]{1,0:T(1,128)} %bitcast.34, bf16[3,1024,128]{2,1,0:T(8,128)(2,1)} %qkv_ref.1, ...), custom_call_target="tpu_custom_call" | custom-call | tf_op jit(solution)/shard_map/project/pallas_call | solution.py:105
  6.7 1.9 %collective-permute-start = (bf16[4,64,128]{2,1,0:T(8,128)(2,1)}, bf16[4,64,128]{2,1,0:T(8,128)(2,1)S(1)}, u32[]{:S(2)}, u32[]{:S(2)}) collective-permute-start(bf16[4,64,128]{2,1,0:T(8,128)(2,1)} %get-tuple-element.30), channel_id=1, source_target_pairs={{0,16},{16,32},{32,48},{48,64},{64,80},{80,96},{96,112},{112,128},... | collective-permute-start | bytes 196616 | tf_op jit(solution)/shard_map/ppermute | solution.py:322
  8.6 3.6 %collective-permute-start.1 = (bf16[4,64,128]{2,1,0:T(8,128)(2,1)}, bf16[4,64,128]{2,1,0:T(8,128)(2,1)S(1)}, u32[]{:S(2)}, u32[]{:S(2)}) collective-permute-start(bf16[4,64,128]{2,1,0:T(8,128)(2,1)} %get-tuple-element.31), channel_id=1, source_target_pairs={{16,0},{32,16},{48,32},{64,48},{80,64},{96,80},{112,96},{128,112},... | collective-permute-start | bytes 196616 | tf_op jit(solution)/shard_map/ppermute | solution.py:322
  12.2 0.2 collective-permute-done.below_ref
  12.5 2.0 %collective-permute-done.1.above_ref = bf16[4,64,128]{2,1,0:T(8,128)(2,1)S(1)} collective-permute-done((bf16[4,64,128]{2,1,0:T(8,128)(2,1)}, bf16[4,64,128]{2,1,0:T(8,128)(2,1)S(1)}, u32[]{:S(2)}, u32[]{:S(2)}) %collective-permute-start.1) | collective-permute-done | bytes 65568 | tf_op jit(solution)/shard_map/ppermute | solution.py:322
  14.4 0.0 copy-done
  14.4 0.0 copy-done.1
  14.4 0.0 copy-done.2
  14.4 0.0 copy-done.6
  14.4 0.0 copy-done.7
  14.5 0.0 copy-done.8
  14.5 0.0 copy-start.3
  14.5 1.6 %copy-done.3 = bf16[1024,1024]{1,0:T(8,128)(2,1)S(1)} copy-done((bf16[1024,1024]{1,0:T(8,128)(2,1)S(1)}, bf16[1024,1024]{1,0:T(8,128)(2,1)}, u32[]{:S(2)}) %copy-start.3) | copy-done | bytes 2097176
  16.1 0.0 copy-start.4
  16.1 1.2 %copy-done.4 = bf16[4,1024,128]{2,1,0:T(8,128)(2,1)S(1)} copy-done((bf16[4,1024,128]{2,1,0:T(8,128)(2,1)S(1)}, bf16[4,1024,128]{2,1,0:T(8,128)(2,1)}, u32[]{:S(2)}) %copy-start.4) | copy-done | bytes 1048600
  17.3 0.0 copy-start.5
  17.3 1.0 %copy-done.5 = f32[1024,128]{1,0:T(8,128)S(1)} copy-done((f32[1024,128]{1,0:T(8,128)S(1)}, f32[1024,128]{1,0:T(8,128)}, u32[]{:S(2)}) %copy-start.5) | copy-done | bytes 524312
  18.3 6.8 %backward.1 = (bf16[4,512,128]{2,1,0:T(8,128)(2,1)S(1)}, bf16[4,512,128]{2,1,0:T(8,128)(2,1)S(1)}, bf16[2,512,128]{2,1,0:T(8,128)(2,1)S(1)}, bf16[2,512,128]{2,1...) custom-call(s32[8]{0:T(128)S(1)} %copy-done.8, ...), custom_call_target="tpu_custom_call" | custom-call | tf_op jit(solution)/shard_map/backward/pallas_call | solution.py:284
  25.1 2.0 %collective-permute-start.6 = (bf16[2,4,4,64,128]{4,3,2,1,0:T(8,128)(2,1)S(1)}, bf16[2,4,4,64,128]{4,3,2,1,0:T(8,128)(2,1)S(1)}, u32[]{:S(2)}, u32[]{:S(2)}) collective-permute-start(bf16[2,4,4,64,128]{4,3,2,1,0:T(8,128)(2,1)S(1)} %get-tuple-element.40), channel_id=1, source_target_pairs={{0,16},{16,0},{32,48},{48,32},{64,80},{80,64},{96,112},{112,96},{1... | collective-permute-start | bytes 1572872 | tf_op jit(solution)/shard_map/ppermute | solution.py:305
  27.2 3.0 %collective-permute-start.2 = (bf16[4,512,128]{2,1,0:T(8,128)(2,1)S(1)}, bf16[4,512,128]{2,1,0:T(8,128)(2,1)S(1)}, u32[]{:S(2)}, u32[]{:S(2)}) collective-permute-start(bf16[4,512,128]{2,1,0:T(8,128)(2,1)S(1)} %get-tuple-element.35), channel_id=1, source_target_pairs={{0,2},{2,0},{4,6},{6,4},{8,10},{10,8},{12,14},{14,12},{1,3},{3,1},... | collective-permute-start | bytes 1572872 | tf_op jit(solution)/shard_map/ppermute | solution.py:305
  30.2 0.0 collective-permute-done.6
  30.2 0.1 fusion.2
  30.3 4.4 %collective-permute-start.7 = (bf16[4,4,64,128]{3,2,1,0:T(8,128)(2,1)S(1)}, bf16[4,4,64,128]{3,2,1,0:T(8,128)(2,1)S(1)}, u32[]{:S(2)}, u32[]{:S(2)}) collective-permute-start(bf16[4,4,64,128]{3,2,1,0:T(8,128)(2,1)S(1)} %fusion.2), channel_id=1, source_target_pairs={{0,32},{16,48},{32,0},{48,16},{64,96},{80,112},{96,64},{112,80},{1... | collective-permute-start | bytes 786440 | tf_op jit(solution)/shard_map/ppermute | solution.py:305
  34.7 3.2 %collective-permute-start.3 = (bf16[2,512,128]{2,1,0:T(8,128)(2,1)S(1)}, bf16[2,512,128]{2,1,0:T(8,128)(2,1)S(1)}, u32[]{:S(2)}, u32[]{:S(2)}) collective-permute-start(bf16[2,512,128]{2,1,0:T(8,128)(2,1)S(1)} %get-tuple-element.36), channel_id=1, source_target_pairs={{0,8},{2,10},{4,12},{6,14},{8,0},{10,2},{12,4},{14,6},{1,9},{3,11}... | collective-permute-start | bytes 786440 | tf_op jit(solution)/shard_map/ppermute | solution.py:305
  37.9 0.7 %collective-permute-start.4 = (bf16[2,512,128]{2,1,0:T(8,128)(2,1)S(1)}, bf16[2,512,128]{2,1,0:T(8,128)(2,1)S(1)}, u32[]{:S(2)}, u32[]{:S(2)}) collective-permute-start(bf16[2,512,128]{2,1,0:T(8,128)(2,1)S(1)} %get-tuple-element.37), channel_id=1, source_target_pairs={{0,4},{2,6},{4,0},{6,2},{8,12},{10,14},{12,8},{14,10},{1,5},{3,7},... | collective-permute-start | bytes 786440 | tf_op jit(solution)/shard_map/ppermute | solution.py:305
  38.6 0.4 collective-permute-start.5
  38.9 2.0 %collective-permute-done.7 = bf16[4,4,64,128]{3,2,1,0:T(8,128)(2,1)S(1)} collective-permute-done((bf16[4,4,64,128]{3,2,1,0:T(8,128)(2,1)S(1)}, bf16[4,4,64,128]{3,2,1,0:T(8,128)(2,1)S(1)}, u32[]{:S(2)}, u32[]{:S(2)}) %collective-permute-start.7) | collective-permute-done | bytes 262176 | tf_op jit(solution)/shard_map/ppermute | solution.py:305
  41.0 0.8 %fusion = bf16[4,4,64,128]{3,2,1,0:T(8,128)(2,1)} fusion(bf16[4,4,64,128]{3,2,1,0:T(8,128)(2,1)S(1)} %collective-permute-done.7, bf16[2,4,4,64,128]{4,3,2,1,0:T(8,128)(2,1)S(1)} %collective-permute-done.6, bf16[2,4,4,64,128]{4,3,2,1,0:T(8,128)(2,1)S(1)} %get-tuple-element.39), kind=kLoop, calls=%fused_computation.1 | loop fusion | flops 1048576 | bytes 1048576 | tf_op jit(solution)/shard_map/convert_element_type | solution.py:330
  41.8 5.2 %all-to-all-start = ((bf16[4,4,64,128]{3,2,1,0:T(8,128)(2,1)}), bf16[4,4,64,128]{3,2,1,0:T(8,128)(2,1)S(1)}, u32[]{:S(2)}, u32[]{:S(2)}) async-start(bf16[4,4,64,128]{3,2,1,0:T(8,128)(2,1)} %fusion), calls=%async_computation | async-start | bytes 524288 | tf_op jit(solution)/shard_map/all_to_all | solution.py:332
  47.0 0.0 collective-permute-done.3
  47.0 3.0 %collective-permute-done.4 = bf16[2,512,128]{2,1,0:T(8,128)(2,1)S(1)} collective-permute-done((bf16[2,512,128]{2,1,0:T(8,128)(2,1)S(1)}, bf16[2,512,128]{2,1,0:T(8,128)(2,1)S(1)}, u32[]{:S(2)}, u32[]{:S(2)}) %collective-permute-start.4) | collective-permute-done | bytes 262176 | tf_op jit(solution)/shard_map/ppermute | solution.py:305
  49.9 0.0 collective-permute-done.5
  49.9 0.0 collective-permute-done.2
  50.0 0.1 fusion.10
  50.1 2.8 %collective-permute-start.11 = (bf16[512,128]{1,0:T(8,128)(2,1)S(1)}, bf16[512,128]{1,0:T(8,128)(2,1)S(1)}, u32[]{:S(2)}, u32[]{:S(2)}) collective-permute-start(bf16[512,128]{1,0:T(8,128)(2,1)S(1)} %get-tuple-element.53), channel_id=1, source_target_pairs={{0,12},{2,14},{4,8},{6,10},{8,4},{10,6},{12,0},{14,2},{1,13},{3,15... | collective-permute-start | bytes 393224 | tf_op jit(solution)/shard_map/ppermute | solution.py:305
  52.9 0.7 %collective-permute-start.9 = (bf16[512,128]{1,0:T(8,128)(2,1)S(1)}, bf16[512,128]{1,0:T(8,128)(2,1)S(1)}, u32[]{:S(2)}, u32[]{:S(2)}) collective-permute-start(bf16[512,128]{1,0:T(8,128)(2,1)S(1)} %get-tuple-element.54), channel_id=1, source_target_pairs={{0,8},{2,10},{4,12},{6,14},{8,0},{10,2},{12,4},{14,6},{1,9},{3,11}... | collective-permute-start | bytes 393224 | tf_op jit(solution)/shard_map/ppermute | solution.py:305
  53.6 0.7 %collective-permute-start.10 = (bf16[512,128]{1,0:T(8,128)(2,1)S(1)}, bf16[512,128]{1,0:T(8,128)(2,1)S(1)}, u32[]{:S(2)}, u32[]{:S(2)}) collective-permute-start(bf16[512,128]{1,0:T(8,128)(2,1)S(1)} %get-tuple-element.55), channel_id=1, source_target_pairs={{0,4},{2,6},{4,0},{6,2},{8,12},{10,14},{12,8},{14,10},{1,5},{3,7},... | collective-permute-start | bytes 393224 | tf_op jit(solution)/shard_map/ppermute | solution.py:305
  54.2 1.1 %convert_add_fusion.1 = f32[2,512,128]{2,1,0:T(8,128)S(1)} fusion(bf16[2,512,128]{2,1,0:T(8,128)(2,1)} %collective-permute-done.5, bf16[2,512,128]{2,1,0:T(8,128)(2,1)S(1)} %collective-permute-done.4, bf16[2,512,128]{2,1,0:T(8,128)(2,1)S(1)} %collective-permute-done.3, bf16[2,512,128]{2,1,0:T(8,128)(2,1)S(1)} %get-tuple-element.33), kind=kLoop, calls=%fused_computation.2 | loop fusion | flops 917504 | bytes 1572864 | tf_op jit(solution)/shard_map/add | solution.py:311
  55.3 2.2 %collective-permute-start.8 = (bf16[512,128]{1,0:T(8,128)(2,1)S(1)}, bf16[512,128]{1,0:T(8,128)(2,1)S(1)}, u32[]{:S(2)}, u32[]{:S(2)}) collective-permute-start(bf16[512,128]{1,0:T(8,128)(2,1)S(1)} %fusion.11), channel_id=1, source_target_pairs={{0,2},{2,0},{4,6},{6,4},{8,10},{10,8},{12,14},{14,12},{1,3},{3,1},... | collective-permute-start | bytes 393224 | tf_op jit(solution)/shard_map/ppermute | solution.py:305
  57.5 0.0 all-to-all-done
  57.5 0.6 convert_reduce_fusion.1
  58.1 0.7 %convert_reduce_fusion = f32[3,64,128]{2,1,0:T(8,128)} fusion(bf16[4,4,64,128]{3,2,1,0:T(8,128)(2,1)S(1)} %all-to-all-done), kind=kLoop, calls=%fused_computation.5 | loop fusion | flops 172032 | bytes 294912 | tf_op jit(solution)/shard_map/reduce_sum | solution.py:339
  58.8 3.1 %collective-permute-done.8 = bf16[512,128]{1,0:T(8,128)(2,1)S(1)} collective-permute-done((bf16[512,128]{1,0:T(8,128)(2,1)S(1)}, bf16[512,128]{1,0:T(8,128)(2,1)S(1)}, u32[]{:S(2)}, u32[]{:S(2)}) %collective-permute-start.8) | collective-permute-done | bytes 131104 | tf_op jit(solution)/shard_map/ppermute | solution.py:305
  61.9 0.0 collective-permute-done.11
  61.9 0.0 collective-permute-done.9
  61.9 0.0 collective-permute-done.10
  61.9 0.1 fusion.4
  62.0 0.7 %pad_maximum_fusion = bf16[1024,128]{1,0:T(8,128)(2,1)} fusion(bf16[512,128]{1,0:T(8,128)(2,1)S(1)} %get-tuple-element.57, bf16[512,128]{1,0:T(8,128)(2,1)S(1)} %get-tuple-element.56), kind=kLoop, calls=%fused_computation.12 | loop fusion | flops 524288 | bytes 524288 | tf_op jit(solution)/shard_map/concatenate | solution.py:344
  (1 shorter events, 0.0 us)
Async XLA Ops:
  0.6 13.8 %copy-start = (bf16[1024,1024]{1,0:T(8,128)(2,1)S(1)}, bf16[1024,1024]{1,0:T(8,128)(2,1)}, u32[]{:S(2)}) copy-start(bf16[1024,1024]{1,0:T(8,128)(2,1)} %frames_hbm.3) | copy-start | bytes 6291460
  0.6 13.8 %copy-start.1 = (bf16[1024,1024]{1,0:T(8,128)(2,1)S(1)}, bf16[1024,1024]{1,0:T(8,128)(2,1)}, u32[]{:S(2)}) copy-start(bf16[1024,1024]{1,0:T(8,128)(2,1)} %cot_hbm.3) | copy-start | bytes 6291460
  0.7 13.8 %copy-start.2 = (bf16[3,1024,128]{2,1,0:T(8,128)(2,1)S(1)}, bf16[3,1024,128]{2,1,0:T(8,128)(2,1)}, u32[]{:S(2)}) copy-start(bf16[3,1024,128]{2,1,0:T(8,128)(2,1)} %qkv_ref.1) | copy-start | bytes 2359300
  0.7 13.8 %copy-start.6 = (s32[16384]{0:T(1024)S(1)}, s32[16384]{0:T(1024)}, u32[]{:S(2)}) copy-start(s32[16384]{0:T(1024)} %param.12) | copy-start | bytes 196612
  0.7 13.8 %copy-start.7 = (f32[1024]{0:T(1024)S(1)}, f32[1024]{0:T(1024)}, u32[]{:S(2)}) copy-start(f32[1024]{0:T(1024)} %param.8) | copy-start | bytes 12292
  0.7 13.8 %copy-start.8 = (s32[8]{0:T(128)S(1)}, s32[8]{0:T(128)}, u32[]{:S(2)}) copy-start(s32[8]{0:T(128)} %len_ref.1) | copy-start | bytes 100
  6.7 5.8 %collective-permute-start = (bf16[4,64,128]{2,1,0:T(8,128)(2,1)}, bf16[4,64,128]{2,1,0:T(8,128)(2,1)S(1)}, u32[]{:S(2)}, u32[]{:S(2)}) collective-permute-start(bf16[4,64,128]{2,1,0:T(8,128)(2,1)} %get-tuple-element.30), channel_id=1, source_target_pairs={{0,16},{16,32},{32,48},{48,64},{64,80},{80,96},{96,112},{112,128},... | collective-permute-start | bytes 196616 | tf_op jit(solution)/shard_map/ppermute | solution.py:322
  8.6 5.8 %collective-permute-start.1 = (bf16[4,64,128]{2,1,0:T(8,128)(2,1)}, bf16[4,64,128]{2,1,0:T(8,128)(2,1)S(1)}, u32[]{:S(2)}, u32[]{:S(2)}) collective-permute-start(bf16[4,64,128]{2,1,0:T(8,128)(2,1)} %get-tuple-element.31), channel_id=1, source_target_pairs={{16,0},{32,16},{48,32},{64,48},{80,64},{96,80},{112,96},{128,112},... | collective-permute-start | bytes 196616 | tf_op jit(solution)/shard_map/ppermute | solution.py:322
  14.5 1.6 %copy-start.3 = (bf16[1024,1024]{1,0:T(8,128)(2,1)S(1)}, bf16[1024,1024]{1,0:T(8,128)(2,1)}, u32[]{:S(2)}) copy-start(bf16[1024,1024]{1,0:T(8,128)(2,1)} %get-tuple-element.32.normed_hbm) | copy-start | bytes 6291460
  16.1 1.2 %copy-start.4 = (bf16[4,1024,128]{2,1,0:T(8,128)(2,1)S(1)}, bf16[4,1024,128]{2,1,0:T(8,128)(2,1)}, u32[]{:S(2)}) copy-start(bf16[4,1024,128]{2,1,0:T(8,128)(2,1)} %get-tuple-element.28.proj_ref) | copy-start | bytes 3145732
  17.3 1.0 %copy-start.5 = (f32[1024,128]{1,0:T(8,128)S(1)}, f32[1024,128]{1,0:T(8,128)}, u32[]{:S(2)}) copy-start(f32[1024,128]{1,0:T(8,128)} %get-tuple-element.29.stats_ref) | copy-start | bytes 1572868
  25.1 5.1 %collective-permute-start.6 = (bf16[2,4,4,64,128]{4,3,2,1,0:T(8,128)(2,1)S(1)}, bf16[2,4,4,64,128]{4,3,2,1,0:T(8,128)(2,1)S(1)}, u32[]{:S(2)}, u32[]{:S(2)}) collective-permute-start(bf16[2,4,4,64,128]{4,3,2,1,0:T(8,128)(2,1)S(1)} %get-tuple-element.40), channel_id=1, source_target_pairs={{0,16},{16,0},{32,48},{48,32},{64,80},{80,64},{96,112},{112,96},{1... | collective-permute-start | bytes 1572872 | tf_op jit(solution)/shard_map/ppermute | solution.py:305
  27.2 22.8 %collective-permute-start.2 = (bf16[4,512,128]{2,1,0:T(8,128)(2,1)S(1)}, bf16[4,512,128]{2,1,0:T(8,128)(2,1)S(1)}, u32[]{:S(2)}, u32[]{:S(2)}) collective-permute-start(bf16[4,512,128]{2,1,0:T(8,128)(2,1)S(1)} %get-tuple-element.35), channel_id=1, source_target_pairs={{0,2},{2,0},{4,6},{6,4},{8,10},{10,8},{12,14},{14,12},{1,3},{3,1},... | collective-permute-start | bytes 1572872 | tf_op jit(solution)/shard_map/ppermute | solution.py:305
  30.3 10.7 %collective-permute-start.7 = (bf16[4,4,64,128]{3,2,1,0:T(8,128)(2,1)S(1)}, bf16[4,4,64,128]{3,2,1,0:T(8,128)(2,1)S(1)}, u32[]{:S(2)}, u32[]{:S(2)}) collective-permute-start(bf16[4,4,64,128]{3,2,1,0:T(8,128)(2,1)S(1)} %fusion.2), channel_id=1, source_target_pairs={{0,32},{16,48},{32,0},{48,16},{64,96},{80,112},{96,64},{112,80},{1... | collective-permute-start | bytes 786440 | tf_op jit(solution)/shard_map/ppermute | solution.py:305
  34.7 12.3 %collective-permute-start.3 = (bf16[2,512,128]{2,1,0:T(8,128)(2,1)S(1)}, bf16[2,512,128]{2,1,0:T(8,128)(2,1)S(1)}, u32[]{:S(2)}, u32[]{:S(2)}) collective-permute-start(bf16[2,512,128]{2,1,0:T(8,128)(2,1)S(1)} %get-tuple-element.36), channel_id=1, source_target_pairs={{0,8},{2,10},{4,12},{6,14},{8,0},{10,2},{12,4},{14,6},{1,9},{3,11}... | collective-permute-start | bytes 786440 | tf_op jit(solution)/shard_map/ppermute | solution.py:305
  37.9 12.1 %collective-permute-start.4 = (bf16[2,512,128]{2,1,0:T(8,128)(2,1)S(1)}, bf16[2,512,128]{2,1,0:T(8,128)(2,1)S(1)}, u32[]{:S(2)}, u32[]{:S(2)}) collective-permute-start(bf16[2,512,128]{2,1,0:T(8,128)(2,1)S(1)} %get-tuple-element.37), channel_id=1, source_target_pairs={{0,4},{2,6},{4,0},{6,2},{8,12},{10,14},{12,8},{14,10},{1,5},{3,7},... | collective-permute-start | bytes 786440 | tf_op jit(solution)/shard_map/ppermute | solution.py:305
  38.6 11.4 %collective-permute-start.5 = (bf16[2,512,128]{2,1,0:T(8,128)(2,1)S(1)}, bf16[2,512,128]{2,1,0:T(8,128)(2,1)}, u32[]{:S(2)}, u32[]{:S(2)}) collective-permute-start(bf16[2,512,128]{2,1,0:T(8,128)(2,1)S(1)} %get-tuple-element.38), channel_id=1, source_target_pairs={{0,12},{2,14},{4,8},{6,10},{8,4},{10,6},{12,0},{14,2},{1,13},{3,15... | collective-permute-start | bytes 786440 | tf_op jit(solution)/shard_map/ppermute | solution.py:305
  41.8 15.7 %all-to-all-start = ((bf16[4,4,64,128]{3,2,1,0:T(8,128)(2,1)}), bf16[4,4,64,128]{3,2,1,0:T(8,128)(2,1)S(1)}, u32[]{:S(2)}, u32[]{:S(2)}) async-start(bf16[4,4,64,128]{3,2,1,0:T(8,128)(2,1)} %fusion), calls=%async_computation | async-start | bytes 524288 | tf_op jit(solution)/shard_map/all_to_all | solution.py:332
  50.1 11.8 %collective-permute-start.11 = (bf16[512,128]{1,0:T(8,128)(2,1)S(1)}, bf16[512,128]{1,0:T(8,128)(2,1)S(1)}, u32[]{:S(2)}, u32[]{:S(2)}) collective-permute-start(bf16[512,128]{1,0:T(8,128)(2,1)S(1)} %get-tuple-element.53), channel_id=1, source_target_pairs={{0,12},{2,14},{4,8},{6,10},{8,4},{10,6},{12,0},{14,2},{1,13},{3,15... | collective-permute-start | bytes 393224 | tf_op jit(solution)/shard_map/ppermute | solution.py:305
  52.9 9.0 %collective-permute-start.9 = (bf16[512,128]{1,0:T(8,128)(2,1)S(1)}, bf16[512,128]{1,0:T(8,128)(2,1)S(1)}, u32[]{:S(2)}, u32[]{:S(2)}) collective-permute-start(bf16[512,128]{1,0:T(8,128)(2,1)S(1)} %get-tuple-element.54), channel_id=1, source_target_pairs={{0,8},{2,10},{4,12},{6,14},{8,0},{10,2},{12,4},{14,6},{1,9},{3,11}... | collective-permute-start | bytes 393224 | tf_op jit(solution)/shard_map/ppermute | solution.py:305
  53.6 8.3 %collective-permute-start.10 = (bf16[512,128]{1,0:T(8,128)(2,1)S(1)}, bf16[512,128]{1,0:T(8,128)(2,1)S(1)}, u32[]{:S(2)}, u32[]{:S(2)}) collective-permute-start(bf16[512,128]{1,0:T(8,128)(2,1)S(1)} %get-tuple-element.55), channel_id=1, source_target_pairs={{0,4},{2,6},{4,0},{6,2},{8,12},{10,14},{12,8},{14,10},{1,5},{3,7},... | collective-permute-start | bytes 393224 | tf_op jit(solution)/shard_map/ppermute | solution.py:305
  55.3 6.6 %collective-permute-start.8 = (bf16[512,128]{1,0:T(8,128)(2,1)S(1)}, bf16[512,128]{1,0:T(8,128)(2,1)S(1)}, u32[]{:S(2)}, u32[]{:S(2)}) collective-permute-start(bf16[512,128]{1,0:T(8,128)(2,1)S(1)} %fusion.11), channel_id=1, source_target_pairs={{0,2},{2,0},{4,6},{6,4},{8,10},{10,8},{12,14},{14,12},{1,3},{3,1},... | collective-permute-start | bytes 393224 | tf_op jit(solution)/shard_map/ppermute | solution.py:305

commit v13 on v10

--- a/solution.py
+++ b/solution.py
@@ -278,7 +278,7 @@
 def backward(lengths, proj, stats, halo, gain, qkv_weight, out_weight, pad2d, frames, normed, cotangent):
     count, width = frames.shape
     vmem = pl.BlockSpec(memory_space=pltpu.VMEM)
-    split = count * 3 // 8
+    split = count * 7 // 16
     shapes = [(4, count - split, 128)] * 2 + [(2, split, 128)] * 4 + [(2, 4, 4, width // 16, HS)] * 2
     return pl.pallas_call(
         backward_body,
@@ -335,12 +335,12 @@
     col = [total(near[k], across[k]) for k in range(4)]
     col_in = [swapped(col[k].astype(BF16), "mp", 2 * k) for k in (2, 1, 3)]
     ring_in, _ = lax.optimization_barrier((ring_in, [c.astype(BF16) for c in col[1:]]))
-    theirs = swapped(total(ring[0][1], *[r[1] for r in ring_in]).astype(BF16), "mp", 1)
-    first_half = total(total(ring[0][0], *[r[0] for r in ring_in]), theirs).astype(BF16)
-    weights, _ = lax.optimization_barrier((weights, first_half))
+    both = lax.optimization_barrier(total(ring[0], *ring_in))
+    theirs = swapped(both[1].astype(BF16), "mp", 1)
     qkv_grad = weights[:, :3].astype(F32).sum(axis=0)
     out_grad = weights[:, 3].astype(F32).sum(axis=0)
-    col_in, _ = lax.optimization_barrier((col_in, (qkv_grad, out_grad)))
+    (theirs, col_in), _ = lax.optimization_barrier(((theirs, col_in), (qkv_grad, out_grad)))
+    first_half = total(both[0], theirs).astype(BF16)
     second_half = total(col[0], *col_in).astype(BF16)
     frame_grad = jnp.concatenate([first_half, second_half], axis=0)
     return frame_grad, qkv_grad, out_grad.T

time: 55.8 us -> 53.9 us (0.966)
  the two profiles are of different devices: /device:TPU:96 before, /device:TPU:16 now
where the time goes in v13:
time: 53.9 us; the launch traced here: 53.6 us
  starting transfers between devices  30 us (56%)
  Pallas kernels  11.7 us (22%)
  waiting for transfers between devices  5.43 us (10%)
  other arithmetic  4.28 us (8%)
  local copies, waits for them, and re-layouts  1.27 us (2%)
  between operations  0.89 us (2%)
    ppermute x10, starting transfers between devices, swapped(): lax.ppermute(x, axis, [(i, i ^ bit) for i in range(lax.axis_size(axis))])  16.8 us
    all_to_all x1, starting transfers between devices, on_device(): lax.all_to_all(pair, 'tm', 0, 0, tiled=True, axis_index_groups=groups)  8.92 us
    pallas_call x1, Pallas kernels, backward(): pl.pallas_call(backward_body, in_specs=[pl.BlockSpec(memory_space=pltpu.S...  7.06 us
    pallas_call x1, Pallas kernels, project(): pl.pallas_call(project_body, in_specs=[hbm, vmem, hbm, hbm, hbm, vmem], o...  4.64 us
    ppermute x1, starting transfers between devices, on_device(): lax.ppermute(ends, 'tm', up)  3.05 us
    ppermute x10, waiting for transfers between devices, swapped(): lax.ppermute(x, axis, [(i, i ^ bit) for i in range(lax.axis_size(axis))])  2.75 us
    all_to_all x1, waiting for transfers between devices, on_device(): lax.all_to_all(pair, 'tm', 0, 0, tiled=True, axis_index_groups=groups)  2.67 us
    ppermute x1, starting transfers between devices, on_device(): lax.ppermute(starts, 'tm', down)  1.29 us
  transfers between devices with their start and end apart: 13, of which 3 were waited for; matrix products, arithmetic and copies ran while one was open for 6% of the time, Pallas kernels for 9%

profile of v13, /device:TPU:16, one launch (start us, length us, event | category | flops | bytes accessed | tf_op | source)
XLA Modules:
  0.0 53.6 jit_solution(16945400518016531341)
XLA Ops:
  0.6 0.0 copy-start.3
  0.6 0.0 copy-start.2
  0.7 0.0 copy-start.4
  0.7 0.0 copy-start.5
  0.7 1.2 %slice_bitcast_fusion.3 = (bf16[1,64,1024]{2,1,0:T(8,128)(2,1)S(1)}, bf16[1,64,1024]{2,1,0:T(8,128)(2,1)S(1)}, bf16[1,64,1024]{2,1,0:T(8,128)(2,1)S(1)}, bf16[1,64,1024]{2,1,0:T(8,128)(2,1)S(1)}) fusion(bf16[1024,1024]{1,0:T(8,128)(2,1)} %cot_hbm.3, bf16[1024,1024]{1,0:T(8,128)(2,1)} %frames_hbm.3), kind=kLoop, calls=%fused_computation.29 | loop fusion | bytes 1048576 | tf_op jit(solution)/shard_map/stack | solution.py:318
  1.9 1.3 %collective-permute-start.1 = (bf16[2,64,1024]{2,1,0:T(8,128)(2,1)S(1)}, bf16[2,64,1024]{2,1,0:T(8,128)(2,1)S(1)}, u32[]{:S(2)}, u32[]{:S(2)}) collective-permute-start(bf16[2,64,1024]{2,1,0:T(8,128)(2,1)S(1)} %pad_maximum_fusion.2), channel_id=1, source_target_pairs={{16,0},{32,16},{48,32},{64,48},{80,64},{96,80},{112,96},{128,112},... | collective-permute-start | bytes 786440 | tf_op jit(solution)/shard_map/ppermute | solution.py:320
  3.3 3.0 %collective-permute-start = (bf16[2,64,1024]{2,1,0:T(8,128)(2,1)S(1)}, bf16[2,64,1024]{2,1,0:T(8,128)(2,1)S(1)}, u32[]{:S(2)}, u32[]{:S(2)}) collective-permute-start(bf16[2,64,1024]{2,1,0:T(8,128)(2,1)S(1)} %pad_maximum_fusion.1), channel_id=1, source_target_pairs={{0,16},{16,32},{32,48},{48,64},{64,80},{80,96},{96,112},{112,128},... | collective-permute-start | bytes 786440 | tf_op jit(solution)/shard_map/ppermute | solution.py:320
  6.3 0.0 copy-done.3
  6.3 0.0 copy-done.2
  6.3 0.0 copy-done.4
  6.3 0.0 copy-done.5
  6.4 0.0 copy-start
  6.4 0.0 copy-start.1
  6.4 0.0 copy-start.6
  6.4 4.6 %project.1 = (bf16[4,1024,128]{2,1,0:T(8,128)(2,1)S(1)}, f32[1024,128]{1,0:T(8,128)S(1)}, bf16[1024,1024]{1,0:T(8,128)(2,1)S(1)}) custom-call(bf16[1024,1024]{1,0:T(8,128)(2,1)} %frames_hbm.3, f32[1,1024]{1,0:T(1,128)S(1)} %bitcast.42, bf16[3,1024,128]{2,1,0:T(8,128)(2,1)S(1)} %copy-done.2, bf16[128,1024]{1,0:T(8,128)(2,1)S(1)} %copy-done.3, ...), custom_call_target="tpu_custom_call" | custom-call | tf_op jit(solution)/shard_map/project/pallas_call | solution.py:100
  11.0 0.0 collective-permute-done.1
  11.0 0.0 collective-permute-done
  11.1 0.0 copy-done
  11.1 0.0 copy-done.1
  11.1 0.0 copy-done.6
  11.1 7.1 %backward.1 = (bf16[4,576,128]{2,1,0:T(8,128)(2,1)S(1)}, bf16[4,576,128]{2,1,0:T(8,128)(2,1)S(1)}, bf16[2,448,128]{2,1,0:T(8,128)(2,1)S(1)}, bf16[2,448,128]{2,1...) custom-call(s32[8]{0:T(128)S(1)} %copy-done.6, ...), custom_call_target="tpu_custom_call" | custom-call | tf_op jit(solution)/shard_map/backward/pallas_call | solution.py:283
  18.2 1.6 %collective-permute-start.6 = (bf16[2,4,4,64,128]{4,3,2,1,0:T(8,128)(2,1)S(1)}, bf16[2,4,4,64,128]{4,3,2,1,0:T(8,128)(2,1)S(1)}, u32[]{:S(2)}, u32[]{:S(2)}) collective-permute-start(bf16[2,4,4,64,128]{4,3,2,1,0:T(8,128)(2,1)S(1)} %get-tuple-element.36), channel_id=1, source_target_pairs={{0,16},{16,0},{32,48},{48,32},{64,80},{80,64},{96,112},{112,96},{1... | collective-permute-start | bytes 1572872 | tf_op jit(solution)/shard_map/ppermute | solution.py:304
  19.8 3.0 %collective-permute-start.2 = (bf16[4,576,128]{2,1,0:T(8,128)(2,1)S(1)}, bf16[4,576,128]{2,1,0:T(8,128)(2,1)S(1)}, u32[]{:S(2)}, u32[]{:S(2)}) collective-permute-start(bf16[4,576,128]{2,1,0:T(8,128)(2,1)S(1)} %get-tuple-element.31), channel_id=1, source_target_pairs={{0,2},{2,0},{4,6},{6,4},{8,10},{10,8},{12,14},{14,12},{1,3},{3,1},... | collective-permute-start | bytes 1769480 | tf_op jit(solution)/shard_map/ppermute | solution.py:304
  22.8 0.0 collective-permute-done.6
  22.8 0.1 fusion.5
  22.9 2.0 %collective-permute-start.7 = (bf16[4,4,64,128]{3,2,1,0:T(8,128)(2,1)S(1)}, bf16[4,4,64,128]{3,2,1,0:T(8,128)(2,1)S(1)}, u32[]{:S(2)}, u32[]{:S(2)}) collective-permute-start(bf16[4,4,64,128]{3,2,1,0:T(8,128)(2,1)S(1)} %fusion.5), channel_id=1, source_target_pairs={{0,32},{16,48},{32,0},{48,16},{64,96},{80,112},{96,64},{112,80},{1... | collective-permute-start | bytes 786440 | tf_op jit(solution)/shard_map/ppermute | solution.py:304
  24.9 0.3 collective-permute-start.3
  25.3 2.2 %collective-permute-start.4 = (bf16[2,448,128]{2,1,0:T(8,128)(2,1)S(1)}, bf16[2,448,128]{2,1,0:T(8,128)(2,1)S(1)}, u32[]{:S(2)}, u32[]{:S(2)}) collective-permute-start(bf16[2,448,128]{2,1,0:T(8,128)(2,1)S(1)} %get-tuple-element.33), channel_id=1, source_target_pairs={{0,4},{2,6},{4,0},{6,2},{8,12},{10,14},{12,8},{14,10},{1,5},{3,7},... | collective-permute-start | bytes 688136 | tf_op jit(solution)/shard_map/ppermute | solution.py:304
  27.4 1.6 %collective-permute-start.5 = (bf16[2,448,128]{2,1,0:T(8,128)(2,1)S(1)}, bf16[2,448,128]{2,1,0:T(8,128)(2,1)}, u32[]{:S(2)}, u32[]{:S(2)}) collective-permute-start(bf16[2,448,128]{2,1,0:T(8,128)(2,1)S(1)} %get-tuple-element.34), channel_id=1, source_target_pairs={{0,12},{2,14},{4,8},{6,10},{8,4},{10,6},{12,0},{14,2},{1,13},{3,15... | collective-permute-start | bytes 688136 | tf_op jit(solution)/shard_map/ppermute | solution.py:304
  29.0 2.2 %collective-permute-done.7 = bf16[4,4,64,128]{3,2,1,0:T(8,128)(2,1)S(1)} collective-permute-done((bf16[4,4,64,128]{3,2,1,0:T(8,128)(2,1)S(1)}, bf16[4,4,64,128]{3,2,1,0:T(8,128)(2,1)S(1)}, u32[]{:S(2)}, u32[]{:S(2)}) %collective-permute-start.7) | collective-permute-done | bytes 262176 | tf_op jit(solution)/shard_map/ppermute | solution.py:304
  31.2 0.8 %fusion = bf16[4,4,64,128]{3,2,1,0:T(8,128)(2,1)} fusion(bf16[4,4,64,128]{3,2,1,0:T(8,128)(2,1)S(1)} %collective-permute-done.7, bf16[2,4,4,64,128]{4,3,2,1,0:T(8,128)(2,1)S(1)} %collective-permute-done.6, bf16[2,4,4,64,128]{4,3,2,1,0:T(8,128)(2,1)S(1)} %get-tuple-element.35), kind=kLoop, calls=%fused_computation.2 | loop fusion | flops 1048576 | bytes 1048576 | tf_op jit(solution)/shard_map/convert_element_type | solution.py:331
  32.0 8.9 %all-to-all-start = ((bf16[4,4,64,128]{3,2,1,0:T(8,128)(2,1)}), bf16[4,4,64,128]{3,2,1,0:T(8,128)(2,1)S(1)}, u32[]{:S(2)}, u32[]{:S(2)}) async-start(bf16[4,4,64,128]{3,2,1,0:T(8,128)(2,1)} %fusion), calls=%async_computation | async-start | bytes 524288 | tf_op jit(solution)/shard_map/all_to_all | solution.py:333
  40.9 0.0 collective-permute-done.3
  40.9 0.0 collective-permute-done.4
  41.0 0.0 collective-permute-done.5
  41.0 0.0 collective-permute-done.2
  41.0 0.1 fusion.10
  41.1 0.5 collective-permute-start.11
  41.6 2.9 %collective-permute-start.9 = (bf16[576,128]{1,0:T(8,128)(2,1)S(1)}, bf16[576,128]{1,0:T(8,128)(2,1)S(1)}, u32[]{:S(2)}, u32[]{:S(2)}) collective-permute-start(bf16[576,128]{1,0:T(8,128)(2,1)S(1)} %get-tuple-element.54), channel_id=1, source_target_pairs={{0,8},{2,10},{4,12},{6,14},{8,0},{10,2},{12,4},{14,6},{1,9},{3,11}... | collective-permute-start | bytes 442376 | tf_op jit(solution)/shard_map/ppermute | solution.py:304
  44.5 0.8 %collective-permute-start.10 = (bf16[576,128]{1,0:T(8,128)(2,1)S(1)}, bf16[576,128]{1,0:T(8,128)(2,1)S(1)}, u32[]{:S(2)}, u32[]{:S(2)}) collective-permute-start(bf16[576,128]{1,0:T(8,128)(2,1)S(1)} %get-tuple-element.55), channel_id=1, source_target_pairs={{0,4},{2,6},{4,0},{6,2},{8,12},{10,14},{12,8},{14,10},{1,5},{3,7},... | collective-permute-start | bytes 442376 | tf_op jit(solution)/shard_map/ppermute | solution.py:304
  45.3 1.0 %convert_add_fusion.1 = f32[2,448,128]{2,1,0:T(8,128)S(1)} fusion(bf16[2,448,128]{2,1,0:T(8,128)(2,1)} %collective-permute-done.5, bf16[2,448,128]{2,1,0:T(8,128)(2,1)S(1)} %collective-permute-done.4, bf16[2,448,128]{2,1,0:T(8,128)(2,1)S(1)} %collective-permute-done.3, bf16[2,448,128]{2,1,0:T(8,128)(2,1)S(1)} %get-tuple-element.29), kind=kLoop, calls=%fused_computation.5 | loop fusion | flops 802816 | bytes 1376256 | tf_op jit(solution)/shard_map/add | solution.py:310
  46.3 1.9 %collective-permute-start.8 = (bf16[448,128]{1,0:T(8,128)(2,1)S(1)}, bf16[448,128]{1,0:T(8,128)(2,1)S(1)}, u32[]{:S(2)}, u32[]{:S(2)}) collective-permute-start(bf16[448,128]{1,0:T(8,128)(2,1)S(1)} %fusion.11), channel_id=1, source_target_pairs={{0,2},{2,0},{4,6},{6,4},{8,10},{10,8},{12,14},{14,12},{1,3},{3,1},... | collective-permute-start | bytes 344072 | tf_op jit(solution)/shard_map/ppermute | solution.py:304
  48.2 2.7 %all-to-all-done = bf16[4,4,64,128]{3,2,1,0:T(8,128)(2,1)S(1)} async-done(((bf16[4,4,64,128]{3,2,1,0:T(8,128)(2,1)}), bf16[4,4,64,128]{3,2,1,0:T(8,128)(2,1)S(1)}, u32[]{:S(2)}, u32[]{:S(2)}) %all-to-all-start) | async-done | bytes 262176 | tf_op jit(solution)/shard_map/all_to_all | solution.py:333
  50.9 0.7 %convert_reduce_fusion = f32[3,64,128]{2,1,0:T(8,128)} fusion(bf16[4,4,64,128]{3,2,1,0:T(8,128)(2,1)S(1)} %all-to-all-done), kind=kLoop, calls=%fused_computation.6 | loop fusion | flops 172032 | bytes 294912 | tf_op jit(solution)/shard_map/reduce_sum | solution.py:340
  51.6 0.6 %convert_reduce_fusion.1 = f32[64,128]{1,0:T(8,128)} fusion(bf16[4,4,64,128]{3,2,1,0:T(8,128)(2,1)S(1)} %all-to-all-done), kind=kLoop, calls=%fused_computation.26 | loop fusion | flops 57344 | bytes 98304 | tf_op jit(solution)/shard_map/reduce_sum | solution.py:341
  52.2 0.5 %collective-permute-done.8 = bf16[448,128]{1,0:T(8,128)(2,1)S(1)} collective-permute-done((bf16[448,128]{1,0:T(8,128)(2,1)S(1)}, bf16[448,128]{1,0:T(8,128)(2,1)S(1)}, u32[]{:S(2)}, u32[]{:S(2)}) %collective-permute-start.8) | collective-permute-done | bytes 114720 | tf_op jit(solution)/shard_map/ppermute | solution.py:304
  52.7 0.0 collective-permute-done.11
  52.7 0.0 collective-permute-done.9
  52.7 0.0 collective-permute-done.10
  52.8 0.1 fusion.3
  52.9 0.7 %pad_maximum_fusion.3 = bf16[1024,128]{1,0:T(8,128)(2,1)} fusion(bf16[576,128]{1,0:T(8,128)(2,1)S(1)} %fusion.3, bf16[448,128]{1,0:T(8,128)(2,1)S(1)} %fusion.7), kind=kLoop, calls=%fused_computation.18 | loop fusion | flops 524288 | bytes 524288 | tf_op jit(solution)/shard_map/concatenate | solution.py:345
  (5 shorter events, 0.1 us)
Async XLA Ops:
  0.6 5.7 %copy-start.3 = (bf16[128,1024]{1,0:T(8,128)(2,1)S(1)}, bf16[128,1024]{1,0:T(8,128)(2,1)}, u32[]{:S(2)}) copy-start(bf16[128,1024]{1,0:T(8,128)(2,1)} %out_ref.1) | copy-start | bytes 786436
  0.6 5.7 %copy-start.2 = (bf16[3,1024,128]{2,1,0:T(8,128)(2,1)S(1)}, bf16[3,1024,128]{2,1,0:T(8,128)(2,1)}, u32[]{:S(2)}) copy-start(bf16[3,1024,128]{2,1,0:T(8,128)(2,1)} %qkv_ref.1) | copy-start | bytes 2359300
  0.7 5.7 %copy-start.4 = (s32[16384]{0:T(1024)S(1)}, s32[16384]{0:T(1024)}, u32[]{:S(2)}) copy-start(s32[16384]{0:T(1024)} %param.12) | copy-start | bytes 196612
  0.7 5.7 %copy-start.5 = (f32[1024]{0:T(1024)S(1)}, f32[1024]{0:T(1024)}, u32[]{:S(2)}) copy-start(f32[1024]{0:T(1024)} %param.8) | copy-start | bytes 12292
  1.9 9.1 %collective-permute-start.1 = (bf16[2,64,1024]{2,1,0:T(8,128)(2,1)S(1)}, bf16[2,64,1024]{2,1,0:T(8,128)(2,1)S(1)}, u32[]{:S(2)}, u32[]{:S(2)}) collective-permute-start(bf16[2,64,1024]{2,1,0:T(8,128)(2,1)S(1)} %pad_maximum_fusion.2), channel_id=1, source_target_pairs={{16,0},{32,16},{48,32},{64,48},{80,64},{96,80},{112,96},{128,112},... | collective-permute-start | bytes 786440 | tf_op jit(solution)/shard_map/ppermute | solution.py:320
  3.3 7.8 %collective-permute-start = (bf16[2,64,1024]{2,1,0:T(8,128)(2,1)S(1)}, bf16[2,64,1024]{2,1,0:T(8,128)(2,1)S(1)}, u32[]{:S(2)}, u32[]{:S(2)}) collective-permute-start(bf16[2,64,1024]{2,1,0:T(8,128)(2,1)S(1)} %pad_maximum_fusion.1), channel_id=1, source_target_pairs={{0,16},{16,32},{32,48},{48,64},{64,80},{80,96},{96,112},{112,128},... | collective-permute-start | bytes 786440 | tf_op jit(solution)/shard_map/ppermute | solution.py:320
  6.4 4.7 %copy-start = (bf16[1024,1024]{1,0:T(8,128)(2,1)S(1)}, bf16[1024,1024]{1,0:T(8,128)(2,1)}, u32[]{:S(2)}) copy-start(bf16[1024,1024]{1,0:T(8,128)(2,1)} %frames_hbm.3) | copy-start | bytes 6291460
  6.4 4.7 %copy-start.1 = (bf16[1024,1024]{1,0:T(8,128)(2,1)S(1)}, bf16[1024,1024]{1,0:T(8,128)(2,1)}, u32[]{:S(2)}) copy-start(bf16[1024,1024]{1,0:T(8,128)(2,1)} %cot_hbm.3) | copy-start | bytes 6291460
  6.4 4.7 %copy-start.6 = (s32[8]{0:T(128)S(1)}, s32[8]{0:T(128)}, u32[]{:S(2)}) copy-start(s32[8]{0:T(128)} %len_ref.1) | copy-start | bytes 100
  18.2 4.6 %collective-permute-start.6 = (bf16[2,4,4,64,128]{4,3,2,1,0:T(8,128)(2,1)S(1)}, bf16[2,4,4,64,128]{4,3,2,1,0:T(8,128)(2,1)S(1)}, u32[]{:S(2)}, u32[]{:S(2)}) collective-permute-start(bf16[2,4,4,64,128]{4,3,2,1,0:T(8,128)(2,1)S(1)} %get-tuple-element.36), channel_id=1, source_target_pairs={{0,16},{16,0},{32,48},{48,32},{64,80},{80,64},{96,112},{112,96},{1... | collective-permute-start | bytes 1572872 | tf_op jit(solution)/shard_map/ppermute | solution.py:304
  19.8 21.2 %collective-permute-start.2 = (bf16[4,576,128]{2,1,0:T(8,128)(2,1)S(1)}, bf16[4,576,128]{2,1,0:T(8,128)(2,1)S(1)}, u32[]{:S(2)}, u32[]{:S(2)}) collective-permute-start(bf16[4,576,128]{2,1,0:T(8,128)(2,1)S(1)} %get-tuple-element.31), channel_id=1, source_target_pairs={{0,2},{2,0},{4,6},{6,4},{8,10},{10,8},{12,14},{14,12},{1,3},{3,1},... | collective-permute-start | bytes 1769480 | tf_op jit(solution)/shard_map/ppermute | solution.py:304
  22.9 8.3 %collective-permute-start.7 = (bf16[4,4,64,128]{3,2,1,0:T(8,128)(2,1)S(1)}, bf16[4,4,64,128]{3,2,1,0:T(8,128)(2,1)S(1)}, u32[]{:S(2)}, u32[]{:S(2)}) collective-permute-start(bf16[4,4,64,128]{3,2,1,0:T(8,128)(2,1)S(1)} %fusion.5), channel_id=1, source_target_pairs={{0,32},{16,48},{32,0},{48,16},{64,96},{80,112},{96,64},{112,80},{1... | collective-permute-start | bytes 786440 | tf_op jit(solution)/shard_map/ppermute | solution.py:304
  24.9 16.0 %collective-permute-start.3 = (bf16[2,448,128]{2,1,0:T(8,128)(2,1)S(1)}, bf16[2,448,128]{2,1,0:T(8,128)(2,1)S(1)}, u32[]{:S(2)}, u32[]{:S(2)}) collective-permute-start(bf16[2,448,128]{2,1,0:T(8,128)(2,1)S(1)} %get-tuple-element.32), channel_id=1, source_target_pairs={{0,8},{2,10},{4,12},{6,14},{8,0},{10,2},{12,4},{14,6},{1,9},{3,11}... | collective-permute-start | bytes 688136 | tf_op jit(solution)/shard_map/ppermute | solution.py:304
  25.3 15.7 %collective-permute-start.4 = (bf16[2,448,128]{2,1,0:T(8,128)(2,1)S(1)}, bf16[2,448,128]{2,1,0:T(8,128)(2,1)S(1)}, u32[]{:S(2)}, u32[]{:S(2)}) collective-permute-start(bf16[2,448,128]{2,1,0:T(8,128)(2,1)S(1)} %get-tuple-element.33), channel_id=1, source_target_pairs={{0,4},{2,6},{4,0},{6,2},{8,12},{10,14},{12,8},{14,10},{1,5},{3,7},... | collective-permute-start | bytes 688136 | tf_op jit(solution)/shard_map/ppermute | solution.py:304
  27.4 13.5 %collective-permute-start.5 = (bf16[2,448,128]{2,1,0:T(8,128)(2,1)S(1)}, bf16[2,448,128]{2,1,0:T(8,128)(2,1)}, u32[]{:S(2)}, u32[]{:S(2)}) collective-permute-start(bf16[2,448,128]{2,1,0:T(8,128)(2,1)S(1)} %get-tuple-element.34), channel_id=1, source_target_pairs={{0,12},{2,14},{4,8},{6,10},{8,4},{10,6},{12,0},{14,2},{1,13},{3,15... | collective-permute-start | bytes 688136 | tf_op jit(solution)/shard_map/ppermute | solution.py:304
  32.0 18.9 %all-to-all-start = ((bf16[4,4,64,128]{3,2,1,0:T(8,128)(2,1)}), bf16[4,4,64,128]{3,2,1,0:T(8,128)(2,1)S(1)}, u32[]{:S(2)}, u32[]{:S(2)}) async-start(bf16[4,4,64,128]{3,2,1,0:T(8,128)(2,1)} %fusion), calls=%async_computation | async-start | bytes 524288 | tf_op jit(solution)/shard_map/all_to_all | solution.py:333
  41.1 11.6 %collective-permute-start.11 = (bf16[576,128]{1,0:T(8,128)(2,1)S(1)}, bf16[576,128]{1,0:T(8,128)(2,1)S(1)}, u32[]{:S(2)}, u32[]{:S(2)}) collective-permute-start(bf16[576,128]{1,0:T(8,128)(2,1)S(1)} %get-tuple-element.53), channel_id=1, source_target_pairs={{0,12},{2,14},{4,8},{6,10},{8,4},{10,6},{12,0},{14,2},{1,13},{3,15... | collective-permute-start | bytes 442376 | tf_op jit(solution)/shard_map/ppermute | solution.py:304
  41.6 11.1 %collective-permute-start.9 = (bf16[576,128]{1,0:T(8,128)(2,1)S(1)}, bf16[576,128]{1,0:T(8,128)(2,1)S(1)}, u32[]{:S(2)}, u32[]{:S(2)}) collective-permute-start(bf16[576,128]{1,0:T(8,128)(2,1)S(1)} %get-tuple-element.54), channel_id=1, source_target_pairs={{0,8},{2,10},{4,12},{6,14},{8,0},{10,2},{12,4},{14,6},{1,9},{3,11}... | collective-permute-start | bytes 442376 | tf_op jit(solution)/shard_map/ppermute | solution.py:304
  44.5 8.2 %collective-permute-start.10 = (bf16[576,128]{1,0:T(8,128)(2,1)S(1)}, bf16[576,128]{1,0:T(8,128)(2,1)S(1)}, u32[]{:S(2)}, u32[]{:S(2)}) collective-permute-start(bf16[576,128]{1,0:T(8,128)(2,1)S(1)} %get-tuple-element.55), channel_id=1, source_target_pairs={{0,4},{2,6},{4,0},{6,2},{8,12},{10,14},{12,8},{14,10},{1,5},{3,7},... | collective-permute-start | bytes 442376 | tf_op jit(solution)/shard_map/ppermute | solution.py:304
  46.3 6.4 %collective-permute-start.8 = (bf16[448,128]{1,0:T(8,128)(2,1)S(1)}, bf16[448,128]{1,0:T(8,128)(2,1)S(1)}, u32[]{:S(2)}, u32[]{:S(2)}) collective-permute-start(bf16[448,128]{1,0:T(8,128)(2,1)S(1)} %fusion.11), channel_id=1, source_target_pairs={{0,2},{2,0},{4,6},{6,4},{8,10},{10,8},{12,14},{14,12},{1,3},{3,1},... | collective-permute-start | bytes 344072 | tf_op jit(solution)/shard_map/ppermute | solution.py:304
